TPU v7x, 128 devices: a whole 4x4x4 slice. The times are simulated.
128 devices in a mesh: member: 8 (over y, core), tile: 16 (over z, x).
Axes of the slice: x: 4, y: 4, z: 4, core: 2. Of those that a mesh axis runs over, the one named last changes fastest.
Arguments:
- perturb: bfloat16 [128, 256, 2560], P('member', 'tile'), may hold values from -0.5 to 0.5
- weights: float32 [128, 64, 1280], P('member', 'tile'), may hold values from -1.2 to 1.2
- column_map: bfloat16 [1280, 2560], replicated, may hold values from -0.15625 to 0.15625
- background: float32 [256, 2560], P('tile', 'member'), may hold values from -6 to 6
- stencil_index: int32 [16, 128, 8, 8], P('tile'), may hold values from 0 to 4798, as said below
- row_fraction: float32 [16, 128, 8, 8], P('tile'), may hold values from 0 to 1
- column_fraction: float32 [16, 128, 8, 8], P('tile'), may hold values from 0 to 1
- block_lengths: int32 [16, 128, 8], P('tile'), may hold values from 0 to 8, as said below
- obs_value: float32 [128, 128, 8], P(('member', 'tile')), may hold values from -6 to 6
- obs_error: float32 [128, 128, 8], P(('member', 'tile')), may hold values from 0.3 to 1
- instrument_gain: float32 [128], P(('member', 'tile')), may hold values from 0.2 to 0.8
Outputs:
- analysis_weights: float32 [128, 64, 1280], P('member', 'tile')
- analysis_increment: float32 [256, 2560], P('tile', 'member')
Inputs may be any that keep to these rules, and one draw needn't show every extreme that they name: stencil_index = r * 320 + c with 0 <= r < 15 and 0 <= c < 319. `block_lengths`: in every draw some owner (one tile and one member index) has all its blocks full.
All inputs are finite; a program needn't handle non-finite values.
Results may differ from a plain program's by a relative error of at most 0.0022.
Values may be sent and summed in bfloat16 or wider, within the bound.
No kernel may reach another device: no remote copies, remote signals or barrier semaphores. Data moves between devices by JAX's collectives and lax.ppermute only.
A program may use at most 64 MiB of HBM per device.

v0:
```python
import jax
import jax.numpy as jnp
from jax import lax
from jax.sharding import PartitionSpec as P

RATIO = 4
KSM = 3


DIFFUSION = 0.45


def padded_2(block, sides, width):
    for axis, dim in sides:
        count = lax.axis_size(axis)
        forward = [(i, i + 1) for i in range(count - 1)]
        backward = [(target, source) for source, target in forward]
        low = lax.ppermute(
            lax.slice_in_dim(block, block.shape[dim] - width, None, axis=dim), axis, forward
        )
        high = lax.ppermute(lax.slice_in_dim(block, 0, width, axis=dim), axis, backward)
        block = jnp.concatenate([low, block, high], axis=dim)
    return block


def rows_halo(grid_values, width_rows):
    return padded_2(grid_values, (("tile", 1),), width_rows)


def smoothed(grid_values, extra_rows):
    for pass_index in range(KSM):
        padded = rows_halo(grid_values, 1)
        grid_values = grid_values + DIFFUSION * (padded[:, :-2] + padded[:, 2:] - 2.0 * grid_values)
    if extra_rows > 0:
        rounded_rows = grid_values.astype(jnp.bfloat16)
        grid_values = padded_2(rounded_rows, (("tile", 1),), extra_rows)
    return grid_values


def refine(extended):
    members_here, row_count, col_count = extended.shape
    lower_rows = extended[:, :-2]
    middle = extended[:, 1:-1]
    upper_rows = extended[:, 2:]
    pieces = []
    for offset in range(RATIO):
        shift_value = (offset + 0.5) / RATIO - 0.5
        if shift_value < 0:
            pieces.append((1.0 + shift_value) * middle - shift_value * lower_rows)
        else:
            pieces.append((1.0 - shift_value) * middle + shift_value * upper_rows)
    return jnp.stack(pieces, axis=2).reshape(members_here, (row_count - 2) * RATIO, col_count)


def refine_adjoint(fine_field):
    members_here, fine_count, col_count = fine_field.shape
    row_count = fine_count // RATIO
    blocks = fine_field.reshape(members_here, row_count, RATIO, col_count)
    middle = jnp.zeros_like(blocks[:, :, 0])
    lower_rows = jnp.zeros_like(middle)
    upper_rows = jnp.zeros_like(middle)
    for offset in range(RATIO):
        shift_value = (offset + 0.5) / RATIO - 0.5
        fine_layer = blocks[:, :, offset]
        if shift_value < 0:
            middle = middle + (1.0 + shift_value) * fine_layer
            lower_rows = lower_rows - shift_value * fine_layer
        else:
            middle = middle + (1.0 - shift_value) * fine_layer
            upper_rows = upper_rows + shift_value * fine_layer
    return (
        jnp.pad(middle, ((0, 0), (1, 1), (0, 0)))
        + jnp.pad(lower_rows, ((0, 0), (0, 2), (0, 0)))
        + jnp.pad(upper_rows, ((0, 0), (2, 0), (0, 0)))
    )


def forward(coarse, perturb, column_map):
    extended = smoothed(coarse, 1)
    members_here, row_count, coarse_cols = extended.shape
    mapped = jnp.dot(
        extended.reshape(-1, coarse_cols), column_map, preferred_element_type=jnp.float32
    )
    fine_field = refine(mapped.reshape(members_here, row_count, -1))
    member_term = jnp.sum(fine_field * perturb, axis=0)
    return lax.psum_scatter(member_term, "member", scatter_dimension=1, tiled=True)


def adjoint_map(spread_field, perturb, column_map):
    edge_terms = refine_adjoint(perturb * spread_field)
    rim_rows = jnp.stack([edge_terms[:, 0], edge_terms[:, -1]], axis=1)
    beside_all = rows_halo(rim_rows, 1)
    inner_rows = edge_terms[:, 1:-1]
    inner_rows = inner_rows.at[:, 0].add(beside_all[:, 0]).at[:, -1].add(beside_all[:, 3])
    members_here, row_count, fine_cols = inner_rows.shape
    pulled = lax.dot_general(
        inner_rows.astype(jnp.bfloat16).reshape(-1, fine_cols),
        column_map,
        (((1,), (1,)), ((), ())),
        preferred_element_type=jnp.float32,
    )
    return smoothed(pulled.reshape(members_here, row_count, -1), 0)


def bilinear_factors(index, row_frac, column_frac, region_width, row_count):
    row_pos = (index // region_width)[..., None]
    column_pos = (index % region_width)[..., None]
    row_ids = lax.broadcasted_iota(jnp.int32, index.shape + (row_count,), index.ndim)
    column_ids = lax.broadcasted_iota(jnp.int32, index.shape + (region_width,), index.ndim)
    row_factor = jnp.where(row_ids == row_pos, 1.0 - row_frac[..., None], 0.0) + jnp.where(
        row_ids == row_pos + 1, row_frac[..., None], 0.0
    )
    column_factor = jnp.where(
        column_ids == column_pos, 1.0 - column_frac[..., None], 0.0
    ) + jnp.where(column_ids == column_pos + 1, column_frac[..., None], 0.0)
    return (row_factor, column_factor)


def interpolate_region(field_region, index, row_frac, column_frac):
    row_count, region_width = field_region.shape
    row_factor, column_factor = bilinear_factors(
        index, row_frac, column_frac, region_width, row_count
    )
    along = jnp.einsum("bsr,rc->bsc", row_factor, field_region, precision=lax.Precision.HIGHEST)
    return jnp.sum(along * column_factor, axis=-1)


def spread_tile(residual, index, row_frac, column_frac, region_width, row_count):
    row_factor, column_factor = bilinear_factors(
        index, row_frac, column_frac, region_width, row_count
    )
    weighted = row_factor * residual[..., None]
    regions = jnp.einsum("bmsr,bmsc->rmc", weighted, column_factor, precision=lax.Precision.HIGHEST)
    return regions.reshape(row_count, -1)


def innovation(obs_state, obs_value, obs_error, instrument):
    bounded = jnp.tanh(obs_state)
    derivative = 1.0 + instrument * (1.0 - bounded * bounded)
    misfit = obs_state + instrument * bounded - obs_value
    precision_obs = 1.0 / (obs_error * obs_error)
    return (derivative * misfit * precision_obs, derivative * derivative * precision_obs)


def global_sum(values):
    return lax.psum(values, ("member", "tile"))


def shards(
    perturb,
    weights,
    column_map,
    background,
    stencil_index,
    row_fraction,
    column_fraction,
    block_lengths,
    obs_value,
    obs_error,
    instrument_gain,
):
    member_pos = lax.axis_index("member")
    member_count = lax.axis_size("member")
    tile_count = lax.axis_size("tile")
    fine_rows, region_width = background.shape
    local_index = stencil_index[0]
    local_row = row_fraction[0]
    local_col = column_fraction[0]
    slot_ids = lax.broadcasted_iota(jnp.int32, local_index.shape, 2)
    valid_slots = (slot_ids < block_lengths[0][:, :, None]).astype(jnp.float32)
    own_index = lax.dynamic_index_in_dim(local_index, member_pos, 1, False)
    own_row = lax.dynamic_index_in_dim(local_row, member_pos, 1, False)
    own_col = lax.dynamic_index_in_dim(local_col, member_pos, 1, False)
    own_valid = lax.dynamic_index_in_dim(valid_slots, member_pos, 1, False)

    def fan_out(values):
        arranged = jnp.transpose(values.reshape(member_count, tile_count, -1), (1, 0, 2))
        widened = jnp.broadcast_to(arranged[None], (member_count,) + arranged.shape)
        return widened.reshape(member_count * tile_count, member_count, -1)

    coarse = weights
    increment = forward(coarse, perturb, column_map)
    obs_state = interpolate_region(background + increment, own_index, own_row, own_col)
    received = lax.all_to_all(
        obs_state, ("member", "tile"), split_axis=0, concat_axis=0, tiled=True
    )
    residual, obs_weight = innovation(received, obs_value[0], obs_error[0], instrument_gain[0])
    residual, obs_weight = (
        lax.all_to_all(
            fan_out(residual), ("member", "tile"), split_axis=0, concat_axis=0, tiled=True
        ),
        lax.all_to_all(
            fan_out(obs_weight), ("member", "tile"), split_axis=0, concat_axis=0, tiled=True
        ),
    )
    spread_field = spread_tile(
        residual * valid_slots, local_index, local_row, local_col, region_width, fine_rows
    )
    gradient = coarse + adjoint_map(spread_field, perturb, column_map)
    grad_square = jnp.sum(gradient * gradient)
    grad_total = global_sum(grad_square)
    grad_image = forward(gradient, perturb, column_map)
    grad_obs = interpolate_region(grad_image, own_index, own_row, own_col)
    own_weight = lax.dynamic_index_in_dim(obs_weight, member_pos, 1, False)
    curvature = jnp.sum(own_valid * own_weight * grad_obs * grad_obs)
    curve_total = global_sum(curvature)
    step_size = grad_total / (grad_total + curve_total)
    coarse = coarse - step_size * gradient
    increment = increment - step_size * grad_image
    return (coarse, increment)


def solution(mesh):
    placed = (
        P("member", "tile", None),
        P("member", "tile", None),
        P(),
        P("tile", "member"),
        P("tile", None, None, None),
        P("tile", None, None, None),
        P("tile", None, None, None),
        P("tile", None, None),
        P(("member", "tile"), None, None),
        P(("member", "tile"), None, None),
        P(("member", "tile")),
    )
    return jax.shard_map(
        shards,
        mesh=mesh,
        in_specs=placed,
        out_specs=(P("member", "tile", None), P("tile", "member")),
        check_vma=False,
    )
```

profile of v0, /device:TPU:1, one launch (start us, length us, event | category | flops | bytes accessed | tf_op | source)
XLA Modules:
  0.0 360.1 jit_solution(11399913175671601973)
XLA Ops:
  8.3 3.9 %collective-permute-start = (f32[16,1,1280]{2,0,1:T(8,128)S(1)}, f32[16,1,1280]{2,0,1:T(8,128)S(1)}, u32[]{:S(2)}, u32[]{:S(2)}) collective-permute-start(f32[16,1,1280]{2,0,1:T(8,128)S(1)} %get-tuple-element.79), channel_id=1, source_target_pairs={{0,1},{1,2},{2,3},{3,4},{4,5},{5,6},{6,7},{7,8},{8,9},{9,10},{10,1... | collective-permute-start | bytes 245768 | tf_op jit(solution)/shard_map/ppermute | solution.py:18
  13.7 3.7 %collective-permute-done.1 = f32[16,1,1280]{2,0,1:T(8,128)S(1)} collective-permute-done((f32[16,1,1280]{2,0,1:T(8,128)S(1)}, f32[16,1,1280]{2,0,1:T(8,128)S(1)}, u32[]{:S(2)}, u32[]{:S(2)}) %collective-permute-start.1) | collective-permute-done | bytes 81952 | tf_op jit(solution)/shard_map/ppermute | solution.py:21
  22.1 3.7 %collective-permute-done.3 = f32[16,1,1280]{2,0,1:T(8,128)S(1)} collective-permute-done((f32[16,1,1280]{2,0,1:T(8,128)S(1)}, f32[16,1,1280]{2,0,1:T(8,128)S(1)}, u32[]{:S(2)}, u32[]{:S(2)}) %collective-permute-start.3) | collective-permute-done | bytes 81952 | tf_op jit(solution)/shard_map/ppermute | solution.py:21
  25.9 5.0 %collective-permute-start.4 = (f32[16,1,1280]{2,0,1:T(8,128)S(1)}, f32[16,1,1280]{2,0,1:T(8,128)S(1)}, u32[]{:S(2)}, u32[]{:S(2)}) collective-permute-start(f32[16,1,1280]{2,0,1:T(8,128)S(1)} %get-tuple-element.75), channel_id=1, source_target_pairs={{0,1},{1,2},{2,3},{3,4},{4,5},{5,6},{6,7},{7,8},{8,9},{9,10},{10,1... | collective-permute-start | bytes 245768 | tf_op jit(solution)/shard_map/ppermute | solution.py:18
  36.2 4.0 %collective-permute-start.6 = (bf16[16,1,1280]{2,0,1:T(8,128)(2,1)S(1)}, bf16[16,1,1280]{2,0,1:T(8,128)(2,1)S(1)}, u32[]{:S(2)}, u32[]{:S(2)}) collective-permute-start(bf16[16,1,1280]{2,0,1:T(8,128)(2,1)S(1)} %get-tuple-element.83), channel_id=1, source_target_pairs={{0,1},{1,2},{2,3},{3,4},{4,5},{5,6},{6,7},{7,8},{8,9},{9,10},{10,1... | collective-permute-start | bytes 122888 | tf_op jit(solution)/shard_map/ppermute | solution.py:18
  45.2 4.0 %fusion.8 = f32[16,6,2560]{2,0,1:T(8,128)S(1)} fusion(bf16[1280,2560]{1,0:T(8,128)(2,1)} %param.17, bf16[16,1,1280]{2,0,1:T(8,128)(2,1)S(1)} %collective-permute-done.7, bf16[16,4,1280]{2,0,1:T(8,128)(2,1)S(1)} %fusion.56, bf16[16,1,1280]{2,0,1:T(8,128)(2,1)S(1)} %collective-permute-done.6), kind=kOutput, calls=%fused_computation.10 | convolution fusion | flops 629391360 | bytes 7782400 | tf_op jit(solution)/shard_map/dot_general | solution.py:81
  54.1 38.6 %reduce-scatter.7.cloned.1.call-done = f32[320,16]{1,0:T(8,128)} async-done(((f32[2560,16]{1,0:T(8,128)}), f32[320,16]{1,0:T(8,128)}) %reduce-scatter.7.cloned.1.call-update) | async-done | bytes 20496
  95.9 9.8 %all-to-all-start = ((f32[128,1,8]{2,1,0:T(1,128)}), f32[128,1,8]{2,1,0:T(1,128)S(1)}, u32[]{:S(2)}, u32[]{:S(2)}) async-start(f32[128,1,8]{2,1,0:T(1,128)} %copy.126), calls=%async_computation | async-start | bytes 131072 | tf_op jit(solution)/shard_map/all_to_all | solution.py:184
  106.5 8.9 %all-to-all-done = f32[128,1,8]{2,1,0:T(1,128)S(1)} async-done(((f32[128,1,8]{2,1,0:T(1,128)}), f32[128,1,8]{2,1,0:T(1,128)S(1)}, u32[]{:S(2)}, u32[]{:S(2)}) %all-to-all-start) | async-done | bytes 4128 | tf_op jit(solution)/shard_map/all_to_all | solution.py:184
  116.5 4.3 %all-to-all-start.1 = ((f32[128,8,8]{2,1,0:T(8,128)}), f32[128,8,8]{2,1,0:T(8,128)S(1)}, u32[]{:S(2)}, u32[]{:S(2)}) async-start(f32[128,8,8]{2,1,0:T(8,128)} %bitcast.22), calls=%async_computation.1 | async-start | bytes 1048576 | tf_op jit(solution)/shard_map/all_to_all | solution.py:189
  120.8 14.1 %all-to-all-done.1 = f32[128,8,8]{2,1,0:T(8,128)S(1)} async-done(((f32[128,8,8]{2,1,0:T(8,128)}), f32[128,8,8]{2,1,0:T(8,128)S(1)}, u32[]{:S(2)}, u32[]{:S(2)}) %all-to-all-start.1) | async-done | bytes 32800 | tf_op jit(solution)/shard_map/all_to_all | solution.py:189
  135.1 11.3 %fusion.19 = f32[16,8,320]{2,0,1:T(8,128)S(1)} fusion(f32[128,8,8]{0,2,1:T(8,128)S(1)} %bitcast.162, s32[128,8,8]{0,2,1:T(8,128)S(1)} %get-tuple-element.89, f32[128,8,8]{0,2,1:T(8,128)S(1)} %get-tuple-element.96, s32[128,8,8]{0,2,1:T(8,128)S(1)} %get-tuple-element.90, f32[128,8,8]{0,2,1:T(8,128)S(1)} %broadcast_select_fusion, ...), kind=kOutput, calls=%fused_computation.31 | convolution fusion | flops 517210112 | bytes 458752 | tf_op jit(solution)/shard_map/bmsr,bmsc->rmc/dot_general | solution.py:133
  153.3 3.9 %collective-permute-done.9 = f32[16,1,2560]{2,0,1:T(8,128)S(1)} collective-permute-done((f32[16,1,2560]{2,0,1:T(8,128)S(1)}, f32[16,1,2560]{2,0,1:T(8,128)S(1)}, u32[]{:S(2)}, u32[]{:S(2)}) %collective-permute-start.9) | collective-permute-done | bytes 163872 | tf_op jit(solution)/shard_map/ppermute | solution.py:21
  167.3 3.9 %collective-permute-start.12 = (f32[16,1,1280]{2,0,1:T(8,128)S(1)}, f32[16,1,1280]{2,0,1:T(8,128)S(1)}, u32[]{:S(2)}, u32[]{:S(2)}) collective-permute-start(f32[16,1,1280]{2,0,1:T(8,128)S(1)} %get-tuple-element.71), channel_id=1, source_target_pairs={{0,1},{1,2},{2,3},{3,4},{4,5},{5,6},{6,7},{7,8},{8,9},{9,10},{10,1... | collective-permute-start | bytes 245768 | tf_op jit(solution)/shard_map/ppermute | solution.py:18
  176.5 4.3 %collective-permute-start.14 = (f32[16,1,1280]{2,0,1:T(8,128)S(1)}, f32[16,1,1280]{2,0,1:T(8,128)S(1)}, u32[]{:S(2)}, u32[]{:S(2)}) collective-permute-start(f32[16,1,1280]{2,0,1:T(8,128)S(1)} %get-tuple-element.69), channel_id=1, source_target_pairs={{0,1},{1,2},{2,3},{3,4},{4,5},{5,6},{6,7},{7,8},{8,9},{9,10},{10,1... | collective-permute-start | bytes 245768 | tf_op jit(solution)/shard_map/ppermute | solution.py:18
  186.7 3.7 %collective-permute-start.16 = (f32[16,1,1280]{2,0,1:T(8,128)S(1)}, f32[16,1,1280]{2,0,1:T(8,128)S(1)}, u32[]{:S(2)}, u32[]{:S(2)}) collective-permute-start(f32[16,1,1280]{2,0,1:T(8,128)S(1)} %get-tuple-element.67), channel_id=1, source_target_pairs={{0,1},{1,2},{2,3},{3,4},{4,5},{5,6},{6,7},{7,8},{8,9},{9,10},{10,1... | collective-permute-start | bytes 245768 | tf_op jit(solution)/shard_map/ppermute | solution.py:18
  195.7 4.0 %collective-permute-start.18 = (f32[16,1,1280]{2,0,1:T(8,128)S(1)}, f32[16,1,1280]{2,0,1:T(8,128)S(1)}, u32[]{:S(2)}, u32[]{:S(2)}) collective-permute-start(f32[16,1,1280]{2,0,1:T(8,128)S(1)} %get-tuple-element.65), channel_id=1, source_target_pairs={{0,1},{1,2},{2,3},{3,4},{4,5},{5,6},{6,7},{7,8},{8,9},{9,10},{10,1... | collective-permute-start | bytes 245768 | tf_op jit(solution)/shard_map/ppermute | solution.py:18
  205.0 4.0 %collective-permute-start.20 = (f32[16,1,1280]{2,0,1:T(8,128)S(1)}, f32[16,1,1280]{2,0,1:T(8,128)S(1)}, u32[]{:S(2)}, u32[]{:S(2)}) collective-permute-start(f32[16,1,1280]{2,0,1:T(8,128)S(1)} %get-tuple-element.63), channel_id=1, source_target_pairs={{0,1},{1,2},{2,3},{3,4},{4,5},{5,6},{6,7},{7,8},{8,9},{9,10},{10,1... | collective-permute-start | bytes 245768 | tf_op jit(solution)/shard_map/ppermute | solution.py:18
  214.3 4.0 %collective-permute-start.22 = (bf16[16,1,1280]{2,0,1:T(8,128)(2,1)S(1)}, bf16[16,1,1280]{2,0,1:T(8,128)(2,1)S(1)}, u32[]{:S(2)}, u32[]{:S(2)}) collective-permute-start(bf16[16,1,1280]{2,0,1:T(8,128)(2,1)S(1)} %get-tuple-element.81), channel_id=1, source_target_pairs={{0,1},{1,2},{2,3},{3,4},{4,5},{5,6},{6,7},{7,8},{8,9},{9,10},{10,1... | collective-permute-start | bytes 122888 | tf_op jit(solution)/shard_map/ppermute | solution.py:18
  220.6 18.2 %all-to-all-start.2 = ((f32[128,8,8]{2,1,0:T(8,128)}), f32[128,8,8]{2,1,0:T(8,128)S(1)}, u32[]{:S(2)}, u32[]{:S(2)}) async-start(f32[128,8,8]{2,1,0:T(8,128)} %bitcast.31), calls=%async_computation.2 | async-start | bytes 1048576 | tf_op jit(solution)/shard_map/all_to_all | solution.py:192
  238.9 4.0 %fusion.4 = f32[16,6,2560]{2,0,1:T(8,128)S(1)} fusion(bf16[1280,2560]{1,0:T(8,128)(2,1)} %param.17, bf16[16,1,1280]{2,0,1:T(8,128)(2,1)S(1)} %collective-permute-done.23, bf16[16,4,1280]{2,0,1:T(8,128)(2,1)S(1)} %fusion.30, bf16[16,1,1280]{2,0,1:T(8,128)(2,1)S(1)} %collective-permute-done.22), kind=kOutput, calls=%fused_computation.6 | convolution fusion | flops 629391360 | bytes 7782400 | tf_op jit(solution)/shard_map/dot_general | solution.py:81
  246.6 6.3 %all-to-all-done.2 = f32[128,8,8]{2,1,0:T(8,128)S(1)} async-done(((f32[128,8,8]{2,1,0:T(8,128)}), f32[128,8,8]{2,1,0:T(8,128)S(1)}, u32[]{:S(2)}, u32[]{:S(2)}) %all-to-all-start.2) | async-done | bytes 32800 | tf_op jit(solution)/shard_map/all_to_all | solution.py:192
  253.0 25.0 %reduce-scatter.9.cloned.1.call-done = f32[320,16]{1,0:T(8,128)} async-done(((f32[2560,16]{1,0:T(8,128)}), f32[320,16]{1,0:T(8,128)}) %reduce-scatter.9.cloned.1.call-update) | async-done | bytes 20496
  282.0 67.6 %all-reduce.3 = (f32[]{:T(128)}, f32[]{:T(128)}) all-reduce(f32[]{:T(128)} %get-tuple-element.40, f32[]{:T(128)} %fusion.103), channel_id=1, replica_groups=mesh['member'=8,'tile'=16] {'member','tile'}, use_global_device_ids=true, to_apply=%region_4.5 | all-reduce | flops 2 | bytes 16 | tf_op jit(solution)/shard_map/psum | solution.py:146
  (131 shorter events, 82.0 us)
Async XLA Ops:
  7.2 85.5 %reduce-scatter.7.cloned.1.call-start = ((), (), s32[]{:S(2)}) async-start(), calls=%async_computation.5 | async-start | bytes 1474560
  8.3 5.4 %collective-permute-start = (f32[16,1,1280]{2,0,1:T(8,128)S(1)}, f32[16,1,1280]{2,0,1:T(8,128)S(1)}, u32[]{:S(2)}, u32[]{:S(2)}) collective-permute-start(f32[16,1,1280]{2,0,1:T(8,128)S(1)} %get-tuple-element.79), channel_id=1, source_target_pairs={{0,1},{1,2},{2,3},{3,4},{4,5},{5,6},{6,7},{7,8},{8,9},{9,10},{10,1... | collective-permute-start | bytes 245768 | tf_op jit(solution)/shard_map/ppermute | solution.py:18
  12.2 5.2 %collective-permute-start.1 = (f32[16,1,1280]{2,0,1:T(8,128)S(1)}, f32[16,1,1280]{2,0,1:T(8,128)S(1)}, u32[]{:S(2)}, u32[]{:S(2)}) collective-permute-start(f32[16,1,1280]{2,0,1:T(8,128)S(1)} %get-tuple-element.80), channel_id=1, source_target_pairs={{1,0},{2,1},{3,2},{4,3},{5,4},{6,5},{7,6},{8,7},{9,8},{10,9},{11,1... | collective-permute-start | bytes 245768 | tf_op jit(solution)/shard_map/ppermute | solution.py:21
  20.6 5.2 %collective-permute-start.3 = (f32[16,1,1280]{2,0,1:T(8,128)S(1)}, f32[16,1,1280]{2,0,1:T(8,128)S(1)}, u32[]{:S(2)}, u32[]{:S(2)}) collective-permute-start(f32[16,1,1280]{2,0,1:T(8,128)S(1)} %get-tuple-element.78), channel_id=1, source_target_pairs={{1,0},{2,1},{3,2},{4,3},{5,4},{6,5},{7,6},{8,7},{9,8},{10,9},{11,1... | collective-permute-start | bytes 245768 | tf_op jit(solution)/shard_map/ppermute | solution.py:21
  25.9 6.5 %collective-permute-start.4 = (f32[16,1,1280]{2,0,1:T(8,128)S(1)}, f32[16,1,1280]{2,0,1:T(8,128)S(1)}, u32[]{:S(2)}, u32[]{:S(2)}) collective-permute-start(f32[16,1,1280]{2,0,1:T(8,128)S(1)} %get-tuple-element.75), channel_id=1, source_target_pairs={{0,1},{1,2},{2,3},{3,4},{4,5},{5,6},{6,7},{7,8},{8,9},{9,10},{10,1... | collective-permute-start | bytes 245768 | tf_op jit(solution)/shard_map/ppermute | solution.py:18
  30.9 5.2 %collective-permute-start.5 = (f32[16,1,1280]{2,0,1:T(8,128)S(1)}, f32[16,1,1280]{2,0,1:T(8,128)S(1)}, u32[]{:S(2)}, u32[]{:S(2)}) collective-permute-start(f32[16,1,1280]{2,0,1:T(8,128)S(1)} %get-tuple-element.76), channel_id=1, source_target_pairs={{1,0},{2,1},{3,2},{4,3},{5,4},{6,5},{7,6},{8,7},{9,8},{10,9},{11,1... | collective-permute-start | bytes 245768 | tf_op jit(solution)/shard_map/ppermute | solution.py:21
  36.2 5.4 %collective-permute-start.6 = (bf16[16,1,1280]{2,0,1:T(8,128)(2,1)S(1)}, bf16[16,1,1280]{2,0,1:T(8,128)(2,1)S(1)}, u32[]{:S(2)}, u32[]{:S(2)}) collective-permute-start(bf16[16,1,1280]{2,0,1:T(8,128)(2,1)S(1)} %get-tuple-element.83), channel_id=1, source_target_pairs={{0,1},{1,2},{2,3},{3,4},{4,5},{5,6},{6,7},{7,8},{8,9},{9,10},{10,1... | collective-permute-start | bytes 122888 | tf_op jit(solution)/shard_map/ppermute | solution.py:18
  95.9 19.6 %all-to-all-start = ((f32[128,1,8]{2,1,0:T(1,128)}), f32[128,1,8]{2,1,0:T(1,128)S(1)}, u32[]{:S(2)}, u32[]{:S(2)}) async-start(f32[128,1,8]{2,1,0:T(1,128)} %copy.126), calls=%async_computation | async-start | bytes 131072 | tf_op jit(solution)/shard_map/all_to_all | solution.py:184
  116.5 18.4 %all-to-all-start.1 = ((f32[128,8,8]{2,1,0:T(8,128)}), f32[128,8,8]{2,1,0:T(8,128)S(1)}, u32[]{:S(2)}, u32[]{:S(2)}) async-start(f32[128,8,8]{2,1,0:T(8,128)} %bitcast.22), calls=%async_computation.1 | async-start | bytes 1048576 | tf_op jit(solution)/shard_map/all_to_all | solution.py:189
  147.9 5.4 %collective-permute-start.8 = (f32[16,1,2560]{2,0,1:T(8,128)S(1)}, f32[16,1,2560]{2,0,1:T(8,128)S(1)}, u32[]{:S(2)}, u32[]{:S(2)}) collective-permute-start(f32[16,1,2560]{2,0,1:T(8,128)S(1)} %get-tuple-element.54), channel_id=1, source_target_pairs={{0,1},{1,2},{2,3},{3,4},{4,5},{5,6},{6,7},{7,8},{8,9},{9,10},{10,1... | collective-permute-start | bytes 491528 | tf_op jit(solution)/shard_map/ppermute | solution.py:18
  150.4 6.8 %collective-permute-start.9 = (f32[16,1,2560]{2,0,1:T(8,128)S(1)}, f32[16,1,2560]{2,0,1:T(8,128)S(1)}, u32[]{:S(2)}, u32[]{:S(2)}) collective-permute-start(f32[16,1,2560]{2,0,1:T(8,128)S(1)} %get-tuple-element.53), channel_id=1, source_target_pairs={{1,0},{2,1},{3,2},{4,3},{5,4},{6,5},{7,6},{8,7},{9,8},{10,9},{11,1... | collective-permute-start | bytes 491528 | tf_op jit(solution)/shard_map/ppermute | solution.py:21
  162.0 5.2 %collective-permute-start.11 = (f32[16,1,1280]{2,0,1:T(8,128)S(1)}, f32[16,1,1280]{2,0,1:T(8,128)S(1)}, u32[]{:S(2)}, u32[]{:S(2)}) collective-permute-start(f32[16,1,1280]{2,0,1:T(8,128)S(1)} %get-tuple-element.74), channel_id=1, source_target_pairs={{1,0},{2,1},{3,2},{4,3},{5,4},{6,5},{7,6},{8,7},{9,8},{10,9},{11,1... | collective-permute-start | bytes 245768 | tf_op jit(solution)/shard_map/ppermute | solution.py:21
  167.3 5.4 %collective-permute-start.12 = (f32[16,1,1280]{2,0,1:T(8,128)S(1)}, f32[16,1,1280]{2,0,1:T(8,128)S(1)}, u32[]{:S(2)}, u32[]{:S(2)}) collective-permute-start(f32[16,1,1280]{2,0,1:T(8,128)S(1)} %get-tuple-element.71), channel_id=1, source_target_pairs={{0,1},{1,2},{2,3},{3,4},{4,5},{5,6},{6,7},{7,8},{8,9},{9,10},{10,1... | collective-permute-start | bytes 245768 | tf_op jit(solution)/shard_map/ppermute | solution.py:18
  171.2 5.2 %collective-permute-start.13 = (f32[16,1,1280]{2,0,1:T(8,128)S(1)}, f32[16,1,1280]{2,0,1:T(8,128)S(1)}, u32[]{:S(2)}, u32[]{:S(2)}) collective-permute-start(f32[16,1,1280]{2,0,1:T(8,128)S(1)} %get-tuple-element.72), channel_id=1, source_target_pairs={{1,0},{2,1},{3,2},{4,3},{5,4},{6,5},{7,6},{8,7},{9,8},{10,9},{11,1... | collective-permute-start | bytes 245768 | tf_op jit(solution)/shard_map/ppermute | solution.py:21
  176.5 5.8 %collective-permute-start.14 = (f32[16,1,1280]{2,0,1:T(8,128)S(1)}, f32[16,1,1280]{2,0,1:T(8,128)S(1)}, u32[]{:S(2)}, u32[]{:S(2)}) collective-permute-start(f32[16,1,1280]{2,0,1:T(8,128)S(1)} %get-tuple-element.69), channel_id=1, source_target_pairs={{0,1},{1,2},{2,3},{3,4},{4,5},{5,6},{6,7},{7,8},{8,9},{9,10},{10,1... | collective-permute-start | bytes 245768 | tf_op jit(solution)/shard_map/ppermute | solution.py:18
  180.8 5.2 %collective-permute-start.15 = (f32[16,1,1280]{2,0,1:T(8,128)S(1)}, f32[16,1,1280]{2,0,1:T(8,128)S(1)}, u32[]{:S(2)}, u32[]{:S(2)}) collective-permute-start(f32[16,1,1280]{2,0,1:T(8,128)S(1)} %get-tuple-element.70), channel_id=1, source_target_pairs={{1,0},{2,1},{3,2},{4,3},{5,4},{6,5},{7,6},{8,7},{9,8},{10,9},{11,1... | collective-permute-start | bytes 245768 | tf_op jit(solution)/shard_map/ppermute | solution.py:21
  186.7 5.2 %collective-permute-start.16 = (f32[16,1,1280]{2,0,1:T(8,128)S(1)}, f32[16,1,1280]{2,0,1:T(8,128)S(1)}, u32[]{:S(2)}, u32[]{:S(2)}) collective-permute-start(f32[16,1,1280]{2,0,1:T(8,128)S(1)} %get-tuple-element.67), channel_id=1, source_target_pairs={{0,1},{1,2},{2,3},{3,4},{4,5},{5,6},{6,7},{7,8},{8,9},{9,10},{10,1... | collective-permute-start | bytes 245768 | tf_op jit(solution)/shard_map/ppermute | solution.py:18
  190.5 5.2 %collective-permute-start.17 = (f32[16,1,1280]{2,0,1:T(8,128)S(1)}, f32[16,1,1280]{2,0,1:T(8,128)S(1)}, u32[]{:S(2)}, u32[]{:S(2)}) collective-permute-start(f32[16,1,1280]{2,0,1:T(8,128)S(1)} %get-tuple-element.68), channel_id=1, source_target_pairs={{1,0},{2,1},{3,2},{4,3},{5,4},{6,5},{7,6},{8,7},{9,8},{10,9},{11,1... | collective-permute-start | bytes 245768 | tf_op jit(solution)/shard_map/ppermute | solution.py:21
  195.7 5.5 %collective-permute-start.18 = (f32[16,1,1280]{2,0,1:T(8,128)S(1)}, f32[16,1,1280]{2,0,1:T(8,128)S(1)}, u32[]{:S(2)}, u32[]{:S(2)}) collective-permute-start(f32[16,1,1280]{2,0,1:T(8,128)S(1)} %get-tuple-element.65), channel_id=1, source_target_pairs={{0,1},{1,2},{2,3},{3,4},{4,5},{5,6},{6,7},{7,8},{8,9},{9,10},{10,1... | collective-permute-start | bytes 245768 | tf_op jit(solution)/shard_map/ppermute | solution.py:18
  205.0 5.5 %collective-permute-start.20 = (f32[16,1,1280]{2,0,1:T(8,128)S(1)}, f32[16,1,1280]{2,0,1:T(8,128)S(1)}, u32[]{:S(2)}, u32[]{:S(2)}) collective-permute-start(f32[16,1,1280]{2,0,1:T(8,128)S(1)} %get-tuple-element.63), channel_id=1, source_target_pairs={{0,1},{1,2},{2,3},{3,4},{4,5},{5,6},{6,7},{7,8},{8,9},{9,10},{10,1... | collective-permute-start | bytes 245768 | tf_op jit(solution)/shard_map/ppermute | solution.py:18
  214.3 24.6 %collective-permute-start.22 = (bf16[16,1,1280]{2,0,1:T(8,128)(2,1)S(1)}, bf16[16,1,1280]{2,0,1:T(8,128)(2,1)S(1)}, u32[]{:S(2)}, u32[]{:S(2)}) collective-permute-start(bf16[16,1,1280]{2,0,1:T(8,128)(2,1)S(1)} %get-tuple-element.81), channel_id=1, source_target_pairs={{0,1},{1,2},{2,3},{3,4},{4,5},{5,6},{6,7},{7,8},{8,9},{9,10},{10,1... | collective-permute-start | bytes 122888 | tf_op jit(solution)/shard_map/ppermute | solution.py:18
  218.4 20.5 %collective-permute-start.23 = (bf16[16,1,1280]{2,0,1:T(8,128)(2,1)S(1)}, bf16[16,1,1280]{2,0,1:T(8,128)(2,1)S(1)}, u32[]{:S(2)}, u32[]{:S(2)}) collective-permute-start(bf16[16,1,1280]{2,0,1:T(8,128)(2,1)S(1)} %get-tuple-element.82), channel_id=1, source_target_pairs={{1,0},{2,1},{3,2},{4,3},{5,4},{6,5},{7,6},{8,7},{9,8},{10,9},{11,1... | collective-permute-start | bytes 122888 | tf_op jit(solution)/shard_map/ppermute | solution.py:21
  220.6 32.3 %all-to-all-start.2 = ((f32[128,8,8]{2,1,0:T(8,128)}), f32[128,8,8]{2,1,0:T(8,128)S(1)}, u32[]{:S(2)}, u32[]{:S(2)}) async-start(f32[128,8,8]{2,1,0:T(8,128)} %bitcast.31), calls=%async_computation.2 | async-start | bytes 1048576 | tf_op jit(solution)/shard_map/all_to_all | solution.py:192
  238.8 39.2 %reduce-scatter.9.cloned.1.call-start = ((), (), s32[]{:S(2)}) async-start(), calls=%async_computation.6 | async-start | bytes 1474560
  (16 other events, 300.3 us)
Sparse Core Ops, SparseCore 0:
  54.1 38.4 reduce-scatter.6
  246.7 31.3 reduce-scatter.8
where the time goes:
time: 361 us; the launch traced here: 360 us
  waiting for transfers between devices  137 us (38%)
  starting transfers between devices  93.4 us (26%)
  blocking collectives  67.6 us (19%)
  matrix products  25.3 us (7%)
  between operations  17.3 us (5%)
  local copies, waits for them, and re-layouts  12 us (3%)
  other arithmetic  7.7 us (2%)
    psum x1, blocking collectives, global_sum(): return lax.psum(values, ('member', 'tile'))  67.6 us
    unnamed x4, waiting for transfers between devices  63.6 us
    ppermute x12, starting transfers between devices, padded_2(): lax.ppermute(lax.slice_in_dim(block, block.shape[dim] - width, None, axis...  45.2 us
    ppermute x12, waiting for transfers between devices, padded_2(): lax.ppermute(lax.slice_in_dim(block, 0, width, axis=dim), axis, backward)  41.1 us
    all_to_all x1, starting transfers between devices, shards(): lax.all_to_all(fan_out(obs_weight), ('member', 'tile'), split_axis=0, con...  18.2 us
    ppermute x12, starting transfers between devices, padded_2(): lax.ppermute(lax.slice_in_dim(block, 0, width, axis=dim), axis, backward)  15.7 us
    all_to_all x1, waiting for transfers between devices, shards(): lax.all_to_all(fan_out(residual), ('member', 'tile'), split_axis=0, conca...  14.1 us
    dot_general x1, matrix products, spread_tile(): jnp.einsum('bmsr,bmsc->rmc', weighted, column_factor, precision=lax.Preci...  11.3 us
  transfers between devices with their start and end apart: 29, of which 26 were waited for; matrix products, arithmetic and copies ran while one was open for 3% of the time, Pallas kernels for 0%

commit v1 on v0

v1 whole, which is shorter than its diff:
```python
import jax
import jax.numpy as jnp
import numpy as np
from jax import lax
from jax.sharding import PartitionSpec as P

RATIO = 4
KSM = 3
DIFFUSION = 0.45
NTILE = 16
NMEMBER = 8
NCORE = 2
NY = NMEMBER // NCORE
FLOAT, HALF = jnp.float32, jnp.bfloat16


def turn(values, step, axis):
    count = lax.axis_size(axis)
    return lax.ppermute(values, axis, [(i, (i + step) % count) for i in range(count)])


def swap_core(values):
    return lax.ppermute(values, "member", [(i, i ^ 1) for i in range(NMEMBER)])


def sum_y(values):
    return (
        values
        + turn(values, NCORE, "member")
        + turn(values, 2 * NCORE, "member")
        + turn(values, 3 * NCORE, "member")
    )


def row_mask(tile_pos, first, count):
    rows = tile_pos * 4 + first + jnp.arange(count)
    return ((rows >= 0) & (rows < 4 * NTILE)).astype(FLOAT)[None, :, None]


def sweeps(values, tile_pos, first):
    for _ in range(KSM):
        values = values * row_mask(tile_pos, first, values.shape[1])
        middle = values[:, 1:-1]
        values = middle + DIFFUSION * (values[:, :-2] + values[:, 2:] - 2.0 * middle)
        first += 1
    return values * row_mask(tile_pos, first, values.shape[1])


def refine(extended):
    members_here, row_count, col_count = extended.shape
    lower_rows = extended[:, :-2]
    middle = extended[:, 1:-1]
    upper_rows = extended[:, 2:]
    pieces = []
    for offset in range(RATIO):
        shift_value = (offset + 0.5) / RATIO - 0.5
        if shift_value < 0:
            pieces.append((1.0 + shift_value) * middle - shift_value * lower_rows)
        else:
            pieces.append((1.0 - shift_value) * middle + shift_value * upper_rows)
    return jnp.stack(pieces, axis=2).reshape(members_here, (row_count - 2) * RATIO, col_count)


def refine_adjoint(fine_field):
    members_here, fine_count, col_count = fine_field.shape
    row_count = fine_count // RATIO
    blocks = fine_field.reshape(members_here, row_count, RATIO, col_count)
    middle = jnp.zeros_like(blocks[:, :, 0])
    lower_rows = jnp.zeros_like(middle)
    upper_rows = jnp.zeros_like(middle)
    for offset in range(RATIO):
        shift_value = (offset + 0.5) / RATIO - 0.5
        fine_layer = blocks[:, :, offset]
        if shift_value < 0:
            middle = middle + (1.0 + shift_value) * fine_layer
            lower_rows = lower_rows - shift_value * fine_layer
        else:
            middle = middle + (1.0 - shift_value) * fine_layer
            upper_rows = upper_rows + shift_value * fine_layer
    return (
        jnp.pad(middle, ((0, 0), (1, 1), (0, 0)))
        + jnp.pad(lower_rows, ((0, 0), (0, 2), (0, 0)))
        + jnp.pad(upper_rows, ((0, 0), (2, 0), (0, 0)))
    )


def partial_forward(low, own, high, tile_pos, perturb, column_map):
    smooth = sweeps(jnp.concatenate([low.astype(FLOAT), own, high.astype(FLOAT)], axis=1), tile_pos, -4)
    members_here, row_count, coarse_cols = smooth.shape
    mapped = jnp.dot(
        smooth.astype(HALF).reshape(-1, coarse_cols), column_map, preferred_element_type=FLOAT
    )
    fine_field = refine(mapped.reshape(members_here, row_count, -1))
    return jnp.sum(fine_field * perturb, axis=0)


def by_parity(field):
    rows, cols = field.shape
    width = cols // NMEMBER
    return jnp.transpose(field.reshape(rows, NY, NCORE, width), (2, 1, 0, 3))


def owner_sum(field, core_pos):
    parts = by_parity(field)
    mine = lax.dynamic_index_in_dim(parts, core_pos, 0, False)
    other = lax.dynamic_index_in_dim(parts, 1 - core_pos, 0, False)
    return sum_y(mine + swap_core(other))


def column_pick(column, width):
    ids = lax.broadcasted_iota(jnp.int32, column.shape[:1] + (width,) + column.shape[1:], 1)
    return (ids == column[:, None]).astype(HALF)


def split_half(values):
    high = lax.reduce_precision(values, 8, 7)
    return high.astype(HALF), (values - high).astype(HALF)


def interpolate(fields, picks, row_factor, column_frac):
    nxt = jnp.concatenate([fields[:, :, 1:], fields[:, :, :1]], axis=2)
    both = jnp.concatenate([fields, nxt], axis=1)
    high, low = split_half(both)
    got = jnp.einsum(
        "yrc,ycn->yrn", jnp.concatenate([high, low], axis=1), picks, preferred_element_type=FLOAT
    )
    rows = fields.shape[1]
    left = got[:, :rows] + got[:, 2 * rows : 3 * rows]
    right = got[:, rows : 2 * rows] + got[:, 3 * rows :]
    mixed = left * (1.0 - column_frac[:, None]) + right * column_frac[:, None]
    return jnp.sum(mixed * row_factor, axis=1)


def spread_regions(residual, picks, row_factor, column_frac):
    weighted = row_factor * residual[:, None]
    both = jnp.concatenate(
        [weighted * (1.0 - column_frac[:, None]), weighted * column_frac[:, None]], axis=1
    )
    high, low = split_half(both)
    got = jnp.einsum(
        "yrn,ycn->yrc", jnp.concatenate([high, low], axis=1), picks, preferred_element_type=FLOAT
    )
    rows = row_factor.shape[1]
    left = got[:, :rows] + got[:, 2 * rows : 3 * rows]
    right = got[:, rows : 2 * rows] + got[:, 3 * rows :]
    return left + jnp.concatenate([right[:, :, -1:], right[:, :, :-1]], axis=2)


def innovation(obs_state, obs_value, obs_error, instrument):
    bounded = jnp.tanh(obs_state)
    derivative = 1.0 + instrument * (1.0 - bounded * bounded)
    misfit = obs_state + instrument * bounded - obs_value
    precision_obs = 1.0 / (obs_error * obs_error)
    return (derivative * misfit * precision_obs, derivative * derivative * precision_obs)


def shards(
    perturb,
    weights,
    column_map,
    background,
    stencil_index,
    row_fraction,
    column_fraction,
    block_lengths,
    obs_value,
    obs_error,
    instrument_gain,
):
    member_pos = lax.axis_index("member")
    core_pos = member_pos % NCORE
    y_pos = member_pos // NCORE
    tile_pos = lax.axis_index("tile")
    fine_rows, width = background.shape
    slots = obs_value.shape[2]
    devices = obs_value.shape[1]

    half_weights = weights.astype(HALF)
    low, high = turn(half_weights, 1, "tile"), turn(half_weights, -1, "tile")

    stacked = jnp.stack([obs_value[0], obs_error[0]])
    stacked = stacked.reshape(2, NY, NCORE, NTILE, slots)
    stacked = jnp.transpose(stacked, (2, 3, 0, 1, 4)).reshape(NCORE, NTILE, 2 * NY * slots)
    gains = jnp.broadcast_to(instrument_gain, (NCORE, NTILE, 2 * NY * slots))
    stacked = jnp.concatenate([stacked, gains], axis=-1)
    sent = jnp.broadcast_to(stacked[None], (NY,) + stacked.shape).reshape(devices, -1)
    got = lax.all_to_all(sent, ("member", "tile"), split_axis=0, concat_axis=0, tiled=True)
    got = got.T
    values = got[: NY * slots].reshape(NY, slots * devices)
    errors = got[NY * slots : 2 * NY * slots].reshape(NY, slots * devices)
    gains = got[2 * NY * slots : 3 * NY * slots].reshape(NY, slots * devices)

    def of_core(array):
        mine = lax.dynamic_index_in_dim(
            array.reshape(devices, NY, NCORE, slots), core_pos, 2, False
        )
        return jnp.transpose(mine, (1, 2, 0)).reshape(NY, slots * devices)

    index = of_core(stencil_index[0])
    row_frac = of_core(row_fraction[0])
    column_frac = of_core(column_fraction[0])
    slot_ids = lax.broadcasted_iota(jnp.int32, stencil_index.shape[1:], 2)
    live = of_core((slot_ids < block_lengths[0][:, :, None]).astype(FLOAT))
    row_pos = index // width
    picks = column_pick(index % width, width)
    row_ids = lax.broadcasted_iota(jnp.int32, (NY, fine_rows, slots * devices), 1)
    row_factor = jnp.where(row_ids == row_pos[:, None], 1.0 - row_frac[:, None], 0.0) + jnp.where(
        row_ids == row_pos[:, None] + 1, row_frac[:, None], 0.0
    )

    base = background

    increment = owner_sum(
        partial_forward(low, weights, high, tile_pos, perturb, column_map), core_pos
    )
    regions = jnp.stack([base, turn(base, NCORE, "member"), turn(base, 2 * NCORE, "member"),
                         turn(base, 3 * NCORE, "member")])
    order = (y_pos - jnp.arange(NY)) % NY
    regions = jnp.take(regions, order, axis=0)
    state = interpolate(regions + increment, picks, row_factor, column_frac)
    residual, obs_weight = innovation(state, values, errors, gains)
    mine = spread_regions(residual * live, picks, row_factor, column_frac)
    other = swap_core(mine)
    even = jnp.where(core_pos == 0, mine, other)
    odd = jnp.where(core_pos == 0, other, mine)
    spread = jnp.transpose(jnp.stack([even, odd], axis=1), (2, 0, 1, 3)).reshape(fine_rows, -1)

    pulled = refine_adjoint(perturb * spread).astype(HALF)
    members_here, row_count, fine_cols = pulled.shape
    part = lax.dot_general(
        pulled.reshape(-1, fine_cols),
        column_map,
        (((1,), (1,)), ((), ())),
        preferred_element_type=FLOAT,
    ).reshape(members_here, row_count, -1)
    from_low = turn(part[:, 2:].astype(HALF), 1, "tile").astype(FLOAT)
    from_high = turn(part[:, :4].astype(HALF), -1, "tile").astype(FLOAT)
    full = (
        jnp.pad(part, ((0, 0), (2, 2), (0, 0)))
        + jnp.pad(from_low * (tile_pos > 0), ((0, 0), (0, 6), (0, 0)))
        + jnp.pad(from_high * (tile_pos < NTILE - 1), ((0, 0), (6, 0), (0, 0)))
    )
    gradient = weights + sweeps(full, tile_pos, -3)
    half_gradient = gradient.astype(HALF)
    grad_low, grad_high = turn(half_gradient, 1, "tile"), turn(half_gradient, -1, "tile")
    grad_square = jnp.sum(gradient * gradient)
    grad_image = owner_sum(
        partial_forward(grad_low, gradient, grad_high, tile_pos, perturb, column_map), core_pos
    )

    def own(array):
        return lax.dynamic_slice_in_dim(array, y_pos, 1, 0)

    grad_own = own(grad_image)
    grad_obs = interpolate(grad_own, own(picks), own(row_factor), own(column_frac))
    curvature = jnp.sum(own(live) * own(obs_weight) * grad_obs * grad_obs)
    pair = jnp.where(jnp.arange(128) < 64, grad_square, curvature)
    shared = lax.all_to_all(
        jnp.broadcast_to(pair[None], (devices, 128)),
        ("member", "tile"),
        split_axis=0,
        concat_axis=0,
        tiled=True,
    )
    totals = jnp.sum(shared, axis=0)
    step_size = totals[0] / (totals[0] + totals[127])
    return (weights - step_size * gradient, own(increment)[0] - step_size * grad_own[0])


def solution(mesh):
    placed = (
        P("member", "tile", None),
        P("member", "tile", None),
        P(),
        P("tile", "member"),
        P("tile", None, None, None),
        P("tile", None, None, None),
        P("tile", None, None, None),
        P("tile", None, None),
        P(("member", "tile"), None, None),
        P(("member", "tile"), None, None),
        P(("member", "tile")),
    )
    return jax.shard_map(
        shards,
        mesh=mesh,
        in_specs=placed,
        out_specs=(P("member", "tile", None), P("tile", "member")),
        check_vma=False,
    )
```

time: 361 us -> 121 us (0.34)
  waiting for transfers between devices: 137 us -> 14.9 us
  starting transfers between devices: 93.4 us -> 40.7 us
  blocking collectives: 67.6 us -> 18.2 us
  matrix products: 25.3 us -> 7.93 us
  between operations: 17.3 us -> 4.13 us
  other arithmetic: 7.7 us -> 19.7 us
    psum x1 -> x0, blocking collectives: 67.6 us -> none  [global_sum(): return lax.psum(values, ('member', 'tile'))]
    unnamed x4 -> x0, waiting for transfers between devices: 63.6 us -> none
    all_to_all x3 -> x1, waiting for transfers between devices: 29.4 us -> 0.01 us  [shards(): lax.all_to_all(sent, ('member', 'tile'), split_axis=0, concat_axis=0, til...]
    ppermute x24 -> x18, waiting for transfers between devices: 43.8 us -> 14.9 us  [the longest x15 12.7 us: turn(): lax.ppermute(values, axis, [(i, (i + step) % count) for i in range(count)])]
    all_to_all x3 -> x1, starting transfers between devices: 32.4 us -> 5.18 us  [shards(): lax.all_to_all(sent, ('member', 'tile'), split_axis=0, concat_axis=0, til...]
    ppermute x24 -> x18, starting transfers between devices: 60.9 us -> 35.5 us  [the longest x15 30.9 us: turn(): lax.ppermute(values, axis, [(i, (i + step) % count) for i in range(count)])]
    all_to_all x0 -> x1, blocking collectives: none -> 18.2 us  [shards(): lax.all_to_all(jnp.broadcast_to(pair[None], (devices, 128)), ('member', '...]
    dot_general x6, matrix products: 25.3 us -> 7.93 us  [the longest x2 2.44 us: partial_forward(): jnp.dot(smooth.astype(HALF).reshape(-1, coarse_cols), column_map, preferr...]
  transfers between devices with their start and end apart: 29 -> 19, of which waited for: 26 -> 11; matrix products, arithmetic and copies ran while one was open for 3% -> 11% of each run, Pallas kernels for 0% -> 0%
where the time goes in v1:
time: 121 us; the launch traced here: 120 us
  starting transfers between devices  40.7 us (34%)
  other arithmetic  19.7 us (16%)
  blocking collectives  18.2 us (15%)
  waiting for transfers between devices  14.9 us (12%)
  local copies, waits for them, and re-layouts  14.7 us (12%)
  matrix products  7.93 us (7%)
  between operations  4.13 us (3%)
    ppermute x15, starting transfers between devices, turn(): lax.ppermute(values, axis, [(i, (i + step) % count) for i in range(count)])  30.9 us
    all_to_all x1, blocking collectives, shards(): lax.all_to_all(jnp.broadcast_to(pair[None], (devices, 128)), ('member', '...  18.2 us
    ppermute x15, waiting for transfers between devices, turn(): lax.ppermute(values, axis, [(i, (i + step) % count) for i in range(count)])  12.7 us
    unnamed x60, local copies, waits for them, and re-layouts  10 us
    all_to_all x1, starting transfers between devices, shards(): lax.all_to_all(sent, ('member', 'tile'), split_axis=0, concat_axis=0, til...  5.18 us
    ppermute x3, starting transfers between devices, swap_core(): return lax.ppermute(values, 'member', [(i, i ^ 1) for i in range(NMEMBER)])  4.63 us
    dot_general x2, matrix products, partial_forward(): jnp.dot(smooth.astype(HALF).reshape(-1, coarse_cols), column_map, preferr...  2.44 us
  transfers between devices with their start and end apart: 19, of which 11 were waited for; matrix products, arithmetic and copies ran while one was open for 11% of the time, Pallas kernels for 0%

profile of v1, /device:TPU:1, one launch (start us, length us, event | category | flops | bytes accessed | tf_op | source)
XLA Modules:
  0.0 120.2 jit_solution(3759023067685383425)
XLA Ops:
  1.7 2.1 %collective-permute-start.3 = (bf16[16,4,1280]{2,0,1:T(8,128)(2,1)S(1)}, bf16[16,4,1280]{2,0,1:T(8,128)(2,1)S(1)}, u32[]{:S(2)}, u32[]{:S(2)}) collective-permute-start(bf16[16,4,1280]{2,0,1:T(8,128)(2,1)S(1)} %copy.208), channel_id=1, source_target_pairs={{0,1},{1,2},{2,3},{3,4},{4,5},{5,6},{6,7},{7,8},{8,9},{9,10},{10,1... | collective-permute-start | bytes 491528 | tf_op jit(solution)/shard_map/ppermute | solution.py:19
  3.8 4.8 %collective-permute-start.4 = (bf16[16,4,1280]{2,0,1:T(8,128)(2,1)S(1)}, bf16[16,4,1280]{2,0,1:T(8,128)(2,1)S(1)}, u32[]{:S(2)}, u32[]{:S(2)}) collective-permute-start(bf16[16,4,1280]{2,0,1:T(8,128)(2,1)S(1)} %copy.208), channel_id=1, source_target_pairs={{0,15},{1,0},{2,1},{3,2},{4,3},{5,4},{6,5},{7,6},{8,7},{9,8},{10,9... | collective-permute-start | bytes 491528 | tf_op jit(solution)/shard_map/ppermute | solution.py:19
  8.6 1.3 %collective-permute-start = (f32[16,320]{1,0:T(8,128)}, f32[16,320]{1,0:T(8,128)S(1)}, u32[]{:S(2)}, u32[]{:S(2)}) collective-permute-start(f32[16,320]{1,0:T(8,128)} %param.14), channel_id=1, source_target_pairs={{0,32},{16,48},{32,64},{48,80},{64,96},{80,112},{96,0},{112,16},{1... | collective-permute-start | bytes 61448 | tf_op jit(solution)/shard_map/ppermute | solution.py:19
  9.9 2.6 %collective-permute-start.1 = (f32[16,320]{1,0:T(8,128)}, f32[16,320]{1,0:T(8,128)S(1)}, u32[]{:S(2)}, u32[]{:S(2)}) collective-permute-start(f32[16,320]{1,0:T(8,128)} %param.14), channel_id=1, source_target_pairs={{0,64},{16,80},{32,96},{48,112},{64,0},{80,16},{96,32},{112,48},{1... | collective-permute-start | bytes 61448 | tf_op jit(solution)/shard_map/ppermute | solution.py:19
  15.8 5.2 %all-to-all-start = ((f32[128,1,128]{2,1,0:T(1,128)}), f32[128,1,128]{2,1,0:T(1,128)S(1)}, u32[]{:S(2)}, u32[]{:S(2)}) async-start(f32[128,1,128]{2,1,0:T(1,128)} %bitcast.14), calls=%async_computation | async-start | bytes 131072 | tf_op jit(solution)/shard_map/all_to_all | solution.py:187
  25.8 2.3 %copy-done = bf16[1280,2560]{1,0:T(8,128)(2,1)S(1)} copy-done((bf16[1280,2560]{1,0:T(8,128)(2,1)S(1)}, bf16[1280,2560]{1,0:T(8,128)(2,1)}, u32[]{:S(2)}) %copy-start) | copy-done | bytes 6553624
  32.8 1.3 %collective-permute-start.5 = (f32[4,16,320]{2,1,0:T(8,128)S(1)}, f32[4,16,320]{2,1,0:T(8,128)S(1)}, u32[]{:S(2)}, u32[]{:S(2)}) collective-permute-start(f32[4,16,320]{2,1,0:T(8,128)S(1)} %bitcast.209), channel_id=1, source_target_pairs={{0,16},{16,0},{32,48},{48,32},{64,80},{80,64},{96,112},{112,96},{1... | collective-permute-start | bytes 245768 | tf_op jit(solution)/shard_map/ppermute | solution.py:23
  35.7 2.5 %collective-permute-start.7 = (f32[4,16,320]{2,1,0:T(8,128)S(1)}, f32[4,16,320]{2,1,0:T(8,128)S(1)}, u32[]{:S(2)}, u32[]{:S(2)}) collective-permute-start(f32[4,16,320]{2,1,0:T(8,128)S(1)} %fusion.80), channel_id=1, source_target_pairs={{0,64},{16,80},{32,96},{48,112},{64,0},{80,16},{96,32},{112,48},{1... | collective-permute-start | bytes 245768 | tf_op jit(solution)/shard_map/ppermute | solution.py:19
  40.4 2.6 %collective-permute-done.7 = f32[4,16,320]{2,1,0:T(8,128)S(1)} collective-permute-done((f32[4,16,320]{2,1,0:T(8,128)S(1)}, f32[4,16,320]{2,1,0:T(8,128)S(1)}, u32[]{:S(2)}, u32[]{:S(2)}) %collective-permute-start.7) | collective-permute-done | bytes 81952 | tf_op jit(solution)/shard_map/ppermute | solution.py:19
  46.7 1.5 %collective-permute-start.9 = (f32[4,16,320]{2,1,0:T(8,128)S(1)}, f32[4,16,320]{2,1,0:T(8,128)S(1)}, u32[]{:S(2)}, u32[]{:S(2)}) collective-permute-start(f32[4,16,320]{2,1,0:T(8,128)S(1)} %fusion.78), channel_id=1, source_target_pairs={{0,16},{16,0},{32,48},{48,32},{64,80},{80,64},{96,112},{112,96},{1... | collective-permute-start | bytes 245768 | tf_op jit(solution)/shard_map/ppermute | solution.py:23
  49.5 2.3 %convert_multiply_fusion.1 = f32[16,16,2560]{2,0,1:T(8,128)S(1)} fusion(f32[16,2560]{1,0:T(8,128)S(1)} %mul.433, bf16[16,16,2560]{2,1,0:T(8,128)(2,1)} %param.11), kind=kLoop, calls=%fused_computation.9 | loop fusion | flops 1310720 | bytes 4096000 | tf_op jit(solution)/shard_map/mul | solution.py:228
  52.2 2.1 %fusion.112 = (bf16[16,6,1280]{2,0,1:T(8,128)(2,1)S(1)}, f32[16,6,1280]{2,0,1:T(8,128)S(1)}) fusion(bf16[1280,2560]{1,0:T(8,128)(2,1)S(1)} %bitcast.196, f32[16,4,2560]{2,0,1:T(8,128)S(1)} %get-tuple-element.24, f32[16,4,2560]{2,0,1:T(8,128)S(1)} %get-tuple-element.23, f32[16,4,2560]{2,0,1:T(8,128)S(1)} %get-tuple-element.22), kind=kOutput, calls=%fused_computation.235 | convolution fusion | flops 630005760 | bytes 9256960 | tf_op jit(solution)/shard_map/dot_general | solution.py:230
  55.5 4.3 %collective-permute-start.11 = (bf16[16,4,1280]{2,0,1:T(8,128)(2,1)S(1)}, bf16[16,4,1280]{2,0,1:T(8,128)(2,1)S(1)}, u32[]{:S(2)}, u32[]{:S(2)}) collective-permute-start(bf16[16,4,1280]{2,0,1:T(8,128)(2,1)S(1)} %get-tuple-element.36), channel_id=1, source_target_pairs={{0,15},{1,0},{2,1},{3,2},{4,3},{5,4},{6,5},{7,6},{8,7},{9,8},{10,9... | collective-permute-start | bytes 491528 | tf_op jit(solution)/shard_map/ppermute | solution.py:19
  59.7 4.1 %collective-permute-done.10 = bf16[16,4,1280]{2,0,1:T(8,128)(2,1)S(1)} collective-permute-done((bf16[16,4,1280]{2,0,1:T(8,128)(2,1)S(1)}, bf16[16,4,1280]{2,0,1:T(8,128)(2,1)S(1)}, u32[]{:S(2)}, u32[]{:S(2)}) %collective-permute-start.10) | collective-permute-done | bytes 163872 | tf_op jit(solution)/shard_map/ppermute | solution.py:19
  66.0 4.8 %collective-permute-start.13 = (bf16[16,4,1280]{2,0,1:T(8,128)(2,1)S(1)}, bf16[16,4,1280]{2,0,1:T(8,128)(2,1)}, u32[]{:S(2)}, u32[]{:S(2)}) collective-permute-start(bf16[16,4,1280]{2,0,1:T(8,128)(2,1)S(1)} %convert_element_type.159), channel_id=1, source_target_pairs={{0,15},{1,0},{2,1},{3,2},{4,3},{5,4},{6,5},{7,6},{8,7},{9,8},{10,9... | collective-permute-start | bytes 491528 | tf_op jit(solution)/shard_map/ppermute | solution.py:19
  70.7 1.8 %iota_compare_fusion = pred[4,320,1024]{2,1,0:T(32,128)(4,1)} fusion(s32[4,1024]{1,0:T(4,128)S(1)} %copy-done.9), kind=kLoop, calls=%fused_computation.7 | loop fusion | flops 1310720 | bytes 1327104 | tf_op jit(solution)/shard_map/eq | solution.py:112
  72.5 1.7 %collective-permute-done.12 = bf16[16,4,1280]{2,0,1:T(8,128)(2,1)} collective-permute-done((bf16[16,4,1280]{2,0,1:T(8,128)(2,1)S(1)}, bf16[16,4,1280]{2,0,1:T(8,128)(2,1)}, u32[]{:S(2)}, u32[]{:S(2)}) %collective-permute-start.12) | collective-permute-done | bytes 163872 | tf_op jit(solution)/shard_map/ppermute | solution.py:19
  83.0 1.9 %collective-permute-start.14 = (f32[4,16,320]{2,1,0:T(8,128)S(1)}, f32[4,16,320]{2,1,0:T(8,128)S(1)}, u32[]{:S(2)}, u32[]{:S(2)}) collective-permute-start(f32[4,16,320]{2,1,0:T(8,128)S(1)} %bitcast.210), channel_id=1, source_target_pairs={{0,16},{16,0},{32,48},{48,32},{64,80},{80,64},{96,112},{112,96},{1... | collective-permute-start | bytes 245768 | tf_op jit(solution)/shard_map/ppermute | solution.py:23
  86.6 2.2 %collective-permute-start.16 = (f32[4,16,320]{2,1,0:T(8,128)S(1)}, f32[4,16,320]{2,1,0:T(8,128)S(1)}, u32[]{:S(2)}, u32[]{:S(2)}) collective-permute-start(f32[4,16,320]{2,1,0:T(8,128)S(1)} %fusion.79), channel_id=1, source_target_pairs={{0,64},{16,80},{32,96},{48,112},{64,0},{80,16},{96,32},{112,48},{1... | collective-permute-start | bytes 245768 | tf_op jit(solution)/shard_map/ppermute | solution.py:19
  88.8 1.5 %collective-permute-start.17 = (f32[4,16,320]{2,1,0:T(8,128)S(1)}, f32[4,16,320]{2,1,0:T(8,128)S(1)}, u32[]{:S(2)}, u32[]{:S(2)}) collective-permute-start(f32[4,16,320]{2,1,0:T(8,128)S(1)} %fusion.79), channel_id=1, source_target_pairs={{0,96},{16,112},{32,0},{48,16},{64,32},{80,48},{96,64},{112,80},{1... | collective-permute-start | bytes 245768 | tf_op jit(solution)/shard_map/ppermute | solution.py:19
  91.1 2.4 %collective-permute-done.16 = f32[4,16,320]{2,1,0:T(8,128)S(1)} collective-permute-done((f32[4,16,320]{2,1,0:T(8,128)S(1)}, f32[4,16,320]{2,1,0:T(8,128)S(1)}, u32[]{:S(2)}, u32[]{:S(2)}) %collective-permute-start.16) | collective-permute-done | bytes 81952 | tf_op jit(solution)/shard_map/ppermute | solution.py:19
  93.8 1.3 %fusion.15 = f32[1,64,1024]{2,1,0:T(8,128)S(1)} fusion(pred[4,320,1024]{2,1,0:T(32,128)(4,1)} %iota_compare_fusion, s32[]{:T(128)S(6)} %select_n.137, bf16[1,32,320]{2,1,0:T(8,128)(2,1)S(1)} %get-tuple-element.52, bf16[1,32,320]{2,1,0:T(8,128)(2,1)S(1)} %get-tuple-element.51), kind=kOutput, calls=%fused_computation.22 | convolution fusion | flops 42024960 | bytes 630788 | tf_op jit(solution)/shard_map/yrc,ycn->yrn/dot_general | solution.py:124
  95.1 1.4 %fusion.96 = f32[]{:T(128)} fusion(f32[1,1024]{1,0:T(1,128)S(1)} %bitcast.220, f32[4,1024]{1,0:T(4,128)} %copy-done.6, s32[]{:T(128)S(6)} %select_n.137, f32[4,1024]{1,0:T(4,128)} %get-tuple-element.53, f32[4,1024]{1,0:T(4,128)S(1)} %bitcast.215), kind=kLoop, calls=%fused_computation.203 | loop fusion | flops 6143 | bytes 16392 | tf_op jit(solution)/shard_map/reduce_sum | solution.py:256
  97.8 18.2 %all_to_all.18 = f32[128,1,128]{2,1,0:T(1,128)S(1)} all-to-all(f32[128,1,128]{2,1,0:T(1,128)S(1)} %broadcast_in_dim.84), channel_id=1, replica_groups=mesh['member'=8,'tile'=16] {'member','tile'}, dimensions={0} | all-to-all | bytes 131072 | tf_op jit(solution)/shard_map/all_to_all | solution.py:258
  (175 shorter events, 40.1 us)
Async XLA Ops:
  1.7 23.6 %collective-permute-start.3 = (bf16[16,4,1280]{2,0,1:T(8,128)(2,1)S(1)}, bf16[16,4,1280]{2,0,1:T(8,128)(2,1)S(1)}, u32[]{:S(2)}, u32[]{:S(2)}) collective-permute-start(bf16[16,4,1280]{2,0,1:T(8,128)(2,1)S(1)} %copy.208), channel_id=1, source_target_pairs={{0,1},{1,2},{2,3},{3,4},{4,5},{5,6},{6,7},{7,8},{8,9},{9,10},{10,1... | collective-permute-start | bytes 491528 | tf_op jit(solution)/shard_map/ppermute | solution.py:19
  3.8 21.5 %collective-permute-start.4 = (bf16[16,4,1280]{2,0,1:T(8,128)(2,1)S(1)}, bf16[16,4,1280]{2,0,1:T(8,128)(2,1)S(1)}, u32[]{:S(2)}, u32[]{:S(2)}) collective-permute-start(bf16[16,4,1280]{2,0,1:T(8,128)(2,1)S(1)} %copy.208), channel_id=1, source_target_pairs={{0,15},{1,0},{2,1},{3,2},{4,3},{5,4},{6,5},{7,6},{8,7},{9,8},{10,9... | collective-permute-start | bytes 491528 | tf_op jit(solution)/shard_map/ppermute | solution.py:19
  8.6 25.5 %collective-permute-start = (f32[16,320]{1,0:T(8,128)}, f32[16,320]{1,0:T(8,128)S(1)}, u32[]{:S(2)}, u32[]{:S(2)}) collective-permute-start(f32[16,320]{1,0:T(8,128)} %param.14), channel_id=1, source_target_pairs={{0,32},{16,48},{32,64},{48,80},{64,96},{80,112},{96,0},{112,16},{1... | collective-permute-start | bytes 61448 | tf_op jit(solution)/shard_map/ppermute | solution.py:19
  9.9 24.2 %collective-permute-start.1 = (f32[16,320]{1,0:T(8,128)}, f32[16,320]{1,0:T(8,128)S(1)}, u32[]{:S(2)}, u32[]{:S(2)}) collective-permute-start(f32[16,320]{1,0:T(8,128)} %param.14), channel_id=1, source_target_pairs={{0,64},{16,80},{32,96},{48,112},{64,0},{80,16},{96,32},{112,48},{1... | collective-permute-start | bytes 61448 | tf_op jit(solution)/shard_map/ppermute | solution.py:19
  12.5 21.6 %collective-permute-start.2 = (f32[16,320]{1,0:T(8,128)}, f32[16,320]{1,0:T(8,128)S(1)}, u32[]{:S(2)}, u32[]{:S(2)}) collective-permute-start(f32[16,320]{1,0:T(8,128)} %param.14), channel_id=1, source_target_pairs={{0,96},{16,112},{32,0},{48,16},{64,32},{80,48},{96,64},{112,80},{1... | collective-permute-start | bytes 61448 | tf_op jit(solution)/shard_map/ppermute | solution.py:19
  15.8 18.9 %all-to-all-start = ((f32[128,1,128]{2,1,0:T(1,128)}), f32[128,1,128]{2,1,0:T(1,128)S(1)}, u32[]{:S(2)}, u32[]{:S(2)}) async-start(f32[128,1,128]{2,1,0:T(1,128)} %bitcast.14), calls=%async_computation | async-start | bytes 131072 | tf_op jit(solution)/shard_map/all_to_all | solution.py:187
  24.1 20.5 %copy-start.4 = (f32[1,4,8,128]{3,2,1,0:T(8,128)}, f32[1,4,8,128]{3,2,1,0:T(8,128)S(1)}, u32[]{:S(2)}) copy-start(f32[1,4,8,128]{3,2,1,0:T(8,128)S(1)} %convert_bitcast_fusion) | copy-start | bytes 49156
  24.1 19.3 %copy-start.7 = (s32[4,1024]{1,0:T(4,128)}, s32[4,1024]{1,0:T(4,128)S(1)}, u32[]{:S(2)}) copy-start(s32[4,1024]{1,0:T(4,128)S(1)} %get-tuple-element.57) | copy-start | bytes 49156
  32.8 2.2 %collective-permute-start.5 = (f32[4,16,320]{2,1,0:T(8,128)S(1)}, f32[4,16,320]{2,1,0:T(8,128)S(1)}, u32[]{:S(2)}, u32[]{:S(2)}) collective-permute-start(f32[4,16,320]{2,1,0:T(8,128)S(1)} %bitcast.209), channel_id=1, source_target_pairs={{0,16},{16,0},{32,48},{48,32},{64,80},{80,64},{96,112},{112,96},{1... | collective-permute-start | bytes 245768 | tf_op jit(solution)/shard_map/ppermute | solution.py:23
  35.1 5.3 %collective-permute-start.6 = (f32[4,16,320]{2,1,0:T(8,128)S(1)}, f32[4,16,320]{2,1,0:T(8,128)S(1)}, u32[]{:S(2)}, u32[]{:S(2)}) collective-permute-start(f32[4,16,320]{2,1,0:T(8,128)S(1)} %fusion.80), channel_id=1, source_target_pairs={{0,32},{16,48},{32,64},{48,80},{64,96},{80,112},{96,0},{112,16},{1... | collective-permute-start | bytes 245768 | tf_op jit(solution)/shard_map/ppermute | solution.py:19
  35.7 7.2 %collective-permute-start.7 = (f32[4,16,320]{2,1,0:T(8,128)S(1)}, f32[4,16,320]{2,1,0:T(8,128)S(1)}, u32[]{:S(2)}, u32[]{:S(2)}) collective-permute-start(f32[4,16,320]{2,1,0:T(8,128)S(1)} %fusion.80), channel_id=1, source_target_pairs={{0,64},{16,80},{32,96},{48,112},{64,0},{80,16},{96,32},{112,48},{1... | collective-permute-start | bytes 245768 | tf_op jit(solution)/shard_map/ppermute | solution.py:19
  38.3 4.8 %collective-permute-start.8 = (f32[4,16,320]{2,1,0:T(8,128)S(1)}, f32[4,16,320]{2,1,0:T(8,128)S(1)}, u32[]{:S(2)}, u32[]{:S(2)}) collective-permute-start(f32[4,16,320]{2,1,0:T(8,128)S(1)} %fusion.80), channel_id=1, source_target_pairs={{0,96},{16,112},{32,0},{48,16},{64,32},{80,48},{96,64},{112,80},{1... | collective-permute-start | bytes 245768 | tf_op jit(solution)/shard_map/ppermute | solution.py:19
  46.7 2.4 %collective-permute-start.9 = (f32[4,16,320]{2,1,0:T(8,128)S(1)}, f32[4,16,320]{2,1,0:T(8,128)S(1)}, u32[]{:S(2)}, u32[]{:S(2)}) collective-permute-start(f32[4,16,320]{2,1,0:T(8,128)S(1)} %fusion.78), channel_id=1, source_target_pairs={{0,16},{16,0},{32,48},{48,32},{64,80},{80,64},{96,112},{112,96},{1... | collective-permute-start | bytes 245768 | tf_op jit(solution)/shard_map/ppermute | solution.py:23
  52.2 11.7 %copy-start.15 = (f32[10]{0:T(128)S(1)}, f32[10]{0:T(128)}, u32[]{:S(2)}) copy-start(f32[10]{0:T(128)} %copy-done.14) | copy-start | bytes 124
  54.3 9.7 %copy-start.18 = (f32[8]{0:T(128)S(1)}, f32[8]{0:T(128)}, u32[]{:S(2)}) copy-start(f32[8]{0:T(128)} %copy-done.17) | copy-start | bytes 100
  54.4 9.5 %collective-permute-start.10 = (bf16[16,4,1280]{2,0,1:T(8,128)(2,1)S(1)}, bf16[16,4,1280]{2,0,1:T(8,128)(2,1)S(1)}, u32[]{:S(2)}, u32[]{:S(2)}) collective-permute-start(bf16[16,4,1280]{2,0,1:T(8,128)(2,1)S(1)} %get-tuple-element.35), channel_id=1, source_target_pairs={{0,1},{1,2},{2,3},{3,4},{4,5},{5,6},{6,7},{7,8},{8,9},{9,10},{10,1... | collective-permute-start | bytes 491528 | tf_op jit(solution)/shard_map/ppermute | solution.py:19
  55.5 8.4 %collective-permute-start.11 = (bf16[16,4,1280]{2,0,1:T(8,128)(2,1)S(1)}, bf16[16,4,1280]{2,0,1:T(8,128)(2,1)S(1)}, u32[]{:S(2)}, u32[]{:S(2)}) collective-permute-start(bf16[16,4,1280]{2,0,1:T(8,128)(2,1)S(1)} %get-tuple-element.36), channel_id=1, source_target_pairs={{0,15},{1,0},{2,1},{3,2},{4,3},{5,4},{6,5},{7,6},{8,7},{9,8},{10,9... | collective-permute-start | bytes 491528 | tf_op jit(solution)/shard_map/ppermute | solution.py:19
  65.1 12.3 %slice-start.2 = ((s8[6553600]{0:T(1024)(128)(4,1)}), s8[2359296]{0:T(1024)(128)(4,1)S(1)}, s32[]{:S(2)}) async-start(s8[6553600]{0:T(1024)(128)(4,1)} %bitcast.197), calls=%async_computation.4 | async-start | bytes 4718592
  65.9 8.3 %collective-permute-start.12 = (bf16[16,4,1280]{2,0,1:T(8,128)(2,1)S(1)}, bf16[16,4,1280]{2,0,1:T(8,128)(2,1)}, u32[]{:S(2)}, u32[]{:S(2)}) collective-permute-start(bf16[16,4,1280]{2,0,1:T(8,128)(2,1)S(1)} %convert_element_type.159), channel_id=1, source_target_pairs={{0,1},{1,2},{2,3},{3,4},{4,5},{5,6},{6,7},{7,8},{8,9},{9,10},{10,1... | collective-permute-start | bytes 491528 | tf_op jit(solution)/shard_map/ppermute | solution.py:19
  66.0 9.2 %collective-permute-start.13 = (bf16[16,4,1280]{2,0,1:T(8,128)(2,1)S(1)}, bf16[16,4,1280]{2,0,1:T(8,128)(2,1)}, u32[]{:S(2)}, u32[]{:S(2)}) collective-permute-start(bf16[16,4,1280]{2,0,1:T(8,128)(2,1)S(1)} %convert_element_type.159), channel_id=1, source_target_pairs={{0,15},{1,0},{2,1},{3,2},{4,3},{5,4},{6,5},{7,6},{8,7},{9,8},{10,9... | collective-permute-start | bytes 491528 | tf_op jit(solution)/shard_map/ppermute | solution.py:19
  83.0 2.8 %collective-permute-start.14 = (f32[4,16,320]{2,1,0:T(8,128)S(1)}, f32[4,16,320]{2,1,0:T(8,128)S(1)}, u32[]{:S(2)}, u32[]{:S(2)}) collective-permute-start(f32[4,16,320]{2,1,0:T(8,128)S(1)} %bitcast.210), channel_id=1, source_target_pairs={{0,16},{16,0},{32,48},{48,32},{64,80},{80,64},{96,112},{112,96},{1... | collective-permute-start | bytes 245768 | tf_op jit(solution)/shard_map/ppermute | solution.py:23
  85.8 5.3 %collective-permute-start.15 = (f32[4,16,320]{2,1,0:T(8,128)S(1)}, f32[4,16,320]{2,1,0:T(8,128)S(1)}, u32[]{:S(2)}, u32[]{:S(2)}) collective-permute-start(f32[4,16,320]{2,1,0:T(8,128)S(1)} %fusion.79), channel_id=1, source_target_pairs={{0,32},{16,48},{32,64},{48,80},{64,96},{80,112},{96,0},{112,16},{1... | collective-permute-start | bytes 245768 | tf_op jit(solution)/shard_map/ppermute | solution.py:19
  86.6 6.8 %collective-permute-start.16 = (f32[4,16,320]{2,1,0:T(8,128)S(1)}, f32[4,16,320]{2,1,0:T(8,128)S(1)}, u32[]{:S(2)}, u32[]{:S(2)}) collective-permute-start(f32[4,16,320]{2,1,0:T(8,128)S(1)} %fusion.79), channel_id=1, source_target_pairs={{0,64},{16,80},{32,96},{48,112},{64,0},{80,16},{96,32},{112,48},{1... | collective-permute-start | bytes 245768 | tf_op jit(solution)/shard_map/ppermute | solution.py:19
  88.8 4.8 %collective-permute-start.17 = (f32[4,16,320]{2,1,0:T(8,128)S(1)}, f32[4,16,320]{2,1,0:T(8,128)S(1)}, u32[]{:S(2)}, u32[]{:S(2)}) collective-permute-start(f32[4,16,320]{2,1,0:T(8,128)S(1)} %fusion.79), channel_id=1, source_target_pairs={{0,96},{16,112},{32,0},{48,16},{64,32},{80,48},{96,64},{112,80},{1... | collective-permute-start | bytes 245768 | tf_op jit(solution)/shard_map/ppermute | solution.py:19
  (20 other events, 65.2 us)

commit v2 on v1

v2 whole, which is shorter than its diff:
```python
import jax
import jax.numpy as jnp
import numpy as np
from jax import lax
from jax.experimental import pallas as pl
from jax.experimental.pallas import tpu as pltpu
from jax.sharding import PartitionSpec as P

RATIO = 4
KSM = 3
DIFFUSION = 0.45
NTILE = 16
NMEMBER = 8
NCORE = 2
NY = NMEMBER // NCORE
MEMBERS_HERE = 16
ROWS = 4
FINE_ROWS = 16
COARSE_COLS = 1280
FINE_COLS = 2560
WIDTH = 320
CHUNK = NCORE * WIDTH
SLOTS = 8
BATCHES = 128
FLOAT, HALF = jnp.float32, jnp.bfloat16


def refine_matrix():
    table = np.zeros((FINE_ROWS, ROWS + 2))
    for row in range(ROWS):
        for offset in range(RATIO):
            shift = (offset + 0.5) / RATIO - 0.5
            fine = RATIO * row + offset
            if shift < 0:
                table[fine, row + 1] += 1.0 + shift
                table[fine, row] -= shift
            else:
                table[fine, row + 1] += 1.0 - shift
                table[fine, row + 2] += shift
    return table


def member_matrix():
    return np.einsum("fr,kl->kfrl", refine_matrix(), np.eye(MEMBERS_HERE)).reshape(
        MEMBERS_HERE * FINE_ROWS, (ROWS + 2) * MEMBERS_HERE
    )


def turn(values, step, axis):
    count = lax.axis_size(axis)
    return lax.ppermute(values, axis, [(i, (i + step) % count) for i in range(count)])


def swap_core(values):
    return lax.ppermute(values, "member", [(i, i ^ 1) for i in range(NMEMBER)])


VMEM = pl.BlockSpec(memory_space=pltpu.VMEM)
SMEM = pl.BlockSpec(memory_space=pltpu.SMEM)


def call(kernel, out_shapes, arguments, smem=0, scratch=()):
    specs = [SMEM] * smem + [VMEM] * (len(arguments) - smem)
    return pl.pallas_call(
        kernel,
        out_shape=out_shapes,
        in_specs=specs,
        out_specs=jax.tree.map(lambda _: VMEM, out_shapes),
        scratch_shapes=list(scratch),
    )(*arguments)


def swept(rows, masks):
    for _ in range(KSM):
        rows = [v if m is None else v * m for v, m in zip(rows, masks)]
        rows = [
            rows[i] + DIFFUSION * (rows[i - 1] + rows[i + 1] - 2.0 * rows[i])
            for i in range(1, len(rows) - 1)
        ]
        masks = masks[1:-1]
    return [v if m is None else v * m for v, m in zip(rows, masks)]


def row_slice(row):
    return pl.ds(row * MEMBERS_HERE, MEMBERS_HERE)


def forward_kernel(
    place_ref, low_ref, own_ref, high_ref, perturb_ref, map_ref, refine_ref, out_ref, smooth_ref
):
    tile_pos, core_pos = place_ref[0], place_ref[1]
    below = jnp.where(tile_pos > 0, 1.0, 0.0)
    above = jnp.where(tile_pos < NTILE - 1, 1.0, 0.0)
    masks = [below] * 4 + [None] * 4 + [above] * 4
    for start in range(0, COARSE_COLS, 128):
        cols = pl.ds(start, 128)
        rows = [low_ref[row_slice(r), cols].astype(FLOAT) for r in range(4)]
        rows += [own_ref[row_slice(r), cols] for r in range(4)]
        rows += [high_ref[row_slice(r), cols].astype(FLOAT) for r in range(4)]
        for r, value in enumerate(swept(rows, masks)[0:]):
            smooth_ref[row_slice(r), cols] = value.astype(HALF)
    smooth = smooth_ref[...]
    for y in range(NY):
        cols = pl.ds(y * CHUNK, CHUNK)
        mapped = jnp.dot(smooth, map_ref[:, cols], preferred_element_type=FLOAT)
        high = mapped.astype(HALF)
        low = (mapped - high.astype(FLOAT)).astype(HALF)
        fine = jnp.dot(
            refine_ref[...], jnp.concatenate([high, low], axis=0), preferred_element_type=FLOAT
        )
        total = None
        for k in range(MEMBERS_HERE):
            term = fine[k * FINE_ROWS : (k + 1) * FINE_ROWS] * perturb_ref[k, :, cols].astype(FLOAT)
            total = term if total is None else total + term
        out_ref[core_pos, y] = total[:, :WIDTH]
        out_ref[1 - core_pos, y] = total[:, WIDTH:]


def partial_forward(place, low, own, high, perturb, column_map):
    matrix = member_matrix()
    matrix = jnp.asarray(np.concatenate([matrix, matrix], axis=1), HALF)
    return call(
        forward_kernel,
        jax.ShapeDtypeStruct((NCORE, NY, FINE_ROWS, WIDTH), FLOAT),
        (place, low, own, high, perturb, column_map, matrix),
        smem=1,
        scratch=[pltpu.VMEM(((ROWS + 2) * MEMBERS_HERE, COARSE_COLS), HALF)],
    )


def adjoint_kernel(
    place_ref, mine_ref, other_ref, perturb_ref, map_ref, back_ref, part_ref, up_ref, down_ref
):
    core_pos = place_ref[1]
    total = None
    for y in range(NY):
        cols = pl.ds(y * CHUNK, CHUNK)
        mine, other = mine_ref[y], other_ref[y]
        first = jnp.where(core_pos == 0, mine, other)
        second = jnp.where(core_pos == 0, other, mine)
        spread = jnp.concatenate([first, second], axis=1)
        highs, lows = [], []
        for k in range(MEMBERS_HERE):
            term = perturb_ref[k, :, cols].astype(FLOAT) * spread
            high = term.astype(HALF)
            highs.append(high)
            lows.append((term - high.astype(FLOAT)).astype(HALF))
        pulled = jnp.dot(
            back_ref[...], jnp.concatenate(highs + lows, axis=0), preferred_element_type=FLOAT
        )
        part = lax.dot_general(
            pulled.astype(HALF),
            map_ref[:, cols],
            (((1,), (1,)), ((), ())),
            preferred_element_type=FLOAT,
        )
        total = part if total is None else total + part
    part_ref[...] = total
    up_ref[...] = total[2 * MEMBERS_HERE :].astype(HALF)
    down_ref[...] = total[: 4 * MEMBERS_HERE].astype(HALF)


def partial_adjoint(place, mine, other, perturb, column_map):
    matrix = member_matrix().T
    matrix = jnp.asarray(np.concatenate([matrix, matrix], axis=1), HALF)
    rim = jax.ShapeDtypeStruct((4 * MEMBERS_HERE, COARSE_COLS), HALF)
    return call(
        adjoint_kernel,
        (jax.ShapeDtypeStruct(((ROWS + 2) * MEMBERS_HERE, COARSE_COLS), FLOAT), rim, rim),
        (place, mine, other, perturb, column_map, matrix),
        smem=1,
    )


def gradient_kernel(place_ref, low_ref, part_ref, high_ref, own_ref, grad_ref, half_ref, square_ref):
    tile_pos = place_ref[0]
    below = jnp.where(tile_pos > 0, 1.0, 0.0)
    above = jnp.where(tile_pos < NTILE - 1, 1.0, 0.0)
    masks = [below] * 3 + [None] * 4 + [above] * 3
    square = None
    for start in range(0, COARSE_COLS, 128):
        cols = pl.ds(start, 128)
        low = [low_ref[row_slice(r), cols].astype(FLOAT) for r in range(4)]
        part = [part_ref[row_slice(r), cols] for r in range(6)]
        high = [high_ref[row_slice(r), cols].astype(FLOAT) for r in range(4)]
        rows = [low[0], low[1], low[2] + part[0], low[3] * below + part[1], part[2], part[3]]
        rows += [part[4] + high[0] * above, part[5] + high[1], high[2], high[3]]
        for r, value in enumerate(swept(rows, masks)):
            gradient = own_ref[row_slice(r), cols] + value
            grad_ref[row_slice(r), cols] = gradient
            half_ref[row_slice(r), cols] = gradient.astype(HALF)
            term = gradient * gradient
            square = term if square is None else square + term
    square_ref[...] = square[:8] + square[8:]


def gradient_of(place, low, part, high, own):
    shape = (ROWS * MEMBERS_HERE, COARSE_COLS)
    return call(
        gradient_kernel,
        (
            jax.ShapeDtypeStruct(shape, FLOAT),
            jax.ShapeDtypeStruct(shape, HALF),
            jax.ShapeDtypeStruct((8, 128), FLOAT),
        ),
        (place, low, part, high, own),
        smem=1,
    )


def column_picks(column):
    ids = lax.broadcasted_iota(jnp.int32, (WIDTH, BATCHES), 0)
    return jnp.concatenate(
        [(ids == column[s : s + 1]).astype(FLOAT).astype(HALF) for s in range(SLOTS)], axis=1
    )


def row_factors(row, fraction):
    ids = lax.broadcasted_iota(jnp.int32, (FINE_ROWS, BATCHES), 0)
    return jnp.concatenate(
        [
            jnp.where(ids == row[s : s + 1], 1.0 - fraction[s : s + 1], 0.0)
            + jnp.where(ids == row[s : s + 1] + 1, fraction[s : s + 1], 0.0)
            for s in range(SLOTS)
        ],
        axis=1,
    )


def on_lanes(values):
    return jnp.concatenate([values[s : s + 1] for s in range(SLOTS)], axis=1)


def on_slots(values):
    return jnp.concatenate(
        [values[:, s * BATCHES : (s + 1) * BATCHES] for s in range(SLOTS)], axis=0
    )


def halves(values):
    high = values.astype(HALF)
    return jnp.concatenate([high, (values - high.astype(FLOAT)).astype(HALF)], axis=0)


def interpolated(field, picks, factors, fraction):
    got = jnp.dot(halves(field), picks, preferred_element_type=FLOAT)
    left = got[:FINE_ROWS] + got[FINE_ROWS:]
    shifted = jnp.concatenate([field[:, 1:], field[:, :1]], axis=1)
    got = jnp.dot(halves(shifted), picks, preferred_element_type=FLOAT)
    right = got[:FINE_ROWS] + got[FINE_ROWS:]
    mixed = left * (1.0 - fraction) + right * fraction
    return on_slots(jnp.sum(mixed * factors, axis=0, keepdims=True))


def located(index):
    row = index // WIDTH
    return row, index - row * WIDTH


def obs_kernel(
    place_ref, a_ref, b_ref, c_ref, d_ref, index_ref, row_ref, column_ref, live_ref, data_ref,
    spread_ref, weight_ref, full_ref,
):
    own = place_ref[2]
    data = jnp.transpose(data_ref[...])
    for y in range(NY):
        field = a_ref[y] + b_ref[y] + c_ref[y] + d_ref[y]
        row, column = located(index_ref[y])
        picks = column_picks(column)
        factors = row_factors(row, row_ref[y])
        fraction = on_lanes(column_ref[y])
        state = interpolated(field, picks, factors, fraction)
        value = data[y * SLOTS : (y + 1) * SLOTS]
        error = data[(NY + y) * SLOTS : (NY + y + 1) * SLOTS]
        gain = data[2 * NY * SLOTS : 2 * NY * SLOTS + SLOTS]
        bounded = jnp.tanh(state)
        derivative = 1.0 + gain * (1.0 - bounded * bounded)
        misfit = state + gain * bounded - value
        precision = live_ref[y] / (error * error)
        residual = derivative * misfit * precision
        weight_ref[y] = derivative * derivative * precision
        full_ref[y] = field
        weighted = factors * on_lanes(residual)
        spread = []
        for part in (weighted * (1.0 - fraction), weighted * fraction):
            got = lax.dot_general(
                halves(part), picks, (((1,), (1,)), ((), ())), preferred_element_type=FLOAT
            )
            spread.append(got[:FINE_ROWS] + got[FINE_ROWS:])
        left, right = spread
        spread_ref[y] = left + jnp.concatenate([right[:, -1:], right[:, :-1]], axis=1)


def obs_spread(place, pieces, index, row_frac, column_frac, live, data):
    regions = jax.ShapeDtypeStruct((NY, FINE_ROWS, WIDTH), FLOAT)
    return call(
        obs_kernel,
        (regions, jax.ShapeDtypeStruct((NY, SLOTS, BATCHES), FLOAT), regions),
        (place, *pieces, index, row_frac, column_frac, live, data),
        smem=1,
    )


def curve_kernel(
    place_ref, a_ref, b_ref, c_ref, d_ref, index_ref, row_ref, column_ref, weight_ref, square_ref,
    field_ref, sent_ref,
):
    own = place_ref[2]
    field = a_ref[...] + b_ref[...] + c_ref[...] + d_ref[...]
    field_ref[...] = field
    row, column = located(index_ref[own])
    observed = interpolated(
        field, column_picks(column), row_factors(row, row_ref[own]), on_lanes(column_ref[own])
    )
    curvature = jnp.sum(weight_ref[own] * observed * observed, keepdims=True)
    square = jnp.sum(square_ref[...], keepdims=True)
    lanes = lax.broadcasted_iota(jnp.int32, (BATCHES, 128), 1)
    sent_ref[...] = jnp.where(lanes < 64, square, curvature)


def curve_of(place, pieces, index, row_frac, column_frac, weight, square):
    return call(
        curve_kernel,
        (
            jax.ShapeDtypeStruct((FINE_ROWS, WIDTH), FLOAT),
            jax.ShapeDtypeStruct((BATCHES, 128), FLOAT),
        ),
        (place, *pieces, index, row_frac, column_frac, weight, square),
        smem=1,
    )


def step_kernel(
    place_ref, shared_ref, own_ref, grad_ref, full_ref, base_ref, image_ref, coarse_ref, increment_ref
):
    totals = jnp.sum(shared_ref[...], axis=0, keepdims=True)
    lanes = lax.broadcasted_iota(jnp.int32, (1, 128), 1)
    square = jnp.sum(jnp.where(lanes == 0, totals, 0.0), keepdims=True)
    curvature = jnp.sum(jnp.where(lanes == 127, totals, 0.0), keepdims=True)
    step = square / (square + curvature)
    coarse_ref[...] = own_ref[...] - step * grad_ref[...]
    increment_ref[...] = full_ref[place_ref[2]] - base_ref[...] - step * image_ref[...]


def stepped(place, shared, own, gradient, full, base, image):
    return call(
        step_kernel,
        (
            jax.ShapeDtypeStruct(own.shape, FLOAT),
            jax.ShapeDtypeStruct((FINE_ROWS, WIDTH), FLOAT),
        ),
        (place, shared, own, gradient, full, base, image),
        smem=1,
    )


def shards(
    perturb,
    weights,
    column_map,
    background,
    stencil_index,
    row_fraction,
    column_fraction,
    block_lengths,
    obs_value,
    obs_error,
    instrument_gain,
):
    member_pos = lax.axis_index("member")
    core_pos = member_pos % NCORE
    y_pos = member_pos // NCORE
    tile_pos = lax.axis_index("tile")
    place = jnp.stack([tile_pos, core_pos, y_pos]).astype(jnp.int32)

    flat = (ROWS * MEMBERS_HERE, COARSE_COLS)
    own = jnp.transpose(weights, (1, 0, 2)).reshape(flat)
    half = own.astype(HALF)
    low, high = turn(half, 1, "tile"), turn(half, -1, "tile")

    stacked = jnp.stack([obs_value[0], obs_error[0]])
    stacked = stacked.reshape(2, NY, NCORE, NTILE, SLOTS)
    stacked = jnp.transpose(stacked, (2, 3, 0, 1, 4)).reshape(NCORE, NTILE, 2 * NY * SLOTS)
    gains = jnp.broadcast_to(instrument_gain, (NCORE, NTILE, 2 * NY * SLOTS))
    stacked = jnp.concatenate([stacked, gains], axis=-1)
    sent = jnp.broadcast_to(stacked[None], (NY,) + stacked.shape).reshape(BATCHES, -1)
    data = lax.all_to_all(sent, ("member", "tile"), split_axis=0, concat_axis=0, tiled=True)

    def of_core(array):
        mine = lax.dynamic_index_in_dim(
            array.reshape(BATCHES, NY, NCORE, SLOTS), core_pos, 2, False
        )
        return jnp.transpose(mine, (1, 2, 0))

    index = of_core(stencil_index[0])
    row_frac = of_core(row_fraction[0])
    column_frac = of_core(column_fraction[0])
    slot_ids = lax.broadcasted_iota(jnp.int32, stencil_index.shape[1:], 2)
    live = of_core((slot_ids < block_lengths[0][:, :, None]).astype(FLOAT))

    first = partial_forward(place, low, own, high, perturb, column_map)
    ours = (jnp.arange(NY) == y_pos).astype(FLOAT)[:, None, None]
    mine = first[0] + swap_core(first[1]) + ours * background
    pieces = [mine] + [turn(mine, NCORE * i, "member") for i in range(1, NY)]
    spread, weight, full = obs_spread(place, pieces, index, row_frac, column_frac, live, data)
    part, up, down = partial_adjoint(place, spread, swap_core(spread), perturb, column_map)
    gradient, half, square = gradient_of(
        place, turn(up, 1, "tile"), part, turn(down, -1, "tile"), own
    )
    second = partial_forward(
        place, turn(half, 1, "tile"), gradient, turn(half, -1, "tile"), perturb, column_map
    )
    mine = second[0] + swap_core(second[1])

    def region(step):
        return lax.dynamic_index_in_dim(mine, (y_pos + step) % NY, 0, False)

    pieces = [region(0)] + [turn(region(i), NCORE * i, "member") for i in range(1, NY)]
    image, sent = curve_of(place, pieces, index, row_frac, column_frac, weight, square)
    shared = lax.all_to_all(sent, ("member", "tile"), split_axis=0, concat_axis=0, tiled=True)
    coarse, increment = stepped(place, shared, own, gradient, full, background, image)
    coarse = jnp.transpose(coarse.reshape(ROWS, MEMBERS_HERE, COARSE_COLS), (1, 0, 2))
    return coarse, increment


def solution(mesh):
    placed = (
        P("member", "tile", None),
        P("member", "tile", None),
        P(),
        P("tile", "member"),
        P("tile", None, None, None),
        P("tile", None, None, None),
        P("tile", None, None, None),
        P("tile", None, None),
        P(("member", "tile"), None, None),
        P(("member", "tile"), None, None),
        P(("member", "tile")),
    )
    return jax.shard_map(
        shards,
        mesh=mesh,
        in_specs=placed,
        out_specs=(P("member", "tile", None), P("tile", "member")),
        check_vma=False,
    )
```

time: 121 us -> 123 us (1.017)
  Pallas kernels: 0 us -> 31.1 us
  other arithmetic: 19.7 us -> 3.81 us
  matrix products: 7.93 us -> 0 us
  waiting for transfers between devices: 14.9 us -> 20 us
  starting transfers between devices: 40.7 us -> 36.9 us
  between operations: 4.13 us -> 1.45 us
  blocking collectives: 18.2 us -> 16.2 us
  local copies, waits for them, and re-layouts: 14.7 us -> 12.8 us
    pallas_call x0 -> x7, Pallas kernels: none -> 31.1 us  [call(): pl.pallas_call(kernel, out_shape=out_shapes, in_specs=specs, out_specs=ja...]
    dot_general x6 -> x0, matrix products: 7.93 us -> none  [the longest x2 2.44 us: partial_forward(): jnp.dot(smooth.astype(HALF).reshape(-1, coarse_cols), column_map, preferr...]
    unnamed x60 -> x37, local copies, waits for them, and re-layouts: 10 us -> 4.02 us
    ppermute x15 -> x12, starting transfers between devices: 30.9 us -> 25.3 us  [turn(): lax.ppermute(values, axis, [(i, (i + step) % count) for i in range(count)])]
    reduce_sum x7 -> x0, other arithmetic: 4.69 us -> none  [the longest x2 2.27 us: partial_forward(): return jnp.sum(fine_field * perturb, axis=0)]
    mul x13 -> x0, other arithmetic: 4.5 us -> none  [the longest x1 2.31 us: shards(): pulled = refine_adjoint(perturb * spread).astype(HALF)]
    ppermute x15 -> x12, waiting for transfers between devices: 12.7 us -> 16.9 us  [turn(): lax.ppermute(values, axis, [(i, (i + step) % count) for i in range(count)])]
    transpose x1 -> x3, local copies, waits for them, and re-layouts: 0.15 us -> 2.99 us  [the longest x2 1.94 us: of_core(): return jnp.transpose(mine, (1, 2, 0))]
  transfers between devices with their start and end apart: 19 -> 16, of which waited for: 11 -> 11; matrix products, arithmetic and copies ran while one was open for 11% -> 6% of each run, Pallas kernels for 0% -> 5%
where the time goes in v2:
time: 123 us; the launch traced here: 122 us
  starting transfers between devices  36.9 us (30%)
  Pallas kernels  31.1 us (25%)
  waiting for transfers between devices  20 us (16%)
  blocking collectives  16.2 us (13%)
  local copies, waits for them, and re-layouts  12.8 us (10%)
  other arithmetic  3.81 us (3%)
  between operations  1.45 us (1%)
    pallas_call x7, Pallas kernels, call(): pl.pallas_call(kernel, out_shape=out_shapes, in_specs=specs, out_specs=ja...  31.1 us
    ppermute x12, starting transfers between devices, turn(): lax.ppermute(values, axis, [(i, (i + step) % count) for i in range(count)])  25.3 us
    ppermute x12, waiting for transfers between devices, turn(): lax.ppermute(values, axis, [(i, (i + step) % count) for i in range(count)])  16.9 us
    all_to_all x1, blocking collectives, shards(): lax.all_to_all(sent, ('member', 'tile'), split_axis=0, concat_axis=0, til...  16.2 us
    all_to_all x1, starting transfers between devices, shards(): lax.all_to_all(sent, ('member', 'tile'), split_axis=0, concat_axis=0, til...  6.66 us
    ppermute x3, starting transfers between devices, swap_core(): return lax.ppermute(values, 'member', [(i, i ^ 1) for i in range(NMEMBER)])  4.92 us
    unnamed x37, local copies, waits for them, and re-layouts  4.02 us
    ppermute x3, waiting for transfers between devices, swap_core(): return lax.ppermute(values, 'member', [(i, i ^ 1) for i in range(NMEMBER)])  3.04 us
  transfers between devices with their start and end apart: 16, of which 11 were waited for; matrix products, arithmetic and copies ran while one was open for 6% of the time, Pallas kernels for 5%

profile of v2, /device:TPU:1, one launch (start us, length us, event | category | flops | bytes accessed | tf_op | source)
XLA Modules:
  0.0 122.2 jit_solution(14903565520349287266)
XLA Ops:
  1.7 2.1 %collective-permute-start = (bf16[64,1280]{1,0:T(8,128)(2,1)S(1)}, bf16[64,1280]{1,0:T(8,128)(2,1)S(1)}, u32[]{:S(2)}, u32[]{:S(2)}) collective-permute-start(bf16[64,1280]{1,0:T(8,128)(2,1)S(1)} %bitcast_convert_fusion), channel_id=1, source_target_pairs={{0,1},{1,2},{2,3},{3,4},{4,5},{5,6},{6,7},{7,8},{8,9},{9,10},{10,1... | collective-permute-start | bytes 491528 | tf_op jit(solution)/shard_map/ppermute | solution.py:51
  3.8 4.8 %collective-permute-start.1 = (bf16[64,1280]{1,0:T(8,128)(2,1)S(1)}, bf16[64,1280]{1,0:T(8,128)(2,1)S(1)}, u32[]{:S(2)}, u32[]{:S(2)}) collective-permute-start(bf16[64,1280]{1,0:T(8,128)(2,1)S(1)} %bitcast_convert_fusion), channel_id=1, source_target_pairs={{0,15},{1,0},{2,1},{3,2},{4,3},{5,4},{6,5},{7,6},{8,7},{9,8},{10,9... | collective-permute-start | bytes 491528 | tf_op jit(solution)/shard_map/ppermute | solution.py:51
  10.9 6.7 %all-to-all-start = ((f32[128,1,128]{2,1,0:T(1,128)}), f32[128,1,128]{2,1,0:T(1,128)S(1)}, u32[]{:S(2)}, u32[]{:S(2)}) async-start(f32[128,1,128]{2,1,0:T(1,128)} %bitcast.22), calls=%async_computation | async-start | bytes 131072 | tf_op jit(solution)/shard_map/all_to_all | solution.py:387
  19.5 1.3 %dynamic-slice_bitcast_fusion.4 = (f32[4,8,128]{2,1,0:T(8,128)}, f32[4,8,128]{2,1,0:T(8,128)}) fusion(f32[128,4,2,8]{0,3,2,1:T(8,128)} %bitcast.82, s32[]{:T(128)S(6)} %select_n.50, f32[128,4,2,8]{0,3,2,1:T(8,128)} %bitcast.83), kind=kLoop, calls=%fused_computation.14 | loop fusion | bytes 65540 | tf_op jit(solution)/shard_map/transpose | solution.py:393
  21.5 6.5 %shard_map.152 = f32[2,4,16,320]{3,2,1,0:T(8,128)} custom-call(s32[3]{0:T(128)} %pad_add_fusion.place_ref, bf16[64,1280]{1,0:T(8,128)(2,1)} %copy-done.6, f32[64,1280]{1,0:T(8,128)} %bitcast.72, bf16[64,1280]{1,0:T(8,128)(2,1)} %copy-done.7, bf16[16,16,2560]{2,1,0:T(8,128)(2,1)} %perturb_ref.5, bf16[1280,2560]{1,0:T(8,128)(2,1)} %map_ref.5, ...), custom_call_target="tpu_custom_call" | custom-call | tf_op jit(solution)/shard_map/pallas_call | solution.py:64
  32.7 2.4 %collective-permute-start.4 = (f32[4,16,320]{2,1,0:T(8,128)S(1)}, f32[4,16,320]{2,1,0:T(8,128)S(1)}, u32[]{:S(2)}, u32[]{:S(2)}) collective-permute-start(f32[4,16,320]{2,1,0:T(8,128)S(1)} %fusion.2.a_ref), channel_id=1, source_target_pairs={{0,64},{16,80},{32,96},{48,112},{64,0},{80,16},{96,32},{112,48},{1... | collective-permute-start | bytes 245768 | tf_op jit(solution)/shard_map/ppermute | solution.py:51
  37.2 2.6 %collective-permute-done.4.c_ref = f32[4,16,320]{2,1,0:T(8,128)S(1)} collective-permute-done((f32[4,16,320]{2,1,0:T(8,128)S(1)}, f32[4,16,320]{2,1,0:T(8,128)S(1)}, u32[]{:S(2)}, u32[]{:S(2)}) %collective-permute-start.4) | collective-permute-done | bytes 81952 | tf_op jit(solution)/shard_map/ppermute | solution.py:51
  40.6 4.8 %shard_map.153 = (f32[4,16,320]{2,1,0:T(8,128)}, f32[4,8,128]{2,1,0:T(8,128)}, f32[4,16,320]{2,1,0:T(8,128)}) custom-call(s32[3]{0:T(128)} %pad_add_fusion.place_ref, f32[4,16,320]{2,1,0:T(8,128)} %copy-done.2, f32[4,16,320]{2,1,0:T(8,128)} %copy-done.12, f32[4,16,320]{2,1,0:T(8,128)} %copy-done.13, f32[4,16,320]{2,1,0:T(8,128)} %copy-done.14, ...), custom_call_target="tpu_custom_call" | custom-call | tf_op jit(solution)/shard_map/pallas_call | solution.py:64
  45.4 1.2 collective-permute-start.6
  48.4 6.8 %shard_map.154 = (f32[96,1280]{1,0:T(8,128)}, bf16[64,1280]{1,0:T(8,128)(2,1)}, bf16[64,1280]{1,0:T(8,128)(2,1)}) custom-call(s32[3]{0:T(128)} %pad_add_fusion.place_ref, f32[4,16,320]{2,1,0:T(8,128)} %get-tuple-element.15.mine_ref, f32[4,16,320]{2,1,0:T(8,128)} %copy-done.10, bf16[16,16,2560]{2,1,0:T(8,128)(2,1)} %perturb_ref.5, ...), custom_call_target="tpu_custom_call" | custom-call | tf_op jit(solution)/shard_map/pallas_call | solution.py:64
  56.2 4.2 %collective-permute-start.8 = (bf16[64,1280]{1,0:T(8,128)(2,1)}, bf16[64,1280]{1,0:T(8,128)(2,1)S(1)}, u32[]{:S(2)}, u32[]{:S(2)}) collective-permute-start(bf16[64,1280]{1,0:T(8,128)(2,1)} %get-tuple-element.18), channel_id=1, source_target_pairs={{0,15},{1,0},{2,1},{3,2},{4,3},{5,4},{6,5},{7,6},{8,7},{9,8},{10,9... | collective-permute-start | bytes 491528 | tf_op jit(solution)/shard_map/ppermute | solution.py:51
  60.4 4.4 %collective-permute-done.7.low_ref = bf16[64,1280]{1,0:T(8,128)(2,1)S(1)} collective-permute-done((bf16[64,1280]{1,0:T(8,128)(2,1)}, bf16[64,1280]{1,0:T(8,128)(2,1)S(1)}, u32[]{:S(2)}, u32[]{:S(2)}) %collective-permute-start.7) | collective-permute-done | bytes 163872 | tf_op jit(solution)/shard_map/ppermute | solution.py:51
  65.5 2.4 %shard_map.155 = (f32[64,1280]{1,0:T(8,128)}, bf16[64,1280]{1,0:T(8,128)(2,1)}, f32[8,128]{1,0:T(8,128)}) custom-call(s32[3]{0:T(128)} %pad_add_fusion.place_ref, bf16[64,1280]{1,0:T(8,128)(2,1)} %copy-done.4, f32[96,1280]{1,0:T(8,128)} %get-tuple-element.17.part_ref, bf16[64,1280]{1,0:T(8,128)(2,1)} %copy-done.5, f32[64,1280]{1,0:T(8,128)} %bitcast.73), custom_call_target="tpu_custom_call" | custom-call | tf_op jit(solution)/shard_map/pallas_call | solution.py:64
  67.9 4.5 %collective-permute-start.10 = (bf16[64,1280]{1,0:T(8,128)(2,1)}, bf16[64,1280]{1,0:T(8,128)(2,1)S(1)}, u32[]{:S(2)}, u32[]{:S(2)}) collective-permute-start(bf16[64,1280]{1,0:T(8,128)(2,1)} %get-tuple-element.19), channel_id=1, source_target_pairs={{0,15},{1,0},{2,1},{3,2},{4,3},{5,4},{6,5},{7,6},{8,7},{9,8},{10,9... | collective-permute-start | bytes 491528 | tf_op jit(solution)/shard_map/ppermute | solution.py:51
  72.4 2.6 %collective-permute-done.10.high_ref = bf16[64,1280]{1,0:T(8,128)(2,1)S(1)} collective-permute-done((bf16[64,1280]{1,0:T(8,128)(2,1)}, bf16[64,1280]{1,0:T(8,128)(2,1)S(1)}, u32[]{:S(2)}, u32[]{:S(2)}) %collective-permute-start.10) | collective-permute-done | bytes 163872 | tf_op jit(solution)/shard_map/ppermute | solution.py:51
  75.0 5.1 %collective-permute-done.9.low_ref = bf16[64,1280]{1,0:T(8,128)(2,1)S(1)} collective-permute-done((bf16[64,1280]{1,0:T(8,128)(2,1)}, bf16[64,1280]{1,0:T(8,128)(2,1)S(1)}, u32[]{:S(2)}, u32[]{:S(2)}) %collective-permute-start.9) | collective-permute-done | bytes 163872 | tf_op jit(solution)/shard_map/ppermute | solution.py:51
  80.8 6.4 %shard_map.156 = f32[2,4,16,320]{3,2,1,0:T(8,128)} custom-call(s32[3]{0:T(128)} %pad_add_fusion.place_ref, bf16[64,1280]{1,0:T(8,128)(2,1)} %copy-done.9, f32[64,1280]{1,0:T(8,128)} %get-tuple-element.20.own_ref.grad_ref, bf16[64,1280]{1,0:T(8,128)(2,1)} %copy-done.8, bf16[16,16,2560]{2,1,0:T(8,128)(2,1)} %perturb_ref.5, bf16[1280,2560]{1,0:T(8,128)(2,1)} %map_ref.5, ...), custom_call_target="tpu_custom_call" | custom-call | tf_op jit(solution)/shard_map/pallas_call | solution.py:64
  88.1 2.6 %collective-permute-start.11 = (f32[4,16,320]{2,1,0:T(8,128)S(1)}, f32[4,16,320]{2,1,0:T(8,128)S(1)}, u32[]{:S(2)}, u32[]{:S(2)}) collective-permute-start(f32[4,16,320]{2,1,0:T(8,128)S(1)} %slice_bitcast_fusion), channel_id=1, source_target_pairs={{0,16},{16,0},{32,48},{48,32},{64,80},{80,64},{96,112},{112,96},{1... | collective-permute-start | bytes 245768 | tf_op jit(solution)/shard_map/ppermute | solution.py:55
  94.2 2.2 %collective-permute-start.13 = (f32[16,320]{1,0:T(8,128)S(1)}, f32[16,320]{1,0:T(8,128)S(1)}, u32[]{:S(2)}, u32[]{:S(2)}) collective-permute-start(f32[16,320]{1,0:T(8,128)S(1)} %get-tuple-element.29), channel_id=1, source_target_pairs={{0,64},{16,80},{32,96},{48,112},{64,0},{80,16},{96,32},{112,48},{1... | collective-permute-start | bytes 61448 | tf_op jit(solution)/shard_map/ppermute | solution.py:51
  96.4 1.2 collective-permute-start.14
  100.0 2.1 %shard_map.157 = (f32[16,320]{1,0:T(8,128)}, f32[128,128]{1,0:T(8,128)}) custom-call(s32[3]{0:T(128)} %pad_add_fusion.place_ref, f32[16,320]{1,0:T(8,128)} %get-tuple-element.31.a_ref, f32[16,320]{1,0:T(8,128)} %copy-done.15, f32[16,320]{1,0:T(8,128)} %copy-done.16, f32[16,320]{1,0:T(8,128)} %copy-done.17, ...), custom_call_target="tpu_custom_call" | custom-call | tf_op jit(solution)/shard_map/pallas_call | solution.py:64
  102.1 16.2 %all_to_all.22 = f32[128,1,128]{2,1,0:T(1,128)} all-to-all(f32[128,1,128]{2,1,0:T(1,128)} %bitcast.81), channel_id=1, replica_groups=mesh['member'=8,'tile'=16] {'member','tile'}, dimensions={0} | all-to-all | bytes 131072 | tf_op jit(solution)/shard_map/all_to_all | solution.py:420
  118.2 2.1 %shard_map.158 = (f32[64,1280]{1,0:T(8,128)}, f32[16,320]{1,0:T(8,128)}) custom-call(s32[3]{0:T(128)} %pad_add_fusion.place_ref, f32[128,128]{1,0:T(8,128)} %bitcast.79, f32[64,1280]{1,0:T(8,128)} %bitcast.74, f32[64,1280]{1,0:T(8,128)} %get-tuple-element.20.own_ref.grad_ref, f32[4,16,320]{2,1,0:T(8,128)} %get-tuple-element.24.full_ref, f32[16,320]{1,0:T(8,128)} %base_ref.1, ...), custom_call_target="tpu_custom_call" | custom-call | tf_op jit(solution)/shard_map/pallas_call | solution.py:64
  120.3 1.9 %copy.44 = f32[4,16,1280]{2,0,1:T(4,128)} copy(f32[4,16,1280]{2,1,0:T(8,128)} %bitcast.77) | data formatting | bytes 655360 | tf_op jit(solution)/shard_map/reshape | solution.py:422
  (73 shorter events, 23.7 us)
Async XLA Ops:
  0.6 35.6 %copy-start = (s32[1,128,8,8]{1,3,2,0:T(8,128)S(1)}, s32[1,128,8,8]{1,3,2,0:T(8,128)}, u32[]{:S(2)}) copy-start(s32[1,128,8,8]{1,3,2,0:T(8,128)} %param.18) | copy-start | bytes 98308
  0.6 30.3 %copy-start.11 = (f32[16,320]{1,0:T(8,128)S(1)}, f32[16,320]{1,0:T(8,128)}, u32[]{:S(2)}) copy-start(f32[16,320]{1,0:T(8,128)} %base_ref.1) | copy-start | bytes 61444
  1.7 19.1 %copy-start.1 = (f32[4,16,1280]{2,1,0:T(8,128)}, f32[4,16,1280]{2,1,0:T(8,128)S(1)}, u32[]{:S(2)}) copy-start(f32[4,16,1280]{2,1,0:T(8,128)S(1)} %copy.30) | copy-start | bytes 983044
  1.7 19.1 %collective-permute-start = (bf16[64,1280]{1,0:T(8,128)(2,1)S(1)}, bf16[64,1280]{1,0:T(8,128)(2,1)S(1)}, u32[]{:S(2)}, u32[]{:S(2)}) collective-permute-start(bf16[64,1280]{1,0:T(8,128)(2,1)S(1)} %bitcast_convert_fusion), channel_id=1, source_target_pairs={{0,1},{1,2},{2,3},{3,4},{4,5},{5,6},{6,7},{7,8},{8,9},{9,10},{10,1... | collective-permute-start | bytes 491528 | tf_op jit(solution)/shard_map/ppermute | solution.py:51
  3.8 17.0 %collective-permute-start.1 = (bf16[64,1280]{1,0:T(8,128)(2,1)S(1)}, bf16[64,1280]{1,0:T(8,128)(2,1)S(1)}, u32[]{:S(2)}, u32[]{:S(2)}) collective-permute-start(bf16[64,1280]{1,0:T(8,128)(2,1)S(1)} %bitcast_convert_fusion), channel_id=1, source_target_pairs={{0,15},{1,0},{2,1},{3,2},{4,3},{5,4},{6,5},{7,6},{8,7},{9,8},{10,9... | collective-permute-start | bytes 491528 | tf_op jit(solution)/shard_map/ppermute | solution.py:51
  10.9 26.0 %all-to-all-start = ((f32[128,1,128]{2,1,0:T(1,128)}), f32[128,1,128]{2,1,0:T(1,128)S(1)}, u32[]{:S(2)}, u32[]{:S(2)}) async-start(f32[128,1,128]{2,1,0:T(1,128)} %bitcast.22), calls=%async_computation | async-start | bytes 131072 | tf_op jit(solution)/shard_map/all_to_all | solution.py:387
  28.9 2.0 %collective-permute-start.2 = (f32[4,16,320]{2,1,0:T(8,128)S(1)}, f32[4,16,320]{2,1,0:T(8,128)S(1)}, u32[]{:S(2)}, u32[]{:S(2)}) collective-permute-start(f32[4,16,320]{2,1,0:T(8,128)S(1)} %slice_bitcast_fusion.2), channel_id=1, source_target_pairs={{0,16},{16,0},{32,48},{48,32},{64,80},{80,64},{96,112},{112,96},{1... | collective-permute-start | bytes 245768 | tf_op jit(solution)/shard_map/ppermute | solution.py:55
  31.9 8.0 %copy-start.2 = (f32[4,16,320]{2,1,0:T(8,128)}, f32[4,16,320]{2,1,0:T(8,128)S(1)}, u32[]{:S(2)}) copy-start(f32[4,16,320]{2,1,0:T(8,128)S(1)} %fusion.2.a_ref) | copy-start | bytes 245764
  31.9 5.3 %collective-permute-start.3 = (f32[4,16,320]{2,1,0:T(8,128)S(1)}, f32[4,16,320]{2,1,0:T(8,128)S(1)}, u32[]{:S(2)}, u32[]{:S(2)}) collective-permute-start(f32[4,16,320]{2,1,0:T(8,128)S(1)} %fusion.2.a_ref), channel_id=1, source_target_pairs={{0,32},{16,48},{32,64},{48,80},{64,96},{80,112},{96,0},{112,16},{1... | collective-permute-start | bytes 245768 | tf_op jit(solution)/shard_map/ppermute | solution.py:51
  32.7 7.1 %collective-permute-start.4 = (f32[4,16,320]{2,1,0:T(8,128)S(1)}, f32[4,16,320]{2,1,0:T(8,128)S(1)}, u32[]{:S(2)}, u32[]{:S(2)}) collective-permute-start(f32[4,16,320]{2,1,0:T(8,128)S(1)} %fusion.2.a_ref), channel_id=1, source_target_pairs={{0,64},{16,80},{32,96},{48,112},{64,0},{80,16},{96,32},{112,48},{1... | collective-permute-start | bytes 245768 | tf_op jit(solution)/shard_map/ppermute | solution.py:51
  35.1 4.8 %collective-permute-start.5 = (f32[4,16,320]{2,1,0:T(8,128)S(1)}, f32[4,16,320]{2,1,0:T(8,128)S(1)}, u32[]{:S(2)}, u32[]{:S(2)}) collective-permute-start(f32[4,16,320]{2,1,0:T(8,128)S(1)} %fusion.2.a_ref), channel_id=1, source_target_pairs={{0,96},{16,112},{32,0},{48,16},{64,32},{80,48},{96,64},{112,80},{1... | collective-permute-start | bytes 245768 | tf_op jit(solution)/shard_map/ppermute | solution.py:51
  36.9 3.1 %copy-start.3 = (f32[128,1,128]{2,1,0:T(1,128)}, f32[128,1,128]{2,1,0:T(1,128)S(1)}, u32[]{:S(2)}) copy-start(f32[128,1,128]{2,1,0:T(1,128)S(1)} %all-to-all-done) | copy-start | bytes 196612
  37.2 2.7 %copy-start.12 = (f32[4,16,320]{2,1,0:T(8,128)}, f32[4,16,320]{2,1,0:T(8,128)S(1)}, u32[]{:S(2)}) copy-start(f32[4,16,320]{2,1,0:T(8,128)S(1)} %collective-permute-done.3.b_ref) | copy-start | bytes 245764
  45.4 2.4 %collective-permute-start.6 = (f32[4,16,320]{2,1,0:T(8,128)}, f32[4,16,320]{2,1,0:T(8,128)S(1)}, u32[]{:S(2)}, u32[]{:S(2)}) collective-permute-start(f32[4,16,320]{2,1,0:T(8,128)} %get-tuple-element.15.mine_ref), channel_id=1, source_target_pairs={{0,16},{16,0},{32,48},{48,32},{64,80},{80,64},{96,112},{112,96},{1... | collective-permute-start | bytes 245768 | tf_op jit(solution)/shard_map/ppermute | solution.py:55
  55.1 9.6 %collective-permute-start.7 = (bf16[64,1280]{1,0:T(8,128)(2,1)}, bf16[64,1280]{1,0:T(8,128)(2,1)S(1)}, u32[]{:S(2)}, u32[]{:S(2)}) collective-permute-start(bf16[64,1280]{1,0:T(8,128)(2,1)} %get-tuple-element.16), channel_id=1, source_target_pairs={{0,1},{1,2},{2,3},{3,4},{4,5},{5,6},{6,7},{7,8},{8,9},{9,10},{10,1... | collective-permute-start | bytes 491528 | tf_op jit(solution)/shard_map/ppermute | solution.py:51
  56.2 8.6 %collective-permute-start.8 = (bf16[64,1280]{1,0:T(8,128)(2,1)}, bf16[64,1280]{1,0:T(8,128)(2,1)S(1)}, u32[]{:S(2)}, u32[]{:S(2)}) collective-permute-start(bf16[64,1280]{1,0:T(8,128)(2,1)} %get-tuple-element.18), channel_id=1, source_target_pairs={{0,15},{1,0},{2,1},{3,2},{4,3},{5,4},{6,5},{7,6},{8,7},{9,8},{10,9... | collective-permute-start | bytes 491528 | tf_op jit(solution)/shard_map/ppermute | solution.py:51
  67.9 7.0 %collective-permute-start.10 = (bf16[64,1280]{1,0:T(8,128)(2,1)}, bf16[64,1280]{1,0:T(8,128)(2,1)S(1)}, u32[]{:S(2)}, u32[]{:S(2)}) collective-permute-start(bf16[64,1280]{1,0:T(8,128)(2,1)} %get-tuple-element.19), channel_id=1, source_target_pairs={{0,15},{1,0},{2,1},{3,2},{4,3},{5,4},{6,5},{7,6},{8,7},{9,8},{10,9... | collective-permute-start | bytes 491528 | tf_op jit(solution)/shard_map/ppermute | solution.py:51
  72.4 7.7 %collective-permute-start.9 = (bf16[64,1280]{1,0:T(8,128)(2,1)}, bf16[64,1280]{1,0:T(8,128)(2,1)S(1)}, u32[]{:S(2)}, u32[]{:S(2)}) collective-permute-start(bf16[64,1280]{1,0:T(8,128)(2,1)} %get-tuple-element.19), channel_id=1, source_target_pairs={{0,1},{1,2},{2,3},{3,4},{4,5},{5,6},{6,7},{7,8},{8,9},{9,10},{10,1... | collective-permute-start | bytes 491528 | tf_op jit(solution)/shard_map/ppermute | solution.py:51
  75.0 5.1 %copy-start.8 = (bf16[64,1280]{1,0:T(8,128)(2,1)}, bf16[64,1280]{1,0:T(8,128)(2,1)S(1)}, u32[]{:S(2)}) copy-start(bf16[64,1280]{1,0:T(8,128)(2,1)S(1)} %collective-permute-done.10.high_ref) | copy-start | bytes 491524
  88.1 3.6 %collective-permute-start.11 = (f32[4,16,320]{2,1,0:T(8,128)S(1)}, f32[4,16,320]{2,1,0:T(8,128)S(1)}, u32[]{:S(2)}, u32[]{:S(2)}) collective-permute-start(f32[4,16,320]{2,1,0:T(8,128)S(1)} %slice_bitcast_fusion), channel_id=1, source_target_pairs={{0,16},{16,0},{32,48},{48,32},{64,80},{80,64},{96,112},{112,96},{1... | collective-permute-start | bytes 245768 | tf_op jit(solution)/shard_map/ppermute | solution.py:55
  93.2 4.4 %collective-permute-start.12 = (f32[16,320]{1,0:T(8,128)S(1)}, f32[16,320]{1,0:T(8,128)S(1)}, u32[]{:S(2)}, u32[]{:S(2)}) collective-permute-start(f32[16,320]{1,0:T(8,128)S(1)} %get-tuple-element.30), channel_id=1, source_target_pairs={{0,32},{16,48},{32,64},{48,80},{64,96},{80,112},{96,0},{112,16},{1... | collective-permute-start | bytes 61448 | tf_op jit(solution)/shard_map/ppermute | solution.py:51
  94.2 4.4 %collective-permute-start.13 = (f32[16,320]{1,0:T(8,128)S(1)}, f32[16,320]{1,0:T(8,128)S(1)}, u32[]{:S(2)}, u32[]{:S(2)}) collective-permute-start(f32[16,320]{1,0:T(8,128)S(1)} %get-tuple-element.29), channel_id=1, source_target_pairs={{0,64},{16,80},{32,96},{48,112},{64,0},{80,16},{96,32},{112,48},{1... | collective-permute-start | bytes 61448 | tf_op jit(solution)/shard_map/ppermute | solution.py:51
  96.4 3.0 %collective-permute-start.14 = (f32[16,320]{1,0:T(8,128)S(1)}, f32[16,320]{1,0:T(8,128)S(1)}, u32[]{:S(2)}, u32[]{:S(2)}) collective-permute-start(f32[16,320]{1,0:T(8,128)S(1)} %get-tuple-element.28), channel_id=1, source_target_pairs={{0,96},{16,112},{32,0},{48,16},{64,32},{80,48},{96,64},{112,80},{1... | collective-permute-start | bytes 61448 | tf_op jit(solution)/shard_map/ppermute | solution.py:51
  97.6 1.8 %copy-start.15 = (f32[16,320]{1,0:T(8,128)}, f32[16,320]{1,0:T(8,128)S(1)}, u32[]{:S(2)}) copy-start(f32[16,320]{1,0:T(8,128)S(1)} %collective-permute-done.12.b_ref) | copy-start | bytes 61444
  (10 other events, 6.7 us)

commit v3 on v2

v3 whole, which is shorter than its diff:
```python
import jax
import jax.numpy as jnp
import numpy as np
from jax import lax
from jax.experimental import pallas as pl
from jax.experimental.pallas import tpu as pltpu
from jax.sharding import PartitionSpec as P

RATIO = 4
KSM = 3
DIFFUSION = 0.45
NTILE = 16
NMEMBER = 8
NCORE = 2
NY = NMEMBER // NCORE
MEMBERS_HERE = 16
ROWS = 4
FINE_ROWS = 16
COARSE_COLS = 1280
WIDTH = 320
CHUNK = NCORE * WIDTH
SLOTS = 8
BATCHES = 128
ROOM = 24 << 20
FLOAT, HALF = jnp.float32, jnp.bfloat16


def refine_matrix():
    table = np.zeros((FINE_ROWS, ROWS + 2))
    for row in range(ROWS):
        for offset in range(RATIO):
            shift = (offset + 0.5) / RATIO - 0.5
            fine = RATIO * row + offset
            if shift < 0:
                table[fine, row + 1] += 1.0 + shift
                table[fine, row] -= shift
            else:
                table[fine, row + 1] += 1.0 - shift
                table[fine, row + 2] += shift
    return table


def member_matrix():
    return np.einsum("fr,kl->kfrl", refine_matrix(), np.eye(MEMBERS_HERE)).reshape(
        MEMBERS_HERE * FINE_ROWS, (ROWS + 2) * MEMBERS_HERE
    )


def turn(values, step, axis):
    count = lax.axis_size(axis)
    return lax.ppermute(values, axis, [(i, (i + step) % count) for i in range(count)])


def swap_core(values):
    return lax.ppermute(values, "member", [(i, i ^ 1) for i in range(NMEMBER)])


NEAR = pl.BlockSpec(memory_space=pltpu.VMEM)
FAR = pl.BlockSpec(memory_space=pltpu.HBM)
SCALAR = pl.BlockSpec(memory_space=pltpu.SMEM)


def near(values):
    return pltpu.with_memory_space_constraint(values, pltpu.VMEM)


def distant(values):
    return pltpu.with_memory_space_constraint(values, pltpu.HBM)


def call(kernel, out_shapes, arguments, far=(), scratch=(), far_out=(), scalar=()):
    specs = [
        SCALAR if i in scalar else FAR if i in far else NEAR for i in range(len(arguments))
    ]
    arguments = tuple(
        x if i in scalar else distant(x) if i in far else near(x)
        for i, x in enumerate(arguments)
    )
    return pl.pallas_call(
        kernel,
        out_shape=tuple(
            jax.ShapeDtypeStruct(shape, kind) if i in far_out else pltpu.VMEM(shape, kind)
            for i, (shape, kind) in enumerate(out_shapes)
        ),
        in_specs=specs,
        out_specs=tuple(NEAR for _ in out_shapes),
        scratch_shapes=list(scratch),
        compiler_params=pltpu.CompilerParams(vmem_limit_bytes=ROOM),
        cost_estimate=pl.CostEstimate(flops=10**9, transcendentals=0, bytes_accessed=8 << 20),
    )(*arguments)


def place():
    member_pos = lax.axis_index("member")
    return lax.axis_index("tile"), lax.rem(member_pos, NCORE), lax.div(member_pos, NCORE)


def edges():
    tile_pos = lax.axis_index("tile")
    return jnp.where(tile_pos > 0, 1.0, 0.0), jnp.where(tile_pos < NTILE - 1, 1.0, 0.0)


def streams(perturb_ref, map_ref, perturb_buf, map_buf, sem):
    copies = []
    for y in range(NY):
        cols = pl.ds(y * CHUNK, CHUNK)
        copies.append(
            (
                pltpu.make_async_copy(map_ref.at[:, cols], map_buf.at[y], sem.at[0, y]),
                pltpu.make_async_copy(
                    perturb_ref.at[:, :, cols], perturb_buf.at[y], sem.at[1, y]
                ),
            )
        )
    return copies


BUFFERS = [
    pltpu.VMEM((NY, MEMBERS_HERE, FINE_ROWS, CHUNK), HALF),
    pltpu.VMEM((NY, COARSE_COLS, CHUNK), HALF),
    pltpu.SemaphoreType.DMA((2, NY)),
]


def swept(rows, masks):
    for _ in range(KSM):
        rows = [v if m is None else v * m for v, m in zip(rows, masks)]
        rows = [
            rows[i] + DIFFUSION * (rows[i - 1] + rows[i + 1] - 2.0 * rows[i])
            for i in range(1, len(rows) - 1)
        ]
        masks = masks[1:-1]
    return [v if m is None else v * m for v, m in zip(rows, masks)]


def row_slice(row):
    return pl.ds(row * MEMBERS_HERE, MEMBERS_HERE)


def forward_kernel(
    low_ref, own_ref, high_ref, refine_ref, perturb_ref, map_ref,
    mine_ref, other_ref, smooth_ref, perturb_buf, map_buf, sem,
):
    copies = streams(perturb_ref, map_ref, perturb_buf, map_buf, sem)
    for pair in copies:
        for copy in pair:
            copy.start()
    _, core_pos, _ = place()
    below, above = edges()
    masks = [below] * 4 + [None] * 4 + [above] * 4
    for start in range(0, COARSE_COLS, 128):
        cols = pl.ds(start, 128)
        rows = [low_ref[row_slice(r), cols].astype(FLOAT) for r in range(4)]
        rows += [own_ref[row_slice(r), cols] for r in range(4)]
        rows += [high_ref[row_slice(r), cols].astype(FLOAT) for r in range(4)]
        for r, value in enumerate(swept(rows, masks)):
            smooth_ref[row_slice(r), cols] = value.astype(HALF)
    smooth = smooth_ref[...]
    for y, (map_copy, perturb_copy) in enumerate(copies):
        map_copy.wait()
        mapped = jnp.dot(smooth, map_buf[y], preferred_element_type=FLOAT)
        high = mapped.astype(HALF)
        low = (mapped - high.astype(FLOAT)).astype(HALF)
        fine = jnp.dot(
            refine_ref[...], jnp.concatenate([high, low], axis=0), preferred_element_type=FLOAT
        )
        perturb_copy.wait()
        total = None
        for k in range(MEMBERS_HERE):
            term = fine[k * FINE_ROWS : (k + 1) * FINE_ROWS] * perturb_buf[y, k].astype(FLOAT)
            total = term if total is None else total + term
        first, second = total[:, :WIDTH], total[:, WIDTH:]
        mine_ref[y] = jnp.where(core_pos == 0, first, second)
        other_ref[y] = jnp.where(core_pos == 0, second, first)


REGIONS = ((NY, FINE_ROWS, WIDTH), FLOAT)


def partial_forward(low, own, high, perturb, column_map):
    matrix = member_matrix()
    matrix = jnp.asarray(np.concatenate([matrix, matrix], axis=1), HALF)
    return call(
        forward_kernel,
        (REGIONS, REGIONS),
        (low, own, high, matrix, perturb, column_map),
        far=(4, 5),
        scratch=[pltpu.VMEM(((ROWS + 2) * MEMBERS_HERE, COARSE_COLS), HALF)] + BUFFERS,
    )


def adjoint_kernel(
    mine_ref, other_ref, back_ref, perturb_ref, map_ref,
    part_ref, up_ref, down_ref, perturb_buf, map_buf, sem,
):
    copies = streams(perturb_ref, map_ref, perturb_buf, map_buf, sem)
    for pair in copies:
        for copy in pair[::-1]:
            copy.start()
    _, core_pos, _ = place()
    total = None
    for y, (map_copy, perturb_copy) in enumerate(copies):
        mine, other = mine_ref[y], other_ref[y]
        first = jnp.where(core_pos == 0, mine, other)
        second = jnp.where(core_pos == 0, other, mine)
        spread = jnp.concatenate([first, second], axis=1)
        perturb_copy.wait()
        highs, lows = [], []
        for k in range(MEMBERS_HERE):
            term = perturb_buf[y, k].astype(FLOAT) * spread
            high = term.astype(HALF)
            highs.append(high)
            lows.append((term - high.astype(FLOAT)).astype(HALF))
        pulled = jnp.dot(
            back_ref[...], jnp.concatenate(highs + lows, axis=0), preferred_element_type=FLOAT
        )
        map_copy.wait()
        part = lax.dot_general(
            pulled.astype(HALF),
            map_buf[y],
            (((1,), (1,)), ((), ())),
            preferred_element_type=FLOAT,
        )
        total = part if total is None else total + part
    part_ref[...] = total
    up_ref[...] = total[2 * MEMBERS_HERE :].astype(HALF)
    down_ref[...] = total[: 4 * MEMBERS_HERE].astype(HALF)


def partial_adjoint(mine, other, perturb, column_map):
    matrix = member_matrix().T
    matrix = jnp.asarray(np.concatenate([matrix, matrix], axis=1), HALF)
    rim = ((4 * MEMBERS_HERE, COARSE_COLS), HALF)
    return call(
        adjoint_kernel,
        ((((ROWS + 2) * MEMBERS_HERE, COARSE_COLS), FLOAT), rim, rim),
        (mine, other, matrix, perturb, column_map),
        far=(3, 4),
        scratch=BUFFERS,
    )


def gradient_kernel(low_ref, part_ref, high_ref, own_ref, grad_ref, half_ref, square_ref):
    below, above = edges()
    masks = [below] * 3 + [None] * 4 + [above] * 3
    square = None
    for start in range(0, COARSE_COLS, 128):
        cols = pl.ds(start, 128)
        low = [low_ref[row_slice(r), cols].astype(FLOAT) for r in range(4)]
        part = [part_ref[row_slice(r), cols] for r in range(6)]
        high = [high_ref[row_slice(r), cols].astype(FLOAT) for r in range(4)]
        rows = [low[0], low[1], low[2] + part[0], low[3] * below + part[1], part[2], part[3]]
        rows += [part[4] + high[0] * above, part[5] + high[1], high[2], high[3]]
        for r, value in enumerate(swept(rows, masks)):
            gradient = own_ref[row_slice(r), cols] + value
            grad_ref[row_slice(r), cols] = gradient
            half_ref[row_slice(r), cols] = gradient.astype(HALF)
            term = gradient * gradient
            square = term if square is None else square + term
    square_ref[...] = square[:8] + square[8:]


def gradient_of(low, part, high, own):
    shape = (ROWS * MEMBERS_HERE, COARSE_COLS)
    return call(
        gradient_kernel,
        ((shape, FLOAT), (shape, HALF), ((8, 128), FLOAT)),
        (low, part, high, own),
    )


def send_kernel(value_ref, error_ref, gain_ref, sent_ref):
    lanes = lax.broadcasted_iota(jnp.int32, (SLOTS, BATCHES), 1)
    block = lanes // (NCORE * NTILE)
    rows = []
    for ref in (value_ref, error_ref):
        values = ref[...]
        turned = [values] + [
            pltpu.roll(values, NCORE * NTILE * i, 1) for i in range(1, NY)
        ]
        for y in range(NY):
            out = turned[0]
            for j in range(NY):
                out = jnp.where(block == j, turned[(j - y) % NY], out)
            rows.append(out)
    gain = jnp.full((2 * NY * SLOTS, BATCHES), gain_ref[0], FLOAT)
    sent_ref[...] = jnp.transpose(jnp.concatenate(rows + [gain], axis=0))


def add_kernel(a_ref, b_ref, base_ref, out_ref):
    _, _, y_pos = place()
    for y in range(NY):
        out_ref[y] = a_ref[y] + b_ref[y]
    out_ref[y_pos] += base_ref[...]


def pick_kernel(a_ref, b_ref, *out_refs):
    _, _, y_pos = place()
    for step, ref in enumerate(out_refs):
        y = lax.rem(y_pos + step, NY)
        ref[...] = a_ref[y] + b_ref[y]


def column_picks(column):
    ids = lax.broadcasted_iota(jnp.int32, (WIDTH, BATCHES), 0)
    return jnp.concatenate(
        [(ids == column[s : s + 1]).astype(FLOAT).astype(HALF) for s in range(SLOTS)], axis=1
    )


def row_factors(row, fraction):
    ids = lax.broadcasted_iota(jnp.int32, (FINE_ROWS, BATCHES), 0)
    return jnp.concatenate(
        [
            jnp.where(ids == row[s : s + 1], 1.0 - fraction[s : s + 1], 0.0)
            + jnp.where(ids == row[s : s + 1] + 1, fraction[s : s + 1], 0.0)
            for s in range(SLOTS)
        ],
        axis=1,
    )


def on_lanes(values):
    return jnp.concatenate([values[s : s + 1] for s in range(SLOTS)], axis=1)


def on_slots(values):
    return jnp.concatenate(
        [values[:, s * BATCHES : (s + 1) * BATCHES] for s in range(SLOTS)], axis=0
    )


def halves(values):
    high = values.astype(HALF)
    return jnp.concatenate([high, (values - high.astype(FLOAT)).astype(HALF)], axis=0)


def interpolated(field, picks, factors, fraction):
    shifted = jnp.concatenate([field[:, 1:], field[:, :1]], axis=1)
    got = jnp.dot(
        halves(jnp.concatenate([field, shifted], axis=0)), picks, preferred_element_type=FLOAT
    )
    got = got[: 2 * FINE_ROWS] + got[2 * FINE_ROWS :]
    left, right = got[:FINE_ROWS], got[FINE_ROWS:]
    mixed = left * (1.0 - fraction) + right * fraction
    return on_slots(jnp.sum(mixed * factors, axis=0, keepdims=True))


def located(index):
    row = index // WIDTH
    return row, index - row * WIDTH


def obs_kernel(
    a_ref, b_ref, c_ref, d_ref, index_ref, row_ref, column_ref, length_ref, data_ref,
    spread_ref, weight_ref, full_ref,
):
    _, core_pos, y_pos = place()
    data = jnp.transpose(data_ref[...])
    gain = data[2 * NY * SLOTS : 2 * NY * SLOTS + SLOTS]
    slots = lax.broadcasted_iota(jnp.int32, (SLOTS, BATCHES), 0)
    for y in range(NY):
        field = a_ref[y] + b_ref[y] + c_ref[y] + d_ref[y]
        group = NCORE * y + core_pos
        row, column = located(index_ref[group])
        picks = column_picks(column)
        factors = row_factors(row, row_ref[group])
        fraction = on_lanes(column_ref[group])
        live = jnp.where(slots < length_ref[pl.ds(group, 1)], 1.0, 0.0)
        state = interpolated(field, picks, factors, fraction)
        value = data[y * SLOTS : (y + 1) * SLOTS]
        error = data[(NY + y) * SLOTS : (NY + y + 1) * SLOTS]
        bounded = jnp.tanh(state)
        derivative = 1.0 + gain * (1.0 - bounded * bounded)
        misfit = state + gain * bounded - value
        precision = live / (error * error)
        residual = derivative * misfit * precision

        @pl.when(y == y_pos)
        def _():
            weight_ref[...] = derivative * derivative * precision
            full_ref[...] = field

        weighted = factors * on_lanes(residual)
        both = jnp.concatenate([weighted * (1.0 - fraction), weighted * fraction], axis=0)
        got = lax.dot_general(
            halves(both), picks, (((1,), (1,)), ((), ())), preferred_element_type=FLOAT
        )
        got = got[: 2 * FINE_ROWS] + got[2 * FINE_ROWS :]
        left, right = got[:FINE_ROWS], got[FINE_ROWS:]
        spread_ref[y] = left + jnp.concatenate([right[:, -1:], right[:, :-1]], axis=1)


def curve_kernel(
    a_ref, b_ref, c_ref, d_ref, index_ref, row_ref, column_ref, weight_ref, square_ref,
    field_ref, sent_ref,
):
    _, core_pos, y_pos = place()
    own = NCORE * y_pos + core_pos
    field = a_ref[...] + b_ref[...] + c_ref[...] + d_ref[...]
    field_ref[...] = field
    row, column = located(index_ref[own])
    observed = interpolated(
        field, column_picks(column), row_factors(row, row_ref[own]), on_lanes(column_ref[own])
    )
    curvature = jnp.sum(weight_ref[...] * observed * observed, keepdims=True)
    square = jnp.sum(square_ref[...], keepdims=True)
    lanes = lax.broadcasted_iota(jnp.int32, (BATCHES, 128), 1)
    sent_ref[...] = jnp.where(lanes < 64, square, curvature)


def step_kernel(
    shared_ref, own_ref, grad_ref, full_ref, base_ref, image_ref, coarse_ref, increment_ref
):
    totals = jnp.sum(shared_ref[...], axis=0, keepdims=True)
    lanes = lax.broadcasted_iota(jnp.int32, (1, 128), 1)
    square = jnp.sum(jnp.where(lanes == 0, totals, 0.0), keepdims=True)
    curvature = jnp.sum(jnp.where(lanes == 127, totals, 0.0), keepdims=True)
    step = square / (square + curvature)
    for r in range(ROWS):
        coarse_ref[:, r, :] = own_ref[row_slice(r)] - step * grad_ref[row_slice(r)]
    increment_ref[...] = full_ref[...] - base_ref[...] - step * image_ref[...]


def shards(
    perturb,
    weights,
    column_map,
    background,
    stencil_index,
    row_fraction,
    column_fraction,
    block_lengths,
    obs_value,
    obs_error,
    instrument_gain,
):
    flat = (ROWS * MEMBERS_HERE, COARSE_COLS)
    own = jnp.transpose(weights, (1, 0, 2)).reshape(flat)
    half = own.astype(HALF)
    low, high = turn(half, 1, "tile"), turn(half, -1, "tile")

    (sent,) = call(
        send_kernel,
        (((BATCHES, BATCHES), FLOAT),),
        (obs_value[0].T, obs_error[0].T, instrument_gain),
        scalar=(2,),
    )
    data = lax.all_to_all(sent, ("member", "tile"), split_axis=0, concat_axis=0, tiled=True)

    index = jnp.transpose(stencil_index[0], (1, 2, 0))
    row_frac = jnp.transpose(row_fraction[0], (1, 2, 0))
    column_frac = jnp.transpose(column_fraction[0], (1, 2, 0))
    lengths = block_lengths[0].T

    mine, other = partial_forward(low, own, high, perturb, column_map)
    (mine,) = call(add_kernel, (REGIONS,), (mine, swap_core(other), background))
    pieces = [mine] + [turn(mine, NCORE * i, "member") for i in range(1, NY)]
    region = ((FINE_ROWS, WIDTH), FLOAT)
    spread, weight, full = call(
        obs_kernel,
        (REGIONS, ((SLOTS, BATCHES), FLOAT), region),
        (*pieces, index, row_frac, column_frac, lengths, data),
    )
    part, up, down = partial_adjoint(spread, swap_core(spread), perturb, column_map)
    gradient, half, square = gradient_of(turn(up, 1, "tile"), part, turn(down, -1, "tile"), own)
    mine, other = partial_forward(
        turn(half, 1, "tile"), gradient, turn(half, -1, "tile"), perturb, column_map
    )
    pieces = call(pick_kernel, (region,) * NY, (mine, swap_core(other)))
    pieces = [pieces[0]] + [turn(pieces[i], NCORE * i, "member") for i in range(1, NY)]
    image, sent = call(
        curve_kernel,
        (region, ((BATCHES, 128), FLOAT)),
        (*pieces, index, row_frac, column_frac, weight, square),
    )
    shared = lax.all_to_all(sent, ("member", "tile"), split_axis=0, concat_axis=0, tiled=True)
    return call(
        step_kernel,
        (((MEMBERS_HERE, ROWS, COARSE_COLS), FLOAT), region),
        (shared, own, gradient, full, background, image),
        far_out=(0, 1),
    )


def solution(mesh):
    placed = (
        P("member", "tile", None),
        P("member", "tile", None),
        P(),
        P("tile", "member"),
        P("tile", None, None, None),
        P("tile", None, None, None),
        P("tile", None, None, None),
        P("tile", None, None),
        P(("member", "tile"), None, None),
        P(("member", "tile"), None, None),
        P(("member", "tile")),
    )
    return jax.shard_map(
        shards,
        mesh=mesh,
        in_specs=placed,
        out_specs=(P("member", "tile", None), P("tile", "member")),
        check_vma=False,
    )
```

time: 123 us -> 104 us (0.85)
  blocking collectives: 16.2 us -> 28.5 us
  Pallas kernels: 31.1 us -> 19.3 us
  local copies, waits for them, and re-layouts: 12.8 us -> 1.99 us
  starting transfers between devices: 36.9 us -> 28.7 us
  waiting for transfers between devices: 20 us -> 23.9 us
  other arithmetic: 3.81 us -> 0.02 us
    all_to_all x1 -> x2, blocking collectives: 16.2 us -> 28.5 us  [shards(): lax.all_to_all(sent, ('member', 'tile'), split_axis=0, concat_axis=0, til...]
    pallas_call x7 -> x10, Pallas kernels: 31.1 us -> 19.3 us  [call(): pl.pallas_call(kernel, out_shape=tuple((jax.ShapeDtypeStruct(shape, kind)...]
    all_to_all x1 -> x0, starting transfers between devices: 6.66 us -> none  [shards(): lax.all_to_all(sent, ('member', 'tile'), split_axis=0, concat_axis=0, til...]
    ppermute x12, waiting for transfers between devices: 16.9 us -> 21.7 us  [turn(): lax.ppermute(values, axis, [(i, (i + step) % count) for i in range(count)])]
    unnamed x37 -> x20, local copies, waits for them, and re-layouts: 4.02 us -> 0.95 us
    squeeze x3 -> x0, local copies, waits for them, and re-layouts: 2.43 us -> none  [the longest x1 0.9 us: shards(): mine = second[0] + swap_core(second[1])]
    ppermute x12, starting transfers between devices: 25.3 us -> 23 us  [turn(): lax.ppermute(values, axis, [(i, (i + step) % count) for i in range(count)])]
    reshape x3 -> x0, local copies, waits for them, and re-layouts: 2.05 us -> none  [the longest x1 1.91 us: shards(): coarse.reshape(ROWS, MEMBERS_HERE, COARSE_COLS)]
  transfers between devices with their start and end apart: 16 -> 15, of which waited for: 11 -> 11; matrix products, arithmetic and copies ran while one was open for 6% -> 0% of each run, Pallas kernels for 5% -> 0%
where the time goes in v3:
time: 104 us
  starting transfers between devices  28.7 us (28%)
  blocking collectives  28.5 us (27%)
  waiting for transfers between devices  23.9 us (23%)
  Pallas kernels  19.3 us (19%)
  local copies, waits for them, and re-layouts  1.99 us (2%)
  between operations  1.49 us (1%)
    all_to_all x2, blocking collectives, shards(): lax.all_to_all(sent, ('member', 'tile'), split_axis=0, concat_axis=0, til...  28.5 us
    ppermute x12, starting transfers between devices, turn(): lax.ppermute(values, axis, [(i, (i + step) % count) for i in range(count)])  23 us
    ppermute x12, waiting for transfers between devices, turn(): lax.ppermute(values, axis, [(i, (i + step) % count) for i in range(count)])  21.7 us
    pallas_call x10, Pallas kernels, call(): pl.pallas_call(kernel, out_shape=tuple((jax.ShapeDtypeStruct(shape, kind)...  19.3 us
    ppermute x3, starting transfers between devices, swap_core(): return lax.ppermute(values, 'member', [(i, i ^ 1) for i in range(NMEMBER)])  5.74 us
    ppermute x3, waiting for transfers between devices, swap_core(): return lax.ppermute(values, 'member', [(i, i ^ 1) for i in range(NMEMBER)])  2.18 us
  transfers between devices with their start and end apart: 15, of which 11 were waited for; matrix products, arithmetic and copies ran while one was open for 0% of the time, Pallas kernels for 0%

profile of v3, /device:TPU:1, one launch (start us, length us, event | category | flops | bytes accessed | tf_op | source)
XLA Modules:
  0.0 103.9 jit_solution(645511903389246188)
XLA Ops:
  0.6 1.0 %copy.17 = f32[4,16,1280]{2,1,0:T(8,128)S(1)} copy(f32[4,16,1280]{2,0,1:T(4,128)} %bitcast.45) | data formatting | bytes 655360 | tf_op jit(solution)/shard_map/transpose | solution.py:439
  1.7 6.8 %collective-permute-start.1 = (bf16[64,1280]{1,0:T(8,128)(2,1)S(1)}, bf16[64,1280]{1,0:T(8,128)(2,1)S(1)}, u32[]{:S(2)}, u32[]{:S(2)}) collective-permute-start(bf16[64,1280]{1,0:T(8,128)(2,1)S(1)} %bitcast_convert_fusion), channel_id=1, source_target_pairs={{0,15},{1,0},{2,1},{3,2},{4,3},{5,4},{6,5},{7,6},{8,7},{9,8},{10,9... | collective-permute-start | bytes 491528 | tf_op jit(solution)/shard_map/ppermute | solution.py:51
  8.6 2.9 %collective-permute-done.1.high_ref = bf16[64,1280]{1,0:T(8,128)(2,1)S(1)} collective-permute-done((bf16[64,1280]{1,0:T(8,128)(2,1)S(1)}, bf16[64,1280]{1,0:T(8,128)(2,1)S(1)}, u32[]{:S(2)}, u32[]{:S(2)}) %collective-permute-start.1) | collective-permute-done | bytes 163872 | tf_op jit(solution)/shard_map/ppermute | solution.py:51
  11.5 5.2 %collective-permute-done.low_ref = bf16[64,1280]{1,0:T(8,128)(2,1)S(1)} collective-permute-done((bf16[64,1280]{1,0:T(8,128)(2,1)S(1)}, bf16[64,1280]{1,0:T(8,128)(2,1)S(1)}, u32[]{:S(2)}, u32[]{:S(2)}) %collective-permute-start) | collective-permute-done | bytes 163872 | tf_op jit(solution)/shard_map/ppermute | solution.py:51
  16.7 0.9 copy-done
  17.6 4.9 %shard_map.149 = (f32[4,16,320]{2,1,0:T(8,128)S(1)}, f32[4,16,320]{2,1,0:T(8,128)S(1)}) custom-call(bf16[64,1280]{1,0:T(8,128)(2,1)S(1)} %collective-permute-done.low_ref, f32[64,1280]{1,0:T(8,128)S(1)} %bitcast.29, bf16[64,1280]{1,0:T(8,128)(2,1)S(1)} %collective-permute-done.1.high_ref, bf16[256,192]{1,0:T(8,128)(2,1)S(1)} %copy-done, ...), custom_call_target="tpu_custom_call" | custom-call | flops 1000000000 | bytes 8388608 | tf_op jit(solution)/shard_map/pallas_call | solution.py:79
  22.5 1.9 %collective-permute-start.2 = (f32[4,16,320]{2,1,0:T(8,128)S(1)}, f32[4,16,320]{2,1,0:T(8,128)S(1)}, u32[]{:S(2)}, u32[]{:S(2)}) collective-permute-start(f32[4,16,320]{2,1,0:T(8,128)S(1)} %get-tuple-element.22), channel_id=1, source_target_pairs={{0,16},{16,0},{32,48},{48,32},{64,80},{80,64},{96,112},{112,96},{1... | collective-permute-start | bytes 245768 | tf_op jit(solution)/shard_map/ppermute | solution.py:55
  25.4 2.8 %collective-permute-start.5 = (f32[4,16,320]{2,1,0:T(8,128)S(1)}, f32[4,16,320]{2,1,0:T(8,128)S(1)}, u32[]{:S(2)}, u32[]{:S(2)}) collective-permute-start(f32[4,16,320]{2,1,0:T(8,128)S(1)} %shard_map.150.a_ref), channel_id=1, source_target_pairs={{0,96},{16,112},{32,0},{48,16},{64,32},{80,48},{96,64},{112,80},{1... | collective-permute-start | bytes 245768 | tf_op jit(solution)/shard_map/ppermute | solution.py:51
  29.4 14.0 %all_to_all.22 = f32[128,1,128]{2,1,0:T(1,128)S(1)} all-to-all(f32[128,1,128]{2,1,0:T(1,128)S(1)} %bitcast.35), channel_id=1, replica_groups=mesh['member'=8,'tile'=16] {'member','tile'}, dimensions={0} | all-to-all | bytes 131072 | tf_op jit(solution)/shard_map/all_to_all | solution.py:449
  43.4 2.4 %shard_map.152 = (f32[4,16,320]{2,1,0:T(8,128)S(1)}, f32[8,128]{1,0:T(8,128)S(1)}, f32[16,320]{1,0:T(8,128)S(1)}) custom-call(f32[4,16,320]{2,1,0:T(8,128)S(1)} %shard_map.150.a_ref, f32[4,16,320]{2,1,0:T(8,128)S(1)} %collective-permute-done.3.b_ref, f32[4,16,320]{2,1,0:T(8,128)S(1)} %collective-permute-done.4.c_ref, ...), custom_call_target="tpu_custom_call" | custom-call | flops 1000000000 | bytes 8388608 | tf_op jit(solution)/shard_map/pallas_call | solution.py:79
  46.7 0.9 collective-permute-done.6.other_ref
  47.6 5.1 %shard_map.153 = (f32[96,1280]{1,0:T(8,128)S(1)}, bf16[64,1280]{1,0:T(8,128)(2,1)S(1)}, bf16[64,1280]{1,0:T(8,128)(2,1)S(1)}) custom-call(f32[4,16,320]{2,1,0:T(8,128)S(1)} %get-tuple-element.23.mine_ref, f32[4,16,320]{2,1,0:T(8,128)S(1)} %collective-permute-done.6.other_ref, bf16[96,512]{1,0:T(8,128)(2,1)S(1)} %copy-done.2, ...), custom_call_target="tpu_custom_call" | custom-call | flops 1000000000 | bytes 8388608 | tf_op jit(solution)/shard_map/pallas_call | solution.py:79
  53.1 4.5 %collective-permute-start.8 = (bf16[64,1280]{1,0:T(8,128)(2,1)S(1)}, bf16[64,1280]{1,0:T(8,128)(2,1)S(1)}, u32[]{:S(2)}, u32[]{:S(2)}) collective-permute-start(bf16[64,1280]{1,0:T(8,128)(2,1)S(1)} %get-tuple-element.26), channel_id=1, source_target_pairs={{0,15},{1,0},{2,1},{3,2},{4,3},{5,4},{6,5},{7,6},{8,7},{9,8},{10,9... | collective-permute-start | bytes 491528 | tf_op jit(solution)/shard_map/ppermute | solution.py:51
  57.6 3.9 %collective-permute-done.7.low_ref = bf16[64,1280]{1,0:T(8,128)(2,1)S(1)} collective-permute-done((bf16[64,1280]{1,0:T(8,128)(2,1)S(1)}, bf16[64,1280]{1,0:T(8,128)(2,1)S(1)}, u32[]{:S(2)}, u32[]{:S(2)}) %collective-permute-start.7) | collective-permute-done | bytes 163872 | tf_op jit(solution)/shard_map/ppermute | solution.py:51
  61.9 4.6 %collective-permute-start.10 = (bf16[64,1280]{1,0:T(8,128)(2,1)S(1)}, bf16[64,1280]{1,0:T(8,128)(2,1)S(1)}, u32[]{:S(2)}, u32[]{:S(2)}) collective-permute-start(bf16[64,1280]{1,0:T(8,128)(2,1)S(1)} %get-tuple-element.27), channel_id=1, source_target_pairs={{0,15},{1,0},{2,1},{3,2},{4,3},{5,4},{6,5},{7,6},{8,7},{9,8},{10,9... | collective-permute-start | bytes 491528 | tf_op jit(solution)/shard_map/ppermute | solution.py:51
  66.5 2.3 %collective-permute-done.10.high_ref = bf16[64,1280]{1,0:T(8,128)(2,1)S(1)} collective-permute-done((bf16[64,1280]{1,0:T(8,128)(2,1)S(1)}, bf16[64,1280]{1,0:T(8,128)(2,1)S(1)}, u32[]{:S(2)}, u32[]{:S(2)}) %collective-permute-start.10) | collective-permute-done | bytes 163872 | tf_op jit(solution)/shard_map/ppermute | solution.py:51
  68.8 5.2 %collective-permute-done.9.low_ref = bf16[64,1280]{1,0:T(8,128)(2,1)S(1)} collective-permute-done((bf16[64,1280]{1,0:T(8,128)(2,1)S(1)}, bf16[64,1280]{1,0:T(8,128)(2,1)S(1)}, u32[]{:S(2)}, u32[]{:S(2)}) %collective-permute-start.9) | collective-permute-done | bytes 163872 | tf_op jit(solution)/shard_map/ppermute | solution.py:51
  74.0 4.8 %shard_map.155 = (f32[4,16,320]{2,1,0:T(8,128)S(1)}, f32[4,16,320]{2,1,0:T(8,128)S(1)}) custom-call(bf16[64,1280]{1,0:T(8,128)(2,1)S(1)} %collective-permute-done.9.low_ref, f32[64,1280]{1,0:T(8,128)S(1)} %get-tuple-element.28.own_ref.grad_ref, bf16[64,1280]{1,0:T(8,128)(2,1)S(1)} %collective-permute-done.10.high_ref, bf16[256,192]{1,0:T(8,128)(2,1)S(1)} %copy-done.1, ...), custom_call_target="tpu_custom_call" | custom-call | flops 1000000000 | bytes 8388608 | tf_op jit(solution)/shard_map/pallas_call | solution.py:79
  78.8 3.0 %collective-permute-start.11 = (f32[4,16,320]{2,1,0:T(8,128)S(1)}, f32[4,16,320]{2,1,0:T(8,128)S(1)}, u32[]{:S(2)}, u32[]{:S(2)}) collective-permute-start(f32[4,16,320]{2,1,0:T(8,128)S(1)} %get-tuple-element.30), channel_id=1, source_target_pairs={{0,16},{16,0},{32,48},{48,32},{64,80},{80,64},{96,112},{112,96},{1... | collective-permute-start | bytes 245768 | tf_op jit(solution)/shard_map/ppermute | solution.py:55
  81.8 0.9 collective-permute-done.11.b_ref
  83.2 1.7 %collective-permute-start.13 = (f32[16,320]{1,0:T(8,128)S(1)}, f32[16,320]{1,0:T(8,128)S(1)}, u32[]{:S(2)}, u32[]{:S(2)}) collective-permute-start(f32[16,320]{1,0:T(8,128)S(1)} %get-tuple-element.33), channel_id=1, source_target_pairs={{0,64},{16,80},{32,96},{48,112},{64,0},{80,16},{96,32},{112,48},{1... | collective-permute-start | bytes 61448 | tf_op jit(solution)/shard_map/ppermute | solution.py:51
  85.7 1.1 %collective-permute-done.12.b_ref = f32[16,320]{1,0:T(8,128)S(1)} collective-permute-done((f32[16,320]{1,0:T(8,128)S(1)}, f32[16,320]{1,0:T(8,128)S(1)}, u32[]{:S(2)}, u32[]{:S(2)}) %collective-permute-start.12) | collective-permute-done | bytes 20512 | tf_op jit(solution)/shard_map/ppermute | solution.py:51
  88.4 14.5 %all_to_all.23 = f32[128,1,128]{2,1,0:T(1,128)S(1)} all-to-all(f32[128,1,128]{2,1,0:T(1,128)S(1)} %bitcast.34), channel_id=1, replica_groups=mesh['member'=8,'tile'=16] {'member','tile'}, dimensions={0} | all-to-all | bytes 131072 | tf_op jit(solution)/shard_map/all_to_all | solution.py:477
  102.9 1.0 shard_map.158
  (40 shorter events, 6.1 us)
Async XLA Ops:
  0.6 24.7 %copy-start.6 = (f32[16,320]{1,0:T(8,128)S(1)}, f32[16,320]{1,0:T(8,128)}, u32[]{:S(2)}) copy-start(f32[16,320]{1,0:T(8,128)} %base_ref.3) | copy-start | bytes 61444
  1.7 27.5 %copy-start.7 = (f32[1,128,8]{1,2,0:T(8,128)S(1)}, f32[1,128,8]{1,2,0:T(8,128)}, u32[]{:S(2)}) copy-start(f32[1,128,8]{1,2,0:T(8,128)} %param.22) | copy-start | bytes 12292
  1.7 27.5 %copy-start.8 = (f32[1,128,8]{1,2,0:T(8,128)S(1)}, f32[1,128,8]{1,2,0:T(8,128)}, u32[]{:S(2)}) copy-start(f32[1,128,8]{1,2,0:T(8,128)} %param.23) | copy-start | bytes 12292
  1.7 9.7 %collective-permute-start.1 = (bf16[64,1280]{1,0:T(8,128)(2,1)S(1)}, bf16[64,1280]{1,0:T(8,128)(2,1)S(1)}, u32[]{:S(2)}, u32[]{:S(2)}) collective-permute-start(bf16[64,1280]{1,0:T(8,128)(2,1)S(1)} %bitcast_convert_fusion), channel_id=1, source_target_pairs={{0,15},{1,0},{2,1},{3,2},{4,3},{5,4},{6,5},{7,6},{8,7},{9,8},{10,9... | collective-permute-start | bytes 491528 | tf_op jit(solution)/shard_map/ppermute | solution.py:51
  8.6 8.1 %collective-permute-start = (bf16[64,1280]{1,0:T(8,128)(2,1)S(1)}, bf16[64,1280]{1,0:T(8,128)(2,1)S(1)}, u32[]{:S(2)}, u32[]{:S(2)}) collective-permute-start(bf16[64,1280]{1,0:T(8,128)(2,1)S(1)} %bitcast_convert_fusion), channel_id=1, source_target_pairs={{0,1},{1,2},{2,3},{3,4},{4,5},{5,6},{6,7},{7,8},{8,9},{9,10},{10,1... | collective-permute-start | bytes 491528 | tf_op jit(solution)/shard_map/ppermute | solution.py:51
  17.6 25.7 %copy-start.3 = (s32[1,128,8,8]{1,3,2,0:T(8,128)S(1)}, s32[1,128,8,8]{1,3,2,0:T(8,128)}, u32[]{:S(2)}) copy-start(s32[1,128,8,8]{1,3,2,0:T(8,128)} %param.18) | copy-start | bytes 98308
  17.6 25.7 %copy-start.4 = (f32[1,128,8,8]{1,3,2,0:T(8,128)S(1)}, f32[1,128,8,8]{1,3,2,0:T(8,128)}, u32[]{:S(2)}) copy-start(f32[1,128,8,8]{1,3,2,0:T(8,128)} %param.19) | copy-start | bytes 98308
  17.6 25.8 %copy-start.5 = (f32[1,128,8,8]{1,3,2,0:T(8,128)S(1)}, f32[1,128,8,8]{1,3,2,0:T(8,128)}, u32[]{:S(2)}) copy-start(f32[1,128,8,8]{1,3,2,0:T(8,128)} %param.20) | copy-start | bytes 98308
  17.6 25.8 %copy-start.9 = (s32[1,128,8]{1,2,0:T(8,128)S(1)}, s32[1,128,8]{1,2,0:T(8,128)}, u32[]{:S(2)}) copy-start(s32[1,128,8]{1,2,0:T(8,128)} %param.21) | copy-start | bytes 12292
  22.5 25.1 %copy-start.2 = (bf16[96,512]{1,0:T(8,128)(2,1)S(1)}, bf16[96,512]{1,0:T(8,128)(2,1)}, u32[]{:S(2)}) copy-start(bf16[96,512]{1,0:T(8,128)(2,1)} %constant.5.clone.back_ref) | copy-start | bytes 294916
  22.5 2.8 %collective-permute-start.2 = (f32[4,16,320]{2,1,0:T(8,128)S(1)}, f32[4,16,320]{2,1,0:T(8,128)S(1)}, u32[]{:S(2)}, u32[]{:S(2)}) collective-permute-start(f32[4,16,320]{2,1,0:T(8,128)S(1)} %get-tuple-element.22), channel_id=1, source_target_pairs={{0,16},{16,0},{32,48},{48,32},{64,80},{80,64},{96,112},{112,96},{1... | collective-permute-start | bytes 245768 | tf_op jit(solution)/shard_map/ppermute | solution.py:55
  25.4 18.0 %collective-permute-start.5 = (f32[4,16,320]{2,1,0:T(8,128)S(1)}, f32[4,16,320]{2,1,0:T(8,128)S(1)}, u32[]{:S(2)}, u32[]{:S(2)}) collective-permute-start(f32[4,16,320]{2,1,0:T(8,128)S(1)} %shard_map.150.a_ref), channel_id=1, source_target_pairs={{0,96},{16,112},{32,0},{48,16},{64,32},{80,48},{96,64},{112,80},{1... | collective-permute-start | bytes 245768 | tf_op jit(solution)/shard_map/ppermute | solution.py:51
  28.2 15.2 %collective-permute-start.4 = (f32[4,16,320]{2,1,0:T(8,128)S(1)}, f32[4,16,320]{2,1,0:T(8,128)S(1)}, u32[]{:S(2)}, u32[]{:S(2)}) collective-permute-start(f32[4,16,320]{2,1,0:T(8,128)S(1)} %shard_map.150.a_ref), channel_id=1, source_target_pairs={{0,64},{16,80},{32,96},{48,112},{64,0},{80,16},{96,32},{112,48},{1... | collective-permute-start | bytes 245768 | tf_op jit(solution)/shard_map/ppermute | solution.py:51
  28.5 14.8 %collective-permute-start.3 = (f32[4,16,320]{2,1,0:T(8,128)S(1)}, f32[4,16,320]{2,1,0:T(8,128)S(1)}, u32[]{:S(2)}, u32[]{:S(2)}) collective-permute-start(f32[4,16,320]{2,1,0:T(8,128)S(1)} %shard_map.150.a_ref), channel_id=1, source_target_pairs={{0,32},{16,48},{32,64},{48,80},{64,96},{80,112},{96,0},{112,16},{1... | collective-permute-start | bytes 245768 | tf_op jit(solution)/shard_map/ppermute | solution.py:51
  45.8 28.2 %copy-start.1 = (bf16[256,192]{1,0:T(8,128)(2,1)S(1)}, bf16[256,192]{1,0:T(8,128)(2,1)}, u32[]{:S(2)}) copy-start(bf16[256,192]{1,0:T(8,128)(2,1)} %constant.4.clone.refine_ref) | copy-start | bytes 294916
  45.8 1.8 %collective-permute-start.6 = (f32[4,16,320]{2,1,0:T(8,128)S(1)}, f32[4,16,320]{2,1,0:T(8,128)S(1)}, u32[]{:S(2)}, u32[]{:S(2)}) collective-permute-start(f32[4,16,320]{2,1,0:T(8,128)S(1)} %get-tuple-element.23.mine_ref), channel_id=1, source_target_pairs={{0,16},{16,0},{32,48},{48,32},{64,80},{80,64},{96,112},{112,96},{1... | collective-permute-start | bytes 245768 | tf_op jit(solution)/shard_map/ppermute | solution.py:55
  52.8 8.8 %collective-permute-start.7 = (bf16[64,1280]{1,0:T(8,128)(2,1)S(1)}, bf16[64,1280]{1,0:T(8,128)(2,1)S(1)}, u32[]{:S(2)}, u32[]{:S(2)}) collective-permute-start(bf16[64,1280]{1,0:T(8,128)(2,1)S(1)} %get-tuple-element.24), channel_id=1, source_target_pairs={{0,1},{1,2},{2,3},{3,4},{4,5},{5,6},{6,7},{7,8},{8,9},{9,10},{10,1... | collective-permute-start | bytes 491528 | tf_op jit(solution)/shard_map/ppermute | solution.py:51
  53.1 8.4 %collective-permute-start.8 = (bf16[64,1280]{1,0:T(8,128)(2,1)S(1)}, bf16[64,1280]{1,0:T(8,128)(2,1)S(1)}, u32[]{:S(2)}, u32[]{:S(2)}) collective-permute-start(bf16[64,1280]{1,0:T(8,128)(2,1)S(1)} %get-tuple-element.26), channel_id=1, source_target_pairs={{0,15},{1,0},{2,1},{3,2},{4,3},{5,4},{6,5},{7,6},{8,7},{9,8},{10,9... | collective-permute-start | bytes 491528 | tf_op jit(solution)/shard_map/ppermute | solution.py:51
  61.9 6.8 %collective-permute-start.10 = (bf16[64,1280]{1,0:T(8,128)(2,1)S(1)}, bf16[64,1280]{1,0:T(8,128)(2,1)S(1)}, u32[]{:S(2)}, u32[]{:S(2)}) collective-permute-start(bf16[64,1280]{1,0:T(8,128)(2,1)S(1)} %get-tuple-element.27), channel_id=1, source_target_pairs={{0,15},{1,0},{2,1},{3,2},{4,3},{5,4},{6,5},{7,6},{8,7},{9,8},{10,9... | collective-permute-start | bytes 491528 | tf_op jit(solution)/shard_map/ppermute | solution.py:51
  66.5 7.5 %collective-permute-start.9 = (bf16[64,1280]{1,0:T(8,128)(2,1)S(1)}, bf16[64,1280]{1,0:T(8,128)(2,1)S(1)}, u32[]{:S(2)}, u32[]{:S(2)}) collective-permute-start(bf16[64,1280]{1,0:T(8,128)(2,1)S(1)} %get-tuple-element.27), channel_id=1, source_target_pairs={{0,1},{1,2},{2,3},{3,4},{4,5},{5,6},{6,7},{7,8},{8,9},{9,10},{10,1... | collective-permute-start | bytes 491528 | tf_op jit(solution)/shard_map/ppermute | solution.py:51
  78.8 3.9 %collective-permute-start.11 = (f32[4,16,320]{2,1,0:T(8,128)S(1)}, f32[4,16,320]{2,1,0:T(8,128)S(1)}, u32[]{:S(2)}, u32[]{:S(2)}) collective-permute-start(f32[4,16,320]{2,1,0:T(8,128)S(1)} %get-tuple-element.30), channel_id=1, source_target_pairs={{0,16},{16,0},{32,48},{48,32},{64,80},{80,64},{96,112},{112,96},{1... | collective-permute-start | bytes 245768 | tf_op jit(solution)/shard_map/ppermute | solution.py:55
  82.8 4.0 %collective-permute-start.12 = (f32[16,320]{1,0:T(8,128)S(1)}, f32[16,320]{1,0:T(8,128)S(1)}, u32[]{:S(2)}, u32[]{:S(2)}) collective-permute-start(f32[16,320]{1,0:T(8,128)S(1)} %get-tuple-element.32), channel_id=1, source_target_pairs={{0,32},{16,48},{32,64},{48,80},{64,96},{80,112},{96,0},{112,16},{1... | collective-permute-start | bytes 61448 | tf_op jit(solution)/shard_map/ppermute | solution.py:51
  83.2 4.2 %collective-permute-start.13 = (f32[16,320]{1,0:T(8,128)S(1)}, f32[16,320]{1,0:T(8,128)S(1)}, u32[]{:S(2)}, u32[]{:S(2)}) collective-permute-start(f32[16,320]{1,0:T(8,128)S(1)} %get-tuple-element.33), channel_id=1, source_target_pairs={{0,64},{16,80},{32,96},{48,112},{64,0},{80,16},{96,32},{112,48},{1... | collective-permute-start | bytes 61448 | tf_op jit(solution)/shard_map/ppermute | solution.py:51
  84.9 3.0 %collective-permute-start.14 = (f32[16,320]{1,0:T(8,128)S(1)}, f32[16,320]{1,0:T(8,128)S(1)}, u32[]{:S(2)}, u32[]{:S(2)}) collective-permute-start(f32[16,320]{1,0:T(8,128)S(1)} %get-tuple-element.34), channel_id=1, source_target_pairs={{0,96},{16,112},{32,0},{48,16},{64,32},{80,48},{96,64},{112,80},{1... | collective-permute-start | bytes 61448 | tf_op jit(solution)/shard_map/ppermute | solution.py:51
  (1 other events, 0.9 us)

commit v4 on v3

--- a/solution.py
+++ b/solution.py
@@ -21,7 +21,7 @@
 CHUNK = NCORE * WIDTH
 SLOTS = 8
 BATCHES = 128
-ROOM = 24 << 20
+ROOM = 12 << 20
 FLOAT, HALF = jnp.float32, jnp.bfloat16
 
 
@@ -51,6 +51,17 @@
     return lax.ppermute(values, axis, [(i, (i + step) % count) for i in range(count)])
 
 
+def swap_near(values):
+    return lax.ppermute(values, "tile", [(i, i ^ 1) for i in range(NTILE)])
+
+
+def swap_far(values):
+    pairs = [(0, 0), (NTILE - 1, NTILE - 1)]
+    for i in range(1, NTILE - 1, 2):
+        pairs += [(i, i + 1), (i + 1, i)]
+    return lax.ppermute(values, "tile", pairs)
+
+
 def swap_core(values):
     return lax.ppermute(values, "member", [(i, i ^ 1) for i in range(NMEMBER)])
 
@@ -100,28 +111,6 @@
     return jnp.where(tile_pos > 0, 1.0, 0.0), jnp.where(tile_pos < NTILE - 1, 1.0, 0.0)
 
 
-def streams(perturb_ref, map_ref, perturb_buf, map_buf, sem):
-    copies = []
-    for y in range(NY):
-        cols = pl.ds(y * CHUNK, CHUNK)
-        copies.append(
-            (
-                pltpu.make_async_copy(map_ref.at[:, cols], map_buf.at[y], sem.at[0, y]),
-                pltpu.make_async_copy(
-                    perturb_ref.at[:, :, cols], perturb_buf.at[y], sem.at[1, y]
-                ),
-            )
-        )
-    return copies
-
-
-BUFFERS = [
-    pltpu.VMEM((NY, MEMBERS_HERE, FINE_ROWS, CHUNK), HALF),
-    pltpu.VMEM((NY, COARSE_COLS, CHUNK), HALF),
-    pltpu.SemaphoreType.DMA((2, NY)),
-]
-
-
 def swept(rows, masks):
     for _ in range(KSM):
         rows = [v if m is None else v * m for v, m in zip(rows, masks)]
@@ -137,37 +126,75 @@
     return pl.ds(row * MEMBERS_HERE, MEMBERS_HERE)
 
 
+def is_even():
+    return lax.rem(lax.axis_index("tile"), 2) == 0
+
+
+def sides(a_ref, b_ref, cols, even):
+    first = [a_ref[row_slice(r), cols].astype(FLOAT) for r in range(4)]
+    second = [b_ref[row_slice(r), cols].astype(FLOAT) for r in range(4)]
+    low = [jnp.where(even, v, u) for u, v in zip(first, second)]
+    high = [jnp.where(even, u, v) for u, v in zip(first, second)]
+    return low, high
+
+
+def streamed_kernel(
+    a_ref, own_ref, b_ref, refine_hbm, perturb_hbm, map_hbm, after_ref,
+    mine_ref, other_ref, refine_ref, perturb_ref, map_ref, smooth_ref, sem,
+):
+    copies = [(pltpu.make_async_copy(refine_hbm, refine_ref, sem.at[0, NY]),)]
+    for y in range(NY):
+        cols = pl.ds(y * CHUNK, CHUNK)
+        copies.append(
+            (
+                pltpu.make_async_copy(map_hbm.at[:, cols], map_ref.at[:, cols], sem.at[0, y]),
+                pltpu.make_async_copy(
+                    perturb_hbm.at[:, :, cols], perturb_ref.at[:, :, cols], sem.at[1, y]
+                ),
+            )
+        )
+    for group in copies[1:2] + copies[:1] + copies[2:]:
+        for copy in group:
+            copy.start()
+
+    def arrived(y):
+        for copy in copies[y + 1] + (copies[0] if y == 0 else ()):
+            copy.wait()
+
+    forward_kernel(
+        a_ref, own_ref, b_ref, refine_ref, perturb_ref, map_ref, mine_ref, other_ref, smooth_ref,
+        arrived=arrived,
+    )
+
+
 def forward_kernel(
-    low_ref, own_ref, high_ref, refine_ref, perturb_ref, map_ref,
-    mine_ref, other_ref, smooth_ref, perturb_buf, map_buf, sem,
-):
-    copies = streams(perturb_ref, map_ref, perturb_buf, map_buf, sem)
-    for pair in copies:
-        for copy in pair:
-            copy.start()
+    a_ref, own_ref, b_ref, refine_ref, perturb_ref, map_ref, mine_ref, other_ref, smooth_ref,
+    arrived=None,
+):
     _, core_pos, _ = place()
+    even = is_even()
     below, above = edges()
     masks = [below] * 4 + [None] * 4 + [above] * 4
     for start in range(0, COARSE_COLS, 128):
         cols = pl.ds(start, 128)
-        rows = [low_ref[row_slice(r), cols].astype(FLOAT) for r in range(4)]
-        rows += [own_ref[row_slice(r), cols] for r in range(4)]
-        rows += [high_ref[row_slice(r), cols].astype(FLOAT) for r in range(4)]
+        low, high = sides(a_ref, b_ref, cols, even)
+        rows = low + [own_ref[row_slice(r), cols] for r in range(4)] + high
         for r, value in enumerate(swept(rows, masks)):
             smooth_ref[row_slice(r), cols] = value.astype(HALF)
     smooth = smooth_ref[...]
-    for y, (map_copy, perturb_copy) in enumerate(copies):
-        map_copy.wait()
-        mapped = jnp.dot(smooth, map_buf[y], preferred_element_type=FLOAT)
+    for y in range(NY):
+        cols = pl.ds(y * CHUNK, CHUNK)
+        if arrived is not None:
+            arrived(y)
+        mapped = jnp.dot(smooth, map_ref[:, cols], preferred_element_type=FLOAT)
         high = mapped.astype(HALF)
         low = (mapped - high.astype(FLOAT)).astype(HALF)
         fine = jnp.dot(
             refine_ref[...], jnp.concatenate([high, low], axis=0), preferred_element_type=FLOAT
         )
-        perturb_copy.wait()
         total = None
         for k in range(MEMBERS_HERE):
-            term = fine[k * FINE_ROWS : (k + 1) * FINE_ROWS] * perturb_buf[y, k].astype(FLOAT)
+            term = fine[k * FINE_ROWS : (k + 1) * FINE_ROWS] * perturb_ref[k, :, cols].astype(FLOAT)
             total = term if total is None else total + term
         first, second = total[:, :WIDTH], total[:, WIDTH:]
         mine_ref[y] = jnp.where(core_pos == 0, first, second)
@@ -177,54 +204,62 @@
 REGIONS = ((NY, FINE_ROWS, WIDTH), FLOAT)
 
 
-def partial_forward(low, own, high, perturb, column_map):
+SMOOTH = pltpu.VMEM(((ROWS + 2) * MEMBERS_HERE, COARSE_COLS), HALF)
+
+
+def first_forward(first, own, second, perturb, column_map, after):
     matrix = member_matrix()
     matrix = jnp.asarray(np.concatenate([matrix, matrix], axis=1), HALF)
+    operators = (matrix, perturb, column_map)
     return call(
-        forward_kernel,
-        (REGIONS, REGIONS),
-        (low, own, high, matrix, perturb, column_map),
-        far=(4, 5),
-        scratch=[pltpu.VMEM(((ROWS + 2) * MEMBERS_HERE, COARSE_COLS), HALF)] + BUFFERS,
+        streamed_kernel,
+        (REGIONS, REGIONS) + tuple((x.shape, x.dtype) for x in operators),
+        (first, own, second) + operators + (after,),
+        far=(3, 4, 5),
+        scratch=[SMOOTH, pltpu.SemaphoreType.DMA((2, NY + 1))],
+    )
+
+
+def later_forward(first, own, second, *operators):
+    return call(
+        forward_kernel, (REGIONS, REGIONS), (first, own, second) + operators, scratch=[SMOOTH]
     )
 
 
 def adjoint_kernel(
     mine_ref, other_ref, back_ref, perturb_ref, map_ref,
-    part_ref, up_ref, down_ref, perturb_buf, map_buf, sem,
-):
-    copies = streams(perturb_ref, map_ref, perturb_buf, map_buf, sem)
-    for pair in copies:
-        for copy in pair[::-1]:
-            copy.start()
+    part_ref, a_ref, b_ref,
+):
     _, core_pos, _ = place()
+    even = is_even()
     total = None
-    for y, (map_copy, perturb_copy) in enumerate(copies):
+    for y in range(NY):
+        cols = pl.ds(y * CHUNK, CHUNK)
         mine, other = mine_ref[y], other_ref[y]
         first = jnp.where(core_pos == 0, mine, other)
         second = jnp.where(core_pos == 0, other, mine)
         spread = jnp.concatenate([first, second], axis=1)
-        perturb_copy.wait()
         highs, lows = [], []
         for k in range(MEMBERS_HERE):
-            term = perturb_buf[y, k].astype(FLOAT) * spread
+            term = perturb_ref[k, :, cols].astype(FLOAT) * spread
             high = term.astype(HALF)
             highs.append(high)
             lows.append((term - high.astype(FLOAT)).astype(HALF))
         pulled = jnp.dot(
             back_ref[...], jnp.concatenate(highs + lows, axis=0), preferred_element_type=FLOAT
         )
-        map_copy.wait()
         part = lax.dot_general(
             pulled.astype(HALF),
-            map_buf[y],
+            map_ref[:, cols],
             (((1,), (1,)), ((), ())),
             preferred_element_type=FLOAT,
         )
         total = part if total is None else total + part
     part_ref[...] = total
-    up_ref[...] = total[2 * MEMBERS_HERE :].astype(HALF)
-    down_ref[...] = total[: 4 * MEMBERS_HERE].astype(HALF)
+    up = total[2 * MEMBERS_HERE :].astype(HALF)
+    down = total[: 4 * MEMBERS_HERE].astype(HALF)
+    a_ref[...] = jnp.where(even, up, down)
+    b_ref[...] = jnp.where(even, down, up)
 
 
 def partial_adjoint(mine, other, perturb, column_map):
@@ -235,20 +270,18 @@
         adjoint_kernel,
         ((((ROWS + 2) * MEMBERS_HERE, COARSE_COLS), FLOAT), rim, rim),
         (mine, other, matrix, perturb, column_map),
-        far=(3, 4),
-        scratch=BUFFERS,
-    )
-
-
-def gradient_kernel(low_ref, part_ref, high_ref, own_ref, grad_ref, half_ref, square_ref):
+    )
+
+
+def gradient_kernel(a_ref, part_ref, b_ref, own_ref, grad_ref, half_ref, square_ref):
     below, above = edges()
     masks = [below] * 3 + [None] * 4 + [above] * 3
+    even = is_even()
     square = None
     for start in range(0, COARSE_COLS, 128):
         cols = pl.ds(start, 128)
-        low = [low_ref[row_slice(r), cols].astype(FLOAT) for r in range(4)]
+        low, high = sides(a_ref, b_ref, cols, even)
         part = [part_ref[row_slice(r), cols] for r in range(6)]
-        high = [high_ref[row_slice(r), cols].astype(FLOAT) for r in range(4)]
         rows = [low[0], low[1], low[2] + part[0], low[3] * below + part[1], part[2], part[3]]
         rows += [part[4] + high[0] * above, part[5] + high[1], high[2], high[3]]
         for r, value in enumerate(swept(rows, masks)):
@@ -269,7 +302,15 @@
     )
 
 
-def send_kernel(value_ref, error_ref, gain_ref, sent_ref):
+def send_kernel(value_hbm, error_hbm, gain_ref, sent_ref, value_ref, error_ref, sem):
+    copies = [
+        pltpu.make_async_copy(value_hbm, value_ref, sem.at[0]),
+        pltpu.make_async_copy(error_hbm, error_ref, sem.at[1]),
+    ]
+    for copy in copies:
+        copy.start()
+    for copy in copies:
+        copy.wait()
     lanes = lax.broadcasted_iota(jnp.int32, (SLOTS, BATCHES), 1)
     block = lanes // (NCORE * NTILE)
     rows = []
@@ -438,13 +479,15 @@
     flat = (ROWS * MEMBERS_HERE, COARSE_COLS)
     own = jnp.transpose(weights, (1, 0, 2)).reshape(flat)
     half = own.astype(HALF)
-    low, high = turn(half, 1, "tile"), turn(half, -1, "tile")
+    near_rows, far_rows = swap_near(half), swap_far(half)
 
     (sent,) = call(
         send_kernel,
         (((BATCHES, BATCHES), FLOAT),),
         (obs_value[0].T, obs_error[0].T, instrument_gain),
+        far=(0, 1),
         scalar=(2,),
+        scratch=[pltpu.VMEM((SLOTS, BATCHES), FLOAT)] * 2 + [pltpu.SemaphoreType.DMA((2,))],
     )
     data = lax.all_to_all(sent, ("member", "tile"), split_axis=0, concat_axis=0, tiled=True)
 
@@ -453,7 +496,9 @@
     column_frac = jnp.transpose(column_fraction[0], (1, 2, 0))
     lengths = block_lengths[0].T
 
-    mine, other = partial_forward(low, own, high, perturb, column_map)
+    mine, other, matrix, perturb, column_map = first_forward(
+        near_rows, own, far_rows, perturb, column_map, data
+    )
     (mine,) = call(add_kernel, (REGIONS,), (mine, swap_core(other), background))
     pieces = [mine] + [turn(mine, NCORE * i, "member") for i in range(1, NY)]
     region = ((FINE_ROWS, WIDTH), FLOAT)
@@ -463,9 +508,9 @@
         (*pieces, index, row_frac, column_frac, lengths, data),
     )
     part, up, down = partial_adjoint(spread, swap_core(spread), perturb, column_map)
-    gradient, half, square = gradient_of(turn(up, 1, "tile"), part, turn(down, -1, "tile"), own)
-    mine, other = partial_forward(
-        turn(half, 1, "tile"), gradient, turn(half, -1, "tile"), perturb, column_map
+    gradient, half, square = gradient_of(swap_near(up), part, swap_far(down), own)
+    mine, other = later_forward(
+        swap_near(half), gradient, swap_far(half), matrix, perturb, column_map
     )
     pieces = call(pick_kernel, (region,) * NY, (mine, swap_core(other)))
     pieces = [pieces[0]] + [turn(pieces[i], NCORE * i, "member") for i in range(1, NY)]

time: 104 us -> 98.8 us (0.950)
  blocking collectives: 28.5 us -> 41.2 us
  starting transfers between devices: 28.7 us -> 22.1 us
  waiting for transfers between devices: 23.9 us -> 18.1 us
  Pallas kernels: 19.3 us -> 14.6 us
    ppermute x12 -> x6, starting transfers between devices: 23 us -> 5.66 us  [turn(): lax.ppermute(values, axis, [(i, (i + step) % count) for i in range(count)])]
    ppermute x12 -> x6, waiting for transfers between devices: 21.7 us -> 8.11 us  [turn(): lax.ppermute(values, axis, [(i, (i + step) % count) for i in range(count)])]
    all_to_all x2, blocking collectives: 28.5 us -> 41.2 us  [shards(): lax.all_to_all(sent, ('member', 'tile'), split_axis=0, concat_axis=0, til...]
    ppermute x0 -> x6, starting transfers between devices: none -> 11.7 us  [the longest x3 9.74 us: swap_near(): return lax.ppermute(values, 'tile', [(i, i ^ 1) for i in range(NTILE)])]
    ppermute x0 -> x6, waiting for transfers between devices: none -> 7.15 us  [the longest x3 7.14 us: swap_near(): return lax.ppermute(values, 'tile', [(i, i ^ 1) for i in range(NTILE)])]
    pallas_call x10, Pallas kernels: 19.3 us -> 14.6 us  [call(): pl.pallas_call(kernel, out_shape=tuple((jax.ShapeDtypeStruct(shape, kind)...]
    ppermute x3, starting transfers between devices: 5.74 us -> 4.66 us  [swap_core(): return lax.ppermute(values, 'member', [(i, i ^ 1) for i in range(NMEMBER)])]
  transfers between devices with their start and end apart: 15 -> 15, of which waited for: 11 -> 11; matrix products, arithmetic and copies ran while one was open for 0% -> 0% of each run, Pallas kernels for 0% -> 1%
where the time goes in v4:
time: 98.8 us; the launch traced here: 98.5 us
  blocking collectives  41.2 us (42%)
  starting transfers between devices  22.1 us (22%)
  waiting for transfers between devices  18.1 us (18%)
  Pallas kernels  14.6 us (15%)
  between operations  1.44 us (1%)
  local copies, waits for them, and re-layouts  1.07 us (1%)
    all_to_all x2, blocking collectives, shards(): lax.all_to_all(sent, ('member', 'tile'), split_axis=0, concat_axis=0, til...  41.2 us
    pallas_call x10, Pallas kernels, call(): pl.pallas_call(kernel, out_shape=tuple((jax.ShapeDtypeStruct(shape, kind)...  14.6 us
    ppermute x3, starting transfers between devices, swap_near(): return lax.ppermute(values, 'tile', [(i, i ^ 1) for i in range(NTILE)])  9.74 us
    ppermute x6, waiting for transfers between devices, turn(): lax.ppermute(values, axis, [(i, (i + step) % count) for i in range(count)])  8.11 us
    ppermute x3, waiting for transfers between devices, swap_near(): return lax.ppermute(values, 'tile', [(i, i ^ 1) for i in range(NTILE)])  7.14 us
    ppermute x6, starting transfers between devices, turn(): lax.ppermute(values, axis, [(i, (i + step) % count) for i in range(count)])  5.66 us
    ppermute x3, starting transfers between devices, swap_core(): return lax.ppermute(values, 'member', [(i, i ^ 1) for i in range(NMEMBER)])  4.66 us
    ppermute x3, waiting for transfers between devices, swap_core(): return lax.ppermute(values, 'member', [(i, i ^ 1) for i in range(NMEMBER)])  2.83 us
  transfers between devices with their start and end apart: 15, of which 11 were waited for; matrix products, arithmetic and copies ran while one was open for 0% of the time, Pallas kernels for 1%

profile of v4, /device:TPU:1, one launch (start us, length us, event | category | flops | bytes accessed | tf_op | source)
XLA Modules:
  0.0 98.5 jit_solution(5931026014031256269)
XLA Ops:
  0.6 1.0 %copy.16 = f32[4,16,1280]{2,1,0:T(8,128)S(1)} copy(f32[4,16,1280]{2,0,1:T(4,128)} %bitcast.44) | data formatting | bytes 655360 | tf_op jit(solution)/shard_map/transpose | solution.py:480
  2.4 4.6 %collective-permute-start = (bf16[64,1280]{1,0:T(8,128)(2,1)S(1)}, bf16[64,1280]{1,0:T(8,128)(2,1)S(1)}, u32[]{:S(2)}, u32[]{:S(2)}) collective-permute-start(bf16[64,1280]{1,0:T(8,128)(2,1)S(1)} %bitcast_convert_fusion), channel_id=1, source_target_pairs={{0,1},{1,0},{2,3},{3,2},{4,5},{5,4},{6,7},{7,6},{8,9},{9,8},{10,11... | collective-permute-start | bytes 491528 | tf_op jit(solution)/shard_map/ppermute | solution.py:55
  7.6 0.9 shard_map.140
  8.5 20.4 %all_to_all.22 = f32[128,1,128]{2,1,0:T(1,128)S(1)} all-to-all(f32[128,1,128]{2,1,0:T(1,128)S(1)} %bitcast.36), channel_id=1, replica_groups=mesh['member'=8,'tile'=16] {'member','tile'}, dimensions={0} | all-to-all | bytes 131072 | tf_op jit(solution)/shard_map/all_to_all | solution.py:492
  29.0 4.5 %shard_map.141 = (f32[4,16,320]{2,1,0:T(8,128)S(1)}, f32[4,16,320]{2,1,0:T(8,128)S(1)}, bf16[256,192]{1,0:T(8,128)(2,1)S(1)}, bf16[16,16,2560]{2,1,0:T(8,128)(2,1)S(1)}, bf16[1280,2560]{1,0:T(8,128)(2,1)S(1)}) custom-call(bf16[64,1280]{1,0:T(8,128)(2,1)S(1)} %collective-permute-done.a_ref, f32[64,1280]{1,0:T(8,128)S(1)} %bitcast.29, ...), custom_call_target="tpu_custom_call" | custom-call | flops 1000000000 | bytes 8388608 | tf_op jit(solution)/shard_map/pallas_call | solution.py:90
  34.4 0.9 collective-permute-done.2.b_ref
  36.2 1.3 %collective-permute-start.4 = (f32[4,16,320]{2,1,0:T(8,128)S(1)}, f32[4,16,320]{2,1,0:T(8,128)S(1)}, u32[]{:S(2)}, u32[]{:S(2)}) collective-permute-start(f32[4,16,320]{2,1,0:T(8,128)S(1)} %shard_map.142.a_ref), channel_id=1, source_target_pairs={{0,64},{16,80},{32,96},{48,112},{64,0},{80,16},{96,32},{112,48},{1... | collective-permute-start | bytes 245768 | tf_op jit(solution)/shard_map/ppermute | solution.py:51
  37.6 1.9 %collective-permute-done.5.d_ref = f32[4,16,320]{2,1,0:T(8,128)S(1)} collective-permute-done((f32[4,16,320]{2,1,0:T(8,128)S(1)}, f32[4,16,320]{2,1,0:T(8,128)S(1)}, u32[]{:S(2)}, u32[]{:S(2)}) %collective-permute-start.5) | collective-permute-done | bytes 81952 | tf_op jit(solution)/shard_map/ppermute | solution.py:51
  39.4 1.8 %collective-permute-done.4.c_ref = f32[4,16,320]{2,1,0:T(8,128)S(1)} collective-permute-done((f32[4,16,320]{2,1,0:T(8,128)S(1)}, f32[4,16,320]{2,1,0:T(8,128)S(1)}, u32[]{:S(2)}, u32[]{:S(2)}) %collective-permute-start.4) | collective-permute-done | bytes 81952 | tf_op jit(solution)/shard_map/ppermute | solution.py:51
  41.2 2.8 %collective-permute-done.3.b_ref = f32[4,16,320]{2,1,0:T(8,128)S(1)} collective-permute-done((f32[4,16,320]{2,1,0:T(8,128)S(1)}, f32[4,16,320]{2,1,0:T(8,128)S(1)}, u32[]{:S(2)}, u32[]{:S(2)}) %collective-permute-start.3) | collective-permute-done | bytes 81952 | tf_op jit(solution)/shard_map/ppermute | solution.py:51
  44.1 2.4 %shard_map.143 = (f32[4,16,320]{2,1,0:T(8,128)S(1)}, f32[8,128]{1,0:T(8,128)S(1)}, f32[16,320]{1,0:T(8,128)S(1)}) custom-call(f32[4,16,320]{2,1,0:T(8,128)S(1)} %shard_map.142.a_ref, f32[4,16,320]{2,1,0:T(8,128)S(1)} %collective-permute-done.3.b_ref, f32[4,16,320]{2,1,0:T(8,128)S(1)} %collective-permute-done.4.c_ref, ...), custom_call_target="tpu_custom_call" | custom-call | flops 1000000000 | bytes 8388608 | tf_op jit(solution)/shard_map/pallas_call | solution.py:90
  46.5 1.1 %collective-permute-start.6 = (f32[4,16,320]{2,1,0:T(8,128)S(1)}, f32[4,16,320]{2,1,0:T(8,128)S(1)}, u32[]{:S(2)}, u32[]{:S(2)}) collective-permute-start(f32[4,16,320]{2,1,0:T(8,128)S(1)} %get-tuple-element.26.mine_ref), channel_id=1, source_target_pairs={{0,16},{16,0},{32,48},{48,32},{64,80},{80,64},{96,112},{112,96},{1... | collective-permute-start | bytes 245768 | tf_op jit(solution)/shard_map/ppermute | solution.py:66
  47.6 0.9 collective-permute-done.6.other_ref
  48.5 2.5 %shard_map.144 = (f32[96,1280]{1,0:T(8,128)S(1)}, bf16[64,1280]{1,0:T(8,128)(2,1)S(1)}, bf16[64,1280]{1,0:T(8,128)(2,1)S(1)}) custom-call(f32[4,16,320]{2,1,0:T(8,128)S(1)} %get-tuple-element.26.mine_ref, f32[4,16,320]{2,1,0:T(8,128)S(1)} %collective-permute-done.6.other_ref, bf16[96,512]{1,0:T(8,128)(2,1)S(1)} %copy-done, ...), custom_call_target="tpu_custom_call" | custom-call | flops 1000000000 | bytes 8388608 | tf_op jit(solution)/shard_map/pallas_call | solution.py:90
  52.1 4.4 %collective-permute-done.7.a_ref = bf16[64,1280]{1,0:T(8,128)(2,1)S(1)} collective-permute-done((bf16[64,1280]{1,0:T(8,128)(2,1)S(1)}, bf16[64,1280]{1,0:T(8,128)(2,1)S(1)}, u32[]{:S(2)}, u32[]{:S(2)}) %collective-permute-start.7) | collective-permute-done | bytes 163872 | tf_op jit(solution)/shard_map/ppermute | solution.py:55
  57.6 4.8 %collective-permute-start.9 = (bf16[64,1280]{1,0:T(8,128)(2,1)S(1)}, bf16[64,1280]{1,0:T(8,128)(2,1)S(1)}, u32[]{:S(2)}, u32[]{:S(2)}) collective-permute-start(bf16[64,1280]{1,0:T(8,128)(2,1)S(1)} %get-tuple-element.32), channel_id=1, source_target_pairs={{0,1},{1,0},{2,3},{3,2},{4,5},{5,4},{6,7},{7,6},{8,9},{9,8},{10,11... | collective-permute-start | bytes 491528 | tf_op jit(solution)/shard_map/ppermute | solution.py:55
  62.4 2.7 %collective-permute-done.9.a_ref = bf16[64,1280]{1,0:T(8,128)(2,1)S(1)} collective-permute-done((bf16[64,1280]{1,0:T(8,128)(2,1)S(1)}, bf16[64,1280]{1,0:T(8,128)(2,1)S(1)}, u32[]{:S(2)}, u32[]{:S(2)}) %collective-permute-start.9) | collective-permute-done | bytes 163872 | tf_op jit(solution)/shard_map/ppermute | solution.py:55
  65.1 2.3 %shard_map.146 = (f32[4,16,320]{2,1,0:T(8,128)S(1)}, f32[4,16,320]{2,1,0:T(8,128)S(1)}) custom-call(bf16[64,1280]{1,0:T(8,128)(2,1)S(1)} %collective-permute-done.9.a_ref, f32[64,1280]{1,0:T(8,128)S(1)} %get-tuple-element.33.own_ref.grad_ref, bf16[64,1280]{1,0:T(8,128)(2,1)S(1)} %collective-permute-done.10.b_ref, ...), custom_call_target="tpu_custom_call" | custom-call | flops 1000000000 | bytes 8388608 | tf_op jit(solution)/shard_map/pallas_call | solution.py:90
  67.5 2.7 %collective-permute-start.11 = (f32[4,16,320]{2,1,0:T(8,128)S(1)}, f32[4,16,320]{2,1,0:T(8,128)S(1)}, u32[]{:S(2)}, u32[]{:S(2)}) collective-permute-start(f32[4,16,320]{2,1,0:T(8,128)S(1)} %get-tuple-element.36), channel_id=1, source_target_pairs={{0,16},{16,0},{32,48},{48,32},{64,80},{80,64},{96,112},{112,96},{1... | collective-permute-start | bytes 245768 | tf_op jit(solution)/shard_map/ppermute | solution.py:66
  70.2 0.9 collective-permute-done.11.b_ref
  71.2 1.5 %collective-permute-start.13 = (f32[16,320]{1,0:T(8,128)S(1)}, f32[16,320]{1,0:T(8,128)S(1)}, u32[]{:S(2)}, u32[]{:S(2)}) collective-permute-start(f32[16,320]{1,0:T(8,128)S(1)} %get-tuple-element.39), channel_id=1, source_target_pairs={{0,64},{16,80},{32,96},{48,112},{64,0},{80,16},{96,32},{112,48},{1... | collective-permute-start | bytes 61448 | tf_op jit(solution)/shard_map/ppermute | solution.py:51
  72.7 1.9 %collective-permute-start.14 = (f32[16,320]{1,0:T(8,128)S(1)}, f32[16,320]{1,0:T(8,128)S(1)}, u32[]{:S(2)}, u32[]{:S(2)}) collective-permute-start(f32[16,320]{1,0:T(8,128)S(1)} %get-tuple-element.40), channel_id=1, source_target_pairs={{0,96},{16,112},{32,0},{48,16},{64,32},{80,48},{96,64},{112,80},{1... | collective-permute-start | bytes 61448 | tf_op jit(solution)/shard_map/ppermute | solution.py:51
  76.8 20.8 %all_to_all.23 = f32[128,1,128]{2,1,0:T(1,128)S(1)} all-to-all(f32[128,1,128]{2,1,0:T(1,128)S(1)} %bitcast.35), channel_id=1, replica_groups=mesh['member'=8,'tile'=16] {'member','tile'}, dimensions={0} | all-to-all | bytes 131072 | tf_op jit(solution)/shard_map/all_to_all | solution.py:522
  97.5 1.0 shard_map.149
  (32 shorter events, 6.8 us)
Async XLA Ops:
  1.7 33.7 %copy-start.4 = (f32[16,320]{1,0:T(8,128)S(1)}, f32[16,320]{1,0:T(8,128)}, u32[]{:S(2)}) copy-start(f32[16,320]{1,0:T(8,128)} %base_ref.3) | copy-start | bytes 61444
  1.7 27.3 %collective-permute-start.1 = (bf16[64,1280]{1,0:T(8,128)(2,1)S(1)}, bf16[64,1280]{1,0:T(8,128)(2,1)S(1)}, u32[]{:S(2)}, u32[]{:S(2)}) collective-permute-start(bf16[64,1280]{1,0:T(8,128)(2,1)S(1)} %bitcast_convert_fusion), channel_id=1, source_target_pairs={{0,0},{15,15},{1,2},{2,1},{3,4},{4,3},{5,6},{6,5},{7,8},{8,7},{9,1... | collective-permute-start | bytes 491528 | tf_op jit(solution)/shard_map/ppermute | solution.py:62
  2.4 26.6 %collective-permute-start = (bf16[64,1280]{1,0:T(8,128)(2,1)S(1)}, bf16[64,1280]{1,0:T(8,128)(2,1)S(1)}, u32[]{:S(2)}, u32[]{:S(2)}) collective-permute-start(bf16[64,1280]{1,0:T(8,128)(2,1)S(1)} %bitcast_convert_fusion), channel_id=1, source_target_pairs={{0,1},{1,0},{2,3},{3,2},{4,5},{5,4},{6,7},{7,6},{8,9},{9,8},{10,11... | collective-permute-start | bytes 491528 | tf_op jit(solution)/shard_map/ppermute | solution.py:55
  8.5 35.5 %copy-start.1 = (s32[1,128,8,8]{1,3,2,0:T(8,128)S(1)}, s32[1,128,8,8]{1,3,2,0:T(8,128)}, u32[]{:S(2)}) copy-start(s32[1,128,8,8]{1,3,2,0:T(8,128)} %param.17) | copy-start | bytes 98308
  8.5 35.5 %copy-start.2 = (f32[1,128,8,8]{1,3,2,0:T(8,128)S(1)}, f32[1,128,8,8]{1,3,2,0:T(8,128)}, u32[]{:S(2)}) copy-start(f32[1,128,8,8]{1,3,2,0:T(8,128)} %param.18) | copy-start | bytes 98308
  8.5 35.5 %copy-start.3 = (f32[1,128,8,8]{1,3,2,0:T(8,128)S(1)}, f32[1,128,8,8]{1,3,2,0:T(8,128)}, u32[]{:S(2)}) copy-start(f32[1,128,8,8]{1,3,2,0:T(8,128)} %param.19) | copy-start | bytes 98308
  8.5 35.5 %copy-start.5 = (s32[1,128,8]{1,2,0:T(8,128)S(1)}, s32[1,128,8]{1,2,0:T(8,128)}, u32[]{:S(2)}) copy-start(s32[1,128,8]{1,2,0:T(8,128)} %param.20) | copy-start | bytes 12292
  29.0 19.5 %copy-start = (bf16[96,512]{1,0:T(8,128)(2,1)S(1)}, bf16[96,512]{1,0:T(8,128)(2,1)}, u32[]{:S(2)}) copy-start(bf16[96,512]{1,0:T(8,128)(2,1)} %constant.5.clone.back_ref) | copy-start | bytes 294916
  33.5 1.8 %collective-permute-start.2 = (f32[4,16,320]{2,1,0:T(8,128)S(1)}, f32[4,16,320]{2,1,0:T(8,128)S(1)}, u32[]{:S(2)}, u32[]{:S(2)}) collective-permute-start(f32[4,16,320]{2,1,0:T(8,128)S(1)} %get-tuple-element.25), channel_id=1, source_target_pairs={{0,16},{16,0},{32,48},{48,32},{64,80},{80,64},{96,112},{112,96},{1... | collective-permute-start | bytes 245768 | tf_op jit(solution)/shard_map/ppermute | solution.py:66
  35.3 4.1 %collective-permute-start.5 = (f32[4,16,320]{2,1,0:T(8,128)S(1)}, f32[4,16,320]{2,1,0:T(8,128)S(1)}, u32[]{:S(2)}, u32[]{:S(2)}) collective-permute-start(f32[4,16,320]{2,1,0:T(8,128)S(1)} %shard_map.142.a_ref), channel_id=1, source_target_pairs={{0,96},{16,112},{32,0},{48,16},{64,32},{80,48},{96,64},{112,80},{1... | collective-permute-start | bytes 245768 | tf_op jit(solution)/shard_map/ppermute | solution.py:51
  36.2 5.0 %collective-permute-start.4 = (f32[4,16,320]{2,1,0:T(8,128)S(1)}, f32[4,16,320]{2,1,0:T(8,128)S(1)}, u32[]{:S(2)}, u32[]{:S(2)}) collective-permute-start(f32[4,16,320]{2,1,0:T(8,128)S(1)} %shard_map.142.a_ref), channel_id=1, source_target_pairs={{0,64},{16,80},{32,96},{48,112},{64,0},{80,16},{96,32},{112,48},{1... | collective-permute-start | bytes 245768 | tf_op jit(solution)/shard_map/ppermute | solution.py:51
  37.6 6.5 %collective-permute-start.3 = (f32[4,16,320]{2,1,0:T(8,128)S(1)}, f32[4,16,320]{2,1,0:T(8,128)S(1)}, u32[]{:S(2)}, u32[]{:S(2)}) collective-permute-start(f32[4,16,320]{2,1,0:T(8,128)S(1)} %shard_map.142.a_ref), channel_id=1, source_target_pairs={{0,32},{16,48},{32,64},{48,80},{64,96},{80,112},{96,0},{112,16},{1... | collective-permute-start | bytes 245768 | tf_op jit(solution)/shard_map/ppermute | solution.py:51
  46.5 2.0 %collective-permute-start.6 = (f32[4,16,320]{2,1,0:T(8,128)S(1)}, f32[4,16,320]{2,1,0:T(8,128)S(1)}, u32[]{:S(2)}, u32[]{:S(2)}) collective-permute-start(f32[4,16,320]{2,1,0:T(8,128)S(1)} %get-tuple-element.26.mine_ref), channel_id=1, source_target_pairs={{0,16},{16,0},{32,48},{48,32},{64,80},{80,64},{96,112},{112,96},{1... | collective-permute-start | bytes 245768 | tf_op jit(solution)/shard_map/ppermute | solution.py:66
  51.1 5.5 %collective-permute-start.7 = (bf16[64,1280]{1,0:T(8,128)(2,1)S(1)}, bf16[64,1280]{1,0:T(8,128)(2,1)S(1)}, u32[]{:S(2)}, u32[]{:S(2)}) collective-permute-start(bf16[64,1280]{1,0:T(8,128)(2,1)S(1)} %get-tuple-element.29), channel_id=1, source_target_pairs={{0,1},{1,0},{2,3},{3,2},{4,5},{5,4},{6,7},{7,6},{8,9},{9,8},{10,11... | collective-permute-start | bytes 491528 | tf_op jit(solution)/shard_map/ppermute | solution.py:55
  51.5 5.1 %collective-permute-start.8 = (bf16[64,1280]{1,0:T(8,128)(2,1)S(1)}, bf16[64,1280]{1,0:T(8,128)(2,1)S(1)}, u32[]{:S(2)}, u32[]{:S(2)}) collective-permute-start(bf16[64,1280]{1,0:T(8,128)(2,1)S(1)} %get-tuple-element.31), channel_id=1, source_target_pairs={{0,0},{15,15},{1,2},{2,1},{3,4},{4,3},{5,6},{6,5},{7,8},{8,7},{9,1... | collective-permute-start | bytes 491528 | tf_op jit(solution)/shard_map/ppermute | solution.py:62
  57.0 5.5 %collective-permute-start.10 = (bf16[64,1280]{1,0:T(8,128)(2,1)S(1)}, bf16[64,1280]{1,0:T(8,128)(2,1)S(1)}, u32[]{:S(2)}, u32[]{:S(2)}) collective-permute-start(bf16[64,1280]{1,0:T(8,128)(2,1)S(1)} %get-tuple-element.32), channel_id=1, source_target_pairs={{0,0},{15,15},{1,2},{2,1},{3,4},{4,3},{5,6},{6,5},{7,8},{8,7},{9,1... | collective-permute-start | bytes 491528 | tf_op jit(solution)/shard_map/ppermute | solution.py:62
  57.6 7.5 %collective-permute-start.9 = (bf16[64,1280]{1,0:T(8,128)(2,1)S(1)}, bf16[64,1280]{1,0:T(8,128)(2,1)S(1)}, u32[]{:S(2)}, u32[]{:S(2)}) collective-permute-start(bf16[64,1280]{1,0:T(8,128)(2,1)S(1)} %get-tuple-element.32), channel_id=1, source_target_pairs={{0,1},{1,0},{2,3},{3,2},{4,5},{5,4},{6,7},{7,6},{8,9},{9,8},{10,11... | collective-permute-start | bytes 491528 | tf_op jit(solution)/shard_map/ppermute | solution.py:55
  67.5 3.6 %collective-permute-start.11 = (f32[4,16,320]{2,1,0:T(8,128)S(1)}, f32[4,16,320]{2,1,0:T(8,128)S(1)}, u32[]{:S(2)}, u32[]{:S(2)}) collective-permute-start(f32[4,16,320]{2,1,0:T(8,128)S(1)} %get-tuple-element.36), channel_id=1, source_target_pairs={{0,16},{16,0},{32,48},{48,32},{64,80},{80,64},{96,112},{112,96},{1... | collective-permute-start | bytes 245768 | tf_op jit(solution)/shard_map/ppermute | solution.py:66
  71.1 4.0 %collective-permute-start.12 = (f32[16,320]{1,0:T(8,128)S(1)}, f32[16,320]{1,0:T(8,128)S(1)}, u32[]{:S(2)}, u32[]{:S(2)}) collective-permute-start(f32[16,320]{1,0:T(8,128)S(1)} %get-tuple-element.38), channel_id=1, source_target_pairs={{0,32},{16,48},{32,64},{48,80},{64,96},{80,112},{96,0},{112,16},{1... | collective-permute-start | bytes 61448 | tf_op jit(solution)/shard_map/ppermute | solution.py:51
  71.2 4.3 %collective-permute-start.13 = (f32[16,320]{1,0:T(8,128)S(1)}, f32[16,320]{1,0:T(8,128)S(1)}, u32[]{:S(2)}, u32[]{:S(2)}) collective-permute-start(f32[16,320]{1,0:T(8,128)S(1)} %get-tuple-element.39), channel_id=1, source_target_pairs={{0,64},{16,80},{32,96},{48,112},{64,0},{80,16},{96,32},{112,48},{1... | collective-permute-start | bytes 61448 | tf_op jit(solution)/shard_map/ppermute | solution.py:51
  72.7 3.5 %collective-permute-start.14 = (f32[16,320]{1,0:T(8,128)S(1)}, f32[16,320]{1,0:T(8,128)S(1)}, u32[]{:S(2)}, u32[]{:S(2)}) collective-permute-start(f32[16,320]{1,0:T(8,128)S(1)} %get-tuple-element.40), channel_id=1, source_target_pairs={{0,96},{16,112},{32,0},{48,16},{64,32},{80,48},{96,64},{112,80},{1... | collective-permute-start | bytes 61448 | tf_op jit(solution)/shard_map/ppermute | solution.py:51

commit v5 on v4

--- a/solution.py
+++ b/solution.py
@@ -60,6 +60,12 @@
     for i in range(1, NTILE - 1, 2):
         pairs += [(i, i + 1), (i + 1, i)]
     return lax.ppermute(values, "tile", pairs)
+
+
+def swap_both(near_values, far_values):
+    near_rows = swap_near(near_values)
+    far_rows = swap_far(far_values)
+    return near_rows, far_rows
 
 
 def swap_core(values):
@@ -479,7 +485,7 @@
     flat = (ROWS * MEMBERS_HERE, COARSE_COLS)
     own = jnp.transpose(weights, (1, 0, 2)).reshape(flat)
     half = own.astype(HALF)
-    near_rows, far_rows = swap_near(half), swap_far(half)
+    near_rows, far_rows = swap_both(half, half)
 
     (sent,) = call(
         send_kernel,
@@ -508,10 +514,10 @@
         (*pieces, index, row_frac, column_frac, lengths, data),
     )
     part, up, down = partial_adjoint(spread, swap_core(spread), perturb, column_map)
-    gradient, half, square = gradient_of(swap_near(up), part, swap_far(down), own)
-    mine, other = later_forward(
-        swap_near(half), gradient, swap_far(half), matrix, perturb, column_map
-    )
+    near_rows, far_rows = swap_both(up, down)
+    gradient, half, square = gradient_of(near_rows, part, far_rows, own)
+    near_rows, far_rows = swap_both(half, half)
+    mine, other = later_forward(near_rows, gradient, far_rows, matrix, perturb, column_map)
     pieces = call(pick_kernel, (region,) * NY, (mine, swap_core(other)))
     pieces = [pieces[0]] + [turn(pieces[i], NCORE * i, "member") for i in range(1, NY)]
     image, sent = call(

time: 98.8 us -> 98.8 us (level)
  no operation moved by 1% of the time
where the time goes in v5:
time: 98.8 us; the launch traced here: 98.5 us
  blocking collectives  41.2 us (42%)
  starting transfers between devices  22.1 us (22%)
  waiting for transfers between devices  18.1 us (18%)
  Pallas kernels  14.6 us (15%)
  between operations  1.44 us (1%)
  local copies, waits for them, and re-layouts  1.07 us (1%)
    all_to_all x2, blocking collectives, shards(): lax.all_to_all(sent, ('member', 'tile'), split_axis=0, concat_axis=0, til...  41.2 us
    pallas_call x10, Pallas kernels, call(): pl.pallas_call(kernel, out_shape=tuple((jax.ShapeDtypeStruct(shape, kind)...  14.6 us
    ppermute x3, starting transfers between devices, swap_near(): return lax.ppermute(values, 'tile', [(i, i ^ 1) for i in range(NTILE)])  9.74 us
    ppermute x6, waiting for transfers between devices, turn(): lax.ppermute(values, axis, [(i, (i + step) % count) for i in range(count)])  8.11 us
    ppermute x3, waiting for transfers between devices, swap_near(): return lax.ppermute(values, 'tile', [(i, i ^ 1) for i in range(NTILE)])  7.14 us
    ppermute x6, starting transfers between devices, turn(): lax.ppermute(values, axis, [(i, (i + step) % count) for i in range(count)])  5.66 us
    ppermute x3, starting transfers between devices, swap_core(): return lax.ppermute(values, 'member', [(i, i ^ 1) for i in range(NMEMBER)])  4.66 us
    ppermute x3, waiting for transfers between devices, swap_core(): return lax.ppermute(values, 'member', [(i, i ^ 1) for i in range(NMEMBER)])  2.83 us
  transfers between devices with their start and end apart: 15, of which 11 were waited for; matrix products, arithmetic and copies ran while one was open for 0% of the time, Pallas kernels for 1%

profile of v5, /device:TPU:1, one launch (start us, length us, event | category | flops | bytes accessed | tf_op | source)
XLA Modules:
  0.0 98.5 jit_solution(5931026014031256269)
XLA Ops:
  0.6 1.0 %copy.16 = f32[4,16,1280]{2,1,0:T(8,128)S(1)} copy(f32[4,16,1280]{2,0,1:T(4,128)} %bitcast.44) | data formatting | bytes 655360 | tf_op jit(solution)/shard_map/transpose | solution.py:486
  2.4 4.6 %collective-permute-start = (bf16[64,1280]{1,0:T(8,128)(2,1)S(1)}, bf16[64,1280]{1,0:T(8,128)(2,1)S(1)}, u32[]{:S(2)}, u32[]{:S(2)}) collective-permute-start(bf16[64,1280]{1,0:T(8,128)(2,1)S(1)} %bitcast_convert_fusion), channel_id=1, source_target_pairs={{0,1},{1,0},{2,3},{3,2},{4,5},{5,4},{6,7},{7,6},{8,9},{9,8},{10,11... | collective-permute-start | bytes 491528 | tf_op jit(solution)/shard_map/ppermute | solution.py:55
  7.6 0.9 shard_map.140
  8.5 20.4 %all_to_all.22 = f32[128,1,128]{2,1,0:T(1,128)S(1)} all-to-all(f32[128,1,128]{2,1,0:T(1,128)S(1)} %bitcast.36), channel_id=1, replica_groups=mesh['member'=8,'tile'=16] {'member','tile'}, dimensions={0} | all-to-all | bytes 131072 | tf_op jit(solution)/shard_map/all_to_all | solution.py:498
  29.0 4.5 %shard_map.141 = (f32[4,16,320]{2,1,0:T(8,128)S(1)}, f32[4,16,320]{2,1,0:T(8,128)S(1)}, bf16[256,192]{1,0:T(8,128)(2,1)S(1)}, bf16[16,16,2560]{2,1,0:T(8,128)(2,1)S(1)}, bf16[1280,2560]{1,0:T(8,128)(2,1)S(1)}) custom-call(bf16[64,1280]{1,0:T(8,128)(2,1)S(1)} %collective-permute-done.a_ref, f32[64,1280]{1,0:T(8,128)S(1)} %bitcast.29, ...), custom_call_target="tpu_custom_call" | custom-call | flops 1000000000 | bytes 8388608 | tf_op jit(solution)/shard_map/pallas_call | solution.py:96
  34.4 0.9 collective-permute-done.2.b_ref
  36.2 1.3 %collective-permute-start.4 = (f32[4,16,320]{2,1,0:T(8,128)S(1)}, f32[4,16,320]{2,1,0:T(8,128)S(1)}, u32[]{:S(2)}, u32[]{:S(2)}) collective-permute-start(f32[4,16,320]{2,1,0:T(8,128)S(1)} %shard_map.142.a_ref), channel_id=1, source_target_pairs={{0,64},{16,80},{32,96},{48,112},{64,0},{80,16},{96,32},{112,48},{1... | collective-permute-start | bytes 245768 | tf_op jit(solution)/shard_map/ppermute | solution.py:51
  37.6 1.9 %collective-permute-done.5.d_ref = f32[4,16,320]{2,1,0:T(8,128)S(1)} collective-permute-done((f32[4,16,320]{2,1,0:T(8,128)S(1)}, f32[4,16,320]{2,1,0:T(8,128)S(1)}, u32[]{:S(2)}, u32[]{:S(2)}) %collective-permute-start.5) | collective-permute-done | bytes 81952 | tf_op jit(solution)/shard_map/ppermute | solution.py:51
  39.4 1.8 %collective-permute-done.4.c_ref = f32[4,16,320]{2,1,0:T(8,128)S(1)} collective-permute-done((f32[4,16,320]{2,1,0:T(8,128)S(1)}, f32[4,16,320]{2,1,0:T(8,128)S(1)}, u32[]{:S(2)}, u32[]{:S(2)}) %collective-permute-start.4) | collective-permute-done | bytes 81952 | tf_op jit(solution)/shard_map/ppermute | solution.py:51
  41.2 2.8 %collective-permute-done.3.b_ref = f32[4,16,320]{2,1,0:T(8,128)S(1)} collective-permute-done((f32[4,16,320]{2,1,0:T(8,128)S(1)}, f32[4,16,320]{2,1,0:T(8,128)S(1)}, u32[]{:S(2)}, u32[]{:S(2)}) %collective-permute-start.3) | collective-permute-done | bytes 81952 | tf_op jit(solution)/shard_map/ppermute | solution.py:51
  44.1 2.4 %shard_map.143 = (f32[4,16,320]{2,1,0:T(8,128)S(1)}, f32[8,128]{1,0:T(8,128)S(1)}, f32[16,320]{1,0:T(8,128)S(1)}) custom-call(f32[4,16,320]{2,1,0:T(8,128)S(1)} %shard_map.142.a_ref, f32[4,16,320]{2,1,0:T(8,128)S(1)} %collective-permute-done.3.b_ref, f32[4,16,320]{2,1,0:T(8,128)S(1)} %collective-permute-done.4.c_ref, ...), custom_call_target="tpu_custom_call" | custom-call | flops 1000000000 | bytes 8388608 | tf_op jit(solution)/shard_map/pallas_call | solution.py:96
  46.5 1.1 %collective-permute-start.6 = (f32[4,16,320]{2,1,0:T(8,128)S(1)}, f32[4,16,320]{2,1,0:T(8,128)S(1)}, u32[]{:S(2)}, u32[]{:S(2)}) collective-permute-start(f32[4,16,320]{2,1,0:T(8,128)S(1)} %get-tuple-element.26.mine_ref), channel_id=1, source_target_pairs={{0,16},{16,0},{32,48},{48,32},{64,80},{80,64},{96,112},{112,96},{1... | collective-permute-start | bytes 245768 | tf_op jit(solution)/shard_map/ppermute | solution.py:72
  47.6 0.9 collective-permute-done.6.other_ref
  48.5 2.5 %shard_map.144 = (f32[96,1280]{1,0:T(8,128)S(1)}, bf16[64,1280]{1,0:T(8,128)(2,1)S(1)}, bf16[64,1280]{1,0:T(8,128)(2,1)S(1)}) custom-call(f32[4,16,320]{2,1,0:T(8,128)S(1)} %get-tuple-element.26.mine_ref, f32[4,16,320]{2,1,0:T(8,128)S(1)} %collective-permute-done.6.other_ref, bf16[96,512]{1,0:T(8,128)(2,1)S(1)} %copy-done, ...), custom_call_target="tpu_custom_call" | custom-call | flops 1000000000 | bytes 8388608 | tf_op jit(solution)/shard_map/pallas_call | solution.py:96
  52.1 4.4 %collective-permute-done.7.a_ref = bf16[64,1280]{1,0:T(8,128)(2,1)S(1)} collective-permute-done((bf16[64,1280]{1,0:T(8,128)(2,1)S(1)}, bf16[64,1280]{1,0:T(8,128)(2,1)S(1)}, u32[]{:S(2)}, u32[]{:S(2)}) %collective-permute-start.7) | collective-permute-done | bytes 163872 | tf_op jit(solution)/shard_map/ppermute | solution.py:55
  57.6 4.8 %collective-permute-start.9 = (bf16[64,1280]{1,0:T(8,128)(2,1)S(1)}, bf16[64,1280]{1,0:T(8,128)(2,1)S(1)}, u32[]{:S(2)}, u32[]{:S(2)}) collective-permute-start(bf16[64,1280]{1,0:T(8,128)(2,1)S(1)} %get-tuple-element.32), channel_id=1, source_target_pairs={{0,1},{1,0},{2,3},{3,2},{4,5},{5,4},{6,7},{7,6},{8,9},{9,8},{10,11... | collective-permute-start | bytes 491528 | tf_op jit(solution)/shard_map/ppermute | solution.py:55
  62.4 2.7 %collective-permute-done.9.a_ref = bf16[64,1280]{1,0:T(8,128)(2,1)S(1)} collective-permute-done((bf16[64,1280]{1,0:T(8,128)(2,1)S(1)}, bf16[64,1280]{1,0:T(8,128)(2,1)S(1)}, u32[]{:S(2)}, u32[]{:S(2)}) %collective-permute-start.9) | collective-permute-done | bytes 163872 | tf_op jit(solution)/shard_map/ppermute | solution.py:55
  65.1 2.3 %shard_map.146 = (f32[4,16,320]{2,1,0:T(8,128)S(1)}, f32[4,16,320]{2,1,0:T(8,128)S(1)}) custom-call(bf16[64,1280]{1,0:T(8,128)(2,1)S(1)} %collective-permute-done.9.a_ref, f32[64,1280]{1,0:T(8,128)S(1)} %get-tuple-element.33.own_ref.grad_ref, bf16[64,1280]{1,0:T(8,128)(2,1)S(1)} %collective-permute-done.10.b_ref, ...), custom_call_target="tpu_custom_call" | custom-call | flops 1000000000 | bytes 8388608 | tf_op jit(solution)/shard_map/pallas_call | solution.py:96
  67.5 2.7 %collective-permute-start.11 = (f32[4,16,320]{2,1,0:T(8,128)S(1)}, f32[4,16,320]{2,1,0:T(8,128)S(1)}, u32[]{:S(2)}, u32[]{:S(2)}) collective-permute-start(f32[4,16,320]{2,1,0:T(8,128)S(1)} %get-tuple-element.36), channel_id=1, source_target_pairs={{0,16},{16,0},{32,48},{48,32},{64,80},{80,64},{96,112},{112,96},{1... | collective-permute-start | bytes 245768 | tf_op jit(solution)/shard_map/ppermute | solution.py:72
  70.2 0.9 collective-permute-done.11.b_ref
  71.2 1.5 %collective-permute-start.13 = (f32[16,320]{1,0:T(8,128)S(1)}, f32[16,320]{1,0:T(8,128)S(1)}, u32[]{:S(2)}, u32[]{:S(2)}) collective-permute-start(f32[16,320]{1,0:T(8,128)S(1)} %get-tuple-element.39), channel_id=1, source_target_pairs={{0,64},{16,80},{32,96},{48,112},{64,0},{80,16},{96,32},{112,48},{1... | collective-permute-start | bytes 61448 | tf_op jit(solution)/shard_map/ppermute | solution.py:51
  72.7 1.9 %collective-permute-start.14 = (f32[16,320]{1,0:T(8,128)S(1)}, f32[16,320]{1,0:T(8,128)S(1)}, u32[]{:S(2)}, u32[]{:S(2)}) collective-permute-start(f32[16,320]{1,0:T(8,128)S(1)} %get-tuple-element.40), channel_id=1, source_target_pairs={{0,96},{16,112},{32,0},{48,16},{64,32},{80,48},{96,64},{112,80},{1... | collective-permute-start | bytes 61448 | tf_op jit(solution)/shard_map/ppermute | solution.py:51
  76.8 20.8 %all_to_all.23 = f32[128,1,128]{2,1,0:T(1,128)S(1)} all-to-all(f32[128,1,128]{2,1,0:T(1,128)S(1)} %bitcast.35), channel_id=1, replica_groups=mesh['member'=8,'tile'=16] {'member','tile'}, dimensions={0} | all-to-all | bytes 131072 | tf_op jit(solution)/shard_map/all_to_all | solution.py:528
  97.5 1.0 shard_map.149
  (32 shorter events, 6.8 us)
Async XLA Ops:
  1.7 33.7 %copy-start.4 = (f32[16,320]{1,0:T(8,128)S(1)}, f32[16,320]{1,0:T(8,128)}, u32[]{:S(2)}) copy-start(f32[16,320]{1,0:T(8,128)} %base_ref.3) | copy-start | bytes 61444
  1.7 27.3 %collective-permute-start.1 = (bf16[64,1280]{1,0:T(8,128)(2,1)S(1)}, bf16[64,1280]{1,0:T(8,128)(2,1)S(1)}, u32[]{:S(2)}, u32[]{:S(2)}) collective-permute-start(bf16[64,1280]{1,0:T(8,128)(2,1)S(1)} %bitcast_convert_fusion), channel_id=1, source_target_pairs={{0,0},{15,15},{1,2},{2,1},{3,4},{4,3},{5,6},{6,5},{7,8},{8,7},{9,1... | collective-permute-start | bytes 491528 | tf_op jit(solution)/shard_map/ppermute | solution.py:62
  2.4 26.6 %collective-permute-start = (bf16[64,1280]{1,0:T(8,128)(2,1)S(1)}, bf16[64,1280]{1,0:T(8,128)(2,1)S(1)}, u32[]{:S(2)}, u32[]{:S(2)}) collective-permute-start(bf16[64,1280]{1,0:T(8,128)(2,1)S(1)} %bitcast_convert_fusion), channel_id=1, source_target_pairs={{0,1},{1,0},{2,3},{3,2},{4,5},{5,4},{6,7},{7,6},{8,9},{9,8},{10,11... | collective-permute-start | bytes 491528 | tf_op jit(solution)/shard_map/ppermute | solution.py:55
  8.5 35.5 %copy-start.1 = (s32[1,128,8,8]{1,3,2,0:T(8,128)S(1)}, s32[1,128,8,8]{1,3,2,0:T(8,128)}, u32[]{:S(2)}) copy-start(s32[1,128,8,8]{1,3,2,0:T(8,128)} %param.17) | copy-start | bytes 98308
  8.5 35.5 %copy-start.2 = (f32[1,128,8,8]{1,3,2,0:T(8,128)S(1)}, f32[1,128,8,8]{1,3,2,0:T(8,128)}, u32[]{:S(2)}) copy-start(f32[1,128,8,8]{1,3,2,0:T(8,128)} %param.18) | copy-start | bytes 98308
  8.5 35.5 %copy-start.3 = (f32[1,128,8,8]{1,3,2,0:T(8,128)S(1)}, f32[1,128,8,8]{1,3,2,0:T(8,128)}, u32[]{:S(2)}) copy-start(f32[1,128,8,8]{1,3,2,0:T(8,128)} %param.19) | copy-start | bytes 98308
  8.5 35.5 %copy-start.5 = (s32[1,128,8]{1,2,0:T(8,128)S(1)}, s32[1,128,8]{1,2,0:T(8,128)}, u32[]{:S(2)}) copy-start(s32[1,128,8]{1,2,0:T(8,128)} %param.20) | copy-start | bytes 12292
  29.0 19.5 %copy-start = (bf16[96,512]{1,0:T(8,128)(2,1)S(1)}, bf16[96,512]{1,0:T(8,128)(2,1)}, u32[]{:S(2)}) copy-start(bf16[96,512]{1,0:T(8,128)(2,1)} %constant.5.clone.back_ref) | copy-start | bytes 294916
  33.5 1.8 %collective-permute-start.2 = (f32[4,16,320]{2,1,0:T(8,128)S(1)}, f32[4,16,320]{2,1,0:T(8,128)S(1)}, u32[]{:S(2)}, u32[]{:S(2)}) collective-permute-start(f32[4,16,320]{2,1,0:T(8,128)S(1)} %get-tuple-element.25), channel_id=1, source_target_pairs={{0,16},{16,0},{32,48},{48,32},{64,80},{80,64},{96,112},{112,96},{1... | collective-permute-start | bytes 245768 | tf_op jit(solution)/shard_map/ppermute | solution.py:72
  35.3 4.1 %collective-permute-start.5 = (f32[4,16,320]{2,1,0:T(8,128)S(1)}, f32[4,16,320]{2,1,0:T(8,128)S(1)}, u32[]{:S(2)}, u32[]{:S(2)}) collective-permute-start(f32[4,16,320]{2,1,0:T(8,128)S(1)} %shard_map.142.a_ref), channel_id=1, source_target_pairs={{0,96},{16,112},{32,0},{48,16},{64,32},{80,48},{96,64},{112,80},{1... | collective-permute-start | bytes 245768 | tf_op jit(solution)/shard_map/ppermute | solution.py:51
  36.2 5.0 %collective-permute-start.4 = (f32[4,16,320]{2,1,0:T(8,128)S(1)}, f32[4,16,320]{2,1,0:T(8,128)S(1)}, u32[]{:S(2)}, u32[]{:S(2)}) collective-permute-start(f32[4,16,320]{2,1,0:T(8,128)S(1)} %shard_map.142.a_ref), channel_id=1, source_target_pairs={{0,64},{16,80},{32,96},{48,112},{64,0},{80,16},{96,32},{112,48},{1... | collective-permute-start | bytes 245768 | tf_op jit(solution)/shard_map/ppermute | solution.py:51
  37.6 6.5 %collective-permute-start.3 = (f32[4,16,320]{2,1,0:T(8,128)S(1)}, f32[4,16,320]{2,1,0:T(8,128)S(1)}, u32[]{:S(2)}, u32[]{:S(2)}) collective-permute-start(f32[4,16,320]{2,1,0:T(8,128)S(1)} %shard_map.142.a_ref), channel_id=1, source_target_pairs={{0,32},{16,48},{32,64},{48,80},{64,96},{80,112},{96,0},{112,16},{1... | collective-permute-start | bytes 245768 | tf_op jit(solution)/shard_map/ppermute | solution.py:51
  46.5 2.0 %collective-permute-start.6 = (f32[4,16,320]{2,1,0:T(8,128)S(1)}, f32[4,16,320]{2,1,0:T(8,128)S(1)}, u32[]{:S(2)}, u32[]{:S(2)}) collective-permute-start(f32[4,16,320]{2,1,0:T(8,128)S(1)} %get-tuple-element.26.mine_ref), channel_id=1, source_target_pairs={{0,16},{16,0},{32,48},{48,32},{64,80},{80,64},{96,112},{112,96},{1... | collective-permute-start | bytes 245768 | tf_op jit(solution)/shard_map/ppermute | solution.py:72
  51.1 5.5 %collective-permute-start.7 = (bf16[64,1280]{1,0:T(8,128)(2,1)S(1)}, bf16[64,1280]{1,0:T(8,128)(2,1)S(1)}, u32[]{:S(2)}, u32[]{:S(2)}) collective-permute-start(bf16[64,1280]{1,0:T(8,128)(2,1)S(1)} %get-tuple-element.29), channel_id=1, source_target_pairs={{0,1},{1,0},{2,3},{3,2},{4,5},{5,4},{6,7},{7,6},{8,9},{9,8},{10,11... | collective-permute-start | bytes 491528 | tf_op jit(solution)/shard_map/ppermute | solution.py:55
  51.5 5.1 %collective-permute-start.8 = (bf16[64,1280]{1,0:T(8,128)(2,1)S(1)}, bf16[64,1280]{1,0:T(8,128)(2,1)S(1)}, u32[]{:S(2)}, u32[]{:S(2)}) collective-permute-start(bf16[64,1280]{1,0:T(8,128)(2,1)S(1)} %get-tuple-element.31), channel_id=1, source_target_pairs={{0,0},{15,15},{1,2},{2,1},{3,4},{4,3},{5,6},{6,5},{7,8},{8,7},{9,1... | collective-permute-start | bytes 491528 | tf_op jit(solution)/shard_map/ppermute | solution.py:62
  57.0 5.5 %collective-permute-start.10 = (bf16[64,1280]{1,0:T(8,128)(2,1)S(1)}, bf16[64,1280]{1,0:T(8,128)(2,1)S(1)}, u32[]{:S(2)}, u32[]{:S(2)}) collective-permute-start(bf16[64,1280]{1,0:T(8,128)(2,1)S(1)} %get-tuple-element.32), channel_id=1, source_target_pairs={{0,0},{15,15},{1,2},{2,1},{3,4},{4,3},{5,6},{6,5},{7,8},{8,7},{9,1... | collective-permute-start | bytes 491528 | tf_op jit(solution)/shard_map/ppermute | solution.py:62
  57.6 7.5 %collective-permute-start.9 = (bf16[64,1280]{1,0:T(8,128)(2,1)S(1)}, bf16[64,1280]{1,0:T(8,128)(2,1)S(1)}, u32[]{:S(2)}, u32[]{:S(2)}) collective-permute-start(bf16[64,1280]{1,0:T(8,128)(2,1)S(1)} %get-tuple-element.32), channel_id=1, source_target_pairs={{0,1},{1,0},{2,3},{3,2},{4,5},{5,4},{6,7},{7,6},{8,9},{9,8},{10,11... | collective-permute-start | bytes 491528 | tf_op jit(solution)/shard_map/ppermute | solution.py:55
  67.5 3.6 %collective-permute-start.11 = (f32[4,16,320]{2,1,0:T(8,128)S(1)}, f32[4,16,320]{2,1,0:T(8,128)S(1)}, u32[]{:S(2)}, u32[]{:S(2)}) collective-permute-start(f32[4,16,320]{2,1,0:T(8,128)S(1)} %get-tuple-element.36), channel_id=1, source_target_pairs={{0,16},{16,0},{32,48},{48,32},{64,80},{80,64},{96,112},{112,96},{1... | collective-permute-start | bytes 245768 | tf_op jit(solution)/shard_map/ppermute | solution.py:72
  71.1 4.0 %collective-permute-start.12 = (f32[16,320]{1,0:T(8,128)S(1)}, f32[16,320]{1,0:T(8,128)S(1)}, u32[]{:S(2)}, u32[]{:S(2)}) collective-permute-start(f32[16,320]{1,0:T(8,128)S(1)} %get-tuple-element.38), channel_id=1, source_target_pairs={{0,32},{16,48},{32,64},{48,80},{64,96},{80,112},{96,0},{112,16},{1... | collective-permute-start | bytes 61448 | tf_op jit(solution)/shard_map/ppermute | solution.py:51
  71.2 4.3 %collective-permute-start.13 = (f32[16,320]{1,0:T(8,128)S(1)}, f32[16,320]{1,0:T(8,128)S(1)}, u32[]{:S(2)}, u32[]{:S(2)}) collective-permute-start(f32[16,320]{1,0:T(8,128)S(1)} %get-tuple-element.39), channel_id=1, source_target_pairs={{0,64},{16,80},{32,96},{48,112},{64,0},{80,16},{96,32},{112,48},{1... | collective-permute-start | bytes 61448 | tf_op jit(solution)/shard_map/ppermute | solution.py:51
  72.7 3.5 %collective-permute-start.14 = (f32[16,320]{1,0:T(8,128)S(1)}, f32[16,320]{1,0:T(8,128)S(1)}, u32[]{:S(2)}, u32[]{:S(2)}) collective-permute-start(f32[16,320]{1,0:T(8,128)S(1)} %get-tuple-element.40), channel_id=1, source_target_pairs={{0,96},{16,112},{32,0},{48,16},{64,32},{80,48},{96,64},{112,80},{1... | collective-permute-start | bytes 61448 | tf_op jit(solution)/shard_map/ppermute | solution.py:51

commit v6 on v5

--- a/solution.py
+++ b/solution.py
@@ -22,6 +22,7 @@
 SLOTS = 8
 BATCHES = 128
 ROOM = 12 << 20
+EVEN, ODD = pl.ds(0, NTILE, stride=2), pl.ds(1, NTILE, stride=2)
 FLOAT, HALF = jnp.float32, jnp.bfloat16
 
 
@@ -145,7 +146,7 @@
 
 
 def streamed_kernel(
-    a_ref, own_ref, b_ref, refine_hbm, perturb_hbm, map_hbm, after_ref,
+    a_ref, own_ref, b_ref, refine_hbm, perturb_hbm, map_hbm, data_ref,
     mine_ref, other_ref, refine_ref, perturb_ref, map_ref, smooth_ref, sem,
 ):
     copies = [(pltpu.make_async_copy(refine_hbm, refine_ref, sem.at[0, NY]),)]
@@ -162,6 +163,17 @@
     for group in copies[1:2] + copies[:1] + copies[2:]:
         for copy in group:
             copy.start()
+
+    _, core_pos, _ = place()
+    data, gain = data_ref[EVEN], data_ref[ODD]
+    lanes = lax.broadcasted_iota(jnp.int32, data.shape, 1)
+    home = RIDE + 2 * NTILE * core_pos
+    for y in range(NY):
+        for ref, parity in ((mine_ref, core_pos), (other_ref, 1 - core_pos)):
+            shift = lax.rem(home + BATCHES - NTILE * (NCORE * y + parity), BATCHES)
+            moved = jnp.where(lanes == home + 2 * SLOTS, gain, pltpu.roll(data, shift, 1))
+            kept = (lanes >= home) & (lanes <= home + 2 * SLOTS)
+            ref[y, :, 256:] = jnp.where(kept, moved, 0.0)
 
     def arrived(y):
         for copy in copies[y + 1] + (copies[0] if y == 0 else ()):
@@ -203,24 +215,26 @@
             term = fine[k * FINE_ROWS : (k + 1) * FINE_ROWS] * perturb_ref[k, :, cols].astype(FLOAT)
             total = term if total is None else total + term
         first, second = total[:, :WIDTH], total[:, WIDTH:]
-        mine_ref[y] = jnp.where(core_pos == 0, first, second)
-        other_ref[y] = jnp.where(core_pos == 0, second, first)
+        mine_ref[y, :, :WIDTH] = jnp.where(core_pos == 0, first, second)
+        other_ref[y, :, :WIDTH] = jnp.where(core_pos == 0, second, first)
 
 
 REGIONS = ((NY, FINE_ROWS, WIDTH), FLOAT)
+LADEN = ((NY, FINE_ROWS, 384), FLOAT)
+RIDE = 64
 
 
 SMOOTH = pltpu.VMEM(((ROWS + 2) * MEMBERS_HERE, COARSE_COLS), HALF)
 
 
-def first_forward(first, own, second, perturb, column_map, after):
+def first_forward(first, own, second, perturb, column_map, data):
     matrix = member_matrix()
     matrix = jnp.asarray(np.concatenate([matrix, matrix], axis=1), HALF)
     operators = (matrix, perturb, column_map)
     return call(
         streamed_kernel,
-        (REGIONS, REGIONS) + tuple((x.shape, x.dtype) for x in operators),
-        (first, own, second) + operators + (after,),
+        (LADEN, LADEN) + tuple((x.shape, x.dtype) for x in operators),
+        (first, own, second) + operators + (data,),
         far=(3, 4, 5),
         scratch=[SMOOTH, pltpu.SemaphoreType.DMA((2, NY + 1))],
     )
@@ -317,28 +331,19 @@
         copy.start()
     for copy in copies:
         copy.wait()
-    lanes = lax.broadcasted_iota(jnp.int32, (SLOTS, BATCHES), 1)
-    block = lanes // (NCORE * NTILE)
     rows = []
-    for ref in (value_ref, error_ref):
-        values = ref[...]
-        turned = [values] + [
-            pltpu.roll(values, NCORE * NTILE * i, 1) for i in range(1, NY)
-        ]
-        for y in range(NY):
-            out = turned[0]
-            for j in range(NY):
-                out = jnp.where(block == j, turned[(j - y) % NY], out)
-            rows.append(out)
-    gain = jnp.full((2 * NY * SLOTS, BATCHES), gain_ref[0], FLOAT)
-    sent_ref[...] = jnp.transpose(jnp.concatenate(rows + [gain], axis=0))
+    for group in range(NMEMBER):
+        for ref in (value_ref, error_ref):
+            rows.append(pltpu.roll(ref[...], (BATCHES - NTILE * group) % BATCHES, 1))
+    sent_ref[EVEN] = jnp.transpose(jnp.concatenate(rows, axis=0))[:NTILE]
+    sent_ref[ODD] = jnp.full((NTILE, 128), gain_ref[0], FLOAT)
 
 
 def add_kernel(a_ref, b_ref, base_ref, out_ref):
     _, _, y_pos = place()
     for y in range(NY):
         out_ref[y] = a_ref[y] + b_ref[y]
-    out_ref[y_pos] += base_ref[...]
+    out_ref[y_pos, :, :WIDTH] += base_ref[...]
 
 
 def pick_kernel(a_ref, b_ref, *out_refs):
@@ -399,15 +404,24 @@
 
 
 def obs_kernel(
-    a_ref, b_ref, c_ref, d_ref, index_ref, row_ref, column_ref, length_ref, data_ref,
-    spread_ref, weight_ref, full_ref,
+    a_ref, b_ref, c_ref, d_ref, index_ref, row_ref, column_ref, length_ref,
+    spread_ref, weight_ref, full_ref, data_ref,
 ):
     _, core_pos, y_pos = place()
-    data = jnp.transpose(data_ref[...])
-    gain = data[2 * NY * SLOTS : 2 * NY * SLOTS + SLOTS]
     slots = lax.broadcasted_iota(jnp.int32, (SLOTS, BATCHES), 0)
     for y in range(NY):
-        field = a_ref[y] + b_ref[y] + c_ref[y] + d_ref[y]
+        field = sum(ref[y, :, :WIDTH] for ref in (b_ref, c_ref, d_ref)) + a_ref[y, :, :WIDTH]
+        for step, ref in enumerate((a_ref, b_ref, c_ref, d_ref)):
+            source = lax.rem(y_pos + NY - step, NY) * (NCORE * NTILE)
+            load = ref[y, :, 256:]
+            for core in range(NCORE):
+                start = pl.multiple_of(source + core * NTILE, NTILE)
+                data_ref[y, pl.ds(start, NTILE)] = pltpu.roll(
+                    load, (BATCHES - RIDE - 2 * NTILE * core) % BATCHES, 1
+                )
+        data = jnp.transpose(data_ref[y])
+        value, error = data[:SLOTS], data[SLOTS : 2 * SLOTS]
+        gain = data[2 * SLOTS : 2 * SLOTS + 1]
         group = NCORE * y + core_pos
         row, column = located(index_ref[group])
         picks = column_picks(column)
@@ -415,8 +429,6 @@
         fraction = on_lanes(column_ref[group])
         live = jnp.where(slots < length_ref[pl.ds(group, 1)], 1.0, 0.0)
         state = interpolated(field, picks, factors, fraction)
-        value = data[y * SLOTS : (y + 1) * SLOTS]
-        error = data[(NY + y) * SLOTS : (NY + y + 1) * SLOTS]
         bounded = jnp.tanh(state)
         derivative = 1.0 + gain * (1.0 - bounded * bounded)
         misfit = state + gain * bounded - value
@@ -489,13 +501,13 @@
 
     (sent,) = call(
         send_kernel,
-        (((BATCHES, BATCHES), FLOAT),),
+        (((2 * NTILE, 128), FLOAT),),
         (obs_value[0].T, obs_error[0].T, instrument_gain),
         far=(0, 1),
         scalar=(2,),
         scratch=[pltpu.VMEM((SLOTS, BATCHES), FLOAT)] * 2 + [pltpu.SemaphoreType.DMA((2,))],
     )
-    data = lax.all_to_all(sent, ("member", "tile"), split_axis=0, concat_axis=0, tiled=True)
+    data = lax.all_to_all(sent, "tile", split_axis=0, concat_axis=0, tiled=True)
 
     index = jnp.transpose(stencil_index[0], (1, 2, 0))
     row_frac = jnp.transpose(row_fraction[0], (1, 2, 0))
@@ -505,13 +517,14 @@
     mine, other, matrix, perturb, column_map = first_forward(
         near_rows, own, far_rows, perturb, column_map, data
     )
-    (mine,) = call(add_kernel, (REGIONS,), (mine, swap_core(other), background))
+    (mine,) = call(add_kernel, (LADEN,), (mine, swap_core(other), background))
     pieces = [mine] + [turn(mine, NCORE * i, "member") for i in range(1, NY)]
     region = ((FINE_ROWS, WIDTH), FLOAT)
     spread, weight, full = call(
         obs_kernel,
         (REGIONS, ((SLOTS, BATCHES), FLOAT), region),
-        (*pieces, index, row_frac, column_frac, lengths, data),
+        (*pieces, index, row_frac, column_frac, lengths),
+        scratch=[pltpu.VMEM((NY, BATCHES, 128), FLOAT)],
     )
     part, up, down = partial_adjoint(spread, swap_core(spread), perturb, column_map)
     near_rows, far_rows = swap_both(up, down)

time: 98.8 us -> 95.6 us (0.968)
  blocking collectives: 41.2 us -> 34.3 us
  starting transfers between devices: 22.1 us -> 24.3 us
  waiting for transfers between devices: 18.1 us -> 19.5 us
    all_to_all x2 -> x1, blocking collectives: 41.2 us -> 20.7 us  [shards(): lax.all_to_all(sent, ('member', 'tile'), split_axis=0, concat_axis=0, til...]
    all_to_all x0 -> x1, blocking collectives: none -> 13.6 us  [shards(): data = lax.all_to_all(sent, 'tile', split_axis=0, concat_axis=0, tiled=True)]
    ppermute x3, starting transfers between devices: 4.66 us -> 6.14 us  [swap_core(): return lax.ppermute(values, 'member', [(i, i ^ 1) for i in range(NMEMBER)])]
    ppermute x6, waiting for transfers between devices: 8.11 us -> 9.51 us  [turn(): lax.ppermute(values, axis, [(i, (i + step) % count) for i in range(count)])]
where the time goes in v6:
time: 95.6 us; the launch traced here: 95.2 us
  blocking collectives  34.3 us (36%)
  starting transfers between devices  24.3 us (25%)
  waiting for transfers between devices  19.5 us (20%)
  Pallas kernels  14.6 us (15%)
  between operations  1.44 us (2%)
  local copies, waits for them, and re-layouts  1.07 us (1%)
    all_to_all x1, blocking collectives, shards(): lax.all_to_all(sent, ('member', 'tile'), split_axis=0, concat_axis=0, til...  20.7 us
    pallas_call x10, Pallas kernels, call(): pl.pallas_call(kernel, out_shape=tuple((jax.ShapeDtypeStruct(shape, kind)...  14.6 us
    all_to_all x1, blocking collectives, shards(): data = lax.all_to_all(sent, 'tile', split_axis=0, concat_axis=0, tiled=True)  13.6 us
    ppermute x3, starting transfers between devices, swap_near(): return lax.ppermute(values, 'tile', [(i, i ^ 1) for i in range(NTILE)])  9.62 us
    ppermute x6, waiting for transfers between devices, turn(): lax.ppermute(values, axis, [(i, (i + step) % count) for i in range(count)])  9.51 us
    ppermute x3, waiting for transfers between devices, swap_near(): return lax.ppermute(values, 'tile', [(i, i ^ 1) for i in range(NTILE)])  7.15 us
    ppermute x6, starting transfers between devices, turn(): lax.ppermute(values, axis, [(i, (i + step) % count) for i in range(count)])  6.58 us
    ppermute x3, starting transfers between devices, swap_core(): return lax.ppermute(values, 'member', [(i, i ^ 1) for i in range(NMEMBER)])  6.14 us
  transfers between devices with their start and end apart: 15, of which 11 were waited for; matrix products, arithmetic and copies ran while one was open for 0% of the time, Pallas kernels for 1%

profile of v6, /device:TPU:1, one launch (start us, length us, event | category | flops | bytes accessed | tf_op | source)
XLA Modules:
  0.0 95.2 jit_solution(6164138603933330647)
XLA Ops:
  0.6 1.0 %copy.16 = f32[4,16,1280]{2,1,0:T(8,128)S(1)} copy(f32[4,16,1280]{2,0,1:T(4,128)} %bitcast.41) | data formatting | bytes 655360 | tf_op jit(solution)/shard_map/transpose | solution.py:498
  2.4 4.6 %collective-permute-start = (bf16[64,1280]{1,0:T(8,128)(2,1)S(1)}, bf16[64,1280]{1,0:T(8,128)(2,1)S(1)}, u32[]{:S(2)}, u32[]{:S(2)}) collective-permute-start(bf16[64,1280]{1,0:T(8,128)(2,1)S(1)} %bitcast_convert_fusion), channel_id=1, source_target_pairs={{0,1},{1,0},{2,3},{3,2},{4,5},{5,4},{6,7},{7,6},{8,9},{9,8},{10,11... | collective-permute-start | bytes 491528 | tf_op jit(solution)/shard_map/ppermute | solution.py:56
  8.5 13.6 %all_to_all.22 = f32[16,2,128]{2,1,0:T(2,128)S(1)} all-to-all(f32[16,2,128]{2,1,0:T(2,128)S(1)} %bitcast.33), channel_id=1, replica_groups=mesh['member'=8,'tile'=16] {'tile'}, dimensions={0} | all-to-all | bytes 32768 | tf_op jit(solution)/shard_map/all_to_all | solution.py:510
  22.1 4.5 %shard_map.141 = (f32[4,16,384]{2,1,0:T(8,128)S(1)}, f32[4,16,384]{2,1,0:T(8,128)S(1)}, bf16[256,192]{1,0:T(8,128)(2,1)S(1)}, bf16[16,16,2560]{2,1,0:T(8,128)(2,1)S(1)}, bf16[1280,2560]{1,0:T(8,128)(2,1)S(1)}) custom-call(bf16[64,1280]{1,0:T(8,128)(2,1)S(1)} %collective-permute-done.a_ref, f32[64,1280]{1,0:T(8,128)S(1)} %bitcast.27, ...), custom_call_target="tpu_custom_call" | custom-call | flops 1000000000 | bytes 8388608 | tf_op jit(solution)/shard_map/pallas_call | solution.py:97
  26.6 2.7 %collective-permute-start.2 = (f32[4,16,384]{2,1,0:T(8,128)S(1)}, f32[4,16,384]{2,1,0:T(8,128)S(1)}, u32[]{:S(2)}, u32[]{:S(2)}) collective-permute-start(f32[4,16,384]{2,1,0:T(8,128)S(1)} %get-tuple-element.25), channel_id=1, source_target_pairs={{0,16},{16,0},{32,48},{48,32},{64,80},{80,64},{96,112},{112,96},{1... | collective-permute-start | bytes 294920 | tf_op jit(solution)/shard_map/ppermute | solution.py:73
  29.4 0.9 collective-permute-done.2.b_ref
  30.4 2.8 %collective-permute-start.5 = (f32[4,16,384]{2,1,0:T(8,128)S(1)}, f32[4,16,384]{2,1,0:T(8,128)S(1)}, u32[]{:S(2)}, u32[]{:S(2)}) collective-permute-start(f32[4,16,384]{2,1,0:T(8,128)S(1)} %shard_map.142.a_ref), channel_id=1, source_target_pairs={{0,96},{16,112},{32,0},{48,16},{64,32},{80,48},{96,64},{112,80},{1... | collective-permute-start | bytes 294920 | tf_op jit(solution)/shard_map/ppermute | solution.py:52
  34.2 2.7 %collective-permute-done.5.d_ref = f32[4,16,384]{2,1,0:T(8,128)S(1)} collective-permute-done((f32[4,16,384]{2,1,0:T(8,128)S(1)}, f32[4,16,384]{2,1,0:T(8,128)S(1)}, u32[]{:S(2)}, u32[]{:S(2)}) %collective-permute-start.5) | collective-permute-done | bytes 98336 | tf_op jit(solution)/shard_map/ppermute | solution.py:52
  36.9 1.3 %collective-permute-done.4.c_ref = f32[4,16,384]{2,1,0:T(8,128)S(1)} collective-permute-done((f32[4,16,384]{2,1,0:T(8,128)S(1)}, f32[4,16,384]{2,1,0:T(8,128)S(1)}, u32[]{:S(2)}, u32[]{:S(2)}) %collective-permute-start.4) | collective-permute-done | bytes 98336 | tf_op jit(solution)/shard_map/ppermute | solution.py:52
  38.2 3.1 %collective-permute-done.3.b_ref = f32[4,16,384]{2,1,0:T(8,128)S(1)} collective-permute-done((f32[4,16,384]{2,1,0:T(8,128)S(1)}, f32[4,16,384]{2,1,0:T(8,128)S(1)}, u32[]{:S(2)}, u32[]{:S(2)}) %collective-permute-start.3) | collective-permute-done | bytes 98336 | tf_op jit(solution)/shard_map/ppermute | solution.py:52
  41.4 2.4 %shard_map.143 = (f32[4,16,320]{2,1,0:T(8,128)S(1)}, f32[8,128]{1,0:T(8,128)S(1)}, f32[16,320]{1,0:T(8,128)S(1)}) custom-call(f32[4,16,384]{2,1,0:T(8,128)S(1)} %shard_map.142.a_ref, f32[4,16,384]{2,1,0:T(8,128)S(1)} %collective-permute-done.3.b_ref, f32[4,16,384]{2,1,0:T(8,128)S(1)} %collective-permute-done.4.c_ref, ...), custom_call_target="tpu_custom_call" | custom-call | flops 1000000000 | bytes 8388608 | tf_op jit(solution)/shard_map/pallas_call | solution.py:97
  44.5 0.9 collective-permute-done.6.other_ref
  45.5 2.6 %shard_map.144 = (f32[96,1280]{1,0:T(8,128)S(1)}, bf16[64,1280]{1,0:T(8,128)(2,1)S(1)}, bf16[64,1280]{1,0:T(8,128)(2,1)S(1)}) custom-call(f32[4,16,320]{2,1,0:T(8,128)S(1)} %get-tuple-element.26.mine_ref, f32[4,16,320]{2,1,0:T(8,128)S(1)} %collective-permute-done.6.other_ref, bf16[96,512]{1,0:T(8,128)(2,1)S(1)} %copy-done, ...), custom_call_target="tpu_custom_call" | custom-call | flops 1000000000 | bytes 8388608 | tf_op jit(solution)/shard_map/pallas_call | solution.py:97
  49.1 4.4 %collective-permute-done.7.a_ref = bf16[64,1280]{1,0:T(8,128)(2,1)S(1)} collective-permute-done((bf16[64,1280]{1,0:T(8,128)(2,1)S(1)}, bf16[64,1280]{1,0:T(8,128)(2,1)S(1)}, u32[]{:S(2)}, u32[]{:S(2)}) %collective-permute-start.7) | collective-permute-done | bytes 163872 | tf_op jit(solution)/shard_map/ppermute | solution.py:56
  54.6 4.7 %collective-permute-start.9 = (bf16[64,1280]{1,0:T(8,128)(2,1)S(1)}, bf16[64,1280]{1,0:T(8,128)(2,1)S(1)}, u32[]{:S(2)}, u32[]{:S(2)}) collective-permute-start(bf16[64,1280]{1,0:T(8,128)(2,1)S(1)} %get-tuple-element.32), channel_id=1, source_target_pairs={{0,1},{1,0},{2,3},{3,2},{4,5},{5,4},{6,7},{7,6},{8,9},{9,8},{10,11... | collective-permute-start | bytes 491528 | tf_op jit(solution)/shard_map/ppermute | solution.py:56
  59.3 2.7 %collective-permute-done.9.a_ref = bf16[64,1280]{1,0:T(8,128)(2,1)S(1)} collective-permute-done((bf16[64,1280]{1,0:T(8,128)(2,1)S(1)}, bf16[64,1280]{1,0:T(8,128)(2,1)S(1)}, u32[]{:S(2)}, u32[]{:S(2)}) %collective-permute-start.9) | collective-permute-done | bytes 163872 | tf_op jit(solution)/shard_map/ppermute | solution.py:56
  62.0 2.3 %shard_map.146 = (f32[4,16,320]{2,1,0:T(8,128)S(1)}, f32[4,16,320]{2,1,0:T(8,128)S(1)}) custom-call(bf16[64,1280]{1,0:T(8,128)(2,1)S(1)} %collective-permute-done.9.a_ref, f32[64,1280]{1,0:T(8,128)S(1)} %get-tuple-element.33.own_ref.grad_ref, bf16[64,1280]{1,0:T(8,128)(2,1)S(1)} %collective-permute-done.10.b_ref, ...), custom_call_target="tpu_custom_call" | custom-call | flops 1000000000 | bytes 8388608 | tf_op jit(solution)/shard_map/pallas_call | solution.py:97
  64.3 2.7 %collective-permute-start.11 = (f32[4,16,320]{2,1,0:T(8,128)S(1)}, f32[4,16,320]{2,1,0:T(8,128)S(1)}, u32[]{:S(2)}, u32[]{:S(2)}) collective-permute-start(f32[4,16,320]{2,1,0:T(8,128)S(1)} %get-tuple-element.36), channel_id=1, source_target_pairs={{0,16},{16,0},{32,48},{48,32},{64,80},{80,64},{96,112},{112,96},{1... | collective-permute-start | bytes 245768 | tf_op jit(solution)/shard_map/ppermute | solution.py:73
  67.0 0.9 collective-permute-done.11.b_ref
  68.1 1.4 %collective-permute-start.13 = (f32[16,320]{1,0:T(8,128)S(1)}, f32[16,320]{1,0:T(8,128)S(1)}, u32[]{:S(2)}, u32[]{:S(2)}) collective-permute-start(f32[16,320]{1,0:T(8,128)S(1)} %get-tuple-element.39), channel_id=1, source_target_pairs={{0,64},{16,80},{32,96},{48,112},{64,0},{80,16},{96,32},{112,48},{1... | collective-permute-start | bytes 61448 | tf_op jit(solution)/shard_map/ppermute | solution.py:52
  69.5 1.2 %collective-permute-start.14 = (f32[16,320]{1,0:T(8,128)S(1)}, f32[16,320]{1,0:T(8,128)S(1)}, u32[]{:S(2)}, u32[]{:S(2)}) collective-permute-start(f32[16,320]{1,0:T(8,128)S(1)} %get-tuple-element.40), channel_id=1, source_target_pairs={{0,96},{16,112},{32,0},{48,16},{64,32},{80,48},{96,64},{112,80},{1... | collective-permute-start | bytes 61448 | tf_op jit(solution)/shard_map/ppermute | solution.py:52
  70.7 1.2 %collective-permute-done.12.b_ref = f32[16,320]{1,0:T(8,128)S(1)} collective-permute-done((f32[16,320]{1,0:T(8,128)S(1)}, f32[16,320]{1,0:T(8,128)S(1)}, u32[]{:S(2)}, u32[]{:S(2)}) %collective-permute-start.12) | collective-permute-done | bytes 20512 | tf_op jit(solution)/shard_map/ppermute | solution.py:52
  73.6 20.7 %all_to_all.23 = f32[128,1,128]{2,1,0:T(1,128)S(1)} all-to-all(f32[128,1,128]{2,1,0:T(1,128)S(1)} %bitcast.32), channel_id=1, replica_groups=mesh['member'=8,'tile'=16] {'member','tile'}, dimensions={0} | all-to-all | bytes 131072 | tf_op jit(solution)/shard_map/all_to_all | solution.py:541
  94.3 1.0 %shard_map.149 = (f32[16,4,1280]{2,1,0:T(4,128)}, f32[16,320]{1,0:T(8,128)}) custom-call(f32[128,128]{1,0:T(8,128)S(1)} %bitcast.31, f32[64,1280]{1,0:T(8,128)S(1)} %bitcast.29, f32[64,1280]{1,0:T(8,128)S(1)} %get-tuple-element.33.own_ref.grad_ref, f32[16,320]{1,0:T(8,128)S(1)} %get-tuple-element.44.full_ref, f32[16,320]{1,0:T(8,128)S(1)} %copy-done.4, ...), custom_call_target="tpu_custom_call" | custom-call | flops 1000000000 | bytes 8388608 | tf_op jit(solution)/shard_map/pallas_call | solution.py:97
  (32 shorter events, 7.2 us)
Async XLA Ops:
  1.7 28.7 %copy-start.4 = (f32[16,320]{1,0:T(8,128)S(1)}, f32[16,320]{1,0:T(8,128)}, u32[]{:S(2)}) copy-start(f32[16,320]{1,0:T(8,128)} %base_ref.3) | copy-start | bytes 61444
  1.7 20.4 %collective-permute-start.1 = (bf16[64,1280]{1,0:T(8,128)(2,1)S(1)}, bf16[64,1280]{1,0:T(8,128)(2,1)S(1)}, u32[]{:S(2)}, u32[]{:S(2)}) collective-permute-start(bf16[64,1280]{1,0:T(8,128)(2,1)S(1)} %bitcast_convert_fusion), channel_id=1, source_target_pairs={{0,0},{15,15},{1,2},{2,1},{3,4},{4,3},{5,6},{6,5},{7,8},{8,7},{9,1... | collective-permute-start | bytes 491528 | tf_op jit(solution)/shard_map/ppermute | solution.py:63
  2.4 19.7 %collective-permute-start = (bf16[64,1280]{1,0:T(8,128)(2,1)S(1)}, bf16[64,1280]{1,0:T(8,128)(2,1)S(1)}, u32[]{:S(2)}, u32[]{:S(2)}) collective-permute-start(bf16[64,1280]{1,0:T(8,128)(2,1)S(1)} %bitcast_convert_fusion), channel_id=1, source_target_pairs={{0,1},{1,0},{2,3},{3,2},{4,5},{5,4},{6,7},{7,6},{8,9},{9,8},{10,11... | collective-permute-start | bytes 491528 | tf_op jit(solution)/shard_map/ppermute | solution.py:56
  8.5 32.9 %copy-start.1 = (s32[1,128,8,8]{1,3,2,0:T(8,128)S(1)}, s32[1,128,8,8]{1,3,2,0:T(8,128)}, u32[]{:S(2)}) copy-start(s32[1,128,8,8]{1,3,2,0:T(8,128)} %param.17) | copy-start | bytes 98308
  8.5 32.9 %copy-start.2 = (f32[1,128,8,8]{1,3,2,0:T(8,128)S(1)}, f32[1,128,8,8]{1,3,2,0:T(8,128)}, u32[]{:S(2)}) copy-start(f32[1,128,8,8]{1,3,2,0:T(8,128)} %param.18) | copy-start | bytes 98308
  8.5 32.9 %copy-start.3 = (f32[1,128,8,8]{1,3,2,0:T(8,128)S(1)}, f32[1,128,8,8]{1,3,2,0:T(8,128)}, u32[]{:S(2)}) copy-start(f32[1,128,8,8]{1,3,2,0:T(8,128)} %param.19) | copy-start | bytes 98308
  8.5 32.9 %copy-start.5 = (s32[1,128,8]{1,2,0:T(8,128)S(1)}, s32[1,128,8]{1,2,0:T(8,128)}, u32[]{:S(2)}) copy-start(s32[1,128,8]{1,2,0:T(8,128)} %param.20) | copy-start | bytes 12292
  22.1 23.4 %copy-start = (bf16[96,512]{1,0:T(8,128)(2,1)S(1)}, bf16[96,512]{1,0:T(8,128)(2,1)}, u32[]{:S(2)}) copy-start(bf16[96,512]{1,0:T(8,128)(2,1)} %constant.5.clone.back_ref) | copy-start | bytes 294916
  26.6 3.7 %collective-permute-start.2 = (f32[4,16,384]{2,1,0:T(8,128)S(1)}, f32[4,16,384]{2,1,0:T(8,128)S(1)}, u32[]{:S(2)}, u32[]{:S(2)}) collective-permute-start(f32[4,16,384]{2,1,0:T(8,128)S(1)} %get-tuple-element.25), channel_id=1, source_target_pairs={{0,16},{16,0},{32,48},{48,32},{64,80},{80,64},{96,112},{112,96},{1... | collective-permute-start | bytes 294920 | tf_op jit(solution)/shard_map/ppermute | solution.py:73
  30.4 6.6 %collective-permute-start.5 = (f32[4,16,384]{2,1,0:T(8,128)S(1)}, f32[4,16,384]{2,1,0:T(8,128)S(1)}, u32[]{:S(2)}, u32[]{:S(2)}) collective-permute-start(f32[4,16,384]{2,1,0:T(8,128)S(1)} %shard_map.142.a_ref), channel_id=1, source_target_pairs={{0,96},{16,112},{32,0},{48,16},{64,32},{80,48},{96,64},{112,80},{1... | collective-permute-start | bytes 294920 | tf_op jit(solution)/shard_map/ppermute | solution.py:52
  33.2 5.1 %collective-permute-start.4 = (f32[4,16,384]{2,1,0:T(8,128)S(1)}, f32[4,16,384]{2,1,0:T(8,128)S(1)}, u32[]{:S(2)}, u32[]{:S(2)}) collective-permute-start(f32[4,16,384]{2,1,0:T(8,128)S(1)} %shard_map.142.a_ref), channel_id=1, source_target_pairs={{0,64},{16,80},{32,96},{48,112},{64,0},{80,16},{96,32},{112,48},{1... | collective-permute-start | bytes 294920 | tf_op jit(solution)/shard_map/ppermute | solution.py:52
  33.5 7.8 %collective-permute-start.3 = (f32[4,16,384]{2,1,0:T(8,128)S(1)}, f32[4,16,384]{2,1,0:T(8,128)S(1)}, u32[]{:S(2)}, u32[]{:S(2)}) collective-permute-start(f32[4,16,384]{2,1,0:T(8,128)S(1)} %shard_map.142.a_ref), channel_id=1, source_target_pairs={{0,32},{16,48},{32,64},{48,80},{64,96},{80,112},{96,0},{112,16},{1... | collective-permute-start | bytes 294920 | tf_op jit(solution)/shard_map/ppermute | solution.py:52
  43.8 1.6 %collective-permute-start.6 = (f32[4,16,320]{2,1,0:T(8,128)S(1)}, f32[4,16,320]{2,1,0:T(8,128)S(1)}, u32[]{:S(2)}, u32[]{:S(2)}) collective-permute-start(f32[4,16,320]{2,1,0:T(8,128)S(1)} %get-tuple-element.26.mine_ref), channel_id=1, source_target_pairs={{0,16},{16,0},{32,48},{48,32},{64,80},{80,64},{96,112},{112,96},{1... | collective-permute-start | bytes 245768 | tf_op jit(solution)/shard_map/ppermute | solution.py:73
  48.0 5.5 %collective-permute-start.7 = (bf16[64,1280]{1,0:T(8,128)(2,1)S(1)}, bf16[64,1280]{1,0:T(8,128)(2,1)S(1)}, u32[]{:S(2)}, u32[]{:S(2)}) collective-permute-start(bf16[64,1280]{1,0:T(8,128)(2,1)S(1)} %get-tuple-element.29), channel_id=1, source_target_pairs={{0,1},{1,0},{2,3},{3,2},{4,5},{5,4},{6,7},{7,6},{8,9},{9,8},{10,11... | collective-permute-start | bytes 491528 | tf_op jit(solution)/shard_map/ppermute | solution.py:56
  48.4 5.1 %collective-permute-start.8 = (bf16[64,1280]{1,0:T(8,128)(2,1)S(1)}, bf16[64,1280]{1,0:T(8,128)(2,1)S(1)}, u32[]{:S(2)}, u32[]{:S(2)}) collective-permute-start(bf16[64,1280]{1,0:T(8,128)(2,1)S(1)} %get-tuple-element.31), channel_id=1, source_target_pairs={{0,0},{15,15},{1,2},{2,1},{3,4},{4,3},{5,6},{6,5},{7,8},{8,7},{9,1... | collective-permute-start | bytes 491528 | tf_op jit(solution)/shard_map/ppermute | solution.py:63
  53.9 5.4 %collective-permute-start.10 = (bf16[64,1280]{1,0:T(8,128)(2,1)S(1)}, bf16[64,1280]{1,0:T(8,128)(2,1)S(1)}, u32[]{:S(2)}, u32[]{:S(2)}) collective-permute-start(bf16[64,1280]{1,0:T(8,128)(2,1)S(1)} %get-tuple-element.32), channel_id=1, source_target_pairs={{0,0},{15,15},{1,2},{2,1},{3,4},{4,3},{5,6},{6,5},{7,8},{8,7},{9,1... | collective-permute-start | bytes 491528 | tf_op jit(solution)/shard_map/ppermute | solution.py:63
  54.6 7.4 %collective-permute-start.9 = (bf16[64,1280]{1,0:T(8,128)(2,1)S(1)}, bf16[64,1280]{1,0:T(8,128)(2,1)S(1)}, u32[]{:S(2)}, u32[]{:S(2)}) collective-permute-start(bf16[64,1280]{1,0:T(8,128)(2,1)S(1)} %get-tuple-element.32), channel_id=1, source_target_pairs={{0,1},{1,0},{2,3},{3,2},{4,5},{5,4},{6,7},{7,6},{8,9},{9,8},{10,11... | collective-permute-start | bytes 491528 | tf_op jit(solution)/shard_map/ppermute | solution.py:56
  64.3 3.6 %collective-permute-start.11 = (f32[4,16,320]{2,1,0:T(8,128)S(1)}, f32[4,16,320]{2,1,0:T(8,128)S(1)}, u32[]{:S(2)}, u32[]{:S(2)}) collective-permute-start(f32[4,16,320]{2,1,0:T(8,128)S(1)} %get-tuple-element.36), channel_id=1, source_target_pairs={{0,16},{16,0},{32,48},{48,32},{64,80},{80,64},{96,112},{112,96},{1... | collective-permute-start | bytes 245768 | tf_op jit(solution)/shard_map/ppermute | solution.py:73
  68.0 4.0 %collective-permute-start.12 = (f32[16,320]{1,0:T(8,128)S(1)}, f32[16,320]{1,0:T(8,128)S(1)}, u32[]{:S(2)}, u32[]{:S(2)}) collective-permute-start(f32[16,320]{1,0:T(8,128)S(1)} %get-tuple-element.38), channel_id=1, source_target_pairs={{0,32},{16,48},{32,64},{48,80},{64,96},{80,112},{96,0},{112,16},{1... | collective-permute-start | bytes 61448 | tf_op jit(solution)/shard_map/ppermute | solution.py:52
  68.1 4.3 %collective-permute-start.13 = (f32[16,320]{1,0:T(8,128)S(1)}, f32[16,320]{1,0:T(8,128)S(1)}, u32[]{:S(2)}, u32[]{:S(2)}) collective-permute-start(f32[16,320]{1,0:T(8,128)S(1)} %get-tuple-element.39), channel_id=1, source_target_pairs={{0,64},{16,80},{32,96},{48,112},{64,0},{80,16},{96,32},{112,48},{1... | collective-permute-start | bytes 61448 | tf_op jit(solution)/shard_map/ppermute | solution.py:52
  69.5 3.6 %collective-permute-start.14 = (f32[16,320]{1,0:T(8,128)S(1)}, f32[16,320]{1,0:T(8,128)S(1)}, u32[]{:S(2)}, u32[]{:S(2)}) collective-permute-start(f32[16,320]{1,0:T(8,128)S(1)} %get-tuple-element.40), channel_id=1, source_target_pairs={{0,96},{16,112},{32,0},{48,16},{64,32},{80,48},{96,64},{112,80},{1... | collective-permute-start | bytes 61448 | tf_op jit(solution)/shard_map/ppermute | solution.py:52

commit v7 on v6

--- a/solution.py
+++ b/solution.py
@@ -22,6 +22,7 @@
 SLOTS = 8
 BATCHES = 128
 ROOM = 12 << 20
+WORK = 2 * 10**10
 EVEN, ODD = pl.ds(0, NTILE, stride=2), pl.ds(1, NTILE, stride=2)
 FLOAT, HALF = jnp.float32, jnp.bfloat16
 
@@ -86,7 +87,7 @@
     return pltpu.with_memory_space_constraint(values, pltpu.HBM)
 
 
-def call(kernel, out_shapes, arguments, far=(), scratch=(), far_out=(), scalar=()):
+def call(kernel, out_shapes, arguments, far=(), scratch=(), far_out=(), scalar=(), work=10**9):
     specs = [
         SCALAR if i in scalar else FAR if i in far else NEAR for i in range(len(arguments))
     ]
@@ -104,7 +105,7 @@
         out_specs=tuple(NEAR for _ in out_shapes),
         scratch_shapes=list(scratch),
         compiler_params=pltpu.CompilerParams(vmem_limit_bytes=ROOM),
-        cost_estimate=pl.CostEstimate(flops=10**9, transcendentals=0, bytes_accessed=8 << 20),
+        cost_estimate=pl.CostEstimate(flops=work, transcendentals=0, bytes_accessed=work >> 7),
     )(*arguments)
 
 
@@ -145,25 +146,9 @@
     return low, high
 
 
-def streamed_kernel(
-    a_ref, own_ref, b_ref, refine_hbm, perturb_hbm, map_hbm, data_ref,
-    mine_ref, other_ref, refine_ref, perturb_ref, map_ref, smooth_ref, sem,
-):
-    copies = [(pltpu.make_async_copy(refine_hbm, refine_ref, sem.at[0, NY]),)]
-    for y in range(NY):
-        cols = pl.ds(y * CHUNK, CHUNK)
-        copies.append(
-            (
-                pltpu.make_async_copy(map_hbm.at[:, cols], map_ref.at[:, cols], sem.at[0, y]),
-                pltpu.make_async_copy(
-                    perturb_hbm.at[:, :, cols], perturb_ref.at[:, :, cols], sem.at[1, y]
-                ),
-            )
-        )
-    for group in copies[1:2] + copies[:1] + copies[2:]:
-        for copy in group:
-            copy.start()
-
+def laden_kernel(
+    a_ref, own_ref, b_ref, refine_ref, perturb_ref, map_ref, data_ref, mine_ref, other_ref, smooth_ref
+):
     _, core_pos, _ = place()
     data, gain = data_ref[EVEN], data_ref[ODD]
     lanes = lax.broadcasted_iota(jnp.int32, data.shape, 1)
@@ -174,20 +159,13 @@
             moved = jnp.where(lanes == home + 2 * SLOTS, gain, pltpu.roll(data, shift, 1))
             kept = (lanes >= home) & (lanes <= home + 2 * SLOTS)
             ref[y, :, 256:] = jnp.where(kept, moved, 0.0)
-
-    def arrived(y):
-        for copy in copies[y + 1] + (copies[0] if y == 0 else ()):
-            copy.wait()
-
     forward_kernel(
-        a_ref, own_ref, b_ref, refine_ref, perturb_ref, map_ref, mine_ref, other_ref, smooth_ref,
-        arrived=arrived,
+        a_ref, own_ref, b_ref, refine_ref, perturb_ref, map_ref, mine_ref, other_ref, smooth_ref
     )
 
 
 def forward_kernel(
-    a_ref, own_ref, b_ref, refine_ref, perturb_ref, map_ref, mine_ref, other_ref, smooth_ref,
-    arrived=None,
+    a_ref, own_ref, b_ref, refine_ref, perturb_ref, map_ref, mine_ref, other_ref, smooth_ref
 ):
     _, core_pos, _ = place()
     even = is_even()
@@ -202,8 +180,6 @@
     smooth = smooth_ref[...]
     for y in range(NY):
         cols = pl.ds(y * CHUNK, CHUNK)
-        if arrived is not None:
-            arrived(y)
         mapped = jnp.dot(smooth, map_ref[:, cols], preferred_element_type=FLOAT)
         high = mapped.astype(HALF)
         low = (mapped - high.astype(FLOAT)).astype(HALF)
@@ -227,23 +203,8 @@
 SMOOTH = pltpu.VMEM(((ROWS + 2) * MEMBERS_HERE, COARSE_COLS), HALF)
 
 
-def first_forward(first, own, second, perturb, column_map, data):
-    matrix = member_matrix()
-    matrix = jnp.asarray(np.concatenate([matrix, matrix], axis=1), HALF)
-    operators = (matrix, perturb, column_map)
-    return call(
-        streamed_kernel,
-        (LADEN, LADEN) + tuple((x.shape, x.dtype) for x in operators),
-        (first, own, second) + operators + (data,),
-        far=(3, 4, 5),
-        scratch=[SMOOTH, pltpu.SemaphoreType.DMA((2, NY + 1))],
-    )
-
-
-def later_forward(first, own, second, *operators):
-    return call(
-        forward_kernel, (REGIONS, REGIONS), (first, own, second) + operators, scratch=[SMOOTH]
-    )
+def partial_forward(kernel, shape, *arguments):
+    return call(kernel, (shape, shape), arguments, scratch=[SMOOTH])
 
 
 def adjoint_kernel(
@@ -494,6 +455,9 @@
     obs_error,
     instrument_gain,
 ):
+    perturb, column_map = near(perturb), near(column_map)
+    matrix = member_matrix()
+    matrix = near(jnp.asarray(np.concatenate([matrix, matrix], axis=1), HALF))
     flat = (ROWS * MEMBERS_HERE, COARSE_COLS)
     own = jnp.transpose(weights, (1, 0, 2)).reshape(flat)
     half = own.astype(HALF)
@@ -505,6 +469,7 @@
         (obs_value[0].T, obs_error[0].T, instrument_gain),
         far=(0, 1),
         scalar=(2,),
+        work=WORK,
         scratch=[pltpu.VMEM((SLOTS, BATCHES), FLOAT)] * 2 + [pltpu.SemaphoreType.DMA((2,))],
     )
     data = lax.all_to_all(sent, "tile", split_axis=0, concat_axis=0, tiled=True)
@@ -514,8 +479,8 @@
     column_frac = jnp.transpose(column_fraction[0], (1, 2, 0))
     lengths = block_lengths[0].T
 
-    mine, other, matrix, perturb, column_map = first_forward(
-        near_rows, own, far_rows, perturb, column_map, data
+    mine, other = partial_forward(
+        laden_kernel, LADEN, near_rows, own, far_rows, matrix, perturb, column_map, data
     )
     (mine,) = call(add_kernel, (LADEN,), (mine, swap_core(other), background))
     pieces = [mine] + [turn(mine, NCORE * i, "member") for i in range(1, NY)]
@@ -530,7 +495,9 @@
     near_rows, far_rows = swap_both(up, down)
     gradient, half, square = gradient_of(near_rows, part, far_rows, own)
     near_rows, far_rows = swap_both(half, half)
-    mine, other = later_forward(near_rows, gradient, far_rows, matrix, perturb, column_map)
+    mine, other = partial_forward(
+        forward_kernel, REGIONS, near_rows, gradient, far_rows, matrix, perturb, column_map
+    )
     pieces = call(pick_kernel, (region,) * NY, (mine, swap_core(other)))
     pieces = [pieces[0]] + [turn(pieces[i], NCORE * i, "member") for i in range(1, NY)]
     image, sent = call(

time: 95.6 us -> 93.8 us (0.981)
  Pallas kernels: 14.6 us -> 12.6 us
    pallas_call x10, Pallas kernels: 14.6 us -> 12.6 us  [call(): pl.pallas_call(kernel, out_shape=tuple((jax.ShapeDtypeStruct(shape, kind)...]
where the time goes in v7:
time: 93.8 us; the launch traced here: 93.5 us
  blocking collectives  34.3 us (37%)
  starting transfers between devices  24.4 us (26%)
  waiting for transfers between devices  19.5 us (21%)
  Pallas kernels  12.6 us (13%)
  between operations  1.51 us (2%)
  local copies, waits for them, and re-layouts  1.25 us (1%)
    all_to_all x1, blocking collectives, shards(): lax.all_to_all(sent, ('member', 'tile'), split_axis=0, concat_axis=0, til...  20.7 us
    all_to_all x1, blocking collectives, shards(): data = lax.all_to_all(sent, 'tile', split_axis=0, concat_axis=0, tiled=True)  13.6 us
    pallas_call x10, Pallas kernels, call(): pl.pallas_call(kernel, out_shape=tuple((jax.ShapeDtypeStruct(shape, kind)...  12.6 us
    ppermute x3, starting transfers between devices, swap_near(): return lax.ppermute(values, 'tile', [(i, i ^ 1) for i in range(NTILE)])  9.6 us
    ppermute x6, waiting for transfers between devices, turn(): lax.ppermute(values, axis, [(i, (i + step) % count) for i in range(count)])  9.51 us
    ppermute x3, waiting for transfers between devices, swap_near(): return lax.ppermute(values, 'tile', [(i, i ^ 1) for i in range(NTILE)])  7.16 us
    ppermute x6, starting transfers between devices, turn(): lax.ppermute(values, axis, [(i, (i + step) % count) for i in range(count)])  6.59 us
    ppermute x3, starting transfers between devices, swap_core(): return lax.ppermute(values, 'member', [(i, i ^ 1) for i in range(NMEMBER)])  6.11 us
  transfers between devices with their start and end apart: 15, of which 11 were waited for; matrix products, arithmetic and copies ran while one was open for 0% of the time, Pallas kernels for 1%

profile of v7, /device:TPU:1, one launch (start us, length us, event | category | flops | bytes accessed | tf_op | source)
XLA Modules:
  0.0 93.5 jit_solution(1556046795448366786)
XLA Ops:
  0.6 1.2 %copy.16 = f32[4,16,1280]{2,1,0:T(8,128)S(1)} copy(f32[4,16,1280]{2,0,1:T(4,128)} %bitcast.43) | data formatting | bytes 655360 | tf_op jit(solution)/shard_map/transpose | solution.py:462
  2.7 4.6 %collective-permute-start = (bf16[64,1280]{1,0:T(8,128)(2,1)S(1)}, bf16[64,1280]{1,0:T(8,128)(2,1)S(1)}, u32[]{:S(2)}, u32[]{:S(2)}) collective-permute-start(bf16[64,1280]{1,0:T(8,128)(2,1)S(1)} %bitcast_convert_fusion), channel_id=1, source_target_pairs={{0,1},{1,0},{2,3},{3,2},{4,5},{5,4},{6,7},{7,6},{8,9},{9,8},{10,11... | collective-permute-start | bytes 491528 | tf_op jit(solution)/shard_map/ppermute | solution.py:57
  7.9 1.0 %shard_map.140 = f32[32,128]{1,0:T(8,128)S(1)} custom-call(f32[8,128]{1,0:T(8,128)} %bitcast.44, f32[8,128]{1,0:T(8,128)} %bitcast.45, f32[1]{0:T(128)S(6)} %copy.18.gain_ref), custom_call_target="tpu_custom_call" | custom-call | flops 20000000000 | bytes 156250000 | tf_op jit(solution)/shard_map/pallas_call | solution.py:98
  9.0 13.6 %all_to_all.22 = f32[16,2,128]{2,1,0:T(2,128)S(1)} all-to-all(f32[16,2,128]{2,1,0:T(2,128)S(1)} %bitcast.35), channel_id=1, replica_groups=mesh['member'=8,'tile'=16] {'tile'}, dimensions={0} | all-to-all | bytes 32768 | tf_op jit(solution)/shard_map/all_to_all | solution.py:475
  22.6 2.3 %shard_map.141 = (f32[4,16,384]{2,1,0:T(8,128)S(1)}, f32[4,16,384]{2,1,0:T(8,128)S(1)}) custom-call(bf16[64,1280]{1,0:T(8,128)(2,1)S(1)} %collective-permute-done.a_ref, f32[64,1280]{1,0:T(8,128)S(1)} %bitcast.29, bf16[64,1280]{1,0:T(8,128)(2,1)S(1)} %collective-permute-done.1.b_ref, bf16[256,192]{1,0:T(8,128)(2,1)S(1)} %copy-done.1, ...), custom_call_target="tpu_custom_call" | custom-call | flops 1000000000 | bytes 7812500 | tf_op jit(solution)/shard_map/pallas_call | solution.py:98
  24.9 2.7 %collective-permute-start.2 = (f32[4,16,384]{2,1,0:T(8,128)S(1)}, f32[4,16,384]{2,1,0:T(8,128)S(1)}, u32[]{:S(2)}, u32[]{:S(2)}) collective-permute-start(f32[4,16,384]{2,1,0:T(8,128)S(1)} %get-tuple-element.22), channel_id=1, source_target_pairs={{0,16},{16,0},{32,48},{48,32},{64,80},{80,64},{96,112},{112,96},{1... | collective-permute-start | bytes 294920 | tf_op jit(solution)/shard_map/ppermute | solution.py:74
  27.7 0.9 %collective-permute-done.2.b_ref = f32[4,16,384]{2,1,0:T(8,128)S(1)} collective-permute-done((f32[4,16,384]{2,1,0:T(8,128)S(1)}, f32[4,16,384]{2,1,0:T(8,128)S(1)}, u32[]{:S(2)}, u32[]{:S(2)}) %collective-permute-start.2) | collective-permute-done | bytes 98336 | tf_op jit(solution)/shard_map/ppermute | solution.py:74
  28.6 2.8 %collective-permute-start.5 = (f32[4,16,384]{2,1,0:T(8,128)S(1)}, f32[4,16,384]{2,1,0:T(8,128)S(1)}, u32[]{:S(2)}, u32[]{:S(2)}) collective-permute-start(f32[4,16,384]{2,1,0:T(8,128)S(1)} %shard_map.142.a_ref), channel_id=1, source_target_pairs={{0,96},{16,112},{32,0},{48,16},{64,32},{80,48},{96,64},{112,80},{1... | collective-permute-start | bytes 294920 | tf_op jit(solution)/shard_map/ppermute | solution.py:53
  32.5 2.7 %collective-permute-done.5.d_ref = f32[4,16,384]{2,1,0:T(8,128)S(1)} collective-permute-done((f32[4,16,384]{2,1,0:T(8,128)S(1)}, f32[4,16,384]{2,1,0:T(8,128)S(1)}, u32[]{:S(2)}, u32[]{:S(2)}) %collective-permute-start.5) | collective-permute-done | bytes 98336 | tf_op jit(solution)/shard_map/ppermute | solution.py:53
  35.2 1.3 %collective-permute-done.4.c_ref = f32[4,16,384]{2,1,0:T(8,128)S(1)} collective-permute-done((f32[4,16,384]{2,1,0:T(8,128)S(1)}, f32[4,16,384]{2,1,0:T(8,128)S(1)}, u32[]{:S(2)}, u32[]{:S(2)}) %collective-permute-start.4) | collective-permute-done | bytes 98336 | tf_op jit(solution)/shard_map/ppermute | solution.py:53
  36.5 3.1 %collective-permute-done.3.b_ref = f32[4,16,384]{2,1,0:T(8,128)S(1)} collective-permute-done((f32[4,16,384]{2,1,0:T(8,128)S(1)}, f32[4,16,384]{2,1,0:T(8,128)S(1)}, u32[]{:S(2)}, u32[]{:S(2)}) %collective-permute-start.3) | collective-permute-done | bytes 98336 | tf_op jit(solution)/shard_map/ppermute | solution.py:53
  39.7 2.4 %shard_map.143 = (f32[4,16,320]{2,1,0:T(8,128)S(1)}, f32[8,128]{1,0:T(8,128)S(1)}, f32[16,320]{1,0:T(8,128)S(1)}) custom-call(f32[4,16,384]{2,1,0:T(8,128)S(1)} %shard_map.142.a_ref, f32[4,16,384]{2,1,0:T(8,128)S(1)} %collective-permute-done.3.b_ref, f32[4,16,384]{2,1,0:T(8,128)S(1)} %collective-permute-done.4.c_ref, ...), custom_call_target="tpu_custom_call" | custom-call | flops 1000000000 | bytes 7812500 | tf_op jit(solution)/shard_map/pallas_call | solution.py:98
  43.8 2.6 %shard_map.144 = (f32[96,1280]{1,0:T(8,128)S(1)}, bf16[64,1280]{1,0:T(8,128)(2,1)S(1)}, bf16[64,1280]{1,0:T(8,128)(2,1)S(1)}) custom-call(f32[4,16,320]{2,1,0:T(8,128)S(1)} %get-tuple-element.23.mine_ref, f32[4,16,320]{2,1,0:T(8,128)S(1)} %collective-permute-done.6.other_ref, bf16[96,512]{1,0:T(8,128)(2,1)S(1)} %copy-done.2, ...), custom_call_target="tpu_custom_call" | custom-call | flops 1000000000 | bytes 7812500 | tf_op jit(solution)/shard_map/pallas_call | solution.py:98
  47.3 4.5 %collective-permute-done.7.a_ref = bf16[64,1280]{1,0:T(8,128)(2,1)S(1)} collective-permute-done((bf16[64,1280]{1,0:T(8,128)(2,1)S(1)}, bf16[64,1280]{1,0:T(8,128)(2,1)S(1)}, u32[]{:S(2)}, u32[]{:S(2)}) %collective-permute-start.7) | collective-permute-done | bytes 163872 | tf_op jit(solution)/shard_map/ppermute | solution.py:57
  52.9 4.7 %collective-permute-start.9 = (bf16[64,1280]{1,0:T(8,128)(2,1)S(1)}, bf16[64,1280]{1,0:T(8,128)(2,1)S(1)}, u32[]{:S(2)}, u32[]{:S(2)}) collective-permute-start(bf16[64,1280]{1,0:T(8,128)(2,1)S(1)} %get-tuple-element.27), channel_id=1, source_target_pairs={{0,1},{1,0},{2,3},{3,2},{4,5},{5,4},{6,7},{7,6},{8,9},{9,8},{10,11... | collective-permute-start | bytes 491528 | tf_op jit(solution)/shard_map/ppermute | solution.py:57
  57.6 2.7 %collective-permute-done.9.a_ref = bf16[64,1280]{1,0:T(8,128)(2,1)S(1)} collective-permute-done((bf16[64,1280]{1,0:T(8,128)(2,1)S(1)}, bf16[64,1280]{1,0:T(8,128)(2,1)S(1)}, u32[]{:S(2)}, u32[]{:S(2)}) %collective-permute-start.9) | collective-permute-done | bytes 163872 | tf_op jit(solution)/shard_map/ppermute | solution.py:57
  60.3 2.3 %shard_map.146 = (f32[4,16,320]{2,1,0:T(8,128)S(1)}, f32[4,16,320]{2,1,0:T(8,128)S(1)}) custom-call(bf16[64,1280]{1,0:T(8,128)(2,1)S(1)} %collective-permute-done.9.a_ref, f32[64,1280]{1,0:T(8,128)S(1)} %get-tuple-element.28.own_ref.grad_ref, bf16[64,1280]{1,0:T(8,128)(2,1)S(1)} %collective-permute-done.10.b_ref, bf16[256,192]{1,0:T(8,128)(2,1)S(1)} %copy-done.1, ...), custom_call_target="tpu_custom_call" | custom-call | flops 1000000000 | bytes 7812500 | tf_op jit(solution)/shard_map/pallas_call | solution.py:98
  62.6 2.7 %collective-permute-start.11 = (f32[4,16,320]{2,1,0:T(8,128)S(1)}, f32[4,16,320]{2,1,0:T(8,128)S(1)}, u32[]{:S(2)}, u32[]{:S(2)}) collective-permute-start(f32[4,16,320]{2,1,0:T(8,128)S(1)} %get-tuple-element.30), channel_id=1, source_target_pairs={{0,16},{16,0},{32,48},{48,32},{64,80},{80,64},{96,112},{112,96},{1... | collective-permute-start | bytes 245768 | tf_op jit(solution)/shard_map/ppermute | solution.py:74
  65.3 0.9 %collective-permute-done.11.b_ref = f32[4,16,320]{2,1,0:T(8,128)S(1)} collective-permute-done((f32[4,16,320]{2,1,0:T(8,128)S(1)}, f32[4,16,320]{2,1,0:T(8,128)S(1)}, u32[]{:S(2)}, u32[]{:S(2)}) %collective-permute-start.11) | collective-permute-done | bytes 81952 | tf_op jit(solution)/shard_map/ppermute | solution.py:74
  66.3 1.4 %collective-permute-start.13 = (f32[16,320]{1,0:T(8,128)S(1)}, f32[16,320]{1,0:T(8,128)S(1)}, u32[]{:S(2)}, u32[]{:S(2)}) collective-permute-start(f32[16,320]{1,0:T(8,128)S(1)} %get-tuple-element.33), channel_id=1, source_target_pairs={{0,64},{16,80},{32,96},{48,112},{64,0},{80,16},{96,32},{112,48},{1... | collective-permute-start | bytes 61448 | tf_op jit(solution)/shard_map/ppermute | solution.py:53
  67.8 1.2 %collective-permute-start.14 = (f32[16,320]{1,0:T(8,128)S(1)}, f32[16,320]{1,0:T(8,128)S(1)}, u32[]{:S(2)}, u32[]{:S(2)}) collective-permute-start(f32[16,320]{1,0:T(8,128)S(1)} %get-tuple-element.34), channel_id=1, source_target_pairs={{0,96},{16,112},{32,0},{48,16},{64,32},{80,48},{96,64},{112,80},{1... | collective-permute-start | bytes 61448 | tf_op jit(solution)/shard_map/ppermute | solution.py:53
  69.0 1.2 %collective-permute-done.12.b_ref = f32[16,320]{1,0:T(8,128)S(1)} collective-permute-done((f32[16,320]{1,0:T(8,128)S(1)}, f32[16,320]{1,0:T(8,128)S(1)}, u32[]{:S(2)}, u32[]{:S(2)}) %collective-permute-start.12) | collective-permute-done | bytes 20512 | tf_op jit(solution)/shard_map/ppermute | solution.py:53
  71.9 20.7 %all_to_all.23 = f32[128,1,128]{2,1,0:T(1,128)S(1)} all-to-all(f32[128,1,128]{2,1,0:T(1,128)S(1)} %bitcast.34), channel_id=1, replica_groups=mesh['member'=8,'tile'=16] {'member','tile'}, dimensions={0} | all-to-all | bytes 131072 | tf_op jit(solution)/shard_map/all_to_all | solution.py:508
  92.6 1.0 %shard_map.149 = (f32[16,4,1280]{2,1,0:T(4,128)}, f32[16,320]{1,0:T(8,128)}) custom-call(f32[128,128]{1,0:T(8,128)S(1)} %bitcast.33, f32[64,1280]{1,0:T(8,128)S(1)} %bitcast.31, f32[64,1280]{1,0:T(8,128)S(1)} %get-tuple-element.28.own_ref.grad_ref, f32[16,320]{1,0:T(8,128)S(1)} %get-tuple-element.38.full_ref, f32[16,320]{1,0:T(8,128)S(1)} %copy-done.6, ...), custom_call_target="tpu_custom_call" | custom-call | flops 1000000000 | bytes 7812500 | tf_op jit(solution)/shard_map/pallas_call | solution.py:98
  (41 shorter events, 7.4 us)
Async XLA Ops:
  0.6 21.9 %slice-start = ((s8[6553600]{0:T(1024)(128)(4,1)}), s8[4194304]{0:T(1024)(128)(4,1)S(1)}, s32[]{:S(2)}) async-start(s8[6553600]{0:T(1024)(128)(4,1)} %bitcast.27), calls=%async_computation.2 | async-start | bytes 8388608
  1.9 20.7 %collective-permute-start.1 = (bf16[64,1280]{1,0:T(8,128)(2,1)S(1)}, bf16[64,1280]{1,0:T(8,128)(2,1)S(1)}, u32[]{:S(2)}, u32[]{:S(2)}) collective-permute-start(bf16[64,1280]{1,0:T(8,128)(2,1)S(1)} %bitcast_convert_fusion), channel_id=1, source_target_pairs={{0,0},{15,15},{1,2},{2,1},{3,4},{4,3},{5,6},{6,5},{7,8},{8,7},{9,1... | collective-permute-start | bytes 491528 | tf_op jit(solution)/shard_map/ppermute | solution.py:64
  2.7 19.9 %collective-permute-start = (bf16[64,1280]{1,0:T(8,128)(2,1)S(1)}, bf16[64,1280]{1,0:T(8,128)(2,1)S(1)}, u32[]{:S(2)}, u32[]{:S(2)}) collective-permute-start(bf16[64,1280]{1,0:T(8,128)(2,1)S(1)} %bitcast_convert_fusion), channel_id=1, source_target_pairs={{0,1},{1,0},{2,3},{3,2},{4,5},{5,4},{6,7},{7,6},{8,9},{9,8},{10,11... | collective-permute-start | bytes 491528 | tf_op jit(solution)/shard_map/ppermute | solution.py:57
  7.9 14.7 %slice-start.1 = ((s8[6553600]{0:T(1024)(128)(4,1)}), s8[2359296]{0:T(1024)(128)(4,1)S(1)}, s32[]{:S(2)}) async-start(s8[6553600]{0:T(1024)(128)(4,1)} %bitcast.27), calls=%async_computation.3 | async-start | bytes 4718592
  7.9 14.7 %copy-start = (bf16[16,16,2560]{2,1,0:T(8,128)(2,1)S(1)}, bf16[16,16,2560]{2,1,0:T(8,128)(2,1)}, u32[]{:S(2)}) copy-start(bf16[16,16,2560]{2,1,0:T(8,128)(2,1)} %perturb_ref.5) | copy-start | bytes 3932164
  8.9 19.7 %copy-start.6 = (f32[16,320]{1,0:T(8,128)S(1)}, f32[16,320]{1,0:T(8,128)}, u32[]{:S(2)}) copy-start(f32[16,320]{1,0:T(8,128)} %base_ref.3) | copy-start | bytes 61444
  8.9 30.7 %copy-start.3 = (s32[1,128,8,8]{1,3,2,0:T(8,128)S(1)}, s32[1,128,8,8]{1,3,2,0:T(8,128)}, u32[]{:S(2)}) copy-start(s32[1,128,8,8]{1,3,2,0:T(8,128)} %param.17) | copy-start | bytes 98308
  9.0 30.7 %copy-start.4 = (f32[1,128,8,8]{1,3,2,0:T(8,128)S(1)}, f32[1,128,8,8]{1,3,2,0:T(8,128)}, u32[]{:S(2)}) copy-start(f32[1,128,8,8]{1,3,2,0:T(8,128)} %param.18) | copy-start | bytes 98308
  9.0 30.7 %copy-start.5 = (f32[1,128,8,8]{1,3,2,0:T(8,128)S(1)}, f32[1,128,8,8]{1,3,2,0:T(8,128)}, u32[]{:S(2)}) copy-start(f32[1,128,8,8]{1,3,2,0:T(8,128)} %param.19) | copy-start | bytes 98308
  9.0 30.7 %copy-start.7 = (s32[1,128,8]{1,2,0:T(8,128)S(1)}, s32[1,128,8]{1,2,0:T(8,128)}, u32[]{:S(2)}) copy-start(s32[1,128,8]{1,2,0:T(8,128)} %param.20) | copy-start | bytes 12292
  22.6 21.1 %copy-start.2 = (bf16[96,512]{1,0:T(8,128)(2,1)S(1)}, bf16[96,512]{1,0:T(8,128)(2,1)}, u32[]{:S(2)}) copy-start(bf16[96,512]{1,0:T(8,128)(2,1)} %constant.5.clone.back_ref) | copy-start | bytes 294916
  24.9 3.7 %collective-permute-start.2 = (f32[4,16,384]{2,1,0:T(8,128)S(1)}, f32[4,16,384]{2,1,0:T(8,128)S(1)}, u32[]{:S(2)}, u32[]{:S(2)}) collective-permute-start(f32[4,16,384]{2,1,0:T(8,128)S(1)} %get-tuple-element.22), channel_id=1, source_target_pairs={{0,16},{16,0},{32,48},{48,32},{64,80},{80,64},{96,112},{112,96},{1... | collective-permute-start | bytes 294920 | tf_op jit(solution)/shard_map/ppermute | solution.py:74
  28.6 6.6 %collective-permute-start.5 = (f32[4,16,384]{2,1,0:T(8,128)S(1)}, f32[4,16,384]{2,1,0:T(8,128)S(1)}, u32[]{:S(2)}, u32[]{:S(2)}) collective-permute-start(f32[4,16,384]{2,1,0:T(8,128)S(1)} %shard_map.142.a_ref), channel_id=1, source_target_pairs={{0,96},{16,112},{32,0},{48,16},{64,32},{80,48},{96,64},{112,80},{1... | collective-permute-start | bytes 294920 | tf_op jit(solution)/shard_map/ppermute | solution.py:53
  31.4 5.1 %collective-permute-start.4 = (f32[4,16,384]{2,1,0:T(8,128)S(1)}, f32[4,16,384]{2,1,0:T(8,128)S(1)}, u32[]{:S(2)}, u32[]{:S(2)}) collective-permute-start(f32[4,16,384]{2,1,0:T(8,128)S(1)} %shard_map.142.a_ref), channel_id=1, source_target_pairs={{0,64},{16,80},{32,96},{48,112},{64,0},{80,16},{96,32},{112,48},{1... | collective-permute-start | bytes 294920 | tf_op jit(solution)/shard_map/ppermute | solution.py:53
  31.8 7.9 %collective-permute-start.3 = (f32[4,16,384]{2,1,0:T(8,128)S(1)}, f32[4,16,384]{2,1,0:T(8,128)S(1)}, u32[]{:S(2)}, u32[]{:S(2)}) collective-permute-start(f32[4,16,384]{2,1,0:T(8,128)S(1)} %shard_map.142.a_ref), channel_id=1, source_target_pairs={{0,32},{16,48},{32,64},{48,80},{64,96},{80,112},{96,0},{112,16},{1... | collective-permute-start | bytes 294920 | tf_op jit(solution)/shard_map/ppermute | solution.py:53
  42.1 1.6 %collective-permute-start.6 = (f32[4,16,320]{2,1,0:T(8,128)S(1)}, f32[4,16,320]{2,1,0:T(8,128)S(1)}, u32[]{:S(2)}, u32[]{:S(2)}) collective-permute-start(f32[4,16,320]{2,1,0:T(8,128)S(1)} %get-tuple-element.23.mine_ref), channel_id=1, source_target_pairs={{0,16},{16,0},{32,48},{48,32},{64,80},{80,64},{96,112},{112,96},{1... | collective-permute-start | bytes 245768 | tf_op jit(solution)/shard_map/ppermute | solution.py:74
  46.3 5.5 %collective-permute-start.7 = (bf16[64,1280]{1,0:T(8,128)(2,1)S(1)}, bf16[64,1280]{1,0:T(8,128)(2,1)S(1)}, u32[]{:S(2)}, u32[]{:S(2)}) collective-permute-start(bf16[64,1280]{1,0:T(8,128)(2,1)S(1)} %get-tuple-element.24), channel_id=1, source_target_pairs={{0,1},{1,0},{2,3},{3,2},{4,5},{5,4},{6,7},{7,6},{8,9},{9,8},{10,11... | collective-permute-start | bytes 491528 | tf_op jit(solution)/shard_map/ppermute | solution.py:57
  46.7 5.1 %collective-permute-start.8 = (bf16[64,1280]{1,0:T(8,128)(2,1)S(1)}, bf16[64,1280]{1,0:T(8,128)(2,1)S(1)}, u32[]{:S(2)}, u32[]{:S(2)}) collective-permute-start(bf16[64,1280]{1,0:T(8,128)(2,1)S(1)} %get-tuple-element.26), channel_id=1, source_target_pairs={{0,0},{15,15},{1,2},{2,1},{3,4},{4,3},{5,6},{6,5},{7,8},{8,7},{9,1... | collective-permute-start | bytes 491528 | tf_op jit(solution)/shard_map/ppermute | solution.py:64
  52.2 5.4 %collective-permute-start.10 = (bf16[64,1280]{1,0:T(8,128)(2,1)S(1)}, bf16[64,1280]{1,0:T(8,128)(2,1)S(1)}, u32[]{:S(2)}, u32[]{:S(2)}) collective-permute-start(bf16[64,1280]{1,0:T(8,128)(2,1)S(1)} %get-tuple-element.27), channel_id=1, source_target_pairs={{0,0},{15,15},{1,2},{2,1},{3,4},{4,3},{5,6},{6,5},{7,8},{8,7},{9,1... | collective-permute-start | bytes 491528 | tf_op jit(solution)/shard_map/ppermute | solution.py:64
  52.9 7.4 %collective-permute-start.9 = (bf16[64,1280]{1,0:T(8,128)(2,1)S(1)}, bf16[64,1280]{1,0:T(8,128)(2,1)S(1)}, u32[]{:S(2)}, u32[]{:S(2)}) collective-permute-start(bf16[64,1280]{1,0:T(8,128)(2,1)S(1)} %get-tuple-element.27), channel_id=1, source_target_pairs={{0,1},{1,0},{2,3},{3,2},{4,5},{5,4},{6,7},{7,6},{8,9},{9,8},{10,11... | collective-permute-start | bytes 491528 | tf_op jit(solution)/shard_map/ppermute | solution.py:57
  62.6 3.6 %collective-permute-start.11 = (f32[4,16,320]{2,1,0:T(8,128)S(1)}, f32[4,16,320]{2,1,0:T(8,128)S(1)}, u32[]{:S(2)}, u32[]{:S(2)}) collective-permute-start(f32[4,16,320]{2,1,0:T(8,128)S(1)} %get-tuple-element.30), channel_id=1, source_target_pairs={{0,16},{16,0},{32,48},{48,32},{64,80},{80,64},{96,112},{112,96},{1... | collective-permute-start | bytes 245768 | tf_op jit(solution)/shard_map/ppermute | solution.py:74
  66.3 4.0 %collective-permute-start.12 = (f32[16,320]{1,0:T(8,128)S(1)}, f32[16,320]{1,0:T(8,128)S(1)}, u32[]{:S(2)}, u32[]{:S(2)}) collective-permute-start(f32[16,320]{1,0:T(8,128)S(1)} %get-tuple-element.32), channel_id=1, source_target_pairs={{0,32},{16,48},{32,64},{48,80},{64,96},{80,112},{96,0},{112,16},{1... | collective-permute-start | bytes 61448 | tf_op jit(solution)/shard_map/ppermute | solution.py:53
  66.3 4.3 %collective-permute-start.13 = (f32[16,320]{1,0:T(8,128)S(1)}, f32[16,320]{1,0:T(8,128)S(1)}, u32[]{:S(2)}, u32[]{:S(2)}) collective-permute-start(f32[16,320]{1,0:T(8,128)S(1)} %get-tuple-element.33), channel_id=1, source_target_pairs={{0,64},{16,80},{32,96},{48,112},{64,0},{80,16},{96,32},{112,48},{1... | collective-permute-start | bytes 61448 | tf_op jit(solution)/shard_map/ppermute | solution.py:53
  67.8 3.6 %collective-permute-start.14 = (f32[16,320]{1,0:T(8,128)S(1)}, f32[16,320]{1,0:T(8,128)S(1)}, u32[]{:S(2)}, u32[]{:S(2)}) collective-permute-start(f32[16,320]{1,0:T(8,128)S(1)} %get-tuple-element.34), channel_id=1, source_target_pairs={{0,96},{16,112},{32,0},{48,16},{64,32},{80,48},{96,64},{112,80},{1... | collective-permute-start | bytes 61448 | tf_op jit(solution)/shard_map/ppermute | solution.py:53
  (1 other events, 14.7 us)

commit v8 on v7

--- a/solution.py
+++ b/solution.py
@@ -48,26 +48,27 @@
     )
 
 
-def turn(values, step, axis):
-    count = lax.axis_size(axis)
-    return lax.ppermute(values, axis, [(i, (i + step) % count) for i in range(count)])
-
-
-def swap_near(values):
-    return lax.ppermute(values, "tile", [(i, i ^ 1) for i in range(NTILE)])
-
-
-def swap_far(values):
-    pairs = [(0, 0), (NTILE - 1, NTILE - 1)]
-    for i in range(1, NTILE - 1, 2):
-        pairs += [(i, i + 1), (i + 1, i)]
-    return lax.ppermute(values, "tile", pairs)
-
-
-def swap_both(near_values, far_values):
-    near_rows = swap_near(near_values)
-    far_rows = swap_far(far_values)
-    return near_rows, far_rows
+def ring():
+    step = []
+    for member in range(NMEMBER):
+        core, here, there = member % NCORE, member * NTILE, (member ^ 1) * NTILE
+        for tile in range(NTILE):
+            onward = tile + 1 - 2 * core
+            inside = 0 <= onward < NTILE
+            step.append((here + tile, here + onward if inside else there + tile))
+    return step
+
+
+def swap_both(first_values, second_values):
+    first = lax.ppermute(first_values, ("member", "tile"), ring())
+    back = [(target, source) for source, target in ring()]
+    second = lax.ppermute(second_values, ("member", "tile"), back)
+    return first, second
+
+
+def across(values, step):
+    pairs = [(i, i ^ (NCORE * step)) for i in range(NMEMBER)]
+    return lax.ppermute(values, "member", pairs)
 
 
 def swap_core(values):
@@ -134,15 +135,15 @@
     return pl.ds(row * MEMBERS_HERE, MEMBERS_HERE)
 
 
-def is_even():
-    return lax.rem(lax.axis_index("tile"), 2) == 0
-
-
-def sides(a_ref, b_ref, cols, even):
+def downward():
+    return lax.rem(lax.axis_index("member"), NCORE) == 1
+
+
+def sides(a_ref, b_ref, cols, down_first):
     first = [a_ref[row_slice(r), cols].astype(FLOAT) for r in range(4)]
     second = [b_ref[row_slice(r), cols].astype(FLOAT) for r in range(4)]
-    low = [jnp.where(even, v, u) for u, v in zip(first, second)]
-    high = [jnp.where(even, u, v) for u, v in zip(first, second)]
+    low = [jnp.where(down_first, v, u) for u, v in zip(first, second)]
+    high = [jnp.where(down_first, u, v) for u, v in zip(first, second)]
     return low, high
 
 
@@ -168,12 +169,12 @@
     a_ref, own_ref, b_ref, refine_ref, perturb_ref, map_ref, mine_ref, other_ref, smooth_ref
 ):
     _, core_pos, _ = place()
-    even = is_even()
+    down_first = downward()
     below, above = edges()
     masks = [below] * 4 + [None] * 4 + [above] * 4
     for start in range(0, COARSE_COLS, 128):
         cols = pl.ds(start, 128)
-        low, high = sides(a_ref, b_ref, cols, even)
+        low, high = sides(a_ref, b_ref, cols, down_first)
         rows = low + [own_ref[row_slice(r), cols] for r in range(4)] + high
         for r, value in enumerate(swept(rows, masks)):
             smooth_ref[row_slice(r), cols] = value.astype(HALF)
@@ -212,7 +213,7 @@
     part_ref, a_ref, b_ref,
 ):
     _, core_pos, _ = place()
-    even = is_even()
+    down_first = downward()
     total = None
     for y in range(NY):
         cols = pl.ds(y * CHUNK, CHUNK)
@@ -239,8 +240,8 @@
     part_ref[...] = total
     up = total[2 * MEMBERS_HERE :].astype(HALF)
     down = total[: 4 * MEMBERS_HERE].astype(HALF)
-    a_ref[...] = jnp.where(even, up, down)
-    b_ref[...] = jnp.where(even, down, up)
+    a_ref[...] = jnp.where(down_first, down, up)
+    b_ref[...] = jnp.where(down_first, up, down)
 
 
 def partial_adjoint(mine, other, perturb, column_map):
@@ -257,11 +258,11 @@
 def gradient_kernel(a_ref, part_ref, b_ref, own_ref, grad_ref, half_ref, square_ref):
     below, above = edges()
     masks = [below] * 3 + [None] * 4 + [above] * 3
-    even = is_even()
+    down_first = downward()
     square = None
     for start in range(0, COARSE_COLS, 128):
         cols = pl.ds(start, 128)
-        low, high = sides(a_ref, b_ref, cols, even)
+        low, high = sides(a_ref, b_ref, cols, down_first)
         part = [part_ref[row_slice(r), cols] for r in range(6)]
         rows = [low[0], low[1], low[2] + part[0], low[3] * below + part[1], part[2], part[3]]
         rows += [part[4] + high[0] * above, part[5] + high[1], high[2], high[3]]
@@ -310,7 +311,7 @@
 def pick_kernel(a_ref, b_ref, *out_refs):
     _, _, y_pos = place()
     for step, ref in enumerate(out_refs):
-        y = lax.rem(y_pos + step, NY)
+        y = lax.bitwise_xor(y_pos, step)
         ref[...] = a_ref[y] + b_ref[y]
 
 
@@ -373,7 +374,7 @@
     for y in range(NY):
         field = sum(ref[y, :, :WIDTH] for ref in (b_ref, c_ref, d_ref)) + a_ref[y, :, :WIDTH]
         for step, ref in enumerate((a_ref, b_ref, c_ref, d_ref)):
-            source = lax.rem(y_pos + NY - step, NY) * (NCORE * NTILE)
+            source = lax.bitwise_xor(y_pos, step) * (NCORE * NTILE)
             load = ref[y, :, 256:]
             for core in range(NCORE):
                 start = pl.multiple_of(source + core * NTILE, NTILE)
@@ -483,7 +484,7 @@
         laden_kernel, LADEN, near_rows, own, far_rows, matrix, perturb, column_map, data
     )
     (mine,) = call(add_kernel, (LADEN,), (mine, swap_core(other), background))
-    pieces = [mine] + [turn(mine, NCORE * i, "member") for i in range(1, NY)]
+    pieces = [mine] + [across(mine, i) for i in range(1, NY)]
     region = ((FINE_ROWS, WIDTH), FLOAT)
     spread, weight, full = call(
         obs_kernel,
@@ -499,7 +500,7 @@
         forward_kernel, REGIONS, near_rows, gradient, far_rows, matrix, perturb, column_map
     )
     pieces = call(pick_kernel, (region,) * NY, (mine, swap_core(other)))
-    pieces = [pieces[0]] + [turn(pieces[i], NCORE * i, "member") for i in range(1, NY)]
+    pieces = [pieces[0]] + [across(pieces[i], i) for i in range(1, NY)]
     image, sent = call(
         curve_kernel,
         (region, ((BATCHES, 128), FLOAT)),

time: 93.8 us -> 91.2 us (0.972)
  starting transfers between devices: 24.4 us -> 20.6 us
  blocking collectives: 34.3 us -> 35.4 us
    ppermute x12, starting transfers between devices: 18.3 us -> 13 us  [the longest x6 7.41 us: across(): return lax.ppermute(values, 'member', pairs)]
    ppermute x3, starting transfers between devices: 6.11 us -> 7.55 us  [swap_core(): return lax.ppermute(values, 'member', [(i, i ^ 1) for i in range(NMEMBER)])]
  transfers between devices with their start and end apart: 15 -> 15, of which waited for: 11 -> 12; matrix products, arithmetic and copies ran while one was open for 0% -> 0% of each run, Pallas kernels for 1% -> 1%
where the time goes in v8:
time: 91.2 us; the launch traced here: 91 us
  blocking collectives  35.4 us (39%)
  starting transfers between devices  20.6 us (23%)
  waiting for transfers between devices  19.7 us (22%)
  Pallas kernels  12.6 us (14%)
  between operations  1.48 us (2%)
  local copies, waits for them, and re-layouts  1.25 us (1%)
    all_to_all x1, blocking collectives, shards(): lax.all_to_all(sent, ('member', 'tile'), split_axis=0, concat_axis=0, til...  21.1 us
    all_to_all x1, blocking collectives, shards(): data = lax.all_to_all(sent, 'tile', split_axis=0, concat_axis=0, tiled=True)  14.2 us
    pallas_call x10, Pallas kernels, call(): pl.pallas_call(kernel, out_shape=tuple((jax.ShapeDtypeStruct(shape, kind)...  12.6 us
    ppermute x3, starting transfers between devices, swap_core(): return lax.ppermute(values, 'member', [(i, i ^ 1) for i in range(NMEMBER)])  7.55 us
    ppermute x6, starting transfers between devices, across(): return lax.ppermute(values, 'member', pairs)  7.41 us
    ppermute x3, waiting for transfers between devices, swap_both(): first = lax.ppermute(first_values, ('member', 'tile'), ring())  7.27 us
    ppermute x6, waiting for transfers between devices, across(): return lax.ppermute(values, 'member', pairs)  7.09 us
    ppermute x3, starting transfers between devices, swap_both(): second = lax.ppermute(second_values, ('member', 'tile'), back)  5.2 us
  transfers between devices with their start and end apart: 15, of which 12 were waited for; matrix products, arithmetic and copies ran while one was open for 0% of the time, Pallas kernels for 1%

profile of v8, /device:TPU:1, one launch (start us, length us, event | category | flops | bytes accessed | tf_op | source)
XLA Modules:
  0.0 91.0 jit_solution(13226792385120639365)
XLA Ops:
  0.6 1.2 %copy.16 = f32[4,16,1280]{2,1,0:T(8,128)S(1)} copy(f32[4,16,1280]{2,0,1:T(4,128)} %bitcast.43) | data formatting | bytes 655360 | tf_op jit(solution)/shard_map/transpose | solution.py:463
  1.9 2.1 %collective-permute-start.1 = (bf16[64,1280]{1,0:T(8,128)(2,1)S(1)}, bf16[64,1280]{1,0:T(8,128)(2,1)S(1)}, u32[]{:S(2)}, u32[]{:S(2)}) collective-permute-start(bf16[64,1280]{1,0:T(8,128)(2,1)S(1)} %bitcast_convert_fusion), channel_id=1, source_target_pairs={{1,0},{2,1},{3,2},{4,3},{5,4},{6,5},{7,6},{8,7},{9,8},{10,9},{11,1... | collective-permute-start | bytes 491528 | tf_op jit(solution)/shard_map/ppermute | solution.py:65
  4.7 1.0 %shard_map.140 = f32[32,128]{1,0:T(8,128)S(1)} custom-call(f32[8,128]{1,0:T(8,128)} %bitcast.44, f32[8,128]{1,0:T(8,128)} %bitcast.45, f32[1]{0:T(128)S(6)} %copy.18.gain_ref), custom_call_target="tpu_custom_call" | custom-call | flops 20000000000 | bytes 156250000 | tf_op jit(solution)/shard_map/pallas_call | solution.py:99
  5.7 14.2 %all_to_all.22 = f32[16,2,128]{2,1,0:T(2,128)S(1)} all-to-all(f32[16,2,128]{2,1,0:T(2,128)S(1)} %bitcast.35), channel_id=1, replica_groups=mesh['member'=8,'tile'=16] {'tile'}, dimensions={0} | all-to-all | bytes 32768 | tf_op jit(solution)/shard_map/all_to_all | solution.py:476
  20.0 2.3 %shard_map.141 = (f32[4,16,384]{2,1,0:T(8,128)S(1)}, f32[4,16,384]{2,1,0:T(8,128)S(1)}) custom-call(bf16[64,1280]{1,0:T(8,128)(2,1)S(1)} %collective-permute-done.a_ref, f32[64,1280]{1,0:T(8,128)S(1)} %bitcast.29, bf16[64,1280]{1,0:T(8,128)(2,1)S(1)} %collective-permute-done.1.b_ref, bf16[256,192]{1,0:T(8,128)(2,1)S(1)} %copy-done.1, ...), custom_call_target="tpu_custom_call" | custom-call | flops 1000000000 | bytes 7812500 | tf_op jit(solution)/shard_map/pallas_call | solution.py:99
  22.3 4.4 %collective-permute-start.2 = (f32[4,16,384]{2,1,0:T(8,128)S(1)}, f32[4,16,384]{2,1,0:T(8,128)S(1)}, u32[]{:S(2)}, u32[]{:S(2)}) collective-permute-start(f32[4,16,384]{2,1,0:T(8,128)S(1)} %get-tuple-element.22), channel_id=1, source_target_pairs={{0,16},{16,0},{32,48},{48,32},{64,80},{80,64},{96,112},{112,96},{1... | collective-permute-start | bytes 294920 | tf_op jit(solution)/shard_map/ppermute | solution.py:75
  26.7 0.9 %collective-permute-done.2.b_ref = f32[4,16,384]{2,1,0:T(8,128)S(1)} collective-permute-done((f32[4,16,384]{2,1,0:T(8,128)S(1)}, f32[4,16,384]{2,1,0:T(8,128)S(1)}, u32[]{:S(2)}, u32[]{:S(2)}) %collective-permute-start.2) | collective-permute-done | bytes 98336 | tf_op jit(solution)/shard_map/ppermute | solution.py:75
  27.7 2.8 %collective-permute-start.5 = (f32[4,16,384]{2,1,0:T(8,128)S(1)}, f32[4,16,384]{2,1,0:T(8,128)S(1)}, u32[]{:S(2)}, u32[]{:S(2)}) collective-permute-start(f32[4,16,384]{2,1,0:T(8,128)S(1)} %shard_map.142.a_ref), channel_id=1, source_target_pairs={{0,96},{16,112},{32,64},{48,80},{64,32},{80,48},{96,0},{112,16},{1... | collective-permute-start | bytes 294920 | tf_op jit(solution)/shard_map/ppermute | solution.py:71
  31.2 3.3 %collective-permute-done.5.d_ref = f32[4,16,384]{2,1,0:T(8,128)S(1)} collective-permute-done((f32[4,16,384]{2,1,0:T(8,128)S(1)}, f32[4,16,384]{2,1,0:T(8,128)S(1)}, u32[]{:S(2)}, u32[]{:S(2)}) %collective-permute-start.5) | collective-permute-done | bytes 98336 | tf_op jit(solution)/shard_map/ppermute | solution.py:71
  34.5 1.0 %collective-permute-done.4.c_ref = f32[4,16,384]{2,1,0:T(8,128)S(1)} collective-permute-done((f32[4,16,384]{2,1,0:T(8,128)S(1)}, f32[4,16,384]{2,1,0:T(8,128)S(1)}, u32[]{:S(2)}, u32[]{:S(2)}) %collective-permute-start.4) | collective-permute-done | bytes 98336 | tf_op jit(solution)/shard_map/ppermute | solution.py:71
  35.8 2.4 %shard_map.143 = (f32[4,16,320]{2,1,0:T(8,128)S(1)}, f32[8,128]{1,0:T(8,128)S(1)}, f32[16,320]{1,0:T(8,128)S(1)}) custom-call(f32[4,16,384]{2,1,0:T(8,128)S(1)} %shard_map.142.a_ref, f32[4,16,384]{2,1,0:T(8,128)S(1)} %collective-permute-done.3.b_ref, f32[4,16,384]{2,1,0:T(8,128)S(1)} %collective-permute-done.4.c_ref, ...), custom_call_target="tpu_custom_call" | custom-call | flops 1000000000 | bytes 7812500 | tf_op jit(solution)/shard_map/pallas_call | solution.py:99
  38.2 2.6 %collective-permute-start.6 = (f32[4,16,320]{2,1,0:T(8,128)S(1)}, f32[4,16,320]{2,1,0:T(8,128)S(1)}, u32[]{:S(2)}, u32[]{:S(2)}) collective-permute-start(f32[4,16,320]{2,1,0:T(8,128)S(1)} %get-tuple-element.23.mine_ref), channel_id=1, source_target_pairs={{0,16},{16,0},{32,48},{48,32},{64,80},{80,64},{96,112},{112,96},{1... | collective-permute-start | bytes 245768 | tf_op jit(solution)/shard_map/ppermute | solution.py:75
  41.8 2.5 %shard_map.144 = (f32[96,1280]{1,0:T(8,128)S(1)}, bf16[64,1280]{1,0:T(8,128)(2,1)S(1)}, bf16[64,1280]{1,0:T(8,128)(2,1)S(1)}) custom-call(f32[4,16,320]{2,1,0:T(8,128)S(1)} %get-tuple-element.23.mine_ref, f32[4,16,320]{2,1,0:T(8,128)S(1)} %collective-permute-done.6.other_ref, bf16[96,512]{1,0:T(8,128)(2,1)S(1)} %copy-done.2, ...), custom_call_target="tpu_custom_call" | custom-call | flops 1000000000 | bytes 7812500 | tf_op jit(solution)/shard_map/pallas_call | solution.py:99
  44.8 1.1 %collective-permute-start.8 = (bf16[64,1280]{1,0:T(8,128)(2,1)S(1)}, bf16[64,1280]{1,0:T(8,128)(2,1)S(1)}, u32[]{:S(2)}, u32[]{:S(2)}) collective-permute-start(bf16[64,1280]{1,0:T(8,128)(2,1)S(1)} %get-tuple-element.26), channel_id=1, source_target_pairs={{1,0},{2,1},{3,2},{4,3},{5,4},{6,5},{7,6},{8,7},{9,8},{10,9},{11,1... | collective-permute-start | bytes 491528 | tf_op jit(solution)/shard_map/ppermute | solution.py:65
  45.9 3.4 %collective-permute-done.7.a_ref = bf16[64,1280]{1,0:T(8,128)(2,1)S(1)} collective-permute-done((bf16[64,1280]{1,0:T(8,128)(2,1)S(1)}, bf16[64,1280]{1,0:T(8,128)(2,1)S(1)}, u32[]{:S(2)}, u32[]{:S(2)}) %collective-permute-start.7) | collective-permute-done | bytes 163872 | tf_op jit(solution)/shard_map/ppermute | solution.py:63
  50.0 2.0 %collective-permute-start.10 = (bf16[64,1280]{1,0:T(8,128)(2,1)S(1)}, bf16[64,1280]{1,0:T(8,128)(2,1)S(1)}, u32[]{:S(2)}, u32[]{:S(2)}) collective-permute-start(bf16[64,1280]{1,0:T(8,128)(2,1)S(1)} %get-tuple-element.27), channel_id=1, source_target_pairs={{1,0},{2,1},{3,2},{4,3},{5,4},{6,5},{7,6},{8,7},{9,8},{10,9},{11,1... | collective-permute-start | bytes 491528 | tf_op jit(solution)/shard_map/ppermute | solution.py:65
  51.9 2.3 %collective-permute-done.10.b_ref = bf16[64,1280]{1,0:T(8,128)(2,1)S(1)} collective-permute-done((bf16[64,1280]{1,0:T(8,128)(2,1)S(1)}, bf16[64,1280]{1,0:T(8,128)(2,1)S(1)}, u32[]{:S(2)}, u32[]{:S(2)}) %collective-permute-start.10) | collective-permute-done | bytes 163872 | tf_op jit(solution)/shard_map/ppermute | solution.py:65
  54.2 3.9 %collective-permute-done.9.a_ref = bf16[64,1280]{1,0:T(8,128)(2,1)S(1)} collective-permute-done((bf16[64,1280]{1,0:T(8,128)(2,1)S(1)}, bf16[64,1280]{1,0:T(8,128)(2,1)S(1)}, u32[]{:S(2)}, u32[]{:S(2)}) %collective-permute-start.9) | collective-permute-done | bytes 163872 | tf_op jit(solution)/shard_map/ppermute | solution.py:63
  58.1 2.3 %shard_map.146 = (f32[4,16,320]{2,1,0:T(8,128)S(1)}, f32[4,16,320]{2,1,0:T(8,128)S(1)}) custom-call(bf16[64,1280]{1,0:T(8,128)(2,1)S(1)} %collective-permute-done.9.a_ref, f32[64,1280]{1,0:T(8,128)S(1)} %get-tuple-element.28.own_ref.grad_ref, bf16[64,1280]{1,0:T(8,128)(2,1)S(1)} %collective-permute-done.10.b_ref, bf16[256,192]{1,0:T(8,128)(2,1)S(1)} %copy-done.1, ...), custom_call_target="tpu_custom_call" | custom-call | flops 1000000000 | bytes 7812500 | tf_op jit(solution)/shard_map/pallas_call | solution.py:99
  62.0 2.5 %collective-permute-start.13 = (f32[16,320]{1,0:T(8,128)S(1)}, f32[16,320]{1,0:T(8,128)S(1)}, u32[]{:S(2)}, u32[]{:S(2)}) collective-permute-start(f32[16,320]{1,0:T(8,128)S(1)} %get-tuple-element.33), channel_id=1, source_target_pairs={{0,64},{16,80},{32,96},{48,112},{64,0},{80,16},{96,32},{112,48},{1... | collective-permute-start | bytes 61448 | tf_op jit(solution)/shard_map/ppermute | solution.py:71
  64.5 1.3 %collective-permute-start.14 = (f32[16,320]{1,0:T(8,128)S(1)}, f32[16,320]{1,0:T(8,128)S(1)}, u32[]{:S(2)}, u32[]{:S(2)}) collective-permute-start(f32[16,320]{1,0:T(8,128)S(1)} %get-tuple-element.34), channel_id=1, source_target_pairs={{0,96},{16,112},{32,64},{48,80},{64,32},{80,48},{96,0},{112,16},{1... | collective-permute-start | bytes 61448 | tf_op jit(solution)/shard_map/ppermute | solution.py:71
  66.3 2.1 %collective-permute-done.14.d_ref = f32[16,320]{1,0:T(8,128)S(1)} collective-permute-done((f32[16,320]{1,0:T(8,128)S(1)}, f32[16,320]{1,0:T(8,128)S(1)}, u32[]{:S(2)}, u32[]{:S(2)}) %collective-permute-start.14) | collective-permute-done | bytes 20512 | tf_op jit(solution)/shard_map/ppermute | solution.py:71
  68.9 21.1 %all_to_all.23 = f32[128,1,128]{2,1,0:T(1,128)S(1)} all-to-all(f32[128,1,128]{2,1,0:T(1,128)S(1)} %bitcast.34), channel_id=1, replica_groups=mesh['member'=8,'tile'=16] {'member','tile'}, dimensions={0} | all-to-all | bytes 131072 | tf_op jit(solution)/shard_map/all_to_all | solution.py:509
  90.1 1.0 %shard_map.149 = (f32[16,4,1280]{2,1,0:T(4,128)}, f32[16,320]{1,0:T(8,128)}) custom-call(f32[128,128]{1,0:T(8,128)S(1)} %bitcast.33, f32[64,1280]{1,0:T(8,128)S(1)} %bitcast.31, f32[64,1280]{1,0:T(8,128)S(1)} %get-tuple-element.28.own_ref.grad_ref, f32[16,320]{1,0:T(8,128)S(1)} %get-tuple-element.38.full_ref, f32[16,320]{1,0:T(8,128)S(1)} %copy-done.6, ...), custom_call_target="tpu_custom_call" | custom-call | flops 1000000000 | bytes 7812500 | tf_op jit(solution)/shard_map/pallas_call | solution.py:99
  (41 shorter events, 5.6 us)
Async XLA Ops:
  0.6 19.3 %slice-start = ((s8[6553600]{0:T(1024)(128)(4,1)}), s8[4194304]{0:T(1024)(128)(4,1)S(1)}, s32[]{:S(2)}) async-start(s8[6553600]{0:T(1024)(128)(4,1)} %bitcast.27), calls=%async_computation.2 | async-start | bytes 8388608
  1.9 18.1 %collective-permute-start.1 = (bf16[64,1280]{1,0:T(8,128)(2,1)S(1)}, bf16[64,1280]{1,0:T(8,128)(2,1)S(1)}, u32[]{:S(2)}, u32[]{:S(2)}) collective-permute-start(bf16[64,1280]{1,0:T(8,128)(2,1)S(1)} %bitcast_convert_fusion), channel_id=1, source_target_pairs={{1,0},{2,1},{3,2},{4,3},{5,4},{6,5},{7,6},{8,7},{9,8},{10,9},{11,1... | collective-permute-start | bytes 491528 | tf_op jit(solution)/shard_map/ppermute | solution.py:65
  4.0 16.0 %collective-permute-start = (bf16[64,1280]{1,0:T(8,128)(2,1)S(1)}, bf16[64,1280]{1,0:T(8,128)(2,1)S(1)}, u32[]{:S(2)}, u32[]{:S(2)}) collective-permute-start(bf16[64,1280]{1,0:T(8,128)(2,1)S(1)} %bitcast_convert_fusion), channel_id=1, source_target_pairs={{0,1},{1,2},{2,3},{3,4},{4,5},{5,6},{6,7},{7,8},{8,9},{9,10},{10,1... | collective-permute-start | bytes 491528 | tf_op jit(solution)/shard_map/ppermute | solution.py:63
  4.6 15.3 %slice-start.1 = ((s8[6553600]{0:T(1024)(128)(4,1)}), s8[2359296]{0:T(1024)(128)(4,1)S(1)}, s32[]{:S(2)}) async-start(s8[6553600]{0:T(1024)(128)(4,1)} %bitcast.27), calls=%async_computation.3 | async-start | bytes 4718592
  4.6 15.3 %copy-start = (bf16[16,16,2560]{2,1,0:T(8,128)(2,1)S(1)}, bf16[16,16,2560]{2,1,0:T(8,128)(2,1)}, u32[]{:S(2)}) copy-start(bf16[16,16,2560]{2,1,0:T(8,128)(2,1)} %perturb_ref.5) | copy-start | bytes 3932164
  5.7 22.0 %copy-start.6 = (f32[16,320]{1,0:T(8,128)S(1)}, f32[16,320]{1,0:T(8,128)}, u32[]{:S(2)}) copy-start(f32[16,320]{1,0:T(8,128)} %base_ref.3) | copy-start | bytes 61444
  5.7 30.1 %copy-start.3 = (s32[1,128,8,8]{1,3,2,0:T(8,128)S(1)}, s32[1,128,8,8]{1,3,2,0:T(8,128)}, u32[]{:S(2)}) copy-start(s32[1,128,8,8]{1,3,2,0:T(8,128)} %param.17) | copy-start | bytes 98308
  5.7 30.1 %copy-start.4 = (f32[1,128,8,8]{1,3,2,0:T(8,128)S(1)}, f32[1,128,8,8]{1,3,2,0:T(8,128)}, u32[]{:S(2)}) copy-start(f32[1,128,8,8]{1,3,2,0:T(8,128)} %param.18) | copy-start | bytes 98308
  5.7 30.1 %copy-start.5 = (f32[1,128,8,8]{1,3,2,0:T(8,128)S(1)}, f32[1,128,8,8]{1,3,2,0:T(8,128)}, u32[]{:S(2)}) copy-start(f32[1,128,8,8]{1,3,2,0:T(8,128)} %param.19) | copy-start | bytes 98308
  5.7 30.0 %copy-start.7 = (s32[1,128,8]{1,2,0:T(8,128)S(1)}, s32[1,128,8]{1,2,0:T(8,128)}, u32[]{:S(2)}) copy-start(s32[1,128,8]{1,2,0:T(8,128)} %param.20) | copy-start | bytes 12292
  20.0 21.8 %copy-start.2 = (bf16[96,512]{1,0:T(8,128)(2,1)S(1)}, bf16[96,512]{1,0:T(8,128)(2,1)}, u32[]{:S(2)}) copy-start(bf16[96,512]{1,0:T(8,128)(2,1)} %constant.5.clone.back_ref) | copy-start | bytes 294916
  22.3 5.4 %collective-permute-start.2 = (f32[4,16,384]{2,1,0:T(8,128)S(1)}, f32[4,16,384]{2,1,0:T(8,128)S(1)}, u32[]{:S(2)}, u32[]{:S(2)}) collective-permute-start(f32[4,16,384]{2,1,0:T(8,128)S(1)} %get-tuple-element.22), channel_id=1, source_target_pairs={{0,16},{16,0},{32,48},{48,32},{64,80},{80,64},{96,112},{112,96},{1... | collective-permute-start | bytes 294920 | tf_op jit(solution)/shard_map/ppermute | solution.py:75
  27.7 6.8 %collective-permute-start.5 = (f32[4,16,384]{2,1,0:T(8,128)S(1)}, f32[4,16,384]{2,1,0:T(8,128)S(1)}, u32[]{:S(2)}, u32[]{:S(2)}) collective-permute-start(f32[4,16,384]{2,1,0:T(8,128)S(1)} %shard_map.142.a_ref), channel_id=1, source_target_pairs={{0,96},{16,112},{32,64},{48,80},{64,32},{80,48},{96,0},{112,16},{1... | collective-permute-start | bytes 294920 | tf_op jit(solution)/shard_map/ppermute | solution.py:71
  30.5 5.0 %collective-permute-start.4 = (f32[4,16,384]{2,1,0:T(8,128)S(1)}, f32[4,16,384]{2,1,0:T(8,128)S(1)}, u32[]{:S(2)}, u32[]{:S(2)}) collective-permute-start(f32[4,16,384]{2,1,0:T(8,128)S(1)} %shard_map.142.a_ref), channel_id=1, source_target_pairs={{0,64},{16,80},{32,96},{48,112},{64,0},{80,16},{96,32},{112,48},{1... | collective-permute-start | bytes 294920 | tf_op jit(solution)/shard_map/ppermute | solution.py:71
  30.9 4.9 %collective-permute-start.3 = (f32[4,16,384]{2,1,0:T(8,128)S(1)}, f32[4,16,384]{2,1,0:T(8,128)S(1)}, u32[]{:S(2)}, u32[]{:S(2)}) collective-permute-start(f32[4,16,384]{2,1,0:T(8,128)S(1)} %shard_map.142.a_ref), channel_id=1, source_target_pairs={{0,32},{16,48},{32,0},{48,16},{64,96},{80,112},{96,64},{112,80},{1... | collective-permute-start | bytes 294920 | tf_op jit(solution)/shard_map/ppermute | solution.py:71
  38.2 3.6 %collective-permute-start.6 = (f32[4,16,320]{2,1,0:T(8,128)S(1)}, f32[4,16,320]{2,1,0:T(8,128)S(1)}, u32[]{:S(2)}, u32[]{:S(2)}) collective-permute-start(f32[4,16,320]{2,1,0:T(8,128)S(1)} %get-tuple-element.23.mine_ref), channel_id=1, source_target_pairs={{0,16},{16,0},{32,48},{48,32},{64,80},{80,64},{96,112},{112,96},{1... | collective-permute-start | bytes 245768 | tf_op jit(solution)/shard_map/ppermute | solution.py:75
  44.4 4.9 %collective-permute-start.7 = (bf16[64,1280]{1,0:T(8,128)(2,1)S(1)}, bf16[64,1280]{1,0:T(8,128)(2,1)S(1)}, u32[]{:S(2)}, u32[]{:S(2)}) collective-permute-start(bf16[64,1280]{1,0:T(8,128)(2,1)S(1)} %get-tuple-element.24), channel_id=1, source_target_pairs={{0,1},{1,2},{2,3},{3,4},{4,5},{5,6},{6,7},{7,8},{8,9},{9,10},{10,1... | collective-permute-start | bytes 491528 | tf_op jit(solution)/shard_map/ppermute | solution.py:63
  44.8 4.8 %collective-permute-start.8 = (bf16[64,1280]{1,0:T(8,128)(2,1)S(1)}, bf16[64,1280]{1,0:T(8,128)(2,1)S(1)}, u32[]{:S(2)}, u32[]{:S(2)}) collective-permute-start(bf16[64,1280]{1,0:T(8,128)(2,1)S(1)} %get-tuple-element.26), channel_id=1, source_target_pairs={{1,0},{2,1},{3,2},{4,3},{5,4},{6,5},{7,6},{8,7},{9,8},{10,9},{11,1... | collective-permute-start | bytes 491528 | tf_op jit(solution)/shard_map/ppermute | solution.py:65
  50.0 4.2 %collective-permute-start.10 = (bf16[64,1280]{1,0:T(8,128)(2,1)S(1)}, bf16[64,1280]{1,0:T(8,128)(2,1)S(1)}, u32[]{:S(2)}, u32[]{:S(2)}) collective-permute-start(bf16[64,1280]{1,0:T(8,128)(2,1)S(1)} %get-tuple-element.27), channel_id=1, source_target_pairs={{1,0},{2,1},{3,2},{4,3},{5,4},{6,5},{7,6},{8,7},{9,8},{10,9},{11,1... | collective-permute-start | bytes 491528 | tf_op jit(solution)/shard_map/ppermute | solution.py:65
  51.9 6.2 %collective-permute-start.9 = (bf16[64,1280]{1,0:T(8,128)(2,1)S(1)}, bf16[64,1280]{1,0:T(8,128)(2,1)S(1)}, u32[]{:S(2)}, u32[]{:S(2)}) collective-permute-start(bf16[64,1280]{1,0:T(8,128)(2,1)S(1)} %get-tuple-element.27), channel_id=1, source_target_pairs={{0,1},{1,2},{2,3},{3,4},{4,5},{5,6},{6,7},{7,8},{8,9},{9,10},{10,1... | collective-permute-start | bytes 491528 | tf_op jit(solution)/shard_map/ppermute | solution.py:63
  60.4 1.5 %collective-permute-start.11 = (f32[4,16,320]{2,1,0:T(8,128)S(1)}, f32[4,16,320]{2,1,0:T(8,128)S(1)}, u32[]{:S(2)}, u32[]{:S(2)}) collective-permute-start(f32[4,16,320]{2,1,0:T(8,128)S(1)} %get-tuple-element.30), channel_id=1, source_target_pairs={{0,16},{16,0},{32,48},{48,32},{64,80},{80,64},{96,112},{112,96},{1... | collective-permute-start | bytes 245768 | tf_op jit(solution)/shard_map/ppermute | solution.py:75
  61.9 3.9 %collective-permute-start.12 = (f32[16,320]{1,0:T(8,128)S(1)}, f32[16,320]{1,0:T(8,128)S(1)}, u32[]{:S(2)}, u32[]{:S(2)}) collective-permute-start(f32[16,320]{1,0:T(8,128)S(1)} %get-tuple-element.32), channel_id=1, source_target_pairs={{0,32},{16,48},{32,0},{48,16},{64,96},{80,112},{96,64},{112,80},{1... | collective-permute-start | bytes 61448 | tf_op jit(solution)/shard_map/ppermute | solution.py:71
  62.0 4.3 %collective-permute-start.13 = (f32[16,320]{1,0:T(8,128)S(1)}, f32[16,320]{1,0:T(8,128)S(1)}, u32[]{:S(2)}, u32[]{:S(2)}) collective-permute-start(f32[16,320]{1,0:T(8,128)S(1)} %get-tuple-element.33), channel_id=1, source_target_pairs={{0,64},{16,80},{32,96},{48,112},{64,0},{80,16},{96,32},{112,48},{1... | collective-permute-start | bytes 61448 | tf_op jit(solution)/shard_map/ppermute | solution.py:71
  64.5 3.9 %collective-permute-start.14 = (f32[16,320]{1,0:T(8,128)S(1)}, f32[16,320]{1,0:T(8,128)S(1)}, u32[]{:S(2)}, u32[]{:S(2)}) collective-permute-start(f32[16,320]{1,0:T(8,128)S(1)} %get-tuple-element.34), channel_id=1, source_target_pairs={{0,96},{16,112},{32,64},{48,80},{64,32},{80,48},{96,0},{112,16},{1... | collective-permute-start | bytes 61448 | tf_op jit(solution)/shard_map/ppermute | solution.py:71
  (1 other events, 15.3 us)

commit v9 on v8

--- a/solution.py
+++ b/solution.py
@@ -284,15 +284,23 @@
     )
 
 
-def send_kernel(value_hbm, error_hbm, gain_ref, sent_ref, value_ref, error_ref, sem):
+def start_kernel(
+    value_hbm, error_hbm, gain_ref, weights_hbm,
+    sent_ref, own_ref, half_ref, value_ref, error_ref, weights_ref, sem,
+):
     copies = [
         pltpu.make_async_copy(value_hbm, value_ref, sem.at[0]),
         pltpu.make_async_copy(error_hbm, error_ref, sem.at[1]),
+        pltpu.make_async_copy(weights_hbm, weights_ref, sem.at[2]),
     ]
     for copy in copies:
         copy.start()
     for copy in copies:
         copy.wait()
+    for r in range(ROWS):
+        values = weights_ref[:, r, :]
+        own_ref[row_slice(r)] = values
+        half_ref[row_slice(r)] = values.astype(HALF)
     rows = []
     for group in range(NMEMBER):
         for ref in (value_ref, error_ref):
@@ -349,24 +357,34 @@
     return jnp.concatenate([high, (values - high.astype(FLOAT)).astype(HALF)], axis=0)
 
 
-def interpolated(field, picks, factors, fraction):
+def located(index):
+    row = index // WIDTH
+    return row, index - row * WIDTH
+
+
+def prepare_kernel(index_ref, row_ref, column_ref, picks_ref, both_ref):
+    _, core_pos, _ = place()
+    for y in range(NY):
+        group = NCORE * y + core_pos
+        row, column = located(index_ref[group])
+        picks_ref[y] = column_picks(column)
+        factors = row_factors(row, row_ref[group])
+        fraction = on_lanes(column_ref[group])
+        both_ref[y, :FINE_ROWS] = factors * (1.0 - fraction)
+        both_ref[y, FINE_ROWS:] = factors * fraction
+
+
+def interpolated(field, picks, both):
     shifted = jnp.concatenate([field[:, 1:], field[:, :1]], axis=1)
     got = jnp.dot(
         halves(jnp.concatenate([field, shifted], axis=0)), picks, preferred_element_type=FLOAT
     )
-    got = got[: 2 * FINE_ROWS] + got[2 * FINE_ROWS :]
-    left, right = got[:FINE_ROWS], got[FINE_ROWS:]
-    mixed = left * (1.0 - fraction) + right * fraction
-    return on_slots(jnp.sum(mixed * factors, axis=0, keepdims=True))
-
-
-def located(index):
-    row = index // WIDTH
-    return row, index - row * WIDTH
+    got = (got[: 2 * FINE_ROWS] + got[2 * FINE_ROWS :]) * both
+    return on_slots(jnp.sum(got, axis=0, keepdims=True))
 
 
 def obs_kernel(
-    a_ref, b_ref, c_ref, d_ref, index_ref, row_ref, column_ref, length_ref,
+    a_ref, b_ref, c_ref, d_ref, picks_ref, both_ref, length_ref,
     spread_ref, weight_ref, full_ref, data_ref,
 ):
     _, core_pos, y_pos = place()
@@ -385,12 +403,9 @@
         value, error = data[:SLOTS], data[SLOTS : 2 * SLOTS]
         gain = data[2 * SLOTS : 2 * SLOTS + 1]
         group = NCORE * y + core_pos
-        row, column = located(index_ref[group])
-        picks = column_picks(column)
-        factors = row_factors(row, row_ref[group])
-        fraction = on_lanes(column_ref[group])
+        picks, both = picks_ref[y], both_ref[y]
         live = jnp.where(slots < length_ref[pl.ds(group, 1)], 1.0, 0.0)
-        state = interpolated(field, picks, factors, fraction)
+        state = interpolated(field, picks, both)
         bounded = jnp.tanh(state)
         derivative = 1.0 + gain * (1.0 - bounded * bounded)
         misfit = state + gain * bounded - value
@@ -402,10 +417,8 @@
             weight_ref[...] = derivative * derivative * precision
             full_ref[...] = field
 
-        weighted = factors * on_lanes(residual)
-        both = jnp.concatenate([weighted * (1.0 - fraction), weighted * fraction], axis=0)
         got = lax.dot_general(
-            halves(both), picks, (((1,), (1,)), ((), ())), preferred_element_type=FLOAT
+            halves(both * on_lanes(residual)), picks, (((1,), (1,)), ((), ())), preferred_element_type=FLOAT
         )
         got = got[: 2 * FINE_ROWS] + got[2 * FINE_ROWS :]
         left, right = got[:FINE_ROWS], got[FINE_ROWS:]
@@ -413,17 +426,12 @@
 
 
 def curve_kernel(
-    a_ref, b_ref, c_ref, d_ref, index_ref, row_ref, column_ref, weight_ref, square_ref,
-    field_ref, sent_ref,
-):
-    _, core_pos, y_pos = place()
-    own = NCORE * y_pos + core_pos
+    a_ref, b_ref, c_ref, d_ref, picks_ref, both_ref, weight_ref, square_ref, field_ref, sent_ref
+):
+    _, _, y_pos = place()
     field = a_ref[...] + b_ref[...] + c_ref[...] + d_ref[...]
     field_ref[...] = field
-    row, column = located(index_ref[own])
-    observed = interpolated(
-        field, column_picks(column), row_factors(row, row_ref[own]), on_lanes(column_ref[own])
-    )
+    observed = interpolated(field, picks_ref[y_pos], both_ref[y_pos])
     curvature = jnp.sum(weight_ref[...] * observed * observed, keepdims=True)
     square = jnp.sum(square_ref[...], keepdims=True)
     lanes = lax.broadcasted_iota(jnp.int32, (BATCHES, 128), 1)
@@ -460,19 +468,18 @@
     matrix = member_matrix()
     matrix = near(jnp.asarray(np.concatenate([matrix, matrix], axis=1), HALF))
     flat = (ROWS * MEMBERS_HERE, COARSE_COLS)
-    own = jnp.transpose(weights, (1, 0, 2)).reshape(flat)
-    half = own.astype(HALF)
-    near_rows, far_rows = swap_both(half, half)
-
-    (sent,) = call(
-        send_kernel,
-        (((2 * NTILE, 128), FLOAT),),
-        (obs_value[0].T, obs_error[0].T, instrument_gain),
-        far=(0, 1),
+    sent, own, half = call(
+        start_kernel,
+        (((2 * NTILE, 128), FLOAT), (flat, FLOAT), (flat, HALF)),
+        (obs_value[0].T, obs_error[0].T, instrument_gain, weights),
+        far=(0, 1, 3),
         scalar=(2,),
         work=WORK,
-        scratch=[pltpu.VMEM((SLOTS, BATCHES), FLOAT)] * 2 + [pltpu.SemaphoreType.DMA((2,))],
-    )
+        scratch=[pltpu.VMEM((SLOTS, BATCHES), FLOAT)] * 2
+        + [pltpu.VMEM((MEMBERS_HERE, ROWS, COARSE_COLS), FLOAT), pltpu.SemaphoreType.DMA((3,))],
+    )
+    near_rows, far_rows = swap_both(half, half)
+
     data = lax.all_to_all(sent, "tile", split_axis=0, concat_axis=0, tiled=True)
 
     index = jnp.transpose(stencil_index[0], (1, 2, 0))
@@ -484,12 +491,22 @@
         laden_kernel, LADEN, near_rows, own, far_rows, matrix, perturb, column_map, data
     )
     (mine,) = call(add_kernel, (LADEN,), (mine, swap_core(other), background))
-    pieces = [mine] + [across(mine, i) for i in range(1, NY)]
+    pieces = [mine]
+    for i in range(1, NY):
+        pieces.append(across(mine, i))
+    picks, both = call(
+        prepare_kernel,
+        (
+            ((NY, WIDTH, SLOTS * BATCHES), HALF),
+            ((NY, 2 * FINE_ROWS, SLOTS * BATCHES), FLOAT),
+        ),
+        (index, row_frac, column_frac),
+    )
     region = ((FINE_ROWS, WIDTH), FLOAT)
     spread, weight, full = call(
         obs_kernel,
         (REGIONS, ((SLOTS, BATCHES), FLOAT), region),
-        (*pieces, index, row_frac, column_frac, lengths),
+        (*pieces, picks, both, lengths),
         scratch=[pltpu.VMEM((NY, BATCHES, 128), FLOAT)],
     )
     part, up, down = partial_adjoint(spread, swap_core(spread), perturb, column_map)
@@ -504,7 +521,7 @@
     image, sent = call(
         curve_kernel,
         (region, ((BATCHES, 128), FLOAT)),
-        (*pieces, index, row_frac, column_frac, weight, square),
+        (*pieces, picks, both, weight, square),
     )
     shared = lax.all_to_all(sent, ("member", "tile"), split_axis=0, concat_axis=0, tiled=True)
     return call(

time: 91.2 us -> 90.2 us (0.989)
  local copies, waits for them, and re-layouts: 1.25 us -> 0.06 us
  Pallas kernels: 12.6 us -> 13.7 us
    transpose x1 -> x0, local copies, waits for them, and re-layouts: 1.19 us -> none  [shards(): own = jnp.transpose(weights, (1, 0, 2)).reshape(flat)]
    pallas_call x10 -> x11, Pallas kernels: 12.6 us -> 13.7 us  [call(): pl.pallas_call(kernel, out_shape=tuple((jax.ShapeDtypeStruct(shape, kind)...]
where the time goes in v9:
time: 90.2 us; the launch traced here: 90 us
  blocking collectives  35.2 us (39%)
  starting transfers between devices  20.6 us (23%)
  waiting for transfers between devices  19 us (21%)
  Pallas kernels  13.7 us (15%)
  between operations  1.46 us (2%)
    all_to_all x1, blocking collectives, shards(): lax.all_to_all(sent, ('member', 'tile'), split_axis=0, concat_axis=0, til...  21.1 us
    all_to_all x1, blocking collectives, shards(): data = lax.all_to_all(sent, 'tile', split_axis=0, concat_axis=0, tiled=True)  14.1 us
    pallas_call x11, Pallas kernels, call(): pl.pallas_call(kernel, out_shape=tuple((jax.ShapeDtypeStruct(shape, kind)...  13.7 us
    ppermute x3, starting transfers between devices, swap_core(): return lax.ppermute(values, 'member', [(i, i ^ 1) for i in range(NMEMBER)])  7.56 us
    ppermute x6, starting transfers between devices, across(): return lax.ppermute(values, 'member', pairs)  7.41 us
    ppermute x3, waiting for transfers between devices, swap_both(): first = lax.ppermute(first_values, ('member', 'tile'), ring())  7.28 us
    ppermute x6, waiting for transfers between devices, across(): return lax.ppermute(values, 'member', pairs)  6.38 us
    ppermute x3, starting transfers between devices, swap_both(): second = lax.ppermute(second_values, ('member', 'tile'), back)  5.2 us
  transfers between devices with their start and end apart: 15, of which 12 were waited for; matrix products, arithmetic and copies ran while one was open for 0% of the time, Pallas kernels for 1%

profile of v9, /device:TPU:1, one launch (start us, length us, event | category | flops | bytes accessed | tf_op | source)
XLA Modules:
  0.0 90.0 jit_solution(6001155617980075564)
XLA Ops:
  1.3 1.7 %shard_map.140 = (f32[32,128]{1,0:T(8,128)S(1)}, f32[64,1280]{1,0:T(8,128)S(1)}, bf16[64,1280]{1,0:T(8,128)(2,1)S(1)}) custom-call(f32[8,128]{1,0:T(8,128)} %bitcast.34, f32[8,128]{1,0:T(8,128)} %bitcast.35, f32[1]{0:T(128)S(6)} %copy.16.gain_ref, f32[16,4,1280]{2,1,0:T(4,128)} %weights_hbm.1), custom_call_target="tpu_custom_call" | custom-call | flops 20000000000 | bytes 156250000 | tf_op jit(solution)/shard_map/pallas_call | solution.py:99
  3.0 2.1 %collective-permute-start.1 = (bf16[64,1280]{1,0:T(8,128)(2,1)S(1)}, bf16[64,1280]{1,0:T(8,128)(2,1)S(1)}, u32[]{:S(2)}, u32[]{:S(2)}) collective-permute-start(bf16[64,1280]{1,0:T(8,128)(2,1)S(1)} %get-tuple-element.26), channel_id=1, source_target_pairs={{1,0},{2,1},{3,2},{4,3},{5,4},{6,5},{7,6},{8,7},{9,8},{10,9},{11,1... | collective-permute-start | bytes 491528 | tf_op jit(solution)/shard_map/ppermute | solution.py:65
  5.1 14.1 %all_to_all.22 = f32[16,2,128]{2,1,0:T(2,128)S(1)} all-to-all(f32[16,2,128]{2,1,0:T(2,128)S(1)} %bitcast.29), channel_id=1, replica_groups=mesh['member'=8,'tile'=16] {'tile'}, dimensions={0} | all-to-all | bytes 32768 | tf_op jit(solution)/shard_map/all_to_all | solution.py:483
  19.3 2.3 %shard_map.141 = (f32[4,16,384]{2,1,0:T(8,128)S(1)}, f32[4,16,384]{2,1,0:T(8,128)S(1)}) custom-call(bf16[64,1280]{1,0:T(8,128)(2,1)S(1)} %collective-permute-done.a_ref, f32[64,1280]{1,0:T(8,128)S(1)} %get-tuple-element.27.own_ref, bf16[64,1280]{1,0:T(8,128)(2,1)S(1)} %collective-permute-done.1.b_ref, bf16[256,192]{1,0:T(8,128)(2,1)S(1)} %copy-done.1, ...), custom_call_target="tpu_custom_call" | custom-call | flops 1000000000 | bytes 7812500 | tf_op jit(solution)/shard_map/pallas_call | solution.py:99
  21.6 4.4 %collective-permute-start.2 = (f32[4,16,384]{2,1,0:T(8,128)S(1)}, f32[4,16,384]{2,1,0:T(8,128)S(1)}, u32[]{:S(2)}, u32[]{:S(2)}) collective-permute-start(f32[4,16,384]{2,1,0:T(8,128)S(1)} %get-tuple-element.30), channel_id=1, source_target_pairs={{0,16},{16,0},{32,48},{48,32},{64,80},{80,64},{96,112},{112,96},{1... | collective-permute-start | bytes 294920 | tf_op jit(solution)/shard_map/ppermute | solution.py:75
  26.0 0.9 %collective-permute-done.2.b_ref = f32[4,16,384]{2,1,0:T(8,128)S(1)} collective-permute-done((f32[4,16,384]{2,1,0:T(8,128)S(1)}, f32[4,16,384]{2,1,0:T(8,128)S(1)}, u32[]{:S(2)}, u32[]{:S(2)}) %collective-permute-start.2) | collective-permute-done | bytes 98336 | tf_op jit(solution)/shard_map/ppermute | solution.py:75
  27.0 2.8 %collective-permute-start.5 = (f32[4,16,384]{2,1,0:T(8,128)S(1)}, f32[4,16,384]{2,1,0:T(8,128)S(1)}, u32[]{:S(2)}, u32[]{:S(2)}) collective-permute-start(f32[4,16,384]{2,1,0:T(8,128)S(1)} %shard_map.142.a_ref), channel_id=1, source_target_pairs={{0,96},{16,112},{32,64},{48,80},{64,32},{80,48},{96,0},{112,16},{1... | collective-permute-start | bytes 294920 | tf_op jit(solution)/shard_map/ppermute | solution.py:71
  31.2 2.6 %collective-permute-done.5.d_ref = f32[4,16,384]{2,1,0:T(8,128)S(1)} collective-permute-done((f32[4,16,384]{2,1,0:T(8,128)S(1)}, f32[4,16,384]{2,1,0:T(8,128)S(1)}, u32[]{:S(2)}, u32[]{:S(2)}) %collective-permute-start.5) | collective-permute-done | bytes 98336 | tf_op jit(solution)/shard_map/ppermute | solution.py:71
  33.8 1.0 %collective-permute-done.4.c_ref = f32[4,16,384]{2,1,0:T(8,128)S(1)} collective-permute-done((f32[4,16,384]{2,1,0:T(8,128)S(1)}, f32[4,16,384]{2,1,0:T(8,128)S(1)}, u32[]{:S(2)}, u32[]{:S(2)}) %collective-permute-start.4) | collective-permute-done | bytes 98336 | tf_op jit(solution)/shard_map/ppermute | solution.py:71
  35.1 2.3 %shard_map.144 = (f32[4,16,320]{2,1,0:T(8,128)S(1)}, f32[8,128]{1,0:T(8,128)S(1)}, f32[16,320]{1,0:T(8,128)S(1)}) custom-call(f32[4,16,384]{2,1,0:T(8,128)S(1)} %shard_map.142.a_ref, f32[4,16,384]{2,1,0:T(8,128)S(1)} %collective-permute-done.3.b_ref, f32[4,16,384]{2,1,0:T(8,128)S(1)} %collective-permute-done.4.c_ref, ...), custom_call_target="tpu_custom_call" | custom-call | flops 1000000000 | bytes 7812500 | tf_op jit(solution)/shard_map/pallas_call | solution.py:99
  37.4 2.6 %collective-permute-start.6 = (f32[4,16,320]{2,1,0:T(8,128)S(1)}, f32[4,16,320]{2,1,0:T(8,128)S(1)}, u32[]{:S(2)}, u32[]{:S(2)}) collective-permute-start(f32[4,16,320]{2,1,0:T(8,128)S(1)} %get-tuple-element.33.mine_ref), channel_id=1, source_target_pairs={{0,16},{16,0},{32,48},{48,32},{64,80},{80,64},{96,112},{112,96},{1... | collective-permute-start | bytes 245768 | tf_op jit(solution)/shard_map/ppermute | solution.py:75
  40.0 0.9 %collective-permute-done.6.other_ref = f32[4,16,320]{2,1,0:T(8,128)S(1)} collective-permute-done((f32[4,16,320]{2,1,0:T(8,128)S(1)}, f32[4,16,320]{2,1,0:T(8,128)S(1)}, u32[]{:S(2)}, u32[]{:S(2)}) %collective-permute-start.6) | collective-permute-done | bytes 81952 | tf_op jit(solution)/shard_map/ppermute | solution.py:75
  41.0 2.5 %shard_map.145 = (f32[96,1280]{1,0:T(8,128)S(1)}, bf16[64,1280]{1,0:T(8,128)(2,1)S(1)}, bf16[64,1280]{1,0:T(8,128)(2,1)S(1)}) custom-call(f32[4,16,320]{2,1,0:T(8,128)S(1)} %get-tuple-element.33.mine_ref, f32[4,16,320]{2,1,0:T(8,128)S(1)} %collective-permute-done.6.other_ref, bf16[96,512]{1,0:T(8,128)(2,1)S(1)} %copy-done.2, ...), custom_call_target="tpu_custom_call" | custom-call | flops 1000000000 | bytes 7812500 | tf_op jit(solution)/shard_map/pallas_call | solution.py:99
  43.9 1.1 %collective-permute-start.8 = (bf16[64,1280]{1,0:T(8,128)(2,1)S(1)}, bf16[64,1280]{1,0:T(8,128)(2,1)S(1)}, u32[]{:S(2)}, u32[]{:S(2)}) collective-permute-start(bf16[64,1280]{1,0:T(8,128)(2,1)S(1)} %get-tuple-element.36), channel_id=1, source_target_pairs={{1,0},{2,1},{3,2},{4,3},{5,4},{6,5},{7,6},{8,7},{9,8},{10,9},{11,1... | collective-permute-start | bytes 491528 | tf_op jit(solution)/shard_map/ppermute | solution.py:65
  45.0 3.4 %collective-permute-done.7.a_ref = bf16[64,1280]{1,0:T(8,128)(2,1)S(1)} collective-permute-done((bf16[64,1280]{1,0:T(8,128)(2,1)S(1)}, bf16[64,1280]{1,0:T(8,128)(2,1)S(1)}, u32[]{:S(2)}, u32[]{:S(2)}) %collective-permute-start.7) | collective-permute-done | bytes 163872 | tf_op jit(solution)/shard_map/ppermute | solution.py:63
  49.1 2.0 %collective-permute-start.10 = (bf16[64,1280]{1,0:T(8,128)(2,1)S(1)}, bf16[64,1280]{1,0:T(8,128)(2,1)S(1)}, u32[]{:S(2)}, u32[]{:S(2)}) collective-permute-start(bf16[64,1280]{1,0:T(8,128)(2,1)S(1)} %get-tuple-element.37), channel_id=1, source_target_pairs={{1,0},{2,1},{3,2},{4,3},{5,4},{6,5},{7,6},{8,7},{9,8},{10,9},{11,1... | collective-permute-start | bytes 491528 | tf_op jit(solution)/shard_map/ppermute | solution.py:65
  51.1 2.3 %collective-permute-done.10.b_ref = bf16[64,1280]{1,0:T(8,128)(2,1)S(1)} collective-permute-done((bf16[64,1280]{1,0:T(8,128)(2,1)S(1)}, bf16[64,1280]{1,0:T(8,128)(2,1)S(1)}, u32[]{:S(2)}, u32[]{:S(2)}) %collective-permute-start.10) | collective-permute-done | bytes 163872 | tf_op jit(solution)/shard_map/ppermute | solution.py:65
  53.3 3.9 %collective-permute-done.9.a_ref = bf16[64,1280]{1,0:T(8,128)(2,1)S(1)} collective-permute-done((bf16[64,1280]{1,0:T(8,128)(2,1)S(1)}, bf16[64,1280]{1,0:T(8,128)(2,1)S(1)}, u32[]{:S(2)}, u32[]{:S(2)}) %collective-permute-start.9) | collective-permute-done | bytes 163872 | tf_op jit(solution)/shard_map/ppermute | solution.py:63
  57.2 2.3 %shard_map.147 = (f32[4,16,320]{2,1,0:T(8,128)S(1)}, f32[4,16,320]{2,1,0:T(8,128)S(1)}) custom-call(bf16[64,1280]{1,0:T(8,128)(2,1)S(1)} %collective-permute-done.9.a_ref, f32[64,1280]{1,0:T(8,128)S(1)} %get-tuple-element.38.own_ref.grad_ref, bf16[64,1280]{1,0:T(8,128)(2,1)S(1)} %collective-permute-done.10.b_ref, bf16[256,192]{1,0:T(8,128)(2,1)S(1)} %copy-done.1, ...), custom_call_target="tpu_custom_call" | custom-call | flops 1000000000 | bytes 7812500 | tf_op jit(solution)/shard_map/pallas_call | solution.py:99
  61.1 2.5 %collective-permute-start.13 = (f32[16,320]{1,0:T(8,128)S(1)}, f32[16,320]{1,0:T(8,128)S(1)}, u32[]{:S(2)}, u32[]{:S(2)}) collective-permute-start(f32[16,320]{1,0:T(8,128)S(1)} %get-tuple-element.43), channel_id=1, source_target_pairs={{0,64},{16,80},{32,96},{48,112},{64,0},{80,16},{96,32},{112,48},{1... | collective-permute-start | bytes 61448 | tf_op jit(solution)/shard_map/ppermute | solution.py:71
  63.6 1.3 %collective-permute-start.14 = (f32[16,320]{1,0:T(8,128)S(1)}, f32[16,320]{1,0:T(8,128)S(1)}, u32[]{:S(2)}, u32[]{:S(2)}) collective-permute-start(f32[16,320]{1,0:T(8,128)S(1)} %get-tuple-element.44), channel_id=1, source_target_pairs={{0,96},{16,112},{32,64},{48,80},{64,32},{80,48},{96,0},{112,16},{1... | collective-permute-start | bytes 61448 | tf_op jit(solution)/shard_map/ppermute | solution.py:71
  65.4 2.1 %collective-permute-done.14.d_ref = f32[16,320]{1,0:T(8,128)S(1)} collective-permute-done((f32[16,320]{1,0:T(8,128)S(1)}, f32[16,320]{1,0:T(8,128)S(1)}, u32[]{:S(2)}, u32[]{:S(2)}) %collective-permute-start.14) | collective-permute-done | bytes 20512 | tf_op jit(solution)/shard_map/ppermute | solution.py:71
  67.9 21.1 %all_to_all.23 = f32[128,1,128]{2,1,0:T(1,128)S(1)} all-to-all(f32[128,1,128]{2,1,0:T(1,128)S(1)} %bitcast.27), channel_id=1, replica_groups=mesh['member'=8,'tile'=16] {'member','tile'}, dimensions={0} | all-to-all | bytes 131072 | tf_op jit(solution)/shard_map/all_to_all | solution.py:526
  89.1 1.0 %shard_map.150 = (f32[16,4,1280]{2,1,0:T(4,128)}, f32[16,320]{1,0:T(8,128)}) custom-call(f32[128,128]{1,0:T(8,128)S(1)} %bitcast.28, f32[64,1280]{1,0:T(8,128)S(1)} %get-tuple-element.27.own_ref, f32[64,1280]{1,0:T(8,128)S(1)} %get-tuple-element.38.own_ref.grad_ref, f32[16,320]{1,0:T(8,128)S(1)} %get-tuple-element.48.full_ref, f32[16,320]{1,0:T(8,128)S(1)} %copy-done.6, ...), custom_call_target="tpu_custom_call" | custom-call | flops 1000000000 | bytes 7812500 | tf_op jit(solution)/shard_map/pallas_call | solution.py:99
  (40 shorter events, 5.2 us)
Async XLA Ops:
  1.3 18.0 %slice-start = ((s8[6553600]{0:T(1024)(128)(4,1)}), s8[4194304]{0:T(1024)(128)(4,1)S(1)}, s32[]{:S(2)}) async-start(s8[6553600]{0:T(1024)(128)(4,1)} %bitcast.24), calls=%async_computation.2 | async-start | bytes 8388608
  1.3 18.0 %slice-start.1 = ((s8[6553600]{0:T(1024)(128)(4,1)}), s8[2359296]{0:T(1024)(128)(4,1)S(1)}, s32[]{:S(2)}) async-start(s8[6553600]{0:T(1024)(128)(4,1)} %bitcast.24), calls=%async_computation.3 | async-start | bytes 4718592
  1.3 18.0 %copy-start = (bf16[16,16,2560]{2,1,0:T(8,128)(2,1)S(1)}, bf16[16,16,2560]{2,1,0:T(8,128)(2,1)}, u32[]{:S(2)}) copy-start(bf16[16,16,2560]{2,1,0:T(8,128)(2,1)} %perturb_ref.5) | copy-start | bytes 3932164
  1.3 18.0 %copy-start.1 = (bf16[256,192]{1,0:T(8,128)(2,1)S(1)}, bf16[256,192]{1,0:T(8,128)(2,1)}, u32[]{:S(2)}) copy-start(bf16[256,192]{1,0:T(8,128)(2,1)} %constant.4.clone.refine_ref) | copy-start | bytes 294916
  3.0 16.2 %collective-permute-start.1 = (bf16[64,1280]{1,0:T(8,128)(2,1)S(1)}, bf16[64,1280]{1,0:T(8,128)(2,1)S(1)}, u32[]{:S(2)}, u32[]{:S(2)}) collective-permute-start(bf16[64,1280]{1,0:T(8,128)(2,1)S(1)} %get-tuple-element.26), channel_id=1, source_target_pairs={{1,0},{2,1},{3,2},{4,3},{5,4},{6,5},{7,6},{8,7},{9,8},{10,9},{11,1... | collective-permute-start | bytes 491528 | tf_op jit(solution)/shard_map/ppermute | solution.py:65
  5.1 14.1 %collective-permute-start = (bf16[64,1280]{1,0:T(8,128)(2,1)S(1)}, bf16[64,1280]{1,0:T(8,128)(2,1)S(1)}, u32[]{:S(2)}, u32[]{:S(2)}) collective-permute-start(bf16[64,1280]{1,0:T(8,128)(2,1)S(1)} %get-tuple-element.26), channel_id=1, source_target_pairs={{0,1},{1,2},{2,3},{3,4},{4,5},{5,6},{6,7},{7,8},{8,9},{9,10},{10,1... | collective-permute-start | bytes 491528 | tf_op jit(solution)/shard_map/ppermute | solution.py:63
  21.6 8.9 %copy-start.3 = (s32[1,128,8,8]{1,3,2,0:T(8,128)S(1)}, s32[1,128,8,8]{1,3,2,0:T(8,128)}, u32[]{:S(2)}) copy-start(s32[1,128,8,8]{1,3,2,0:T(8,128)} %param.17) | copy-start | bytes 98308
  21.6 8.9 %copy-start.4 = (f32[1,128,8,8]{1,3,2,0:T(8,128)S(1)}, f32[1,128,8,8]{1,3,2,0:T(8,128)}, u32[]{:S(2)}) copy-start(f32[1,128,8,8]{1,3,2,0:T(8,128)} %param.18) | copy-start | bytes 98308
  21.6 8.9 %copy-start.5 = (f32[1,128,8,8]{1,3,2,0:T(8,128)S(1)}, f32[1,128,8,8]{1,3,2,0:T(8,128)}, u32[]{:S(2)}) copy-start(f32[1,128,8,8]{1,3,2,0:T(8,128)} %param.19) | copy-start | bytes 98308
  21.6 5.4 %collective-permute-start.2 = (f32[4,16,384]{2,1,0:T(8,128)S(1)}, f32[4,16,384]{2,1,0:T(8,128)S(1)}, u32[]{:S(2)}, u32[]{:S(2)}) collective-permute-start(f32[4,16,384]{2,1,0:T(8,128)S(1)} %get-tuple-element.30), channel_id=1, source_target_pairs={{0,16},{16,0},{32,48},{48,32},{64,80},{80,64},{96,112},{112,96},{1... | collective-permute-start | bytes 294920 | tf_op jit(solution)/shard_map/ppermute | solution.py:75
  27.0 8.1 %copy-start.7 = (s32[1,128,8]{1,2,0:T(8,128)S(1)}, s32[1,128,8]{1,2,0:T(8,128)}, u32[]{:S(2)}) copy-start(s32[1,128,8]{1,2,0:T(8,128)} %param.20) | copy-start | bytes 12292
  27.0 6.8 %collective-permute-start.5 = (f32[4,16,384]{2,1,0:T(8,128)S(1)}, f32[4,16,384]{2,1,0:T(8,128)S(1)}, u32[]{:S(2)}, u32[]{:S(2)}) collective-permute-start(f32[4,16,384]{2,1,0:T(8,128)S(1)} %shard_map.142.a_ref), channel_id=1, source_target_pairs={{0,96},{16,112},{32,64},{48,80},{64,32},{80,48},{96,0},{112,16},{1... | collective-permute-start | bytes 294920 | tf_op jit(solution)/shard_map/ppermute | solution.py:71
  29.8 5.0 %collective-permute-start.4 = (f32[4,16,384]{2,1,0:T(8,128)S(1)}, f32[4,16,384]{2,1,0:T(8,128)S(1)}, u32[]{:S(2)}, u32[]{:S(2)}) collective-permute-start(f32[4,16,384]{2,1,0:T(8,128)S(1)} %shard_map.142.a_ref), channel_id=1, source_target_pairs={{0,64},{16,80},{32,96},{48,112},{64,0},{80,16},{96,32},{112,48},{1... | collective-permute-start | bytes 294920 | tf_op jit(solution)/shard_map/ppermute | solution.py:71
  30.2 4.9 %collective-permute-start.3 = (f32[4,16,384]{2,1,0:T(8,128)S(1)}, f32[4,16,384]{2,1,0:T(8,128)S(1)}, u32[]{:S(2)}, u32[]{:S(2)}) collective-permute-start(f32[4,16,384]{2,1,0:T(8,128)S(1)} %shard_map.142.a_ref), channel_id=1, source_target_pairs={{0,32},{16,48},{32,0},{48,16},{64,96},{80,112},{96,64},{112,80},{1... | collective-permute-start | bytes 294920 | tf_op jit(solution)/shard_map/ppermute | solution.py:71
  31.2 9.7 %copy-start.2 = (bf16[96,512]{1,0:T(8,128)(2,1)S(1)}, bf16[96,512]{1,0:T(8,128)(2,1)}, u32[]{:S(2)}) copy-start(bf16[96,512]{1,0:T(8,128)(2,1)} %constant.5.clone.back_ref) | copy-start | bytes 294916
  37.4 3.6 %collective-permute-start.6 = (f32[4,16,320]{2,1,0:T(8,128)S(1)}, f32[4,16,320]{2,1,0:T(8,128)S(1)}, u32[]{:S(2)}, u32[]{:S(2)}) collective-permute-start(f32[4,16,320]{2,1,0:T(8,128)S(1)} %get-tuple-element.33.mine_ref), channel_id=1, source_target_pairs={{0,16},{16,0},{32,48},{48,32},{64,80},{80,64},{96,112},{112,96},{1... | collective-permute-start | bytes 245768 | tf_op jit(solution)/shard_map/ppermute | solution.py:75
  43.5 4.9 %collective-permute-start.7 = (bf16[64,1280]{1,0:T(8,128)(2,1)S(1)}, bf16[64,1280]{1,0:T(8,128)(2,1)S(1)}, u32[]{:S(2)}, u32[]{:S(2)}) collective-permute-start(bf16[64,1280]{1,0:T(8,128)(2,1)S(1)} %get-tuple-element.34), channel_id=1, source_target_pairs={{0,1},{1,2},{2,3},{3,4},{4,5},{5,6},{6,7},{7,8},{8,9},{9,10},{10,1... | collective-permute-start | bytes 491528 | tf_op jit(solution)/shard_map/ppermute | solution.py:63
  43.9 4.8 %collective-permute-start.8 = (bf16[64,1280]{1,0:T(8,128)(2,1)S(1)}, bf16[64,1280]{1,0:T(8,128)(2,1)S(1)}, u32[]{:S(2)}, u32[]{:S(2)}) collective-permute-start(bf16[64,1280]{1,0:T(8,128)(2,1)S(1)} %get-tuple-element.36), channel_id=1, source_target_pairs={{1,0},{2,1},{3,2},{4,3},{5,4},{6,5},{7,6},{8,7},{9,8},{10,9},{11,1... | collective-permute-start | bytes 491528 | tf_op jit(solution)/shard_map/ppermute | solution.py:65
  49.1 4.2 %collective-permute-start.10 = (bf16[64,1280]{1,0:T(8,128)(2,1)S(1)}, bf16[64,1280]{1,0:T(8,128)(2,1)S(1)}, u32[]{:S(2)}, u32[]{:S(2)}) collective-permute-start(bf16[64,1280]{1,0:T(8,128)(2,1)S(1)} %get-tuple-element.37), channel_id=1, source_target_pairs={{1,0},{2,1},{3,2},{4,3},{5,4},{6,5},{7,6},{8,7},{9,8},{10,9},{11,1... | collective-permute-start | bytes 491528 | tf_op jit(solution)/shard_map/ppermute | solution.py:65
  51.1 6.2 %collective-permute-start.9 = (bf16[64,1280]{1,0:T(8,128)(2,1)S(1)}, bf16[64,1280]{1,0:T(8,128)(2,1)S(1)}, u32[]{:S(2)}, u32[]{:S(2)}) collective-permute-start(bf16[64,1280]{1,0:T(8,128)(2,1)S(1)} %get-tuple-element.37), channel_id=1, source_target_pairs={{0,1},{1,2},{2,3},{3,4},{4,5},{5,6},{6,7},{7,8},{8,9},{9,10},{10,1... | collective-permute-start | bytes 491528 | tf_op jit(solution)/shard_map/ppermute | solution.py:63
  59.5 1.5 %collective-permute-start.11 = (f32[4,16,320]{2,1,0:T(8,128)S(1)}, f32[4,16,320]{2,1,0:T(8,128)S(1)}, u32[]{:S(2)}, u32[]{:S(2)}) collective-permute-start(f32[4,16,320]{2,1,0:T(8,128)S(1)} %get-tuple-element.40), channel_id=1, source_target_pairs={{0,16},{16,0},{32,48},{48,32},{64,80},{80,64},{96,112},{112,96},{1... | collective-permute-start | bytes 245768 | tf_op jit(solution)/shard_map/ppermute | solution.py:75
  61.0 3.9 %collective-permute-start.12 = (f32[16,320]{1,0:T(8,128)S(1)}, f32[16,320]{1,0:T(8,128)S(1)}, u32[]{:S(2)}, u32[]{:S(2)}) collective-permute-start(f32[16,320]{1,0:T(8,128)S(1)} %get-tuple-element.42), channel_id=1, source_target_pairs={{0,32},{16,48},{32,0},{48,16},{64,96},{80,112},{96,64},{112,80},{1... | collective-permute-start | bytes 61448 | tf_op jit(solution)/shard_map/ppermute | solution.py:71
  61.1 4.3 %collective-permute-start.13 = (f32[16,320]{1,0:T(8,128)S(1)}, f32[16,320]{1,0:T(8,128)S(1)}, u32[]{:S(2)}, u32[]{:S(2)}) collective-permute-start(f32[16,320]{1,0:T(8,128)S(1)} %get-tuple-element.43), channel_id=1, source_target_pairs={{0,64},{16,80},{32,96},{48,112},{64,0},{80,16},{96,32},{112,48},{1... | collective-permute-start | bytes 61448 | tf_op jit(solution)/shard_map/ppermute | solution.py:71
  63.6 3.9 %collective-permute-start.14 = (f32[16,320]{1,0:T(8,128)S(1)}, f32[16,320]{1,0:T(8,128)S(1)}, u32[]{:S(2)}, u32[]{:S(2)}) collective-permute-start(f32[16,320]{1,0:T(8,128)S(1)} %get-tuple-element.44), channel_id=1, source_target_pairs={{0,96},{16,112},{32,64},{48,80},{64,32},{80,48},{96,0},{112,16},{1... | collective-permute-start | bytes 61448 | tf_op jit(solution)/shard_map/ppermute | solution.py:71
  (1 other events, 7.7 us)

commit v10 on v9

--- a/solution.py
+++ b/solution.py
@@ -147,27 +147,40 @@
     return low, high
 
 
-def laden_kernel(
-    a_ref, own_ref, b_ref, refine_ref, perturb_ref, map_ref, data_ref, mine_ref, other_ref, smooth_ref
-):
-    _, core_pos, _ = place()
+def window(parity, y):
+    return pl.ds(pl.multiple_of(y * CHUNK + 256 * parity, 128), 384)
+
+
+def load(data_ref, ref, parity, core_pos):
     data, gain = data_ref[EVEN], data_ref[ODD]
     lanes = lax.broadcasted_iota(jnp.int32, data.shape, 1)
     home = RIDE + 2 * NTILE * core_pos
     for y in range(NY):
-        for ref, parity in ((mine_ref, core_pos), (other_ref, 1 - core_pos)):
-            shift = lax.rem(home + BATCHES - NTILE * (NCORE * y + parity), BATCHES)
-            moved = jnp.where(lanes == home + 2 * SLOTS, gain, pltpu.roll(data, shift, 1))
-            kept = (lanes >= home) & (lanes <= home + 2 * SLOTS)
-            ref[y, :, 256:] = jnp.where(kept, moved, 0.0)
-    forward_kernel(
-        a_ref, own_ref, b_ref, refine_ref, perturb_ref, map_ref, mine_ref, other_ref, smooth_ref
-    )
-
-
-def forward_kernel(
-    a_ref, own_ref, b_ref, refine_ref, perturb_ref, map_ref, mine_ref, other_ref, smooth_ref
-):
+        shift = lax.rem(home + BATCHES - NTILE * (NCORE * y + parity), BATCHES)
+        moved = jnp.where(lanes == home + 2 * SLOTS, gain, pltpu.roll(data, shift, 1))
+        kept = (lanes >= home) & (lanes <= home + 2 * SLOTS)
+        ref[y, :, 256:] = jnp.where(kept, moved, 0.0)
+
+
+def regions_of(smooth_ref, refine_ref, perturb_ref, map_ref, parity, out_ref):
+    smooth = smooth_ref[...]
+    for y in range(NY):
+        cols = window(parity, y)
+        mapped = jnp.dot(smooth, map_ref[:, cols], preferred_element_type=FLOAT)
+        high = mapped.astype(HALF)
+        low = (mapped - high.astype(FLOAT)).astype(HALF)
+        fine = jnp.dot(
+            refine_ref[...], jnp.concatenate([high, low], axis=0), preferred_element_type=FLOAT
+        )
+        total = None
+        for k in range(MEMBERS_HERE):
+            term = fine[k * FINE_ROWS : (k + 1) * FINE_ROWS] * perturb_ref[k, :, cols].astype(FLOAT)
+            total = term if total is None else total + term
+        out_ref[y, :, :WIDTH] = jnp.where(parity == 0, total[:, :WIDTH], total[:, 384 - WIDTH :])
+
+
+def other_kernel(a_ref, own_ref, b_ref, refine_ref, perturb_ref, map_ref, *refs):
+    other_ref, smooth_ref = refs[-2:]
     _, core_pos, _ = place()
     down_first = downward()
     below, above = edges()
@@ -178,22 +191,16 @@
         rows = low + [own_ref[row_slice(r), cols] for r in range(4)] + high
         for r, value in enumerate(swept(rows, masks)):
             smooth_ref[row_slice(r), cols] = value.astype(HALF)
-    smooth = smooth_ref[...]
-    for y in range(NY):
-        cols = pl.ds(y * CHUNK, CHUNK)
-        mapped = jnp.dot(smooth, map_ref[:, cols], preferred_element_type=FLOAT)
-        high = mapped.astype(HALF)
-        low = (mapped - high.astype(FLOAT)).astype(HALF)
-        fine = jnp.dot(
-            refine_ref[...], jnp.concatenate([high, low], axis=0), preferred_element_type=FLOAT
-        )
-        total = None
-        for k in range(MEMBERS_HERE):
-            term = fine[k * FINE_ROWS : (k + 1) * FINE_ROWS] * perturb_ref[k, :, cols].astype(FLOAT)
-            total = term if total is None else total + term
-        first, second = total[:, :WIDTH], total[:, WIDTH:]
-        mine_ref[y, :, :WIDTH] = jnp.where(core_pos == 0, first, second)
-        other_ref[y, :, :WIDTH] = jnp.where(core_pos == 0, second, first)
+    if len(refs) > 2:
+        load(refs[0], other_ref, 1 - core_pos, core_pos)
+    regions_of(smooth_ref, refine_ref, perturb_ref, map_ref, 1 - core_pos, other_ref)
+
+
+def mine_kernel(smooth_ref, refine_ref, perturb_ref, map_ref, *refs):
+    _, core_pos, _ = place()
+    if len(refs) > 1:
+        load(refs[0], refs[-1], core_pos, core_pos)
+    regions_of(smooth_ref, refine_ref, perturb_ref, map_ref, core_pos, refs[-1])
 
 
 REGIONS = ((NY, FINE_ROWS, WIDTH), FLOAT)
@@ -201,26 +208,30 @@
 RIDE = 64
 
 
-SMOOTH = pltpu.VMEM(((ROWS + 2) * MEMBERS_HERE, COARSE_COLS), HALF)
-
-
-def partial_forward(kernel, shape, *arguments):
-    return call(kernel, (shape, shape), arguments, scratch=[SMOOTH])
-
-
-def adjoint_kernel(
-    mine_ref, other_ref, back_ref, perturb_ref, map_ref,
-    part_ref, a_ref, b_ref,
-):
-    _, core_pos, _ = place()
-    down_first = downward()
+SMOOTH = (((ROWS + 2) * MEMBERS_HERE, COARSE_COLS), HALF)
+
+
+def partial_forward(shape, first, own, second, operators, data=()):
+    other, smooth = call(other_kernel, (shape, SMOOTH), (first, own, second) + operators + data)
+    there = swap_core(other)
+    (mine,) = call(mine_kernel, (shape,), (smooth,) + operators + data)
+    return mine, there
+
+
+PART = (((ROWS + 2) * MEMBERS_HERE, COARSE_COLS), FLOAT)
+
+
+def pulled_part(values_ref, back_ref, perturb_ref, map_ref, parity):
     total = None
     for y in range(NY):
-        cols = pl.ds(y * CHUNK, CHUNK)
-        mine, other = mine_ref[y], other_ref[y]
-        first = jnp.where(core_pos == 0, mine, other)
-        second = jnp.where(core_pos == 0, other, mine)
-        spread = jnp.concatenate([first, second], axis=1)
+        cols = window(parity, y)
+        values = values_ref[y]
+        rest = jnp.zeros((FINE_ROWS, 384 - WIDTH), FLOAT)
+        spread = jnp.where(
+            parity == 0,
+            jnp.concatenate([values, rest], axis=1),
+            jnp.concatenate([rest, values], axis=1),
+        )
         highs, lows = [], []
         for k in range(MEMBERS_HERE):
             term = perturb_ref[k, :, cols].astype(FLOAT) * spread
@@ -237,6 +248,20 @@
             preferred_element_type=FLOAT,
         )
         total = part if total is None else total + part
+    return total
+
+
+def pull_mine_kernel(mine_ref, back_ref, perturb_ref, map_ref, part_ref):
+    _, core_pos, _ = place()
+    part_ref[...] = pulled_part(mine_ref, back_ref, perturb_ref, map_ref, core_pos)
+
+
+def pull_other_kernel(
+    mine_ref, other_ref, back_ref, perturb_ref, map_ref, part_ref, a_ref, b_ref
+):
+    _, core_pos, _ = place()
+    down_first = downward()
+    total = mine_ref[...] + pulled_part(other_ref, back_ref, perturb_ref, map_ref, 1 - core_pos)
     part_ref[...] = total
     up = total[2 * MEMBERS_HERE :].astype(HALF)
     down = total[: 4 * MEMBERS_HERE].astype(HALF)
@@ -244,15 +269,14 @@
     b_ref[...] = jnp.where(down_first, up, down)
 
 
-def partial_adjoint(mine, other, perturb, column_map):
+def partial_adjoint(spread, perturb, column_map):
     matrix = member_matrix().T
     matrix = jnp.asarray(np.concatenate([matrix, matrix], axis=1), HALF)
+    operators = (matrix, perturb, column_map)
+    there = swap_core(spread)
+    (mine,) = call(pull_mine_kernel, (PART,), (spread,) + operators)
     rim = ((4 * MEMBERS_HERE, COARSE_COLS), HALF)
-    return call(
-        adjoint_kernel,
-        ((((ROWS + 2) * MEMBERS_HERE, COARSE_COLS), FLOAT), rim, rim),
-        (mine, other, matrix, perturb, column_map),
-    )
+    return call(pull_other_kernel, (PART, rim, rim), (mine, there) + operators)
 
 
 def gradient_kernel(a_ref, part_ref, b_ref, own_ref, grad_ref, half_ref, square_ref):
@@ -487,10 +511,9 @@
     column_frac = jnp.transpose(column_fraction[0], (1, 2, 0))
     lengths = block_lengths[0].T
 
-    mine, other = partial_forward(
-        laden_kernel, LADEN, near_rows, own, far_rows, matrix, perturb, column_map, data
-    )
-    (mine,) = call(add_kernel, (LADEN,), (mine, swap_core(other), background))
+    operators = (matrix, perturb, column_map)
+    mine, there = partial_forward(LADEN, near_rows, own, far_rows, operators, (data,))
+    (mine,) = call(add_kernel, (LADEN,), (mine, there, background))
     pieces = [mine]
     for i in range(1, NY):
         pieces.append(across(mine, i))
@@ -509,15 +532,15 @@
         (*pieces, picks, both, lengths),
         scratch=[pltpu.VMEM((NY, BATCHES, 128), FLOAT)],
     )
-    part, up, down = partial_adjoint(spread, swap_core(spread), perturb, column_map)
+    part, up, down = partial_adjoint(spread, perturb, column_map)
     near_rows, far_rows = swap_both(up, down)
     gradient, half, square = gradient_of(near_rows, part, far_rows, own)
     near_rows, far_rows = swap_both(half, half)
-    mine, other = partial_forward(
-        forward_kernel, REGIONS, near_rows, gradient, far_rows, matrix, perturb, column_map
-    )
-    pieces = call(pick_kernel, (region,) * NY, (mine, swap_core(other)))
-    pieces = [pieces[0]] + [across(pieces[i], i) for i in range(1, NY)]
+    mine, there = partial_forward(REGIONS, near_rows, gradient, far_rows, operators)
+    turned = call(pick_kernel, (region,) * NY, (mine, there))
+    pieces = [turned[0]]
+    for i in range(1, NY):
+        pieces.append(across(turned[i], i))
     image, sent = call(
         curve_kernel,
         (region, ((BATCHES, 128), FLOAT)),

time: 90.2 us -> 90.9 us (level)
  Pallas kernels: 13.7 us -> 17.7 us
  waiting for transfers between devices: 19 us -> 16.5 us
    pallas_call x11 -> x14, Pallas kernels: 13.7 us -> 17.7 us  [call(): pl.pallas_call(kernel, out_shape=tuple((jax.ShapeDtypeStruct(shape, kind)...]
    ppermute x3, waiting for transfers between devices: 2.83 us -> 0.01 us  [swap_core(): return lax.ppermute(values, 'member', [(i, i ^ 1) for i in range(NMEMBER)])]
  transfers between devices with their start and end apart: 15 -> 15, of which waited for: 12 -> 7; matrix products, arithmetic and copies ran while one was open for 0% -> 0% of each run, Pallas kernels for 1% -> 7%
where the time goes in v10:
time: 90.9 us; the launch traced here: 90.8 us
  blocking collectives  34.9 us (38%)
  starting transfers between devices  20.1 us (22%)
  Pallas kernels  17.7 us (19%)
  waiting for transfers between devices  16.5 us (18%)
  between operations  1.48 us (2%)
    all_to_all x1, blocking collectives, shards(): lax.all_to_all(sent, ('member', 'tile'), split_axis=0, concat_axis=0, til...  20.8 us
    pallas_call x14, Pallas kernels, call(): pl.pallas_call(kernel, out_shape=tuple((jax.ShapeDtypeStruct(shape, kind)...  17.7 us
    all_to_all x1, blocking collectives, shards(): data = lax.all_to_all(sent, 'tile', split_axis=0, concat_axis=0, tiled=True)  14.1 us
    ppermute x6, starting transfers between devices, across(): return lax.ppermute(values, 'member', pairs)  7.42 us
    ppermute x3, waiting for transfers between devices, swap_both(): first = lax.ppermute(first_values, ('member', 'tile'), ring())  7.28 us
    ppermute x3, starting transfers between devices, swap_core(): return lax.ppermute(values, 'member', [(i, i ^ 1) for i in range(NMEMBER)])  7.2 us
    ppermute x6, waiting for transfers between devices, across(): return lax.ppermute(values, 'member', pairs)  6.97 us
    ppermute x3, starting transfers between devices, swap_both(): second = lax.ppermute(second_values, ('member', 'tile'), back)  5.32 us
  transfers between devices with their start and end apart: 15, of which 7 were waited for; matrix products, arithmetic and copies ran while one was open for 0% of the time, Pallas kernels for 7%

profile of v10, /device:TPU:1, one launch (start us, length us, event | category | flops | bytes accessed | tf_op | source)
XLA Modules:
  0.0 90.8 jit_solution(971571169920818620)
XLA Ops:
  1.3 1.7 %shard_map.140 = (f32[32,128]{1,0:T(8,128)S(1)}, f32[64,1280]{1,0:T(8,128)S(1)}, bf16[64,1280]{1,0:T(8,128)(2,1)S(1)}) custom-call(f32[8,128]{1,0:T(8,128)} %bitcast.35, f32[8,128]{1,0:T(8,128)} %bitcast.36, f32[1]{0:T(128)S(6)} %copy.16.gain_ref, f32[16,4,1280]{2,1,0:T(4,128)} %weights_hbm.1), custom_call_target="tpu_custom_call" | custom-call | flops 20000000000 | bytes 156250000 | tf_op jit(solution)/shard_map/pallas_call | solution.py:99
  3.0 2.1 %collective-permute-start.1 = (bf16[64,1280]{1,0:T(8,128)(2,1)S(1)}, bf16[64,1280]{1,0:T(8,128)(2,1)S(1)}, u32[]{:S(2)}, u32[]{:S(2)}) collective-permute-start(bf16[64,1280]{1,0:T(8,128)(2,1)S(1)} %get-tuple-element.26), channel_id=1, source_target_pairs={{1,0},{2,1},{3,2},{4,3},{5,4},{6,5},{7,6},{8,7},{9,8},{10,9},{11,1... | collective-permute-start | bytes 491528 | tf_op jit(solution)/shard_map/ppermute | solution.py:65
  5.1 14.1 %all_to_all.22 = f32[16,2,128]{2,1,0:T(2,128)S(1)} all-to-all(f32[16,2,128]{2,1,0:T(2,128)S(1)} %bitcast.30), channel_id=1, replica_groups=mesh['member'=8,'tile'=16] {'tile'}, dimensions={0} | all-to-all | bytes 32768 | tf_op jit(solution)/shard_map/all_to_all | solution.py:507
  19.3 2.1 %shard_map.141 = (f32[4,16,384]{2,1,0:T(8,128)S(1)}, bf16[96,1280]{1,0:T(8,128)(2,1)S(1)}) custom-call(bf16[64,1280]{1,0:T(8,128)(2,1)S(1)} %collective-permute-done.a_ref, f32[64,1280]{1,0:T(8,128)S(1)} %get-tuple-element.27.own_ref, bf16[64,1280]{1,0:T(8,128)(2,1)S(1)} %collective-permute-done.1.b_ref, bf16[256,192]{1,0:T(8,128)(2,1)S(1)} %copy-done.1, ...), custom_call_target="tpu_custom_call" | custom-call | flops 1000000000 | bytes 7812500 | tf_op jit(solution)/shard_map/pallas_call | solution.py:99
  21.3 4.4 %collective-permute-start.2 = (f32[4,16,384]{2,1,0:T(8,128)S(1)}, f32[4,16,384]{2,1,0:T(8,128)S(1)}, u32[]{:S(2)}, u32[]{:S(2)}) collective-permute-start(f32[4,16,384]{2,1,0:T(8,128)S(1)} %get-tuple-element.30), channel_id=1, source_target_pairs={{0,16},{16,0},{32,48},{48,32},{64,80},{80,64},{96,112},{112,96},{1... | collective-permute-start | bytes 294920 | tf_op jit(solution)/shard_map/ppermute | solution.py:75
  25.7 1.7 %shard_map.142.a_ref = f32[4,16,384]{2,1,0:T(8,128)S(1)} custom-call(bf16[96,1280]{1,0:T(8,128)(2,1)S(1)} %get-tuple-element.29.smooth_ref, bf16[256,192]{1,0:T(8,128)(2,1)S(1)} %copy-done.1, bf16[16,16,2560]{2,1,0:T(8,128)(2,1)S(1)} %copy-done, bf16[1280,2560]{1,0:T(8,128)(2,1)S(1)} %bitcast.25, f32[32,128]{1,0:T(8,128)S(1)} %bitcast.27), custom_call_target="tpu_custom_call" | custom-call | flops 1000000000 | bytes 7812500 | tf_op jit(solution)/shard_map/pallas_call | solution.py:99
  27.5 2.8 %collective-permute-start.5 = (f32[4,16,384]{2,1,0:T(8,128)S(1)}, f32[4,16,384]{2,1,0:T(8,128)S(1)}, u32[]{:S(2)}, u32[]{:S(2)}) collective-permute-start(f32[4,16,384]{2,1,0:T(8,128)S(1)} %shard_map.143.a_ref), channel_id=1, source_target_pairs={{0,96},{16,112},{32,64},{48,80},{64,32},{80,48},{96,0},{112,16},{1... | collective-permute-start | bytes 294920 | tf_op jit(solution)/shard_map/ppermute | solution.py:71
  31.7 2.7 %collective-permute-done.5.d_ref = f32[4,16,384]{2,1,0:T(8,128)S(1)} collective-permute-done((f32[4,16,384]{2,1,0:T(8,128)S(1)}, f32[4,16,384]{2,1,0:T(8,128)S(1)}, u32[]{:S(2)}, u32[]{:S(2)}) %collective-permute-start.5) | collective-permute-done | bytes 98336 | tf_op jit(solution)/shard_map/ppermute | solution.py:71
  34.4 1.4 %collective-permute-done.4.c_ref = f32[4,16,384]{2,1,0:T(8,128)S(1)} collective-permute-done((f32[4,16,384]{2,1,0:T(8,128)S(1)}, f32[4,16,384]{2,1,0:T(8,128)S(1)}, u32[]{:S(2)}, u32[]{:S(2)}) %collective-permute-start.4) | collective-permute-done | bytes 98336 | tf_op jit(solution)/shard_map/ppermute | solution.py:71
  35.9 2.3 %shard_map.145 = (f32[4,16,320]{2,1,0:T(8,128)S(1)}, f32[8,128]{1,0:T(8,128)S(1)}, f32[16,320]{1,0:T(8,128)S(1)}) custom-call(f32[4,16,384]{2,1,0:T(8,128)S(1)} %shard_map.143.a_ref, f32[4,16,384]{2,1,0:T(8,128)S(1)} %collective-permute-done.3.b_ref, f32[4,16,384]{2,1,0:T(8,128)S(1)} %collective-permute-done.4.c_ref, ...), custom_call_target="tpu_custom_call" | custom-call | flops 1000000000 | bytes 7812500 | tf_op jit(solution)/shard_map/pallas_call | solution.py:99
  38.2 2.0 %collective-permute-start.6 = (f32[4,16,320]{2,1,0:T(8,128)S(1)}, f32[4,16,320]{2,1,0:T(8,128)S(1)}, u32[]{:S(2)}, u32[]{:S(2)}) collective-permute-start(f32[4,16,320]{2,1,0:T(8,128)S(1)} %get-tuple-element.33.mine_ref), channel_id=1, source_target_pairs={{0,16},{16,0},{32,48},{48,32},{64,80},{80,64},{96,112},{112,96},{1... | collective-permute-start | bytes 245768 | tf_op jit(solution)/shard_map/ppermute | solution.py:75
  40.2 1.8 %shard_map.146.mine_ref = f32[96,1280]{1,0:T(8,128)S(1)} custom-call(f32[4,16,320]{2,1,0:T(8,128)S(1)} %get-tuple-element.33.mine_ref, bf16[96,512]{1,0:T(8,128)(2,1)S(1)} %copy-done.2, bf16[16,16,2560]{2,1,0:T(8,128)(2,1)S(1)} %copy-done, bf16[1280,2560]{1,0:T(8,128)(2,1)S(1)} %bitcast.25), custom_call_target="tpu_custom_call" | custom-call | flops 1000000000 | bytes 7812500 | tf_op jit(solution)/shard_map/pallas_call | solution.py:99
  42.0 1.8 %shard_map.147 = (f32[96,1280]{1,0:T(8,128)S(1)}, bf16[64,1280]{1,0:T(8,128)(2,1)S(1)}, bf16[64,1280]{1,0:T(8,128)(2,1)S(1)}) custom-call(f32[96,1280]{1,0:T(8,128)S(1)} %shard_map.146.mine_ref, f32[4,16,320]{2,1,0:T(8,128)S(1)} %collective-permute-done.6.other_ref, bf16[96,512]{1,0:T(8,128)(2,1)S(1)} %copy-done.2, bf16[16,16,2560]{2,1,0:T(8,128)(2,1)S(1)} %copy-done, ...), custom_call_target="tpu_custom_call" | custom-call | flops 1000000000 | bytes 7812500 | tf_op jit(solution)/shard_map/pallas_call | solution.py:99
  44.0 1.4 %collective-permute-start.8 = (bf16[64,1280]{1,0:T(8,128)(2,1)S(1)}, bf16[64,1280]{1,0:T(8,128)(2,1)S(1)}, u32[]{:S(2)}, u32[]{:S(2)}) collective-permute-start(bf16[64,1280]{1,0:T(8,128)(2,1)S(1)} %get-tuple-element.36), channel_id=1, source_target_pairs={{1,0},{2,1},{3,2},{4,3},{5,4},{6,5},{7,6},{8,7},{9,8},{10,9},{11,1... | collective-permute-start | bytes 491528 | tf_op jit(solution)/shard_map/ppermute | solution.py:65
  45.4 3.7 %collective-permute-done.7.a_ref = bf16[64,1280]{1,0:T(8,128)(2,1)S(1)} collective-permute-done((bf16[64,1280]{1,0:T(8,128)(2,1)S(1)}, bf16[64,1280]{1,0:T(8,128)(2,1)S(1)}, u32[]{:S(2)}, u32[]{:S(2)}) %collective-permute-start.7) | collective-permute-done | bytes 163872 | tf_op jit(solution)/shard_map/ppermute | solution.py:63
  49.5 1.8 %collective-permute-start.10 = (bf16[64,1280]{1,0:T(8,128)(2,1)S(1)}, bf16[64,1280]{1,0:T(8,128)(2,1)S(1)}, u32[]{:S(2)}, u32[]{:S(2)}) collective-permute-start(bf16[64,1280]{1,0:T(8,128)(2,1)S(1)} %get-tuple-element.37), channel_id=1, source_target_pairs={{1,0},{2,1},{3,2},{4,3},{5,4},{6,5},{7,6},{8,7},{9,8},{10,9},{11,1... | collective-permute-start | bytes 491528 | tf_op jit(solution)/shard_map/ppermute | solution.py:65
  51.3 2.3 %collective-permute-done.10.b_ref = bf16[64,1280]{1,0:T(8,128)(2,1)S(1)} collective-permute-done((bf16[64,1280]{1,0:T(8,128)(2,1)S(1)}, bf16[64,1280]{1,0:T(8,128)(2,1)S(1)}, u32[]{:S(2)}, u32[]{:S(2)}) %collective-permute-start.10) | collective-permute-done | bytes 163872 | tf_op jit(solution)/shard_map/ppermute | solution.py:65
  53.5 3.6 %collective-permute-done.9.a_ref = bf16[64,1280]{1,0:T(8,128)(2,1)S(1)} collective-permute-done((bf16[64,1280]{1,0:T(8,128)(2,1)S(1)}, bf16[64,1280]{1,0:T(8,128)(2,1)S(1)}, u32[]{:S(2)}, u32[]{:S(2)}) %collective-permute-start.9) | collective-permute-done | bytes 163872 | tf_op jit(solution)/shard_map/ppermute | solution.py:63
  57.1 2.1 %shard_map.149 = (f32[4,16,320]{2,1,0:T(8,128)S(1)}, bf16[96,1280]{1,0:T(8,128)(2,1)S(1)}) custom-call(bf16[64,1280]{1,0:T(8,128)(2,1)S(1)} %collective-permute-done.9.a_ref, f32[64,1280]{1,0:T(8,128)S(1)} %get-tuple-element.38.own_ref.grad_ref, bf16[64,1280]{1,0:T(8,128)(2,1)S(1)} %collective-permute-done.10.b_ref, bf16[256,192]{1,0:T(8,128)(2,1)S(1)} %copy-done.1, ...), custom_call_target="tpu_custom_call" | custom-call | flops 1000000000 | bytes 7812500 | tf_op jit(solution)/shard_map/pallas_call | solution.py:99
  60.0 1.7 %shard_map.150.a_ref = f32[4,16,320]{2,1,0:T(8,128)S(1)} custom-call(bf16[96,1280]{1,0:T(8,128)(2,1)S(1)} %get-tuple-element.39.smooth_ref, bf16[256,192]{1,0:T(8,128)(2,1)S(1)} %copy-done.1, bf16[16,16,2560]{2,1,0:T(8,128)(2,1)S(1)} %copy-done, bf16[1280,2560]{1,0:T(8,128)(2,1)S(1)} %bitcast.25), custom_call_target="tpu_custom_call" | custom-call | flops 1000000000 | bytes 7812500 | tf_op jit(solution)/shard_map/pallas_call | solution.py:99
  62.0 2.6 %collective-permute-start.13 = (f32[16,320]{1,0:T(8,128)S(1)}, f32[16,320]{1,0:T(8,128)S(1)}, u32[]{:S(2)}, u32[]{:S(2)}) collective-permute-start(f32[16,320]{1,0:T(8,128)S(1)} %get-tuple-element.43), channel_id=1, source_target_pairs={{0,64},{16,80},{32,96},{48,112},{64,0},{80,16},{96,32},{112,48},{1... | collective-permute-start | bytes 61448 | tf_op jit(solution)/shard_map/ppermute | solution.py:71
  64.6 1.1 %collective-permute-start.14 = (f32[16,320]{1,0:T(8,128)S(1)}, f32[16,320]{1,0:T(8,128)S(1)}, u32[]{:S(2)}, u32[]{:S(2)}) collective-permute-start(f32[16,320]{1,0:T(8,128)S(1)} %get-tuple-element.44), channel_id=1, source_target_pairs={{0,96},{16,112},{32,64},{48,80},{64,32},{80,48},{96,0},{112,16},{1... | collective-permute-start | bytes 61448 | tf_op jit(solution)/shard_map/ppermute | solution.py:71
  66.4 2.1 %collective-permute-done.14.d_ref = f32[16,320]{1,0:T(8,128)S(1)} collective-permute-done((f32[16,320]{1,0:T(8,128)S(1)}, f32[16,320]{1,0:T(8,128)S(1)}, u32[]{:S(2)}, u32[]{:S(2)}) %collective-permute-start.14) | collective-permute-done | bytes 20512 | tf_op jit(solution)/shard_map/ppermute | solution.py:71
  68.9 20.8 %all_to_all.23 = f32[128,1,128]{2,1,0:T(1,128)S(1)} all-to-all(f32[128,1,128]{2,1,0:T(1,128)S(1)} %bitcast.28), channel_id=1, replica_groups=mesh['member'=8,'tile'=16] {'member','tile'}, dimensions={0} | all-to-all | bytes 131072 | tf_op jit(solution)/shard_map/all_to_all | solution.py:549
  (43 shorter events, 5.2 us)
Async XLA Ops:
  1.3 18.0 %slice-start = ((s8[6553600]{0:T(1024)(128)(4,1)}), s8[4194304]{0:T(1024)(128)(4,1)S(1)}, s32[]{:S(2)}) async-start(s8[6553600]{0:T(1024)(128)(4,1)} %bitcast.24), calls=%async_computation.2 | async-start | bytes 8388608
  1.3 18.0 %slice-start.1 = ((s8[6553600]{0:T(1024)(128)(4,1)}), s8[2359296]{0:T(1024)(128)(4,1)S(1)}, s32[]{:S(2)}) async-start(s8[6553600]{0:T(1024)(128)(4,1)} %bitcast.24), calls=%async_computation.3 | async-start | bytes 4718592
  1.3 18.0 %copy-start = (bf16[16,16,2560]{2,1,0:T(8,128)(2,1)S(1)}, bf16[16,16,2560]{2,1,0:T(8,128)(2,1)}, u32[]{:S(2)}) copy-start(bf16[16,16,2560]{2,1,0:T(8,128)(2,1)} %perturb_ref.11) | copy-start | bytes 3932164
  1.3 18.0 %copy-start.1 = (bf16[256,192]{1,0:T(8,128)(2,1)S(1)}, bf16[256,192]{1,0:T(8,128)(2,1)}, u32[]{:S(2)}) copy-start(bf16[256,192]{1,0:T(8,128)(2,1)} %constant.4.clone.refine_ref) | copy-start | bytes 294916
  3.0 16.2 %collective-permute-start.1 = (bf16[64,1280]{1,0:T(8,128)(2,1)S(1)}, bf16[64,1280]{1,0:T(8,128)(2,1)S(1)}, u32[]{:S(2)}, u32[]{:S(2)}) collective-permute-start(bf16[64,1280]{1,0:T(8,128)(2,1)S(1)} %get-tuple-element.26), channel_id=1, source_target_pairs={{1,0},{2,1},{3,2},{4,3},{5,4},{6,5},{7,6},{8,7},{9,8},{10,9},{11,1... | collective-permute-start | bytes 491528 | tf_op jit(solution)/shard_map/ppermute | solution.py:65
  5.1 14.1 %collective-permute-start = (bf16[64,1280]{1,0:T(8,128)(2,1)S(1)}, bf16[64,1280]{1,0:T(8,128)(2,1)S(1)}, u32[]{:S(2)}, u32[]{:S(2)}) collective-permute-start(bf16[64,1280]{1,0:T(8,128)(2,1)S(1)} %get-tuple-element.26), channel_id=1, source_target_pairs={{0,1},{1,2},{2,3},{3,4},{4,5},{5,6},{6,7},{7,8},{8,9},{9,10},{10,1... | collective-permute-start | bytes 491528 | tf_op jit(solution)/shard_map/ppermute | solution.py:63
  21.3 6.1 %collective-permute-start.2 = (f32[4,16,384]{2,1,0:T(8,128)S(1)}, f32[4,16,384]{2,1,0:T(8,128)S(1)}, u32[]{:S(2)}, u32[]{:S(2)}) collective-permute-start(f32[4,16,384]{2,1,0:T(8,128)S(1)} %get-tuple-element.30), channel_id=1, source_target_pairs={{0,16},{16,0},{32,48},{48,32},{64,80},{80,64},{96,112},{112,96},{1... | collective-permute-start | bytes 294920 | tf_op jit(solution)/shard_map/ppermute | solution.py:75
  27.4 3.6 %copy-start.3 = (s32[1,128,8,8]{1,3,2,0:T(8,128)S(1)}, s32[1,128,8,8]{1,3,2,0:T(8,128)}, u32[]{:S(2)}) copy-start(s32[1,128,8,8]{1,3,2,0:T(8,128)} %param.17) | copy-start | bytes 98308
  27.4 3.6 %copy-start.4 = (f32[1,128,8,8]{1,3,2,0:T(8,128)S(1)}, f32[1,128,8,8]{1,3,2,0:T(8,128)}, u32[]{:S(2)}) copy-start(f32[1,128,8,8]{1,3,2,0:T(8,128)} %param.18) | copy-start | bytes 98308
  27.4 3.6 %copy-start.5 = (f32[1,128,8,8]{1,3,2,0:T(8,128)S(1)}, f32[1,128,8,8]{1,3,2,0:T(8,128)}, u32[]{:S(2)}) copy-start(f32[1,128,8,8]{1,3,2,0:T(8,128)} %param.19) | copy-start | bytes 98308
  27.5 8.4 %copy-start.7 = (s32[1,128,8]{1,2,0:T(8,128)S(1)}, s32[1,128,8]{1,2,0:T(8,128)}, u32[]{:S(2)}) copy-start(s32[1,128,8]{1,2,0:T(8,128)} %param.20) | copy-start | bytes 12292
  27.5 6.9 %collective-permute-start.5 = (f32[4,16,384]{2,1,0:T(8,128)S(1)}, f32[4,16,384]{2,1,0:T(8,128)S(1)}, u32[]{:S(2)}, u32[]{:S(2)}) collective-permute-start(f32[4,16,384]{2,1,0:T(8,128)S(1)} %shard_map.143.a_ref), channel_id=1, source_target_pairs={{0,96},{16,112},{32,64},{48,80},{64,32},{80,48},{96,0},{112,16},{1... | collective-permute-start | bytes 294920 | tf_op jit(solution)/shard_map/ppermute | solution.py:71
  30.3 5.5 %collective-permute-start.4 = (f32[4,16,384]{2,1,0:T(8,128)S(1)}, f32[4,16,384]{2,1,0:T(8,128)S(1)}, u32[]{:S(2)}, u32[]{:S(2)}) collective-permute-start(f32[4,16,384]{2,1,0:T(8,128)S(1)} %shard_map.143.a_ref), channel_id=1, source_target_pairs={{0,64},{16,80},{32,96},{48,112},{64,0},{80,16},{96,32},{112,48},{1... | collective-permute-start | bytes 294920 | tf_op jit(solution)/shard_map/ppermute | solution.py:71
  30.7 5.2 %collective-permute-start.3 = (f32[4,16,384]{2,1,0:T(8,128)S(1)}, f32[4,16,384]{2,1,0:T(8,128)S(1)}, u32[]{:S(2)}, u32[]{:S(2)}) collective-permute-start(f32[4,16,384]{2,1,0:T(8,128)S(1)} %shard_map.143.a_ref), channel_id=1, source_target_pairs={{0,32},{16,48},{32,0},{48,16},{64,96},{80,112},{96,64},{112,80},{1... | collective-permute-start | bytes 294920 | tf_op jit(solution)/shard_map/ppermute | solution.py:71
  31.7 8.5 %copy-start.2 = (bf16[96,512]{1,0:T(8,128)(2,1)S(1)}, bf16[96,512]{1,0:T(8,128)(2,1)}, u32[]{:S(2)}) copy-start(bf16[96,512]{1,0:T(8,128)(2,1)} %constant.5.clone.back_ref) | copy-start | bytes 294916
  38.2 3.8 %collective-permute-start.6 = (f32[4,16,320]{2,1,0:T(8,128)S(1)}, f32[4,16,320]{2,1,0:T(8,128)S(1)}, u32[]{:S(2)}, u32[]{:S(2)}) collective-permute-start(f32[4,16,320]{2,1,0:T(8,128)S(1)} %get-tuple-element.33.mine_ref), channel_id=1, source_target_pairs={{0,16},{16,0},{32,48},{48,32},{64,80},{80,64},{96,112},{112,96},{1... | collective-permute-start | bytes 245768 | tf_op jit(solution)/shard_map/ppermute | solution.py:75
  43.9 5.2 %collective-permute-start.7 = (bf16[64,1280]{1,0:T(8,128)(2,1)S(1)}, bf16[64,1280]{1,0:T(8,128)(2,1)S(1)}, u32[]{:S(2)}, u32[]{:S(2)}) collective-permute-start(bf16[64,1280]{1,0:T(8,128)(2,1)S(1)} %get-tuple-element.34), channel_id=1, source_target_pairs={{0,1},{1,2},{2,3},{3,4},{4,5},{5,6},{6,7},{7,8},{8,9},{9,10},{10,1... | collective-permute-start | bytes 491528 | tf_op jit(solution)/shard_map/ppermute | solution.py:63
  44.0 5.2 %collective-permute-start.8 = (bf16[64,1280]{1,0:T(8,128)(2,1)S(1)}, bf16[64,1280]{1,0:T(8,128)(2,1)S(1)}, u32[]{:S(2)}, u32[]{:S(2)}) collective-permute-start(bf16[64,1280]{1,0:T(8,128)(2,1)S(1)} %get-tuple-element.36), channel_id=1, source_target_pairs={{1,0},{2,1},{3,2},{4,3},{5,4},{6,5},{7,6},{8,7},{9,8},{10,9},{11,1... | collective-permute-start | bytes 491528 | tf_op jit(solution)/shard_map/ppermute | solution.py:65
  49.5 4.0 %collective-permute-start.10 = (bf16[64,1280]{1,0:T(8,128)(2,1)S(1)}, bf16[64,1280]{1,0:T(8,128)(2,1)S(1)}, u32[]{:S(2)}, u32[]{:S(2)}) collective-permute-start(bf16[64,1280]{1,0:T(8,128)(2,1)S(1)} %get-tuple-element.37), channel_id=1, source_target_pairs={{1,0},{2,1},{3,2},{4,3},{5,4},{6,5},{7,6},{8,7},{9,8},{10,9},{11,1... | collective-permute-start | bytes 491528 | tf_op jit(solution)/shard_map/ppermute | solution.py:65
  51.3 5.8 %collective-permute-start.9 = (bf16[64,1280]{1,0:T(8,128)(2,1)S(1)}, bf16[64,1280]{1,0:T(8,128)(2,1)S(1)}, u32[]{:S(2)}, u32[]{:S(2)}) collective-permute-start(bf16[64,1280]{1,0:T(8,128)(2,1)S(1)} %get-tuple-element.37), channel_id=1, source_target_pairs={{0,1},{1,2},{2,3},{3,4},{4,5},{5,6},{6,7},{7,8},{8,9},{9,10},{10,1... | collective-permute-start | bytes 491528 | tf_op jit(solution)/shard_map/ppermute | solution.py:63
  59.2 2.5 %collective-permute-start.11 = (f32[4,16,320]{2,1,0:T(8,128)S(1)}, f32[4,16,320]{2,1,0:T(8,128)S(1)}, u32[]{:S(2)}, u32[]{:S(2)}) collective-permute-start(f32[4,16,320]{2,1,0:T(8,128)S(1)} %get-tuple-element.40), channel_id=1, source_target_pairs={{0,16},{16,0},{32,48},{48,32},{64,80},{80,64},{96,112},{112,96},{1... | collective-permute-start | bytes 245768 | tf_op jit(solution)/shard_map/ppermute | solution.py:75
  61.7 3.9 %collective-permute-start.12 = (f32[16,320]{1,0:T(8,128)S(1)}, f32[16,320]{1,0:T(8,128)S(1)}, u32[]{:S(2)}, u32[]{:S(2)}) collective-permute-start(f32[16,320]{1,0:T(8,128)S(1)} %get-tuple-element.42), channel_id=1, source_target_pairs={{0,32},{16,48},{32,0},{48,16},{64,96},{80,112},{96,64},{112,80},{1... | collective-permute-start | bytes 61448 | tf_op jit(solution)/shard_map/ppermute | solution.py:71
  62.0 4.3 %collective-permute-start.13 = (f32[16,320]{1,0:T(8,128)S(1)}, f32[16,320]{1,0:T(8,128)S(1)}, u32[]{:S(2)}, u32[]{:S(2)}) collective-permute-start(f32[16,320]{1,0:T(8,128)S(1)} %get-tuple-element.43), channel_id=1, source_target_pairs={{0,64},{16,80},{32,96},{48,112},{64,0},{80,16},{96,32},{112,48},{1... | collective-permute-start | bytes 61448 | tf_op jit(solution)/shard_map/ppermute | solution.py:71
  64.6 3.9 %collective-permute-start.14 = (f32[16,320]{1,0:T(8,128)S(1)}, f32[16,320]{1,0:T(8,128)S(1)}, u32[]{:S(2)}, u32[]{:S(2)}) collective-permute-start(f32[16,320]{1,0:T(8,128)S(1)} %get-tuple-element.44), channel_id=1, source_target_pairs={{0,96},{16,112},{32,64},{48,80},{64,32},{80,48},{96,0},{112,16},{1... | collective-permute-start | bytes 61448 | tf_op jit(solution)/shard_map/ppermute | solution.py:71
  (1 other events, 1.8 us)

commit v11 on v9

--- a/solution.py
+++ b/solution.py
@@ -21,7 +21,7 @@
 CHUNK = NCORE * WIDTH
 SLOTS = 8
 BATCHES = 128
-ROOM = 12 << 20
+ROOM = 16 << 20
 WORK = 2 * 10**10
 EVEN, ODD = pl.ds(0, NTILE, stride=2), pl.ds(1, NTILE, stride=2)
 FLOAT, HALF = jnp.float32, jnp.bfloat16
@@ -179,8 +179,8 @@
         for r, value in enumerate(swept(rows, masks)):
             smooth_ref[row_slice(r), cols] = value.astype(HALF)
     smooth = smooth_ref[...]
-    for y in range(NY):
-        cols = pl.ds(y * CHUNK, CHUNK)
+    for pair in range(0, NY, 2):
+        cols = pl.ds(pair * CHUNK, 2 * CHUNK)
         mapped = jnp.dot(smooth, map_ref[:, cols], preferred_element_type=FLOAT)
         high = mapped.astype(HALF)
         low = (mapped - high.astype(FLOAT)).astype(HALF)
@@ -191,9 +191,12 @@
         for k in range(MEMBERS_HERE):
             term = fine[k * FINE_ROWS : (k + 1) * FINE_ROWS] * perturb_ref[k, :, cols].astype(FLOAT)
             total = term if total is None else total + term
-        first, second = total[:, :WIDTH], total[:, WIDTH:]
-        mine_ref[y, :, :WIDTH] = jnp.where(core_pos == 0, first, second)
-        other_ref[y, :, :WIDTH] = jnp.where(core_pos == 0, second, first)
+        for y in range(pair, pair + 2):
+            start = (y - pair) * CHUNK
+            first = total[:, start : start + WIDTH]
+            second = total[:, start + WIDTH : start + CHUNK]
+            mine_ref[y, :, :WIDTH] = jnp.where(core_pos == 0, first, second)
+            other_ref[y, :, :WIDTH] = jnp.where(core_pos == 0, second, first)
 
 
 REGIONS = ((NY, FINE_ROWS, WIDTH), FLOAT)
@@ -215,12 +218,14 @@
     _, core_pos, _ = place()
     down_first = downward()
     total = None
-    for y in range(NY):
-        cols = pl.ds(y * CHUNK, CHUNK)
-        mine, other = mine_ref[y], other_ref[y]
-        first = jnp.where(core_pos == 0, mine, other)
-        second = jnp.where(core_pos == 0, other, mine)
-        spread = jnp.concatenate([first, second], axis=1)
+    for pair in range(0, NY, 2):
+        cols = pl.ds(pair * CHUNK, 2 * CHUNK)
+        regions = []
+        for y in range(pair, pair + 2):
+            mine, other = mine_ref[y], other_ref[y]
+            regions.append(jnp.where(core_pos == 0, mine, other))
+            regions.append(jnp.where(core_pos == 0, other, mine))
+        spread = jnp.concatenate(regions, axis=1)
         highs, lows = [], []
         for k in range(MEMBERS_HERE):
             term = perturb_ref[k, :, cols].astype(FLOAT) * spread
@@ -517,7 +522,10 @@
         forward_kernel, REGIONS, near_rows, gradient, far_rows, matrix, perturb, column_map
     )
     pieces = call(pick_kernel, (region,) * NY, (mine, swap_core(other)))
-    pieces = [pieces[0]] + [across(pieces[i], i) for i in range(1, NY)]
+    turned = pieces
+    pieces = [turned[0]]
+    for i in range(1, NY):
+        pieces.append(across(turned[i], i))
     image, sent = call(
         curve_kernel,
         (region, ((BATCHES, 128), FLOAT)),

time: 90.2 us -> 89.7 us (level)
  no operation moved by 1% of the time
where the time goes in v11:
time: 89.7 us; the launch traced here: 89.5 us
  blocking collectives  35.2 us (39%)
  starting transfers between devices  20.6 us (23%)
  waiting for transfers between devices  19 us (21%)
  Pallas kernels  13.1 us (15%)
  between operations  1.45 us (2%)
    all_to_all x1, blocking collectives, shards(): lax.all_to_all(sent, ('member', 'tile'), split_axis=0, concat_axis=0, til...  21.1 us
    all_to_all x1, blocking collectives, shards(): data = lax.all_to_all(sent, 'tile', split_axis=0, concat_axis=0, tiled=True)  14.1 us
    pallas_call x11, Pallas kernels, call(): pl.pallas_call(kernel, out_shape=tuple((jax.ShapeDtypeStruct(shape, kind)...  13.1 us
    ppermute x3, starting transfers between devices, swap_core(): return lax.ppermute(values, 'member', [(i, i ^ 1) for i in range(NMEMBER)])  7.55 us
    ppermute x6, starting transfers between devices, across(): return lax.ppermute(values, 'member', pairs)  7.41 us
    ppermute x3, waiting for transfers between devices, swap_both(): first = lax.ppermute(first_values, ('member', 'tile'), ring())  7.28 us
    ppermute x6, waiting for transfers between devices, across(): return lax.ppermute(values, 'member', pairs)  6.37 us
    ppermute x3, starting transfers between devices, swap_both(): second = lax.ppermute(second_values, ('member', 'tile'), back)  5.19 us
  transfers between devices with their start and end apart: 15, of which 12 were waited for; matrix products, arithmetic and copies ran while one was open for 0% of the time, Pallas kernels for 1%

profile of v11, /device:TPU:1, one launch (start us, length us, event | category | flops | bytes accessed | tf_op | source)
XLA Modules:
  0.0 89.5 jit_solution(4460342866985548076)
XLA Ops:
  1.3 1.7 %shard_map.140 = (f32[32,128]{1,0:T(8,128)S(1)}, f32[64,1280]{1,0:T(8,128)S(1)}, bf16[64,1280]{1,0:T(8,128)(2,1)S(1)}) custom-call(f32[8,128]{1,0:T(8,128)} %bitcast.34, f32[8,128]{1,0:T(8,128)} %bitcast.35, f32[1]{0:T(128)S(6)} %copy.16.gain_ref, f32[16,4,1280]{2,1,0:T(4,128)} %weights_hbm.1), custom_call_target="tpu_custom_call" | custom-call | flops 20000000000 | bytes 156250000 | tf_op jit(solution)/shard_map/pallas_call | solution.py:99
  3.0 2.1 %collective-permute-start.1 = (bf16[64,1280]{1,0:T(8,128)(2,1)S(1)}, bf16[64,1280]{1,0:T(8,128)(2,1)S(1)}, u32[]{:S(2)}, u32[]{:S(2)}) collective-permute-start(bf16[64,1280]{1,0:T(8,128)(2,1)S(1)} %get-tuple-element.26), channel_id=1, source_target_pairs={{1,0},{2,1},{3,2},{4,3},{5,4},{6,5},{7,6},{8,7},{9,8},{10,9},{11,1... | collective-permute-start | bytes 491528 | tf_op jit(solution)/shard_map/ppermute | solution.py:65
  5.1 14.1 %all_to_all.22 = f32[16,2,128]{2,1,0:T(2,128)S(1)} all-to-all(f32[16,2,128]{2,1,0:T(2,128)S(1)} %bitcast.29), channel_id=1, replica_groups=mesh['member'=8,'tile'=16] {'tile'}, dimensions={0} | all-to-all | bytes 32768 | tf_op jit(solution)/shard_map/all_to_all | solution.py:488
  19.3 1.9 %shard_map.141 = (f32[4,16,384]{2,1,0:T(8,128)S(1)}, f32[4,16,384]{2,1,0:T(8,128)S(1)}) custom-call(bf16[64,1280]{1,0:T(8,128)(2,1)S(1)} %collective-permute-done.a_ref, f32[64,1280]{1,0:T(8,128)S(1)} %get-tuple-element.27.own_ref, bf16[64,1280]{1,0:T(8,128)(2,1)S(1)} %collective-permute-done.1.b_ref, bf16[256,192]{1,0:T(8,128)(2,1)S(1)} %copy-done.1, ...), custom_call_target="tpu_custom_call" | custom-call | flops 1000000000 | bytes 7812500 | tf_op jit(solution)/shard_map/pallas_call | solution.py:99
  21.3 4.4 %collective-permute-start.2 = (f32[4,16,384]{2,1,0:T(8,128)S(1)}, f32[4,16,384]{2,1,0:T(8,128)S(1)}, u32[]{:S(2)}, u32[]{:S(2)}) collective-permute-start(f32[4,16,384]{2,1,0:T(8,128)S(1)} %get-tuple-element.30), channel_id=1, source_target_pairs={{0,16},{16,0},{32,48},{48,32},{64,80},{80,64},{96,112},{112,96},{1... | collective-permute-start | bytes 294920 | tf_op jit(solution)/shard_map/ppermute | solution.py:75
  25.7 0.9 %collective-permute-done.2.b_ref = f32[4,16,384]{2,1,0:T(8,128)S(1)} collective-permute-done((f32[4,16,384]{2,1,0:T(8,128)S(1)}, f32[4,16,384]{2,1,0:T(8,128)S(1)}, u32[]{:S(2)}, u32[]{:S(2)}) %collective-permute-start.2) | collective-permute-done | bytes 98336 | tf_op jit(solution)/shard_map/ppermute | solution.py:75
  26.7 2.8 %collective-permute-start.5 = (f32[4,16,384]{2,1,0:T(8,128)S(1)}, f32[4,16,384]{2,1,0:T(8,128)S(1)}, u32[]{:S(2)}, u32[]{:S(2)}) collective-permute-start(f32[4,16,384]{2,1,0:T(8,128)S(1)} %shard_map.142.a_ref), channel_id=1, source_target_pairs={{0,96},{16,112},{32,64},{48,80},{64,32},{80,48},{96,0},{112,16},{1... | collective-permute-start | bytes 294920 | tf_op jit(solution)/shard_map/ppermute | solution.py:71
  30.9 2.6 %collective-permute-done.5.d_ref = f32[4,16,384]{2,1,0:T(8,128)S(1)} collective-permute-done((f32[4,16,384]{2,1,0:T(8,128)S(1)}, f32[4,16,384]{2,1,0:T(8,128)S(1)}, u32[]{:S(2)}, u32[]{:S(2)}) %collective-permute-start.5) | collective-permute-done | bytes 98336 | tf_op jit(solution)/shard_map/ppermute | solution.py:71
  33.4 1.0 %collective-permute-done.4.c_ref = f32[4,16,384]{2,1,0:T(8,128)S(1)} collective-permute-done((f32[4,16,384]{2,1,0:T(8,128)S(1)}, f32[4,16,384]{2,1,0:T(8,128)S(1)}, u32[]{:S(2)}, u32[]{:S(2)}) %collective-permute-start.4) | collective-permute-done | bytes 98336 | tf_op jit(solution)/shard_map/ppermute | solution.py:71
  34.7 2.3 %shard_map.144 = (f32[4,16,320]{2,1,0:T(8,128)S(1)}, f32[8,128]{1,0:T(8,128)S(1)}, f32[16,320]{1,0:T(8,128)S(1)}) custom-call(f32[4,16,384]{2,1,0:T(8,128)S(1)} %shard_map.142.a_ref, f32[4,16,384]{2,1,0:T(8,128)S(1)} %collective-permute-done.3.b_ref, f32[4,16,384]{2,1,0:T(8,128)S(1)} %collective-permute-done.4.c_ref, ...), custom_call_target="tpu_custom_call" | custom-call | flops 1000000000 | bytes 7812500 | tf_op jit(solution)/shard_map/pallas_call | solution.py:99
  37.0 2.6 %collective-permute-start.6 = (f32[4,16,320]{2,1,0:T(8,128)S(1)}, f32[4,16,320]{2,1,0:T(8,128)S(1)}, u32[]{:S(2)}, u32[]{:S(2)}) collective-permute-start(f32[4,16,320]{2,1,0:T(8,128)S(1)} %get-tuple-element.33.mine_ref), channel_id=1, source_target_pairs={{0,16},{16,0},{32,48},{48,32},{64,80},{80,64},{96,112},{112,96},{1... | collective-permute-start | bytes 245768 | tf_op jit(solution)/shard_map/ppermute | solution.py:75
  39.7 0.9 %collective-permute-done.6.other_ref = f32[4,16,320]{2,1,0:T(8,128)S(1)} collective-permute-done((f32[4,16,320]{2,1,0:T(8,128)S(1)}, f32[4,16,320]{2,1,0:T(8,128)S(1)}, u32[]{:S(2)}, u32[]{:S(2)}) %collective-permute-start.6) | collective-permute-done | bytes 81952 | tf_op jit(solution)/shard_map/ppermute | solution.py:75
  40.6 2.7 %shard_map.145 = (f32[96,1280]{1,0:T(8,128)S(1)}, bf16[64,1280]{1,0:T(8,128)(2,1)S(1)}, bf16[64,1280]{1,0:T(8,128)(2,1)S(1)}) custom-call(f32[4,16,320]{2,1,0:T(8,128)S(1)} %get-tuple-element.33.mine_ref, f32[4,16,320]{2,1,0:T(8,128)S(1)} %collective-permute-done.6.other_ref, bf16[96,512]{1,0:T(8,128)(2,1)S(1)} %copy-done.2, ...), custom_call_target="tpu_custom_call" | custom-call | flops 1000000000 | bytes 7812500 | tf_op jit(solution)/shard_map/pallas_call | solution.py:99
  43.7 1.1 %collective-permute-start.8 = (bf16[64,1280]{1,0:T(8,128)(2,1)S(1)}, bf16[64,1280]{1,0:T(8,128)(2,1)S(1)}, u32[]{:S(2)}, u32[]{:S(2)}) collective-permute-start(bf16[64,1280]{1,0:T(8,128)(2,1)S(1)} %get-tuple-element.36), channel_id=1, source_target_pairs={{1,0},{2,1},{3,2},{4,3},{5,4},{6,5},{7,6},{8,7},{9,8},{10,9},{11,1... | collective-permute-start | bytes 491528 | tf_op jit(solution)/shard_map/ppermute | solution.py:65
  44.8 3.4 %collective-permute-done.7.a_ref = bf16[64,1280]{1,0:T(8,128)(2,1)S(1)} collective-permute-done((bf16[64,1280]{1,0:T(8,128)(2,1)S(1)}, bf16[64,1280]{1,0:T(8,128)(2,1)S(1)}, u32[]{:S(2)}, u32[]{:S(2)}) %collective-permute-start.7) | collective-permute-done | bytes 163872 | tf_op jit(solution)/shard_map/ppermute | solution.py:63
  48.9 2.0 %collective-permute-start.10 = (bf16[64,1280]{1,0:T(8,128)(2,1)S(1)}, bf16[64,1280]{1,0:T(8,128)(2,1)S(1)}, u32[]{:S(2)}, u32[]{:S(2)}) collective-permute-start(bf16[64,1280]{1,0:T(8,128)(2,1)S(1)} %get-tuple-element.37), channel_id=1, source_target_pairs={{1,0},{2,1},{3,2},{4,3},{5,4},{6,5},{7,6},{8,7},{9,8},{10,9},{11,1... | collective-permute-start | bytes 491528 | tf_op jit(solution)/shard_map/ppermute | solution.py:65
  50.9 2.3 %collective-permute-done.10.b_ref = bf16[64,1280]{1,0:T(8,128)(2,1)S(1)} collective-permute-done((bf16[64,1280]{1,0:T(8,128)(2,1)S(1)}, bf16[64,1280]{1,0:T(8,128)(2,1)S(1)}, u32[]{:S(2)}, u32[]{:S(2)}) %collective-permute-start.10) | collective-permute-done | bytes 163872 | tf_op jit(solution)/shard_map/ppermute | solution.py:65
  53.1 3.9 %collective-permute-done.9.a_ref = bf16[64,1280]{1,0:T(8,128)(2,1)S(1)} collective-permute-done((bf16[64,1280]{1,0:T(8,128)(2,1)S(1)}, bf16[64,1280]{1,0:T(8,128)(2,1)S(1)}, u32[]{:S(2)}, u32[]{:S(2)}) %collective-permute-start.9) | collective-permute-done | bytes 163872 | tf_op jit(solution)/shard_map/ppermute | solution.py:63
  57.1 1.9 %shard_map.147 = (f32[4,16,320]{2,1,0:T(8,128)S(1)}, f32[4,16,320]{2,1,0:T(8,128)S(1)}) custom-call(bf16[64,1280]{1,0:T(8,128)(2,1)S(1)} %collective-permute-done.9.a_ref, f32[64,1280]{1,0:T(8,128)S(1)} %get-tuple-element.38.own_ref.grad_ref, bf16[64,1280]{1,0:T(8,128)(2,1)S(1)} %collective-permute-done.10.b_ref, bf16[256,192]{1,0:T(8,128)(2,1)S(1)} %copy-done.1, ...), custom_call_target="tpu_custom_call" | custom-call | flops 1000000000 | bytes 7812500 | tf_op jit(solution)/shard_map/pallas_call | solution.py:99
  60.6 2.5 %collective-permute-start.13 = (f32[16,320]{1,0:T(8,128)S(1)}, f32[16,320]{1,0:T(8,128)S(1)}, u32[]{:S(2)}, u32[]{:S(2)}) collective-permute-start(f32[16,320]{1,0:T(8,128)S(1)} %get-tuple-element.43), channel_id=1, source_target_pairs={{0,64},{16,80},{32,96},{48,112},{64,0},{80,16},{96,32},{112,48},{1... | collective-permute-start | bytes 61448 | tf_op jit(solution)/shard_map/ppermute | solution.py:71
  63.1 1.3 %collective-permute-start.14 = (f32[16,320]{1,0:T(8,128)S(1)}, f32[16,320]{1,0:T(8,128)S(1)}, u32[]{:S(2)}, u32[]{:S(2)}) collective-permute-start(f32[16,320]{1,0:T(8,128)S(1)} %get-tuple-element.44), channel_id=1, source_target_pairs={{0,96},{16,112},{32,64},{48,80},{64,32},{80,48},{96,0},{112,16},{1... | collective-permute-start | bytes 61448 | tf_op jit(solution)/shard_map/ppermute | solution.py:71
  64.8 2.1 %collective-permute-done.14.d_ref = f32[16,320]{1,0:T(8,128)S(1)} collective-permute-done((f32[16,320]{1,0:T(8,128)S(1)}, f32[16,320]{1,0:T(8,128)S(1)}, u32[]{:S(2)}, u32[]{:S(2)}) %collective-permute-start.14) | collective-permute-done | bytes 20512 | tf_op jit(solution)/shard_map/ppermute | solution.py:71
  67.4 21.1 %all_to_all.23 = f32[128,1,128]{2,1,0:T(1,128)S(1)} all-to-all(f32[128,1,128]{2,1,0:T(1,128)S(1)} %bitcast.27), channel_id=1, replica_groups=mesh['member'=8,'tile'=16] {'member','tile'}, dimensions={0} | all-to-all | bytes 131072 | tf_op jit(solution)/shard_map/all_to_all | solution.py:534
  88.5 1.0 %shard_map.150 = (f32[16,4,1280]{2,1,0:T(4,128)}, f32[16,320]{1,0:T(8,128)}) custom-call(f32[128,128]{1,0:T(8,128)S(1)} %bitcast.28, f32[64,1280]{1,0:T(8,128)S(1)} %get-tuple-element.27.own_ref, f32[64,1280]{1,0:T(8,128)S(1)} %get-tuple-element.38.own_ref.grad_ref, f32[16,320]{1,0:T(8,128)S(1)} %get-tuple-element.48.full_ref, f32[16,320]{1,0:T(8,128)S(1)} %copy-done.6, ...), custom_call_target="tpu_custom_call" | custom-call | flops 1000000000 | bytes 7812500 | tf_op jit(solution)/shard_map/pallas_call | solution.py:99
  (40 shorter events, 5.2 us)
Async XLA Ops:
  1.3 18.0 %slice-start = ((s8[6553600]{0:T(1024)(128)(4,1)}), s8[4194304]{0:T(1024)(128)(4,1)S(1)}, s32[]{:S(2)}) async-start(s8[6553600]{0:T(1024)(128)(4,1)} %bitcast.24), calls=%async_computation.2 | async-start | bytes 8388608
  1.3 18.0 %slice-start.1 = ((s8[6553600]{0:T(1024)(128)(4,1)}), s8[2359296]{0:T(1024)(128)(4,1)S(1)}, s32[]{:S(2)}) async-start(s8[6553600]{0:T(1024)(128)(4,1)} %bitcast.24), calls=%async_computation.3 | async-start | bytes 4718592
  1.3 18.0 %copy-start = (bf16[16,16,2560]{2,1,0:T(8,128)(2,1)S(1)}, bf16[16,16,2560]{2,1,0:T(8,128)(2,1)}, u32[]{:S(2)}) copy-start(bf16[16,16,2560]{2,1,0:T(8,128)(2,1)} %perturb_ref.5) | copy-start | bytes 3932164
  1.3 18.0 %copy-start.1 = (bf16[256,192]{1,0:T(8,128)(2,1)S(1)}, bf16[256,192]{1,0:T(8,128)(2,1)}, u32[]{:S(2)}) copy-start(bf16[256,192]{1,0:T(8,128)(2,1)} %constant.4.clone.refine_ref) | copy-start | bytes 294916
  3.0 16.2 %collective-permute-start.1 = (bf16[64,1280]{1,0:T(8,128)(2,1)S(1)}, bf16[64,1280]{1,0:T(8,128)(2,1)S(1)}, u32[]{:S(2)}, u32[]{:S(2)}) collective-permute-start(bf16[64,1280]{1,0:T(8,128)(2,1)S(1)} %get-tuple-element.26), channel_id=1, source_target_pairs={{1,0},{2,1},{3,2},{4,3},{5,4},{6,5},{7,6},{8,7},{9,8},{10,9},{11,1... | collective-permute-start | bytes 491528 | tf_op jit(solution)/shard_map/ppermute | solution.py:65
  5.1 14.1 %collective-permute-start = (bf16[64,1280]{1,0:T(8,128)(2,1)S(1)}, bf16[64,1280]{1,0:T(8,128)(2,1)S(1)}, u32[]{:S(2)}, u32[]{:S(2)}) collective-permute-start(bf16[64,1280]{1,0:T(8,128)(2,1)S(1)} %get-tuple-element.26), channel_id=1, source_target_pairs={{0,1},{1,2},{2,3},{3,4},{4,5},{5,6},{6,7},{7,8},{8,9},{9,10},{10,1... | collective-permute-start | bytes 491528 | tf_op jit(solution)/shard_map/ppermute | solution.py:63
  21.2 8.9 %copy-start.3 = (s32[1,128,8,8]{1,3,2,0:T(8,128)S(1)}, s32[1,128,8,8]{1,3,2,0:T(8,128)}, u32[]{:S(2)}) copy-start(s32[1,128,8,8]{1,3,2,0:T(8,128)} %param.17) | copy-start | bytes 98308
  21.2 8.9 %copy-start.4 = (f32[1,128,8,8]{1,3,2,0:T(8,128)S(1)}, f32[1,128,8,8]{1,3,2,0:T(8,128)}, u32[]{:S(2)}) copy-start(f32[1,128,8,8]{1,3,2,0:T(8,128)} %param.18) | copy-start | bytes 98308
  21.2 8.9 %copy-start.5 = (f32[1,128,8,8]{1,3,2,0:T(8,128)S(1)}, f32[1,128,8,8]{1,3,2,0:T(8,128)}, u32[]{:S(2)}) copy-start(f32[1,128,8,8]{1,3,2,0:T(8,128)} %param.19) | copy-start | bytes 98308
  21.3 5.4 %collective-permute-start.2 = (f32[4,16,384]{2,1,0:T(8,128)S(1)}, f32[4,16,384]{2,1,0:T(8,128)S(1)}, u32[]{:S(2)}, u32[]{:S(2)}) collective-permute-start(f32[4,16,384]{2,1,0:T(8,128)S(1)} %get-tuple-element.30), channel_id=1, source_target_pairs={{0,16},{16,0},{32,48},{48,32},{64,80},{80,64},{96,112},{112,96},{1... | collective-permute-start | bytes 294920 | tf_op jit(solution)/shard_map/ppermute | solution.py:75
  26.6 8.0 %copy-start.7 = (s32[1,128,8]{1,2,0:T(8,128)S(1)}, s32[1,128,8]{1,2,0:T(8,128)}, u32[]{:S(2)}) copy-start(s32[1,128,8]{1,2,0:T(8,128)} %param.20) | copy-start | bytes 12292
  26.7 6.8 %collective-permute-start.5 = (f32[4,16,384]{2,1,0:T(8,128)S(1)}, f32[4,16,384]{2,1,0:T(8,128)S(1)}, u32[]{:S(2)}, u32[]{:S(2)}) collective-permute-start(f32[4,16,384]{2,1,0:T(8,128)S(1)} %shard_map.142.a_ref), channel_id=1, source_target_pairs={{0,96},{16,112},{32,64},{48,80},{64,32},{80,48},{96,0},{112,16},{1... | collective-permute-start | bytes 294920 | tf_op jit(solution)/shard_map/ppermute | solution.py:71
  29.5 5.0 %collective-permute-start.4 = (f32[4,16,384]{2,1,0:T(8,128)S(1)}, f32[4,16,384]{2,1,0:T(8,128)S(1)}, u32[]{:S(2)}, u32[]{:S(2)}) collective-permute-start(f32[4,16,384]{2,1,0:T(8,128)S(1)} %shard_map.142.a_ref), channel_id=1, source_target_pairs={{0,64},{16,80},{32,96},{48,112},{64,0},{80,16},{96,32},{112,48},{1... | collective-permute-start | bytes 294920 | tf_op jit(solution)/shard_map/ppermute | solution.py:71
  29.8 4.9 %collective-permute-start.3 = (f32[4,16,384]{2,1,0:T(8,128)S(1)}, f32[4,16,384]{2,1,0:T(8,128)S(1)}, u32[]{:S(2)}, u32[]{:S(2)}) collective-permute-start(f32[4,16,384]{2,1,0:T(8,128)S(1)} %shard_map.142.a_ref), channel_id=1, source_target_pairs={{0,32},{16,48},{32,0},{48,16},{64,96},{80,112},{96,64},{112,80},{1... | collective-permute-start | bytes 294920 | tf_op jit(solution)/shard_map/ppermute | solution.py:71
  30.9 9.7 %copy-start.2 = (bf16[96,512]{1,0:T(8,128)(2,1)S(1)}, bf16[96,512]{1,0:T(8,128)(2,1)}, u32[]{:S(2)}) copy-start(bf16[96,512]{1,0:T(8,128)(2,1)} %constant.5.clone.back_ref) | copy-start | bytes 294916
  37.0 3.6 %collective-permute-start.6 = (f32[4,16,320]{2,1,0:T(8,128)S(1)}, f32[4,16,320]{2,1,0:T(8,128)S(1)}, u32[]{:S(2)}, u32[]{:S(2)}) collective-permute-start(f32[4,16,320]{2,1,0:T(8,128)S(1)} %get-tuple-element.33.mine_ref), channel_id=1, source_target_pairs={{0,16},{16,0},{32,48},{48,32},{64,80},{80,64},{96,112},{112,96},{1... | collective-permute-start | bytes 245768 | tf_op jit(solution)/shard_map/ppermute | solution.py:75
  43.3 4.9 %collective-permute-start.7 = (bf16[64,1280]{1,0:T(8,128)(2,1)S(1)}, bf16[64,1280]{1,0:T(8,128)(2,1)S(1)}, u32[]{:S(2)}, u32[]{:S(2)}) collective-permute-start(bf16[64,1280]{1,0:T(8,128)(2,1)S(1)} %get-tuple-element.34), channel_id=1, source_target_pairs={{0,1},{1,2},{2,3},{3,4},{4,5},{5,6},{6,7},{7,8},{8,9},{9,10},{10,1... | collective-permute-start | bytes 491528 | tf_op jit(solution)/shard_map/ppermute | solution.py:63
  43.7 4.8 %collective-permute-start.8 = (bf16[64,1280]{1,0:T(8,128)(2,1)S(1)}, bf16[64,1280]{1,0:T(8,128)(2,1)S(1)}, u32[]{:S(2)}, u32[]{:S(2)}) collective-permute-start(bf16[64,1280]{1,0:T(8,128)(2,1)S(1)} %get-tuple-element.36), channel_id=1, source_target_pairs={{1,0},{2,1},{3,2},{4,3},{5,4},{6,5},{7,6},{8,7},{9,8},{10,9},{11,1... | collective-permute-start | bytes 491528 | tf_op jit(solution)/shard_map/ppermute | solution.py:65
  48.9 4.2 %collective-permute-start.10 = (bf16[64,1280]{1,0:T(8,128)(2,1)S(1)}, bf16[64,1280]{1,0:T(8,128)(2,1)S(1)}, u32[]{:S(2)}, u32[]{:S(2)}) collective-permute-start(bf16[64,1280]{1,0:T(8,128)(2,1)S(1)} %get-tuple-element.37), channel_id=1, source_target_pairs={{1,0},{2,1},{3,2},{4,3},{5,4},{6,5},{7,6},{8,7},{9,8},{10,9},{11,1... | collective-permute-start | bytes 491528 | tf_op jit(solution)/shard_map/ppermute | solution.py:65
  50.9 6.2 %collective-permute-start.9 = (bf16[64,1280]{1,0:T(8,128)(2,1)S(1)}, bf16[64,1280]{1,0:T(8,128)(2,1)S(1)}, u32[]{:S(2)}, u32[]{:S(2)}) collective-permute-start(bf16[64,1280]{1,0:T(8,128)(2,1)S(1)} %get-tuple-element.37), channel_id=1, source_target_pairs={{0,1},{1,2},{2,3},{3,4},{4,5},{5,6},{6,7},{7,8},{8,9},{9,10},{10,1... | collective-permute-start | bytes 491528 | tf_op jit(solution)/shard_map/ppermute | solution.py:63
  59.0 1.4 %collective-permute-start.11 = (f32[4,16,320]{2,1,0:T(8,128)S(1)}, f32[4,16,320]{2,1,0:T(8,128)S(1)}, u32[]{:S(2)}, u32[]{:S(2)}) collective-permute-start(f32[4,16,320]{2,1,0:T(8,128)S(1)} %get-tuple-element.40), channel_id=1, source_target_pairs={{0,16},{16,0},{32,48},{48,32},{64,80},{80,64},{96,112},{112,96},{1... | collective-permute-start | bytes 245768 | tf_op jit(solution)/shard_map/ppermute | solution.py:75
  60.5 3.9 %collective-permute-start.12 = (f32[16,320]{1,0:T(8,128)S(1)}, f32[16,320]{1,0:T(8,128)S(1)}, u32[]{:S(2)}, u32[]{:S(2)}) collective-permute-start(f32[16,320]{1,0:T(8,128)S(1)} %get-tuple-element.42), channel_id=1, source_target_pairs={{0,32},{16,48},{32,0},{48,16},{64,96},{80,112},{96,64},{112,80},{1... | collective-permute-start | bytes 61448 | tf_op jit(solution)/shard_map/ppermute | solution.py:71
  60.6 4.3 %collective-permute-start.13 = (f32[16,320]{1,0:T(8,128)S(1)}, f32[16,320]{1,0:T(8,128)S(1)}, u32[]{:S(2)}, u32[]{:S(2)}) collective-permute-start(f32[16,320]{1,0:T(8,128)S(1)} %get-tuple-element.43), channel_id=1, source_target_pairs={{0,64},{16,80},{32,96},{48,112},{64,0},{80,16},{96,32},{112,48},{1... | collective-permute-start | bytes 61448 | tf_op jit(solution)/shard_map/ppermute | solution.py:71
  63.1 3.9 %collective-permute-start.14 = (f32[16,320]{1,0:T(8,128)S(1)}, f32[16,320]{1,0:T(8,128)S(1)}, u32[]{:S(2)}, u32[]{:S(2)}) collective-permute-start(f32[16,320]{1,0:T(8,128)S(1)} %get-tuple-element.44), channel_id=1, source_target_pairs={{0,96},{16,112},{32,64},{48,80},{64,32},{80,48},{96,0},{112,16},{1... | collective-permute-start | bytes 61448 | tf_op jit(solution)/shard_map/ppermute | solution.py:71
  (1 other events, 7.4 us)

commit v12 on v10

--- a/solution.py
+++ b/solution.py
@@ -21,7 +21,7 @@
 CHUNK = NCORE * WIDTH
 SLOTS = 8
 BATCHES = 128
-ROOM = 12 << 20
+ROOM = 16 << 20
 WORK = 2 * 10**10
 EVEN, ODD = pl.ds(0, NTILE, stride=2), pl.ds(1, NTILE, stride=2)
 FLOAT, HALF = jnp.float32, jnp.bfloat16
@@ -164,19 +164,24 @@
 
 def regions_of(smooth_ref, refine_ref, perturb_ref, map_ref, parity, out_ref):
     smooth = smooth_ref[...]
-    for y in range(NY):
-        cols = window(parity, y)
-        mapped = jnp.dot(smooth, map_ref[:, cols], preferred_element_type=FLOAT)
+    for pair in range(0, NY, 2):
+        windows = [window(parity, y) for y in (pair, pair + 1)]
+        columns = jnp.concatenate([map_ref[:, cols] for cols in windows], axis=1)
+        mapped = jnp.dot(smooth, columns, preferred_element_type=FLOAT)
         high = mapped.astype(HALF)
         low = (mapped - high.astype(FLOAT)).astype(HALF)
         fine = jnp.dot(
             refine_ref[...], jnp.concatenate([high, low], axis=0), preferred_element_type=FLOAT
         )
-        total = None
-        for k in range(MEMBERS_HERE):
-            term = fine[k * FINE_ROWS : (k + 1) * FINE_ROWS] * perturb_ref[k, :, cols].astype(FLOAT)
-            total = term if total is None else total + term
-        out_ref[y, :, :WIDTH] = jnp.where(parity == 0, total[:, :WIDTH], total[:, 384 - WIDTH :])
+        for half, cols in enumerate(windows):
+            total = None
+            for k in range(MEMBERS_HERE):
+                term = fine[k * FINE_ROWS : (k + 1) * FINE_ROWS, half * 384 : (half + 1) * 384]
+                term = term * perturb_ref[k, :, cols].astype(FLOAT)
+                total = term if total is None else total + term
+            out_ref[pair + half, :, :WIDTH] = jnp.where(
+                parity == 0, total[:, :WIDTH], total[:, 384 - WIDTH :]
+            )
 
 
 def other_kernel(a_ref, own_ref, b_ref, refine_ref, perturb_ref, map_ref, *refs):
@@ -223,27 +228,31 @@
 
 def pulled_part(values_ref, back_ref, perturb_ref, map_ref, parity):
     total = None
-    for y in range(NY):
-        cols = window(parity, y)
-        values = values_ref[y]
-        rest = jnp.zeros((FINE_ROWS, 384 - WIDTH), FLOAT)
-        spread = jnp.where(
-            parity == 0,
-            jnp.concatenate([values, rest], axis=1),
-            jnp.concatenate([rest, values], axis=1),
-        )
-        highs, lows = [], []
-        for k in range(MEMBERS_HERE):
-            term = perturb_ref[k, :, cols].astype(FLOAT) * spread
-            high = term.astype(HALF)
-            highs.append(high)
-            lows.append((term - high.astype(FLOAT)).astype(HALF))
+    for pair in range(0, NY, 2):
+        windows = [window(parity, y) for y in (pair, pair + 1)]
+        columns = jnp.concatenate([map_ref[:, cols] for cols in windows], axis=1)
+        pulled = []
+        for y, cols in zip((pair, pair + 1), windows):
+            values = values_ref[y]
+            rest = jnp.zeros((FINE_ROWS, 384 - WIDTH), FLOAT)
+            spread = jnp.where(
+                parity == 0,
+                jnp.concatenate([values, rest], axis=1),
+                jnp.concatenate([rest, values], axis=1),
+            )
+            highs, lows = [], []
+            for k in range(MEMBERS_HERE):
+                term = perturb_ref[k, :, cols].astype(FLOAT) * spread
+                high = term.astype(HALF)
+                highs.append(high)
+                lows.append((term - high.astype(FLOAT)).astype(HALF))
+            pulled.append(jnp.concatenate(highs + lows, axis=0))
         pulled = jnp.dot(
-            back_ref[...], jnp.concatenate(highs + lows, axis=0), preferred_element_type=FLOAT
+            back_ref[...], jnp.concatenate(pulled, axis=1), preferred_element_type=FLOAT
         )
         part = lax.dot_general(
             pulled.astype(HALF),
-            map_ref[:, cols],
+            columns,
             (((1,), (1,)), ((), ())),
             preferred_element_type=FLOAT,
         )

time: 90.9 us -> 88.8 us (0.977)
  Pallas kernels: 17.7 us -> 15.8 us
    pallas_call x14, Pallas kernels: 17.7 us -> 15.8 us  [call(): pl.pallas_call(kernel, out_shape=tuple((jax.ShapeDtypeStruct(shape, kind)...]
  transfers between devices with their start and end apart: 15 -> 15, of which waited for: 7 -> 7; matrix products, arithmetic and copies ran while one was open for 0% -> 0% of each run, Pallas kernels for 7% -> 6%
where the time goes in v12:
time: 88.8 us; the launch traced here: 88.6 us
  blocking collectives  34.9 us (39%)
  starting transfers between devices  20.1 us (23%)
  waiting for transfers between devices  16.3 us (18%)
  Pallas kernels  15.8 us (18%)
  between operations  1.47 us (2%)
    all_to_all x1, blocking collectives, shards(): lax.all_to_all(sent, ('member', 'tile'), split_axis=0, concat_axis=0, til...  20.9 us
    pallas_call x14, Pallas kernels, call(): pl.pallas_call(kernel, out_shape=tuple((jax.ShapeDtypeStruct(shape, kind)...  15.8 us
    all_to_all x1, blocking collectives, shards(): data = lax.all_to_all(sent, 'tile', split_axis=0, concat_axis=0, tiled=True)  14.1 us
    ppermute x6, starting transfers between devices, across(): return lax.ppermute(values, 'member', pairs)  7.42 us
    ppermute x3, waiting for transfers between devices, swap_both(): first = lax.ppermute(first_values, ('member', 'tile'), ring())  7.28 us
    ppermute x3, starting transfers between devices, swap_core(): return lax.ppermute(values, 'member', [(i, i ^ 1) for i in range(NMEMBER)])  7.22 us
    ppermute x6, waiting for transfers between devices, across(): return lax.ppermute(values, 'member', pairs)  6.96 us
    ppermute x3, starting transfers between devices, swap_both(): second = lax.ppermute(second_values, ('member', 'tile'), back)  5.15 us
  transfers between devices with their start and end apart: 15, of which 7 were waited for; matrix products, arithmetic and copies ran while one was open for 0% of the time, Pallas kernels for 6%

profile of v12, /device:TPU:1, one launch (start us, length us, event | category | flops | bytes accessed | tf_op | source)
XLA Modules:
  0.0 88.6 jit_solution(11689136895940971439)
XLA Ops:
  1.3 1.7 %shard_map.140 = (f32[32,128]{1,0:T(8,128)S(1)}, f32[64,1280]{1,0:T(8,128)S(1)}, bf16[64,1280]{1,0:T(8,128)(2,1)S(1)}) custom-call(f32[8,128]{1,0:T(8,128)} %bitcast.35, f32[8,128]{1,0:T(8,128)} %bitcast.36, f32[1]{0:T(128)S(6)} %copy.16.gain_ref, f32[16,4,1280]{2,1,0:T(4,128)} %weights_hbm.1), custom_call_target="tpu_custom_call" | custom-call | flops 20000000000 | bytes 156250000 | tf_op jit(solution)/shard_map/pallas_call | solution.py:99
  3.0 2.1 %collective-permute-start.1 = (bf16[64,1280]{1,0:T(8,128)(2,1)S(1)}, bf16[64,1280]{1,0:T(8,128)(2,1)S(1)}, u32[]{:S(2)}, u32[]{:S(2)}) collective-permute-start(bf16[64,1280]{1,0:T(8,128)(2,1)S(1)} %get-tuple-element.26), channel_id=1, source_target_pairs={{1,0},{2,1},{3,2},{4,3},{5,4},{6,5},{7,6},{8,7},{9,8},{10,9},{11,1... | collective-permute-start | bytes 491528 | tf_op jit(solution)/shard_map/ppermute | solution.py:65
  5.1 14.1 %all_to_all.22 = f32[16,2,128]{2,1,0:T(2,128)S(1)} all-to-all(f32[16,2,128]{2,1,0:T(2,128)S(1)} %bitcast.30), channel_id=1, replica_groups=mesh['member'=8,'tile'=16] {'tile'}, dimensions={0} | all-to-all | bytes 32768 | tf_op jit(solution)/shard_map/all_to_all | solution.py:516
  19.3 1.6 %shard_map.141 = (f32[4,16,384]{2,1,0:T(8,128)S(1)}, bf16[96,1280]{1,0:T(8,128)(2,1)S(1)}) custom-call(bf16[64,1280]{1,0:T(8,128)(2,1)S(1)} %collective-permute-done.a_ref, f32[64,1280]{1,0:T(8,128)S(1)} %get-tuple-element.27.own_ref, bf16[64,1280]{1,0:T(8,128)(2,1)S(1)} %collective-permute-done.1.b_ref, bf16[256,192]{1,0:T(8,128)(2,1)S(1)} %copy-done.1, ...), custom_call_target="tpu_custom_call" | custom-call | flops 1000000000 | bytes 7812500 | tf_op jit(solution)/shard_map/pallas_call | solution.py:99
  20.9 4.4 %collective-permute-start.2 = (f32[4,16,384]{2,1,0:T(8,128)S(1)}, f32[4,16,384]{2,1,0:T(8,128)S(1)}, u32[]{:S(2)}, u32[]{:S(2)}) collective-permute-start(f32[4,16,384]{2,1,0:T(8,128)S(1)} %get-tuple-element.30), channel_id=1, source_target_pairs={{0,16},{16,0},{32,48},{48,32},{64,80},{80,64},{96,112},{112,96},{1... | collective-permute-start | bytes 294920 | tf_op jit(solution)/shard_map/ppermute | solution.py:75
  25.3 1.3 %shard_map.142.a_ref = f32[4,16,384]{2,1,0:T(8,128)S(1)} custom-call(bf16[96,1280]{1,0:T(8,128)(2,1)S(1)} %get-tuple-element.29.smooth_ref, bf16[256,192]{1,0:T(8,128)(2,1)S(1)} %copy-done.1, bf16[16,16,2560]{2,1,0:T(8,128)(2,1)S(1)} %copy-done, bf16[1280,2560]{1,0:T(8,128)(2,1)S(1)} %bitcast.25, f32[32,128]{1,0:T(8,128)S(1)} %bitcast.27), custom_call_target="tpu_custom_call" | custom-call | flops 1000000000 | bytes 7812500 | tf_op jit(solution)/shard_map/pallas_call | solution.py:99
  26.6 2.8 %collective-permute-start.5 = (f32[4,16,384]{2,1,0:T(8,128)S(1)}, f32[4,16,384]{2,1,0:T(8,128)S(1)}, u32[]{:S(2)}, u32[]{:S(2)}) collective-permute-start(f32[4,16,384]{2,1,0:T(8,128)S(1)} %shard_map.143.a_ref), channel_id=1, source_target_pairs={{0,96},{16,112},{32,64},{48,80},{64,32},{80,48},{96,0},{112,16},{1... | collective-permute-start | bytes 294920 | tf_op jit(solution)/shard_map/ppermute | solution.py:71
  30.8 2.7 %collective-permute-done.5.d_ref = f32[4,16,384]{2,1,0:T(8,128)S(1)} collective-permute-done((f32[4,16,384]{2,1,0:T(8,128)S(1)}, f32[4,16,384]{2,1,0:T(8,128)S(1)}, u32[]{:S(2)}, u32[]{:S(2)}) %collective-permute-start.5) | collective-permute-done | bytes 98336 | tf_op jit(solution)/shard_map/ppermute | solution.py:71
  33.5 1.4 %collective-permute-done.4.c_ref = f32[4,16,384]{2,1,0:T(8,128)S(1)} collective-permute-done((f32[4,16,384]{2,1,0:T(8,128)S(1)}, f32[4,16,384]{2,1,0:T(8,128)S(1)}, u32[]{:S(2)}, u32[]{:S(2)}) %collective-permute-start.4) | collective-permute-done | bytes 98336 | tf_op jit(solution)/shard_map/ppermute | solution.py:71
  35.0 2.3 %shard_map.145 = (f32[4,16,320]{2,1,0:T(8,128)S(1)}, f32[8,128]{1,0:T(8,128)S(1)}, f32[16,320]{1,0:T(8,128)S(1)}) custom-call(f32[4,16,384]{2,1,0:T(8,128)S(1)} %shard_map.143.a_ref, f32[4,16,384]{2,1,0:T(8,128)S(1)} %collective-permute-done.3.b_ref, f32[4,16,384]{2,1,0:T(8,128)S(1)} %collective-permute-done.4.c_ref, ...), custom_call_target="tpu_custom_call" | custom-call | flops 1000000000 | bytes 7812500 | tf_op jit(solution)/shard_map/pallas_call | solution.py:99
  37.3 2.0 %collective-permute-start.6 = (f32[4,16,320]{2,1,0:T(8,128)S(1)}, f32[4,16,320]{2,1,0:T(8,128)S(1)}, u32[]{:S(2)}, u32[]{:S(2)}) collective-permute-start(f32[4,16,320]{2,1,0:T(8,128)S(1)} %get-tuple-element.33.mine_ref), channel_id=1, source_target_pairs={{0,16},{16,0},{32,48},{48,32},{64,80},{80,64},{96,112},{112,96},{1... | collective-permute-start | bytes 245768 | tf_op jit(solution)/shard_map/ppermute | solution.py:75
  39.3 1.7 %shard_map.146.mine_ref = f32[96,1280]{1,0:T(8,128)S(1)} custom-call(f32[4,16,320]{2,1,0:T(8,128)S(1)} %get-tuple-element.33.mine_ref, bf16[96,512]{1,0:T(8,128)(2,1)S(1)} %copy-done.2, bf16[16,16,2560]{2,1,0:T(8,128)(2,1)S(1)} %copy-done, bf16[1280,2560]{1,0:T(8,128)(2,1)S(1)} %bitcast.25), custom_call_target="tpu_custom_call" | custom-call | flops 1000000000 | bytes 7812500 | tf_op jit(solution)/shard_map/pallas_call | solution.py:99
  41.1 1.7 %shard_map.147 = (f32[96,1280]{1,0:T(8,128)S(1)}, bf16[64,1280]{1,0:T(8,128)(2,1)S(1)}, bf16[64,1280]{1,0:T(8,128)(2,1)S(1)}) custom-call(f32[96,1280]{1,0:T(8,128)S(1)} %shard_map.146.mine_ref, f32[4,16,320]{2,1,0:T(8,128)S(1)} %collective-permute-done.6.other_ref, bf16[96,512]{1,0:T(8,128)(2,1)S(1)} %copy-done.2, bf16[16,16,2560]{2,1,0:T(8,128)(2,1)S(1)} %copy-done, ...), custom_call_target="tpu_custom_call" | custom-call | flops 1000000000 | bytes 7812500 | tf_op jit(solution)/shard_map/pallas_call | solution.py:99
  42.9 1.4 %collective-permute-start.8 = (bf16[64,1280]{1,0:T(8,128)(2,1)S(1)}, bf16[64,1280]{1,0:T(8,128)(2,1)S(1)}, u32[]{:S(2)}, u32[]{:S(2)}) collective-permute-start(bf16[64,1280]{1,0:T(8,128)(2,1)S(1)} %get-tuple-element.36), channel_id=1, source_target_pairs={{1,0},{2,1},{3,2},{4,3},{5,4},{6,5},{7,6},{8,7},{9,8},{10,9},{11,1... | collective-permute-start | bytes 491528 | tf_op jit(solution)/shard_map/ppermute | solution.py:65
  44.4 3.7 %collective-permute-done.7.a_ref = bf16[64,1280]{1,0:T(8,128)(2,1)S(1)} collective-permute-done((bf16[64,1280]{1,0:T(8,128)(2,1)S(1)}, bf16[64,1280]{1,0:T(8,128)(2,1)S(1)}, u32[]{:S(2)}, u32[]{:S(2)}) %collective-permute-start.7) | collective-permute-done | bytes 163872 | tf_op jit(solution)/shard_map/ppermute | solution.py:63
  48.5 1.6 %collective-permute-start.10 = (bf16[64,1280]{1,0:T(8,128)(2,1)S(1)}, bf16[64,1280]{1,0:T(8,128)(2,1)S(1)}, u32[]{:S(2)}, u32[]{:S(2)}) collective-permute-start(bf16[64,1280]{1,0:T(8,128)(2,1)S(1)} %get-tuple-element.37), channel_id=1, source_target_pairs={{1,0},{2,1},{3,2},{4,3},{5,4},{6,5},{7,6},{8,7},{9,8},{10,9},{11,1... | collective-permute-start | bytes 491528 | tf_op jit(solution)/shard_map/ppermute | solution.py:65
  50.3 2.1 %collective-permute-done.10.b_ref = bf16[64,1280]{1,0:T(8,128)(2,1)S(1)} collective-permute-done((bf16[64,1280]{1,0:T(8,128)(2,1)S(1)}, bf16[64,1280]{1,0:T(8,128)(2,1)S(1)}, u32[]{:S(2)}, u32[]{:S(2)}) %collective-permute-start.10) | collective-permute-done | bytes 163872 | tf_op jit(solution)/shard_map/ppermute | solution.py:65
  52.3 3.6 %collective-permute-done.9.a_ref = bf16[64,1280]{1,0:T(8,128)(2,1)S(1)} collective-permute-done((bf16[64,1280]{1,0:T(8,128)(2,1)S(1)}, bf16[64,1280]{1,0:T(8,128)(2,1)S(1)}, u32[]{:S(2)}, u32[]{:S(2)}) %collective-permute-start.9) | collective-permute-done | bytes 163872 | tf_op jit(solution)/shard_map/ppermute | solution.py:63
  55.9 1.6 %shard_map.149 = (f32[4,16,320]{2,1,0:T(8,128)S(1)}, bf16[96,1280]{1,0:T(8,128)(2,1)S(1)}) custom-call(bf16[64,1280]{1,0:T(8,128)(2,1)S(1)} %collective-permute-done.9.a_ref, f32[64,1280]{1,0:T(8,128)S(1)} %get-tuple-element.38.own_ref.grad_ref, bf16[64,1280]{1,0:T(8,128)(2,1)S(1)} %collective-permute-done.10.b_ref, bf16[256,192]{1,0:T(8,128)(2,1)S(1)} %copy-done.1, ...), custom_call_target="tpu_custom_call" | custom-call | flops 1000000000 | bytes 7812500 | tf_op jit(solution)/shard_map/pallas_call | solution.py:99
  58.3 1.3 %shard_map.150.a_ref = f32[4,16,320]{2,1,0:T(8,128)S(1)} custom-call(bf16[96,1280]{1,0:T(8,128)(2,1)S(1)} %get-tuple-element.39.smooth_ref, bf16[256,192]{1,0:T(8,128)(2,1)S(1)} %copy-done.1, bf16[16,16,2560]{2,1,0:T(8,128)(2,1)S(1)} %copy-done, bf16[1280,2560]{1,0:T(8,128)(2,1)S(1)} %bitcast.25), custom_call_target="tpu_custom_call" | custom-call | flops 1000000000 | bytes 7812500 | tf_op jit(solution)/shard_map/pallas_call | solution.py:99
  59.9 2.6 %collective-permute-start.13 = (f32[16,320]{1,0:T(8,128)S(1)}, f32[16,320]{1,0:T(8,128)S(1)}, u32[]{:S(2)}, u32[]{:S(2)}) collective-permute-start(f32[16,320]{1,0:T(8,128)S(1)} %get-tuple-element.43), channel_id=1, source_target_pairs={{0,64},{16,80},{32,96},{48,112},{64,0},{80,16},{96,32},{112,48},{1... | collective-permute-start | bytes 61448 | tf_op jit(solution)/shard_map/ppermute | solution.py:71
  62.5 1.1 %collective-permute-start.14 = (f32[16,320]{1,0:T(8,128)S(1)}, f32[16,320]{1,0:T(8,128)S(1)}, u32[]{:S(2)}, u32[]{:S(2)}) collective-permute-start(f32[16,320]{1,0:T(8,128)S(1)} %get-tuple-element.44), channel_id=1, source_target_pairs={{0,96},{16,112},{32,64},{48,80},{64,32},{80,48},{96,0},{112,16},{1... | collective-permute-start | bytes 61448 | tf_op jit(solution)/shard_map/ppermute | solution.py:71
  64.3 2.1 %collective-permute-done.14.d_ref = f32[16,320]{1,0:T(8,128)S(1)} collective-permute-done((f32[16,320]{1,0:T(8,128)S(1)}, f32[16,320]{1,0:T(8,128)S(1)}, u32[]{:S(2)}, u32[]{:S(2)}) %collective-permute-start.14) | collective-permute-done | bytes 20512 | tf_op jit(solution)/shard_map/ppermute | solution.py:71
  66.8 20.9 %all_to_all.23 = f32[128,1,128]{2,1,0:T(1,128)S(1)} all-to-all(f32[128,1,128]{2,1,0:T(1,128)S(1)} %bitcast.28), channel_id=1, replica_groups=mesh['member'=8,'tile'=16] {'member','tile'}, dimensions={0} | all-to-all | bytes 131072 | tf_op jit(solution)/shard_map/all_to_all | solution.py:558
  (43 shorter events, 5.3 us)
Async XLA Ops:
  1.3 18.0 %slice-start = ((s8[6553600]{0:T(1024)(128)(4,1)}), s8[4194304]{0:T(1024)(128)(4,1)S(1)}, s32[]{:S(2)}) async-start(s8[6553600]{0:T(1024)(128)(4,1)} %bitcast.24), calls=%async_computation.2 | async-start | bytes 8388608
  1.3 18.0 %slice-start.1 = ((s8[6553600]{0:T(1024)(128)(4,1)}), s8[2359296]{0:T(1024)(128)(4,1)S(1)}, s32[]{:S(2)}) async-start(s8[6553600]{0:T(1024)(128)(4,1)} %bitcast.24), calls=%async_computation.3 | async-start | bytes 4718592
  1.3 18.0 %copy-start = (bf16[16,16,2560]{2,1,0:T(8,128)(2,1)S(1)}, bf16[16,16,2560]{2,1,0:T(8,128)(2,1)}, u32[]{:S(2)}) copy-start(bf16[16,16,2560]{2,1,0:T(8,128)(2,1)} %perturb_ref.11) | copy-start | bytes 3932164
  1.3 18.0 %copy-start.1 = (bf16[256,192]{1,0:T(8,128)(2,1)S(1)}, bf16[256,192]{1,0:T(8,128)(2,1)}, u32[]{:S(2)}) copy-start(bf16[256,192]{1,0:T(8,128)(2,1)} %constant.4.clone.refine_ref) | copy-start | bytes 294916
  3.0 16.2 %collective-permute-start.1 = (bf16[64,1280]{1,0:T(8,128)(2,1)S(1)}, bf16[64,1280]{1,0:T(8,128)(2,1)S(1)}, u32[]{:S(2)}, u32[]{:S(2)}) collective-permute-start(bf16[64,1280]{1,0:T(8,128)(2,1)S(1)} %get-tuple-element.26), channel_id=1, source_target_pairs={{1,0},{2,1},{3,2},{4,3},{5,4},{6,5},{7,6},{8,7},{9,8},{10,9},{11,1... | collective-permute-start | bytes 491528 | tf_op jit(solution)/shard_map/ppermute | solution.py:65
  5.1 14.1 %collective-permute-start = (bf16[64,1280]{1,0:T(8,128)(2,1)S(1)}, bf16[64,1280]{1,0:T(8,128)(2,1)S(1)}, u32[]{:S(2)}, u32[]{:S(2)}) collective-permute-start(bf16[64,1280]{1,0:T(8,128)(2,1)S(1)} %get-tuple-element.26), channel_id=1, source_target_pairs={{0,1},{1,2},{2,3},{3,4},{4,5},{5,6},{6,7},{7,8},{8,9},{9,10},{10,1... | collective-permute-start | bytes 491528 | tf_op jit(solution)/shard_map/ppermute | solution.py:63
  20.9 5.7 %collective-permute-start.2 = (f32[4,16,384]{2,1,0:T(8,128)S(1)}, f32[4,16,384]{2,1,0:T(8,128)S(1)}, u32[]{:S(2)}, u32[]{:S(2)}) collective-permute-start(f32[4,16,384]{2,1,0:T(8,128)S(1)} %get-tuple-element.30), channel_id=1, source_target_pairs={{0,16},{16,0},{32,48},{48,32},{64,80},{80,64},{96,112},{112,96},{1... | collective-permute-start | bytes 294920 | tf_op jit(solution)/shard_map/ppermute | solution.py:75
  26.6 3.6 %copy-start.3 = (s32[1,128,8,8]{1,3,2,0:T(8,128)S(1)}, s32[1,128,8,8]{1,3,2,0:T(8,128)}, u32[]{:S(2)}) copy-start(s32[1,128,8,8]{1,3,2,0:T(8,128)} %param.17) | copy-start | bytes 98308
  26.6 3.6 %copy-start.4 = (f32[1,128,8,8]{1,3,2,0:T(8,128)S(1)}, f32[1,128,8,8]{1,3,2,0:T(8,128)}, u32[]{:S(2)}) copy-start(f32[1,128,8,8]{1,3,2,0:T(8,128)} %param.18) | copy-start | bytes 98308
  26.6 3.6 %copy-start.5 = (f32[1,128,8,8]{1,3,2,0:T(8,128)S(1)}, f32[1,128,8,8]{1,3,2,0:T(8,128)}, u32[]{:S(2)}) copy-start(f32[1,128,8,8]{1,3,2,0:T(8,128)} %param.19) | copy-start | bytes 98308
  26.6 8.4 %copy-start.7 = (s32[1,128,8]{1,2,0:T(8,128)S(1)}, s32[1,128,8]{1,2,0:T(8,128)}, u32[]{:S(2)}) copy-start(s32[1,128,8]{1,2,0:T(8,128)} %param.20) | copy-start | bytes 12292
  26.6 6.9 %collective-permute-start.5 = (f32[4,16,384]{2,1,0:T(8,128)S(1)}, f32[4,16,384]{2,1,0:T(8,128)S(1)}, u32[]{:S(2)}, u32[]{:S(2)}) collective-permute-start(f32[4,16,384]{2,1,0:T(8,128)S(1)} %shard_map.143.a_ref), channel_id=1, source_target_pairs={{0,96},{16,112},{32,64},{48,80},{64,32},{80,48},{96,0},{112,16},{1... | collective-permute-start | bytes 294920 | tf_op jit(solution)/shard_map/ppermute | solution.py:71
  29.4 5.5 %collective-permute-start.4 = (f32[4,16,384]{2,1,0:T(8,128)S(1)}, f32[4,16,384]{2,1,0:T(8,128)S(1)}, u32[]{:S(2)}, u32[]{:S(2)}) collective-permute-start(f32[4,16,384]{2,1,0:T(8,128)S(1)} %shard_map.143.a_ref), channel_id=1, source_target_pairs={{0,64},{16,80},{32,96},{48,112},{64,0},{80,16},{96,32},{112,48},{1... | collective-permute-start | bytes 294920 | tf_op jit(solution)/shard_map/ppermute | solution.py:71
  29.8 5.2 %collective-permute-start.3 = (f32[4,16,384]{2,1,0:T(8,128)S(1)}, f32[4,16,384]{2,1,0:T(8,128)S(1)}, u32[]{:S(2)}, u32[]{:S(2)}) collective-permute-start(f32[4,16,384]{2,1,0:T(8,128)S(1)} %shard_map.143.a_ref), channel_id=1, source_target_pairs={{0,32},{16,48},{32,0},{48,16},{64,96},{80,112},{96,64},{112,80},{1... | collective-permute-start | bytes 294920 | tf_op jit(solution)/shard_map/ppermute | solution.py:71
  30.8 8.5 %copy-start.2 = (bf16[96,512]{1,0:T(8,128)(2,1)S(1)}, bf16[96,512]{1,0:T(8,128)(2,1)}, u32[]{:S(2)}) copy-start(bf16[96,512]{1,0:T(8,128)(2,1)} %constant.5.clone.back_ref) | copy-start | bytes 294916
  37.3 3.8 %collective-permute-start.6 = (f32[4,16,320]{2,1,0:T(8,128)S(1)}, f32[4,16,320]{2,1,0:T(8,128)S(1)}, u32[]{:S(2)}, u32[]{:S(2)}) collective-permute-start(f32[4,16,320]{2,1,0:T(8,128)S(1)} %get-tuple-element.33.mine_ref), channel_id=1, source_target_pairs={{0,16},{16,0},{32,48},{48,32},{64,80},{80,64},{96,112},{112,96},{1... | collective-permute-start | bytes 245768 | tf_op jit(solution)/shard_map/ppermute | solution.py:75
  42.8 5.2 %collective-permute-start.7 = (bf16[64,1280]{1,0:T(8,128)(2,1)S(1)}, bf16[64,1280]{1,0:T(8,128)(2,1)S(1)}, u32[]{:S(2)}, u32[]{:S(2)}) collective-permute-start(bf16[64,1280]{1,0:T(8,128)(2,1)S(1)} %get-tuple-element.34), channel_id=1, source_target_pairs={{0,1},{1,2},{2,3},{3,4},{4,5},{5,6},{6,7},{7,8},{8,9},{9,10},{10,1... | collective-permute-start | bytes 491528 | tf_op jit(solution)/shard_map/ppermute | solution.py:63
  42.9 5.1 %collective-permute-start.8 = (bf16[64,1280]{1,0:T(8,128)(2,1)S(1)}, bf16[64,1280]{1,0:T(8,128)(2,1)S(1)}, u32[]{:S(2)}, u32[]{:S(2)}) collective-permute-start(bf16[64,1280]{1,0:T(8,128)(2,1)S(1)} %get-tuple-element.36), channel_id=1, source_target_pairs={{1,0},{2,1},{3,2},{4,3},{5,4},{6,5},{7,6},{8,7},{9,8},{10,9},{11,1... | collective-permute-start | bytes 491528 | tf_op jit(solution)/shard_map/ppermute | solution.py:65
  48.5 3.9 %collective-permute-start.10 = (bf16[64,1280]{1,0:T(8,128)(2,1)S(1)}, bf16[64,1280]{1,0:T(8,128)(2,1)S(1)}, u32[]{:S(2)}, u32[]{:S(2)}) collective-permute-start(bf16[64,1280]{1,0:T(8,128)(2,1)S(1)} %get-tuple-element.37), channel_id=1, source_target_pairs={{1,0},{2,1},{3,2},{4,3},{5,4},{6,5},{7,6},{8,7},{9,8},{10,9},{11,1... | collective-permute-start | bytes 491528 | tf_op jit(solution)/shard_map/ppermute | solution.py:65
  50.1 5.8 %collective-permute-start.9 = (bf16[64,1280]{1,0:T(8,128)(2,1)S(1)}, bf16[64,1280]{1,0:T(8,128)(2,1)S(1)}, u32[]{:S(2)}, u32[]{:S(2)}) collective-permute-start(bf16[64,1280]{1,0:T(8,128)(2,1)S(1)} %get-tuple-element.37), channel_id=1, source_target_pairs={{0,1},{1,2},{2,3},{3,4},{4,5},{5,6},{6,7},{7,8},{8,9},{9,10},{10,1... | collective-permute-start | bytes 491528 | tf_op jit(solution)/shard_map/ppermute | solution.py:63
  57.5 2.1 %collective-permute-start.11 = (f32[4,16,320]{2,1,0:T(8,128)S(1)}, f32[4,16,320]{2,1,0:T(8,128)S(1)}, u32[]{:S(2)}, u32[]{:S(2)}) collective-permute-start(f32[4,16,320]{2,1,0:T(8,128)S(1)} %get-tuple-element.40), channel_id=1, source_target_pairs={{0,16},{16,0},{32,48},{48,32},{64,80},{80,64},{96,112},{112,96},{1... | collective-permute-start | bytes 245768 | tf_op jit(solution)/shard_map/ppermute | solution.py:75
  59.6 3.9 %collective-permute-start.12 = (f32[16,320]{1,0:T(8,128)S(1)}, f32[16,320]{1,0:T(8,128)S(1)}, u32[]{:S(2)}, u32[]{:S(2)}) collective-permute-start(f32[16,320]{1,0:T(8,128)S(1)} %get-tuple-element.42), channel_id=1, source_target_pairs={{0,32},{16,48},{32,0},{48,16},{64,96},{80,112},{96,64},{112,80},{1... | collective-permute-start | bytes 61448 | tf_op jit(solution)/shard_map/ppermute | solution.py:71
  59.9 4.4 %collective-permute-start.13 = (f32[16,320]{1,0:T(8,128)S(1)}, f32[16,320]{1,0:T(8,128)S(1)}, u32[]{:S(2)}, u32[]{:S(2)}) collective-permute-start(f32[16,320]{1,0:T(8,128)S(1)} %get-tuple-element.43), channel_id=1, source_target_pairs={{0,64},{16,80},{32,96},{48,112},{64,0},{80,16},{96,32},{112,48},{1... | collective-permute-start | bytes 61448 | tf_op jit(solution)/shard_map/ppermute | solution.py:71
  62.5 3.9 %collective-permute-start.14 = (f32[16,320]{1,0:T(8,128)S(1)}, f32[16,320]{1,0:T(8,128)S(1)}, u32[]{:S(2)}, u32[]{:S(2)}) collective-permute-start(f32[16,320]{1,0:T(8,128)S(1)} %get-tuple-element.44), channel_id=1, source_target_pairs={{0,96},{16,112},{32,64},{48,80},{64,32},{80,48},{96,0},{112,16},{1... | collective-permute-start | bytes 61448 | tf_op jit(solution)/shard_map/ppermute | solution.py:71
  (1 other events, 1.3 us)

commit v13 on v12

--- a/solution.py
+++ b/solution.py
@@ -21,7 +21,8 @@
 CHUNK = NCORE * WIDTH
 SLOTS = 8
 BATCHES = 128
-ROOM = 16 << 20
+ROOM = 24 << 20
+TOGETHER, PULLED = 4, 4
 WORK = 2 * 10**10
 EVEN, ODD = pl.ds(0, NTILE, stride=2), pl.ds(1, NTILE, stride=2)
 FLOAT, HALF = jnp.float32, jnp.bfloat16
@@ -164,8 +165,8 @@
 
 def regions_of(smooth_ref, refine_ref, perturb_ref, map_ref, parity, out_ref):
     smooth = smooth_ref[...]
-    for pair in range(0, NY, 2):
-        windows = [window(parity, y) for y in (pair, pair + 1)]
+    for pair in range(0, NY, TOGETHER):
+        windows = [window(parity, y) for y in range(pair, pair + TOGETHER)]
         columns = jnp.concatenate([map_ref[:, cols] for cols in windows], axis=1)
         mapped = jnp.dot(smooth, columns, preferred_element_type=FLOAT)
         high = mapped.astype(HALF)
@@ -228,11 +229,11 @@
 
 def pulled_part(values_ref, back_ref, perturb_ref, map_ref, parity):
     total = None
-    for pair in range(0, NY, 2):
-        windows = [window(parity, y) for y in (pair, pair + 1)]
+    for pair in range(0, NY, PULLED):
+        windows = [window(parity, y) for y in range(pair, pair + PULLED)]
         columns = jnp.concatenate([map_ref[:, cols] for cols in windows], axis=1)
         pulled = []
-        for y, cols in zip((pair, pair + 1), windows):
+        for y, cols in zip(range(pair, pair + PULLED), windows):
             values = values_ref[y]
             rest = jnp.zeros((FINE_ROWS, 384 - WIDTH), FLOAT)
             spread = jnp.where(

time: 88.8 us -> 88.3 us (level)
  transfers between devices with their start and end apart: 15 -> 15, of which waited for: 7 -> 7; matrix products, arithmetic and copies ran while one was open for 0% -> 0% of each run, Pallas kernels for 6% -> 5%
where the time goes in v13:
time: 88.3 us; the launch traced here: 88.2 us
  blocking collectives  35.1 us (40%)
  starting transfers between devices  20.4 us (23%)
  waiting for transfers between devices  16.1 us (18%)
  Pallas kernels  15 us (17%)
  between operations  1.5 us (2%)
    all_to_all x1, blocking collectives, shards(): lax.all_to_all(sent, ('member', 'tile'), split_axis=0, concat_axis=0, til...  21 us
    pallas_call x14, Pallas kernels, call(): pl.pallas_call(kernel, out_shape=tuple((jax.ShapeDtypeStruct(shape, kind)...  15 us
    all_to_all x1, blocking collectives, shards(): data = lax.all_to_all(sent, 'tile', split_axis=0, concat_axis=0, tiled=True)  14.1 us
    ppermute x3, starting transfers between devices, swap_core(): return lax.ppermute(values, 'member', [(i, i ^ 1) for i in range(NMEMBER)])  7.57 us
    ppermute x6, starting transfers between devices, across(): return lax.ppermute(values, 'member', pairs)  7.42 us
    ppermute x3, waiting for transfers between devices, swap_both(): first = lax.ppermute(first_values, ('member', 'tile'), ring())  7.27 us
    ppermute x6, waiting for transfers between devices, across(): return lax.ppermute(values, 'member', pairs)  6.74 us
    ppermute x3, starting transfers between devices, swap_both(): second = lax.ppermute(second_values, ('member', 'tile'), back)  5.15 us
  transfers between devices with their start and end apart: 15, of which 7 were waited for; matrix products, arithmetic and copies ran while one was open for 0% of the time, Pallas kernels for 5%

profile of v13, /device:TPU:1, one launch (start us, length us, event | category | flops | bytes accessed | tf_op | source)
XLA Modules:
  0.0 88.2 jit_solution(6353765756628061197)
XLA Ops:
  1.3 1.7 %shard_map.140 = (f32[32,128]{1,0:T(8,128)S(1)}, f32[64,1280]{1,0:T(8,128)S(1)}, bf16[64,1280]{1,0:T(8,128)(2,1)S(1)}) custom-call(f32[8,128]{1,0:T(8,128)} %bitcast.35, f32[8,128]{1,0:T(8,128)} %bitcast.36, f32[1]{0:T(128)S(6)} %copy.16.gain_ref, f32[16,4,1280]{2,1,0:T(4,128)} %weights_hbm.1), custom_call_target="tpu_custom_call" | custom-call | flops 20000000000 | bytes 156250000 | tf_op jit(solution)/shard_map/pallas_call | solution.py:100
  3.0 2.1 %collective-permute-start.1 = (bf16[64,1280]{1,0:T(8,128)(2,1)S(1)}, bf16[64,1280]{1,0:T(8,128)(2,1)S(1)}, u32[]{:S(2)}, u32[]{:S(2)}) collective-permute-start(bf16[64,1280]{1,0:T(8,128)(2,1)S(1)} %get-tuple-element.26), channel_id=1, source_target_pairs={{1,0},{2,1},{3,2},{4,3},{5,4},{6,5},{7,6},{8,7},{9,8},{10,9},{11,1... | collective-permute-start | bytes 491528 | tf_op jit(solution)/shard_map/ppermute | solution.py:66
  5.1 14.1 %all_to_all.22 = f32[16,2,128]{2,1,0:T(2,128)S(1)} all-to-all(f32[16,2,128]{2,1,0:T(2,128)S(1)} %bitcast.30), channel_id=1, replica_groups=mesh['member'=8,'tile'=16] {'tile'}, dimensions={0} | all-to-all | bytes 32768 | tf_op jit(solution)/shard_map/all_to_all | solution.py:517
  19.3 1.4 %shard_map.141 = (f32[4,16,384]{2,1,0:T(8,128)S(1)}, bf16[96,1280]{1,0:T(8,128)(2,1)S(1)}) custom-call(bf16[64,1280]{1,0:T(8,128)(2,1)S(1)} %collective-permute-done.a_ref, f32[64,1280]{1,0:T(8,128)S(1)} %get-tuple-element.27.own_ref, bf16[64,1280]{1,0:T(8,128)(2,1)S(1)} %collective-permute-done.1.b_ref, bf16[256,192]{1,0:T(8,128)(2,1)S(1)} %copy-done.1, ...), custom_call_target="tpu_custom_call" | custom-call | flops 1000000000 | bytes 7812500 | tf_op jit(solution)/shard_map/pallas_call | solution.py:100
  20.7 4.4 %collective-permute-start.2 = (f32[4,16,384]{2,1,0:T(8,128)S(1)}, f32[4,16,384]{2,1,0:T(8,128)S(1)}, u32[]{:S(2)}, u32[]{:S(2)}) collective-permute-start(f32[4,16,384]{2,1,0:T(8,128)S(1)} %get-tuple-element.30), channel_id=1, source_target_pairs={{0,16},{16,0},{32,48},{48,32},{64,80},{80,64},{96,112},{112,96},{1... | collective-permute-start | bytes 294920 | tf_op jit(solution)/shard_map/ppermute | solution.py:76
  25.1 1.1 %shard_map.142.a_ref = f32[4,16,384]{2,1,0:T(8,128)S(1)} custom-call(bf16[96,1280]{1,0:T(8,128)(2,1)S(1)} %get-tuple-element.29.smooth_ref, bf16[256,192]{1,0:T(8,128)(2,1)S(1)} %copy-done.1, bf16[16,16,2560]{2,1,0:T(8,128)(2,1)S(1)} %copy-done, bf16[1280,2560]{1,0:T(8,128)(2,1)S(1)} %bitcast.25, f32[32,128]{1,0:T(8,128)S(1)} %bitcast.27), custom_call_target="tpu_custom_call" | custom-call | flops 1000000000 | bytes 7812500 | tf_op jit(solution)/shard_map/pallas_call | solution.py:100
  26.3 2.8 %collective-permute-start.5 = (f32[4,16,384]{2,1,0:T(8,128)S(1)}, f32[4,16,384]{2,1,0:T(8,128)S(1)}, u32[]{:S(2)}, u32[]{:S(2)}) collective-permute-start(f32[4,16,384]{2,1,0:T(8,128)S(1)} %shard_map.143.a_ref), channel_id=1, source_target_pairs={{0,96},{16,112},{32,64},{48,80},{64,32},{80,48},{96,0},{112,16},{1... | collective-permute-start | bytes 294920 | tf_op jit(solution)/shard_map/ppermute | solution.py:72
  30.5 2.7 %collective-permute-done.5.d_ref = f32[4,16,384]{2,1,0:T(8,128)S(1)} collective-permute-done((f32[4,16,384]{2,1,0:T(8,128)S(1)}, f32[4,16,384]{2,1,0:T(8,128)S(1)}, u32[]{:S(2)}, u32[]{:S(2)}) %collective-permute-start.5) | collective-permute-done | bytes 98336 | tf_op jit(solution)/shard_map/ppermute | solution.py:72
  33.2 1.3 %collective-permute-done.4.c_ref = f32[4,16,384]{2,1,0:T(8,128)S(1)} collective-permute-done((f32[4,16,384]{2,1,0:T(8,128)S(1)}, f32[4,16,384]{2,1,0:T(8,128)S(1)}, u32[]{:S(2)}, u32[]{:S(2)}) %collective-permute-start.4) | collective-permute-done | bytes 98336 | tf_op jit(solution)/shard_map/ppermute | solution.py:72
  34.6 2.3 %shard_map.145 = (f32[4,16,320]{2,1,0:T(8,128)S(1)}, f32[8,128]{1,0:T(8,128)S(1)}, f32[16,320]{1,0:T(8,128)S(1)}) custom-call(f32[4,16,384]{2,1,0:T(8,128)S(1)} %shard_map.143.a_ref, f32[4,16,384]{2,1,0:T(8,128)S(1)} %collective-permute-done.3.b_ref, f32[4,16,384]{2,1,0:T(8,128)S(1)} %collective-permute-done.4.c_ref, ...), custom_call_target="tpu_custom_call" | custom-call | flops 1000000000 | bytes 7812500 | tf_op jit(solution)/shard_map/pallas_call | solution.py:100
  36.9 2.3 %collective-permute-start.6 = (f32[4,16,320]{2,1,0:T(8,128)S(1)}, f32[4,16,320]{2,1,0:T(8,128)S(1)}, u32[]{:S(2)}, u32[]{:S(2)}) collective-permute-start(f32[4,16,320]{2,1,0:T(8,128)S(1)} %get-tuple-element.33.mine_ref), channel_id=1, source_target_pairs={{0,16},{16,0},{32,48},{48,32},{64,80},{80,64},{96,112},{112,96},{1... | collective-permute-start | bytes 245768 | tf_op jit(solution)/shard_map/ppermute | solution.py:76
  39.1 1.7 %shard_map.146.mine_ref = f32[96,1280]{1,0:T(8,128)S(1)} custom-call(f32[4,16,320]{2,1,0:T(8,128)S(1)} %get-tuple-element.33.mine_ref, bf16[96,512]{1,0:T(8,128)(2,1)S(1)} %copy-done.2, bf16[16,16,2560]{2,1,0:T(8,128)(2,1)S(1)} %copy-done, bf16[1280,2560]{1,0:T(8,128)(2,1)S(1)} %bitcast.25), custom_call_target="tpu_custom_call" | custom-call | flops 1000000000 | bytes 7812500 | tf_op jit(solution)/shard_map/pallas_call | solution.py:100
  40.9 1.7 %shard_map.147 = (f32[96,1280]{1,0:T(8,128)S(1)}, bf16[64,1280]{1,0:T(8,128)(2,1)S(1)}, bf16[64,1280]{1,0:T(8,128)(2,1)S(1)}) custom-call(f32[96,1280]{1,0:T(8,128)S(1)} %shard_map.146.mine_ref, f32[4,16,320]{2,1,0:T(8,128)S(1)} %collective-permute-done.6.other_ref, bf16[96,512]{1,0:T(8,128)(2,1)S(1)} %copy-done.2, bf16[16,16,2560]{2,1,0:T(8,128)(2,1)S(1)} %copy-done, ...), custom_call_target="tpu_custom_call" | custom-call | flops 1000000000 | bytes 7812500 | tf_op jit(solution)/shard_map/pallas_call | solution.py:100
  42.7 1.4 %collective-permute-start.8 = (bf16[64,1280]{1,0:T(8,128)(2,1)S(1)}, bf16[64,1280]{1,0:T(8,128)(2,1)S(1)}, u32[]{:S(2)}, u32[]{:S(2)}) collective-permute-start(bf16[64,1280]{1,0:T(8,128)(2,1)S(1)} %get-tuple-element.36), channel_id=1, source_target_pairs={{1,0},{2,1},{3,2},{4,3},{5,4},{6,5},{7,6},{8,7},{9,8},{10,9},{11,1... | collective-permute-start | bytes 491528 | tf_op jit(solution)/shard_map/ppermute | solution.py:66
  44.2 3.7 %collective-permute-done.7.a_ref = bf16[64,1280]{1,0:T(8,128)(2,1)S(1)} collective-permute-done((bf16[64,1280]{1,0:T(8,128)(2,1)S(1)}, bf16[64,1280]{1,0:T(8,128)(2,1)S(1)}, u32[]{:S(2)}, u32[]{:S(2)}) %collective-permute-start.7) | collective-permute-done | bytes 163872 | tf_op jit(solution)/shard_map/ppermute | solution.py:64
  48.3 1.6 %collective-permute-start.10 = (bf16[64,1280]{1,0:T(8,128)(2,1)S(1)}, bf16[64,1280]{1,0:T(8,128)(2,1)S(1)}, u32[]{:S(2)}, u32[]{:S(2)}) collective-permute-start(bf16[64,1280]{1,0:T(8,128)(2,1)S(1)} %get-tuple-element.37), channel_id=1, source_target_pairs={{1,0},{2,1},{3,2},{4,3},{5,4},{6,5},{7,6},{8,7},{9,8},{10,9},{11,1... | collective-permute-start | bytes 491528 | tf_op jit(solution)/shard_map/ppermute | solution.py:66
  50.0 2.1 %collective-permute-done.10.b_ref = bf16[64,1280]{1,0:T(8,128)(2,1)S(1)} collective-permute-done((bf16[64,1280]{1,0:T(8,128)(2,1)S(1)}, bf16[64,1280]{1,0:T(8,128)(2,1)S(1)}, u32[]{:S(2)}, u32[]{:S(2)}) %collective-permute-start.10) | collective-permute-done | bytes 163872 | tf_op jit(solution)/shard_map/ppermute | solution.py:66
  52.1 3.6 %collective-permute-done.9.a_ref = bf16[64,1280]{1,0:T(8,128)(2,1)S(1)} collective-permute-done((bf16[64,1280]{1,0:T(8,128)(2,1)S(1)}, bf16[64,1280]{1,0:T(8,128)(2,1)S(1)}, u32[]{:S(2)}, u32[]{:S(2)}) %collective-permute-start.9) | collective-permute-done | bytes 163872 | tf_op jit(solution)/shard_map/ppermute | solution.py:64
  55.7 1.4 %shard_map.149 = (f32[4,16,320]{2,1,0:T(8,128)S(1)}, bf16[96,1280]{1,0:T(8,128)(2,1)S(1)}) custom-call(bf16[64,1280]{1,0:T(8,128)(2,1)S(1)} %collective-permute-done.9.a_ref, f32[64,1280]{1,0:T(8,128)S(1)} %get-tuple-element.38.own_ref.grad_ref, bf16[64,1280]{1,0:T(8,128)(2,1)S(1)} %collective-permute-done.10.b_ref, bf16[256,192]{1,0:T(8,128)(2,1)S(1)} %copy-done.1, ...), custom_call_target="tpu_custom_call" | custom-call | flops 1000000000 | bytes 7812500 | tf_op jit(solution)/shard_map/pallas_call | solution.py:100
  58.0 1.1 %shard_map.150.a_ref = f32[4,16,320]{2,1,0:T(8,128)S(1)} custom-call(bf16[96,1280]{1,0:T(8,128)(2,1)S(1)} %get-tuple-element.39.smooth_ref, bf16[256,192]{1,0:T(8,128)(2,1)S(1)} %copy-done.1, bf16[16,16,2560]{2,1,0:T(8,128)(2,1)S(1)} %copy-done, bf16[1280,2560]{1,0:T(8,128)(2,1)S(1)} %bitcast.25), custom_call_target="tpu_custom_call" | custom-call | flops 1000000000 | bytes 7812500 | tf_op jit(solution)/shard_map/pallas_call | solution.py:100
  59.3 2.6 %collective-permute-start.13 = (f32[16,320]{1,0:T(8,128)S(1)}, f32[16,320]{1,0:T(8,128)S(1)}, u32[]{:S(2)}, u32[]{:S(2)}) collective-permute-start(f32[16,320]{1,0:T(8,128)S(1)} %get-tuple-element.43), channel_id=1, source_target_pairs={{0,64},{16,80},{32,96},{48,112},{64,0},{80,16},{96,32},{112,48},{1... | collective-permute-start | bytes 61448 | tf_op jit(solution)/shard_map/ppermute | solution.py:72
  61.9 1.2 %collective-permute-start.14 = (f32[16,320]{1,0:T(8,128)S(1)}, f32[16,320]{1,0:T(8,128)S(1)}, u32[]{:S(2)}, u32[]{:S(2)}) collective-permute-start(f32[16,320]{1,0:T(8,128)S(1)} %get-tuple-element.44), channel_id=1, source_target_pairs={{0,96},{16,112},{32,64},{48,80},{64,32},{80,48},{96,0},{112,16},{1... | collective-permute-start | bytes 61448 | tf_op jit(solution)/shard_map/ppermute | solution.py:72
  63.5 2.3 %collective-permute-done.14.d_ref = f32[16,320]{1,0:T(8,128)S(1)} collective-permute-done((f32[16,320]{1,0:T(8,128)S(1)}, f32[16,320]{1,0:T(8,128)S(1)}, u32[]{:S(2)}, u32[]{:S(2)}) %collective-permute-start.14) | collective-permute-done | bytes 20512 | tf_op jit(solution)/shard_map/ppermute | solution.py:72
  66.2 21.0 %all_to_all.23 = f32[128,1,128]{2,1,0:T(1,128)S(1)} all-to-all(f32[128,1,128]{2,1,0:T(1,128)S(1)} %bitcast.28), channel_id=1, replica_groups=mesh['member'=8,'tile'=16] {'member','tile'}, dimensions={0} | all-to-all | bytes 131072 | tf_op jit(solution)/shard_map/all_to_all | solution.py:559
  (43 shorter events, 5.0 us)
Async XLA Ops:
  1.3 18.0 %slice-start = ((s8[6553600]{0:T(1024)(128)(4,1)}), s8[4194304]{0:T(1024)(128)(4,1)S(1)}, s32[]{:S(2)}) async-start(s8[6553600]{0:T(1024)(128)(4,1)} %bitcast.24), calls=%async_computation.2 | async-start | bytes 8388608
  1.3 18.0 %slice-start.1 = ((s8[6553600]{0:T(1024)(128)(4,1)}), s8[2359296]{0:T(1024)(128)(4,1)S(1)}, s32[]{:S(2)}) async-start(s8[6553600]{0:T(1024)(128)(4,1)} %bitcast.24), calls=%async_computation.3 | async-start | bytes 4718592
  1.3 18.0 %copy-start = (bf16[16,16,2560]{2,1,0:T(8,128)(2,1)S(1)}, bf16[16,16,2560]{2,1,0:T(8,128)(2,1)}, u32[]{:S(2)}) copy-start(bf16[16,16,2560]{2,1,0:T(8,128)(2,1)} %perturb_ref.11) | copy-start | bytes 3932164
  1.3 18.0 %copy-start.1 = (bf16[256,192]{1,0:T(8,128)(2,1)S(1)}, bf16[256,192]{1,0:T(8,128)(2,1)}, u32[]{:S(2)}) copy-start(bf16[256,192]{1,0:T(8,128)(2,1)} %constant.4.clone.refine_ref) | copy-start | bytes 294916
  3.0 16.2 %collective-permute-start.1 = (bf16[64,1280]{1,0:T(8,128)(2,1)S(1)}, bf16[64,1280]{1,0:T(8,128)(2,1)S(1)}, u32[]{:S(2)}, u32[]{:S(2)}) collective-permute-start(bf16[64,1280]{1,0:T(8,128)(2,1)S(1)} %get-tuple-element.26), channel_id=1, source_target_pairs={{1,0},{2,1},{3,2},{4,3},{5,4},{6,5},{7,6},{8,7},{9,8},{10,9},{11,1... | collective-permute-start | bytes 491528 | tf_op jit(solution)/shard_map/ppermute | solution.py:66
  5.1 14.1 %collective-permute-start = (bf16[64,1280]{1,0:T(8,128)(2,1)S(1)}, bf16[64,1280]{1,0:T(8,128)(2,1)S(1)}, u32[]{:S(2)}, u32[]{:S(2)}) collective-permute-start(bf16[64,1280]{1,0:T(8,128)(2,1)S(1)} %get-tuple-element.26), channel_id=1, source_target_pairs={{0,1},{1,2},{2,3},{3,4},{4,5},{5,6},{6,7},{7,8},{8,9},{9,10},{10,1... | collective-permute-start | bytes 491528 | tf_op jit(solution)/shard_map/ppermute | solution.py:64
  20.7 5.6 %collective-permute-start.2 = (f32[4,16,384]{2,1,0:T(8,128)S(1)}, f32[4,16,384]{2,1,0:T(8,128)S(1)}, u32[]{:S(2)}, u32[]{:S(2)}) collective-permute-start(f32[4,16,384]{2,1,0:T(8,128)S(1)} %get-tuple-element.30), channel_id=1, source_target_pairs={{0,16},{16,0},{32,48},{48,32},{64,80},{80,64},{96,112},{112,96},{1... | collective-permute-start | bytes 294920 | tf_op jit(solution)/shard_map/ppermute | solution.py:76
  26.2 3.6 %copy-start.3 = (s32[1,128,8,8]{1,3,2,0:T(8,128)S(1)}, s32[1,128,8,8]{1,3,2,0:T(8,128)}, u32[]{:S(2)}) copy-start(s32[1,128,8,8]{1,3,2,0:T(8,128)} %param.17) | copy-start | bytes 98308
  26.2 3.6 %copy-start.4 = (f32[1,128,8,8]{1,3,2,0:T(8,128)S(1)}, f32[1,128,8,8]{1,3,2,0:T(8,128)}, u32[]{:S(2)}) copy-start(f32[1,128,8,8]{1,3,2,0:T(8,128)} %param.18) | copy-start | bytes 98308
  26.2 3.6 %copy-start.5 = (f32[1,128,8,8]{1,3,2,0:T(8,128)S(1)}, f32[1,128,8,8]{1,3,2,0:T(8,128)}, u32[]{:S(2)}) copy-start(f32[1,128,8,8]{1,3,2,0:T(8,128)} %param.19) | copy-start | bytes 98308
  26.3 8.3 %copy-start.7 = (s32[1,128,8]{1,2,0:T(8,128)S(1)}, s32[1,128,8]{1,2,0:T(8,128)}, u32[]{:S(2)}) copy-start(s32[1,128,8]{1,2,0:T(8,128)} %param.20) | copy-start | bytes 12292
  26.3 6.9 %collective-permute-start.5 = (f32[4,16,384]{2,1,0:T(8,128)S(1)}, f32[4,16,384]{2,1,0:T(8,128)S(1)}, u32[]{:S(2)}, u32[]{:S(2)}) collective-permute-start(f32[4,16,384]{2,1,0:T(8,128)S(1)} %shard_map.143.a_ref), channel_id=1, source_target_pairs={{0,96},{16,112},{32,64},{48,80},{64,32},{80,48},{96,0},{112,16},{1... | collective-permute-start | bytes 294920 | tf_op jit(solution)/shard_map/ppermute | solution.py:72
  29.1 5.4 %collective-permute-start.4 = (f32[4,16,384]{2,1,0:T(8,128)S(1)}, f32[4,16,384]{2,1,0:T(8,128)S(1)}, u32[]{:S(2)}, u32[]{:S(2)}) collective-permute-start(f32[4,16,384]{2,1,0:T(8,128)S(1)} %shard_map.143.a_ref), channel_id=1, source_target_pairs={{0,64},{16,80},{32,96},{48,112},{64,0},{80,16},{96,32},{112,48},{1... | collective-permute-start | bytes 294920 | tf_op jit(solution)/shard_map/ppermute | solution.py:72
  29.5 5.1 %collective-permute-start.3 = (f32[4,16,384]{2,1,0:T(8,128)S(1)}, f32[4,16,384]{2,1,0:T(8,128)S(1)}, u32[]{:S(2)}, u32[]{:S(2)}) collective-permute-start(f32[4,16,384]{2,1,0:T(8,128)S(1)} %shard_map.143.a_ref), channel_id=1, source_target_pairs={{0,32},{16,48},{32,0},{48,16},{64,96},{80,112},{96,64},{112,80},{1... | collective-permute-start | bytes 294920 | tf_op jit(solution)/shard_map/ppermute | solution.py:72
  30.5 8.6 %copy-start.2 = (bf16[96,512]{1,0:T(8,128)(2,1)S(1)}, bf16[96,512]{1,0:T(8,128)(2,1)}, u32[]{:S(2)}) copy-start(bf16[96,512]{1,0:T(8,128)(2,1)} %constant.5.clone.back_ref) | copy-start | bytes 294916
  36.9 4.0 %collective-permute-start.6 = (f32[4,16,320]{2,1,0:T(8,128)S(1)}, f32[4,16,320]{2,1,0:T(8,128)S(1)}, u32[]{:S(2)}, u32[]{:S(2)}) collective-permute-start(f32[4,16,320]{2,1,0:T(8,128)S(1)} %get-tuple-element.33.mine_ref), channel_id=1, source_target_pairs={{0,16},{16,0},{32,48},{48,32},{64,80},{80,64},{96,112},{112,96},{1... | collective-permute-start | bytes 245768 | tf_op jit(solution)/shard_map/ppermute | solution.py:76
  42.6 5.2 %collective-permute-start.7 = (bf16[64,1280]{1,0:T(8,128)(2,1)S(1)}, bf16[64,1280]{1,0:T(8,128)(2,1)S(1)}, u32[]{:S(2)}, u32[]{:S(2)}) collective-permute-start(bf16[64,1280]{1,0:T(8,128)(2,1)S(1)} %get-tuple-element.34), channel_id=1, source_target_pairs={{0,1},{1,2},{2,3},{3,4},{4,5},{5,6},{6,7},{7,8},{8,9},{9,10},{10,1... | collective-permute-start | bytes 491528 | tf_op jit(solution)/shard_map/ppermute | solution.py:64
  42.7 5.2 %collective-permute-start.8 = (bf16[64,1280]{1,0:T(8,128)(2,1)S(1)}, bf16[64,1280]{1,0:T(8,128)(2,1)S(1)}, u32[]{:S(2)}, u32[]{:S(2)}) collective-permute-start(bf16[64,1280]{1,0:T(8,128)(2,1)S(1)} %get-tuple-element.36), channel_id=1, source_target_pairs={{1,0},{2,1},{3,2},{4,3},{5,4},{6,5},{7,6},{8,7},{9,8},{10,9},{11,1... | collective-permute-start | bytes 491528 | tf_op jit(solution)/shard_map/ppermute | solution.py:66
  48.3 3.9 %collective-permute-start.10 = (bf16[64,1280]{1,0:T(8,128)(2,1)S(1)}, bf16[64,1280]{1,0:T(8,128)(2,1)S(1)}, u32[]{:S(2)}, u32[]{:S(2)}) collective-permute-start(bf16[64,1280]{1,0:T(8,128)(2,1)S(1)} %get-tuple-element.37), channel_id=1, source_target_pairs={{1,0},{2,1},{3,2},{4,3},{5,4},{6,5},{7,6},{8,7},{9,8},{10,9},{11,1... | collective-permute-start | bytes 491528 | tf_op jit(solution)/shard_map/ppermute | solution.py:66
  49.9 5.8 %collective-permute-start.9 = (bf16[64,1280]{1,0:T(8,128)(2,1)S(1)}, bf16[64,1280]{1,0:T(8,128)(2,1)S(1)}, u32[]{:S(2)}, u32[]{:S(2)}) collective-permute-start(bf16[64,1280]{1,0:T(8,128)(2,1)S(1)} %get-tuple-element.37), channel_id=1, source_target_pairs={{0,1},{1,2},{2,3},{3,4},{4,5},{5,6},{6,7},{7,8},{8,9},{9,10},{10,1... | collective-permute-start | bytes 491528 | tf_op jit(solution)/shard_map/ppermute | solution.py:64
  57.1 2.0 %collective-permute-start.11 = (f32[4,16,320]{2,1,0:T(8,128)S(1)}, f32[4,16,320]{2,1,0:T(8,128)S(1)}, u32[]{:S(2)}, u32[]{:S(2)}) collective-permute-start(f32[4,16,320]{2,1,0:T(8,128)S(1)} %get-tuple-element.40), channel_id=1, source_target_pairs={{0,16},{16,0},{32,48},{48,32},{64,80},{80,64},{96,112},{112,96},{1... | collective-permute-start | bytes 245768 | tf_op jit(solution)/shard_map/ppermute | solution.py:76
  59.1 3.9 %collective-permute-start.12 = (f32[16,320]{1,0:T(8,128)S(1)}, f32[16,320]{1,0:T(8,128)S(1)}, u32[]{:S(2)}, u32[]{:S(2)}) collective-permute-start(f32[16,320]{1,0:T(8,128)S(1)} %get-tuple-element.42), channel_id=1, source_target_pairs={{0,32},{16,48},{32,0},{48,16},{64,96},{80,112},{96,64},{112,80},{1... | collective-permute-start | bytes 61448 | tf_op jit(solution)/shard_map/ppermute | solution.py:72
  59.3 4.2 %collective-permute-start.13 = (f32[16,320]{1,0:T(8,128)S(1)}, f32[16,320]{1,0:T(8,128)S(1)}, u32[]{:S(2)}, u32[]{:S(2)}) collective-permute-start(f32[16,320]{1,0:T(8,128)S(1)} %get-tuple-element.43), channel_id=1, source_target_pairs={{0,64},{16,80},{32,96},{48,112},{64,0},{80,16},{96,32},{112,48},{1... | collective-permute-start | bytes 61448 | tf_op jit(solution)/shard_map/ppermute | solution.py:72
  61.9 3.9 %collective-permute-start.14 = (f32[16,320]{1,0:T(8,128)S(1)}, f32[16,320]{1,0:T(8,128)S(1)}, u32[]{:S(2)}, u32[]{:S(2)}) collective-permute-start(f32[16,320]{1,0:T(8,128)S(1)} %get-tuple-element.44), channel_id=1, source_target_pairs={{0,96},{16,112},{32,64},{48,80},{64,32},{80,48},{96,0},{112,16},{1... | collective-permute-start | bytes 61448 | tf_op jit(solution)/shard_map/ppermute | solution.py:72
  (1 other events, 1.1 us)
